TPU v7x, 32 devices: a whole 2x2x4 slice. The times are simulated.
32 devices in a mesh: shot: 8 (over y, x, core), rcv: 4 (over z).
Axes of the slice: x: 2, y: 2, z: 4, core: 2. Of those that a mesh axis runs over, the one named last changes fastest.
Arguments:
- traces: bfloat16 [256, 512, 256], P('shot', 'rcv'), may hold values from -6 to 6
- shift_index: int32 [256, 512], P('shot', 'rcv'), may hold values from 0 to 63
- deconv: float32 [256, 64], P('shot'), may hold values from -0.75 to 0.75
- focal_start: bfloat16 [8, 512, 256], P(None, 'rcv'), may hold values from -6 to 6
- onset_source: int32 [8, 256], P('rcv', 'shot'), may hold values from 32 to 128
- onset_receiver: int32 [8, 512], P('shot', 'rcv'), may hold values from 32 to 128
Outputs:
- upgoing_first: float32 [8, 256, 256], P('rcv', 'shot')
- downgoing: float32 [8, 512, 256], P('shot', 'rcv')
- upgoing_second: float32 [8, 256, 256], P('rcv', 'shot')
All inputs are finite; a program needn't handle non-finite values.
Results may differ from a plain program's by a relative error of at most 0.028.
Values may be sent and summed in bfloat16 or wider, within the bound.
No kernel may reach another device: no remote copies, remote signals or barrier semaphores. Data moves between devices by JAX's collectives and lax.ppermute only.
A program may use at most 64 MiB of HBM per device.

v0:
```python
import math

import jax
import jax.numpy as jnp
from jax import lax
from jax.sharding import PartitionSpec as P

NT = 256
NF = 128
TAPS = 64
KSHIFT = 64


exact_mode = lax.Precision.HIGHEST


def fourier_tables(length, bin_count):
    sample_ids = jnp.arange(length, dtype=jnp.int32)
    bin_ids = jnp.arange(bin_count, dtype=jnp.int32)
    phases = sample_ids[:, None] * bin_ids[None, :] % length
    angles = 2.0 * math.pi / length * phases.astype(jnp.float32)
    forward = jnp.concatenate([jnp.cos(angles), -jnp.sin(angles)], axis=1)
    weights = jnp.where(bin_ids == 0, 1.0, 2.0).astype(jnp.float32) / length
    inverse = jnp.concatenate(
        [jnp.cos(angles) * weights[None, :], -jnp.sin(angles) * weights[None, :]], axis=1
    ).T
    return (forward, inverse)


def delay_table(tap_count, kind_count):
    tap_index = jnp.arange(tap_count, dtype=jnp.float32)
    fraction = jnp.arange(kind_count, dtype=jnp.float32) * (tap_count / (4.0 * kind_count))
    offset = tap_index[None, :] - 0.375 * tap_count - fraction[:, None]
    window = 0.5 - 0.5 * jnp.cos(2.0 * math.pi * (tap_index + 0.5) / tap_count)
    return jnp.sinc(offset) * window[None, :]


def split_transform(signal, upper_part, lower_part, form):
    high_term = jnp.einsum(form, signal, upper_part, preferred_element_type=jnp.float32)
    low_term = jnp.einsum(form, signal, lower_part, preferred_element_type=jnp.float32)
    return high_term + low_term


def complex_product(left_op, right_op):
    real_part = left_op[0] * right_op[0] - left_op[1] * right_op[1]
    imag_part = left_op[0] * right_op[1] + left_op[1] * right_op[0]
    return jnp.stack([real_part, imag_part])


def apply_forward(matrix, focal_spec):

    def product_term(left_op, right_op):
        return jnp.einsum("fdau,fpd->fapu", left_op, right_op, preferred_element_type=jnp.float32)

    real_part = product_term(matrix[0], focal_spec[0]) - product_term(matrix[1], focal_spec[1])
    imag_part = product_term(matrix[0], focal_spec[1]) + product_term(matrix[1], focal_spec[0])
    return jnp.stack([real_part, imag_part])


def apply_adjoint(matrix, echo_spec):

    def product_term(left_op, right_op):
        return jnp.einsum("fdau,fapu->fpd", left_op, right_op, preferred_element_type=jnp.float32)

    real_part = product_term(matrix[0], echo_spec[0]) + product_term(matrix[1], echo_spec[1])
    imag_part = product_term(matrix[0], echo_spec[1]) - product_term(matrix[1], echo_spec[0])
    stacked = jnp.stack([real_part, imag_part])
    return stacked.reshape(
        stacked.shape[0], stacked.shape[1], stacked.shape[2], 1, stacked.shape[3]
    )


def to_time_field(spectra, onset, inverse):
    flat = spectra.reshape(-1, onset.shape[0], onset.shape[1])
    signal = jnp.einsum("cpu,ct->put", flat, inverse, precision=exact_mode)
    sample_ids = jnp.arange(inverse.shape[1], dtype=jnp.int32)
    folded = jnp.minimum(sample_ids, inverse.shape[1] - sample_ids)
    return jnp.where(folded[None, None, :] < onset[:, :, None], signal, 0.0)


def to_spectrum(signal, forward):
    flat = jnp.einsum("put,tc->cpu", signal, forward, precision=exact_mode)
    return flat.reshape(2, flat.shape[0] // 2, flat.shape[1], flat.shape[2])


def forward_sum(partial_value):
    return lax.psum_scatter(
        partial_value.astype(jnp.bfloat16), "rcv", scatter_dimension=3, tiled=True
    ).astype(jnp.float32)


def focal_rows(pieces):
    return lax.all_gather(pieces, "rcv", axis=3, tiled=True)


def time_layout(spectra):
    return lax.all_to_all(
        spectra.astype(jnp.bfloat16), "shot", split_axis=2, concat_axis=1, tiled=True
    ).astype(spectra.dtype)


def spectrum_layout(spectra):
    return lax.all_to_all(spectra, "shot", split_axis=1, concat_axis=2, tiled=True)


def body(traces, shift_index, deconv, focal_start, onset_source, onset_receiver):
    shot_count = lax.axis_size("shot")
    rcv_count = lax.axis_size("rcv")
    shot_index = lax.axis_index("shot")
    per_owner = NF // shot_count
    source_local = traces.shape[0]
    receiver_local = traces.shape[1]
    focal_total = focal_start.shape[0]
    focal_owned = focal_total // shot_count
    gain_factor = 1.0 / math.sqrt(NT * receiver_local * rcv_count)
    forward, inverse = fourier_tables(NT, NF)
    upper_part = forward.astype(jnp.bfloat16)
    lower_part = (forward - upper_part.astype(jnp.float32)).astype(jnp.bfloat16)
    tap_spec = jnp.dot(delay_table(TAPS, KSHIFT), forward[:TAPS], precision=exact_mode)
    wave_spec = jnp.dot(deconv, forward[:TAPS], precision=exact_mode)
    raw_spec = split_transform(traces, upper_part, lower_part, "srt,tc->crs").reshape(
        2, NF, receiver_local, source_local
    )
    kind_ids = jnp.arange(KSHIFT, dtype=jnp.int32)
    one_hot = (shift_index[:, :, None] == kind_ids[None, None, :]).astype(jnp.float32)
    delays = jnp.einsum("srm,mc->crs", one_hot, tap_spec, precision=exact_mode).reshape(
        2, NF, receiver_local, source_local
    )
    wavelet = wave_spec.T.reshape(2, NF, 1, source_local)
    reflection = (complex_product(complex_product(raw_spec, delays), wavelet) * gain_factor).astype(
        jnp.bfloat16
    )
    owned = lax.all_to_all(reflection, "shot", split_axis=1, concat_axis=3, tiled=True)
    matrix = owned.reshape(2, per_owner, receiver_local, shot_count, source_local)
    upper_band = lax.dynamic_slice_in_dim(
        upper_part.reshape(NT, 2, NF), shot_index * per_owner, per_owner, 2
    ).reshape(NT, 2 * per_owner)
    lower_band = lax.dynamic_slice_in_dim(
        lower_part.reshape(NT, 2, NF), shot_index * per_owner, per_owner, 2
    ).reshape(NT, 2 * per_owner)
    start_spec = split_transform(focal_start, upper_band, lower_band, "prt,tc->cpr").reshape(
        2, per_owner, focal_total, receiver_local
    )
    start_spec = start_spec.astype(jnp.bfloat16)
    summed = forward_sum(apply_forward(matrix, start_spec))
    summed = time_layout(summed)
    upgoing_first = to_time_field(summed, onset_source, inverse)
    echo_spec = to_spectrum(upgoing_first, forward).astype(jnp.bfloat16)
    echo_spec = echo_spec.reshape(2, NF, 1, echo_spec.shape[2], echo_spec.shape[3])
    echo_spec = spectrum_layout(echo_spec)
    echo_all = focal_rows(echo_spec)
    adjoint = apply_adjoint(matrix, echo_all)
    adjoint = time_layout(adjoint)
    focal_own = lax.dynamic_slice_in_dim(
        focal_start, shot_index * focal_owned, focal_owned, 0
    ).astype(jnp.float32)
    downgoing = focal_own + to_time_field(adjoint, onset_receiver, inverse)
    plus_spec = to_spectrum(downgoing, forward).astype(jnp.bfloat16)
    plus_spec = plus_spec.reshape(2, NF, focal_owned, 1, receiver_local)
    plus_spec = spectrum_layout(plus_spec)
    plus_spec = plus_spec.reshape(2, plus_spec.shape[1], focal_total, receiver_local)
    summed_again = forward_sum(apply_forward(matrix, plus_spec))
    summed_again = time_layout(summed_again)
    upgoing_second = to_time_field(summed_again, onset_source, inverse)
    return (upgoing_first, downgoing, upgoing_second)


def solution(mesh):
    placed = (
        P("shot", "rcv", None),
        P("shot", "rcv"),
        P("shot", None),
        P(None, "rcv", None),
        P("rcv", "shot"),
        P("shot", "rcv"),
    )
    return jax.shard_map(
        body,
        mesh=mesh,
        in_specs=placed,
        out_specs=(P("rcv", "shot", None), P("shot", "rcv", None), P("rcv", "shot", None)),
        check_vma=False,
    )
```

profile of v0, /device:TPU:0, one launch (start us, length us, event | category | flops | bytes accessed | tf_op | source)
XLA Modules:
  0.0 180.0 jit_solution(3745824398154742096)
XLA Ops:
  7.2 0.5 sine_negate_fusion
  7.8 1.0 copy-done
  8.8 0.7 fusion.38
  9.5 0.7 add_bitcast_fusion
  10.3 0.2 fusion.104
  10.6 0.3 convolution_bitcast_fusion.5
  10.9 1.8 %convolution_bitcast_fusion = f32[256,128,32]{1,0,2:T(8,128)S(1)} fusion(f32[64,256,1]{1,0,2:T(8,128)S(1)} %convolution_bitcast_fusion.5, s32[32,128]{1,0:T(8,128)S(1)} %copy-done.7), kind=kOutput, calls=%fused_computation.3 | convolution fusion | flops 805568512 | bytes 4276224 | tf_op jit(solution)/shard_map/srm,mc->crs/dot_general | solution.py:126
  12.8 1.5 subtract_bitcast_fusion
  14.3 1.3 add_bitcast_fusion.1
  15.6 0.6 fusion
  16.2 2.7 %copy.58 = bf16[2,128,128,32]{2,3,0,1:T(8,128)(2,1)} copy(bf16[2,128,128,32]{2,1,3,0:T(8,128)(2,1)S(1)} %fusion) | data formatting | bytes 4194304 | tf_op jit(solution)/shard_map/convert_element_type | solution.py:130
  18.8 5.3 %all-to-all-start = ((bf16[2,128,128,32]{2,3,0,1:T(8,128)(2,1)}), bf16[2,128,128,32]{2,3,0,1:T(8,128)(2,1)}, u32[]{:S(2)}, u32[]{:S(2)}) async-start(bf16[2,128,128,32]{2,3,0,1:T(8,128)(2,1)} %copy.58), calls=%async_computation | async-start | bytes 4194304 | tf_op jit(solution)/shard_map/all_to_all | solution.py:133
  24.1 0.2 reduce-scatter.3.cloned.1.call-start
  24.4 0.5 sine_negate_fusion.1
  25.0 0.2 fusion.126
  25.2 0.3 fusion.11
  25.5 25.4 %all-to-all-done = bf16[2,128,128,32]{2,3,0,1:T(8,128)(2,1)} async-done(((bf16[2,128,128,32]{2,3,0,1:T(8,128)(2,1)}), bf16[2,128,128,32]{2,3,0,1:T(8,128)(2,1)}, u32[]{:S(2)}, u32[]{:S(2)}) %all-to-all-start) | async-done | bytes 2097184 | tf_op jit(solution)/shard_map/all_to_all | solution.py:133
  50.9 2.2 %copy.136 = bf16[2,8,16,128,32]{3,4,1,2,0:T(8,128)(2,1)S(1)} copy(bf16[2,8,16,128,32]{3,4,0,2,1:T(8,128)(2,1)} %bitcast.12) | data formatting | bytes 4194304 | tf_op jit(solution)/shard_map/all_to_all | solution.py:133
  53.1 1.4 fusion.23
  54.6 1.5 fusion.22
  56.0 1.5 fusion.8
  57.5 1.5 fusion.7
  59.0 0.1 pad_maximum_fusion
  59.1 0.9 copy.65
  60.0 0.5 broadcast_multiply_fusion.1
  60.6 21.2 %reduce-scatter.3.cloned.1.call-done = bf16[2,16,8,2,32]{4,2,1,0,3:T(8,128)(2,1)} async-done(((bf16[2,16,8,8,32]{4,2,1,0,3:T(8,128)(2,1)}), bf16[2,16,8,2,32]{4,2,1,0,3:T(8,128)(2,1)}) %reduce-scatter.3.cloned.1.call-update) | async-done | bytes 32784 | tf_op jit(solution)/shard_map/reduce_scatter | solution.py:87
  81.8 1.0 copy.139
  82.8 0.8 reshape.232
  83.6 3.6 %all-to-all-start.1 = ((bf16[8,2,1024]{2,1,0:T(2,128)(2,1)}), bf16[8,2,1024]{2,1,0:T(2,128)(2,1)S(1)}, u32[]{:S(2)}, u32[]{:S(2)}) async-start(bf16[8,2,1024]{2,1,0:T(2,128)(2,1)} %reshape.232), calls=%async_computation.2 | async-start | bytes 65536 | tf_op jit(solution)/shard_map/all_to_all | solution.py:97
  87.2 4.8 %all-to-all-done.1 = bf16[8,2,1024]{2,1,0:T(2,128)(2,1)S(1)} async-done(((bf16[8,2,1024]{2,1,0:T(2,128)(2,1)}), bf16[8,2,1024]{2,1,0:T(2,128)(2,1)S(1)}, u32[]{:S(2)}, u32[]{:S(2)}) %all-to-all-start.1) | async-done | bytes 32800 | tf_op jit(solution)/shard_map/all_to_all | solution.py:97
  92.1 0.1 reshape.233
  92.2 0.1 bitcast_bitcast_fusion.1
  92.3 0.3 convolution_select_fusion.2
  92.6 0.4 convolution_convert_fusion.1
  93.0 0.1 copy.71
  93.2 0.2 reshape.234
  93.3 7.2 %all_to_all.93 = bf16[8,2,1024]{2,1,0:T(2,128)(2,1)S(1)} all-to-all(bf16[8,2,1024]{2,1,0:T(2,128)(2,1)S(1)} %reshape.234), channel_id=1, replica_groups=mesh['shot'=8,'rcv'=4] {'shot'}, dimensions={0} | all-to-all | bytes 65536 | tf_op jit(solution)/shard_map/all_to_all | solution.py:103
  100.6 0.1 reshape.235
  100.8 16.1 %all-gather = bf16[2,16,8,1,8,32]{5,2,3,1,0,4:T(8,128)(2,1)S(1)} all-gather(bf16[2,16,8,1,2,32]{5,2,3,1,0,4:T(8,128)(2,1)S(1)} %copy.73), channel_id=2, replica_groups=mesh['shot'=8,'rcv'=4] {'rcv'}, dimensions={4}, use_global_device_ids=true | all-gather | bytes 163840 | tf_op jit(solution)/shard_map/all_gather | solution.py:93
  116.9 0.5 convolution_bitcast_fusion.3
  117.4 0.5 convolution_bitcast_fusion.1
  117.9 0.5 fusion.17
  118.4 0.5 fusion.18
  118.9 0.6 copy.76
  119.5 3.4 %all-to-all-start.3 = ((bf16[2,16,8,1,128]{4,1,3,0,2:T(8,128)(2,1)}), bf16[2,16,8,1,128]{4,1,3,0,2:T(8,128)(2,1)S(1)}, u32[]{:S(2)}, u32[]{:S(2)}) async-start(bf16[2,16,8,1,128]{4,1,3,0,2:T(8,128)(2,1)} %copy.76), calls=%async_computation.4 | async-start | bytes 131072 | tf_op jit(solution)/shard_map/all_to_all | solution.py:97
  122.9 0.0 reduce-scatter.5.cloned.1.call-start
  123.0 4.9 %all-to-all-done.3 = bf16[2,16,8,1,128]{4,1,3,0,2:T(8,128)(2,1)S(1)} async-done(((bf16[2,16,8,1,128]{4,1,3,0,2:T(8,128)(2,1)}), bf16[2,16,8,1,128]{4,1,3,0,2:T(8,128)(2,1)S(1)}, u32[]{:S(2)}, u32[]{:S(2)}) %all-to-all-start.3) | async-done | bytes 65568 | tf_op jit(solution)/shard_map/all_to_all | solution.py:97
  127.9 0.3 fusion.10
  128.2 0.4 fusion.14
  128.5 0.1 copy.78
  128.6 7.4 %all_to_all.94 = bf16[2,128,1,1,128]{4,0,3,2,1:T(2,128)(2,1)S(1)} all-to-all(bf16[2,128,1,1,128]{4,0,3,2,1:T(2,128)(2,1)S(1)} %copy.78), channel_id=1, replica_groups=mesh['shot'=8,'rcv'=4] {'shot'}, dimensions={1} | all-to-all | bytes 131072 | tf_op jit(solution)/shard_map/all_to_all | solution.py:103
  136.1 2.7 %fusion.21 = f32[16,8,8,32]{3,1,2,0:T(8,128)S(1)} fusion(bf16[2,16,128,8,32]{2,4,3,1,0:T(8,128)(2,1)} %bitcast.192, bf16[2,16,8,1,1,128]{5,2,1,4,3,0:T(8,128)(2,1)S(1)} %bitcast.201), kind=kOutput, calls=%fused_computation.49 | convolution fusion | flops 8388608 | bytes 1212416 | tf_op jit(solution)/shard_map/fdau,fpd->fapu/dot_general | solution.py:53
  138.7 1.5 fusion.20
  140.2 1.5 fusion.6
  141.7 1.5 fusion.5
  143.1 0.1 pad_maximum_fusion.1
  143.3 0.9 copy.81
  144.2 18.3 %reduce-scatter.5.cloned.1.call-done = bf16[2,16,8,2,32]{4,2,1,0,3:T(8,128)(2,1)} async-done(((bf16[2,16,8,8,32]{4,2,1,0,3:T(8,128)(2,1)}), bf16[2,16,8,2,32]{4,2,1,0,3:T(8,128)(2,1)}) %reduce-scatter.5.cloned.1.call-update) | async-done | bytes 32784 | tf_op jit(solution)/shard_map/reduce_scatter | solution.py:87
  162.5 1.0 copy.138
  163.6 0.2 reshape.236
  163.7 8.3 %all_to_all.95 = bf16[8,2,1024]{2,1,0:T(2,128)(2,1)S(1)} all-to-all(bf16[8,2,1024]{2,1,0:T(2,128)(2,1)S(1)} %reshape.236), channel_id=1, replica_groups=mesh['shot'=8,'rcv'=4] {'shot'}, dimensions={0} | all-to-all | bytes 65536 | tf_op jit(solution)/shard_map/all_to_all | solution.py:97
  172.0 0.1 reshape.237
  172.2 0.1 bitcast_bitcast_fusion
  172.3 0.9 convolution_select_fusion.1
  (42 shorter events, 0.4 us)
Async XLA Ops:
  7.2 1.6 copy-start
  9.5 0.8 copy-start.8
  9.5 1.4 copy-start.7
  18.8 6.1 %copy-start.4 = (bf16[8,128,256]{2,1,0:T(8,128)(2,1)S(1)}, bf16[8,128,256]{2,1,0:T(8,128)(2,1)}, u32[]{:S(2)}) copy-start(bf16[8,128,256]{2,1,0:T(8,128)(2,1)} %param.9) | copy-start | bytes 1572868
  18.8 32.1 %all-to-all-start = ((bf16[2,128,128,32]{2,3,0,1:T(8,128)(2,1)}), bf16[2,128,128,32]{2,3,0,1:T(8,128)(2,1)}, u32[]{:S(2)}, u32[]{:S(2)}) async-start(bf16[2,128,128,32]{2,3,0,1:T(8,128)(2,1)} %copy.58), calls=%async_computation | async-start | bytes 4194304 | tf_op jit(solution)/shard_map/all_to_all | solution.py:133
  24.1 57.6 %reduce-scatter.3.cloned.1.call-start = ((), (), s32[]{:S(2)}) async-start(), calls=%async_computation.8 | async-start | bytes 655360 | tf_op jit(solution)/shard_map/reduce_scatter | solution.py:87
  53.1 4.4 %copy-start.1 = (bf16[2,8,16,128,32]{3,4,1,2,0:T(8,128)(2,1)}, bf16[2,8,16,128,32]{3,4,1,2,0:T(8,128)(2,1)S(1)}, u32[]{:S(2)}) copy-start(bf16[2,8,16,128,32]{3,4,1,2,0:T(8,128)(2,1)S(1)} %copy.136) | copy-start | bytes 6291460
  59.0 33.4 %copy-start.9 = (s32[2,32]{1,0:T(2,128)S(1)}, s32[2,32]{1,0:T(2,128)}, u32[]{:S(2)}) copy-start(s32[2,32]{1,0:T(2,128)} %param.10) | copy-start | bytes 772
  83.6 8.5 %all-to-all-start.1 = ((bf16[8,2,1024]{2,1,0:T(2,128)(2,1)}), bf16[8,2,1024]{2,1,0:T(2,128)(2,1)S(1)}, u32[]{:S(2)}, u32[]{:S(2)}) async-start(bf16[8,2,1024]{2,1,0:T(2,128)(2,1)} %reshape.232), calls=%async_computation.2 | async-start | bytes 65536 | tf_op jit(solution)/shard_map/all_to_all | solution.py:97
  92.6 24.8 %copy-start.6 = (f32[2,32,256]{2,1,0:T(8,128)}, f32[2,32,256]{2,1,0:T(8,128)S(1)}, u32[]{:S(2)}) copy-start(f32[2,32,256]{2,1,0:T(8,128)S(1)} %convolution_select_fusion.2) | copy-start | bytes 196612
  100.7 16.2 %copy-start.2 = (bf16[2,8,16,128,32]{3,4,1,2,0:T(8,128)(2,1)S(1)}, bf16[2,8,16,128,32]{3,4,1,2,0:T(8,128)(2,1)}, u32[]{:S(2)}) copy-start(bf16[2,8,16,128,32]{3,4,1,2,0:T(8,128)(2,1)} %copy-done.1) | copy-start | bytes 6291460
  117.9 10.0 %copy-start.10 = (s32[1,128]{1,0:T(1,128)S(1)}, s32[1,128]{1,0:T(1,128)}, u32[]{:S(2)}) copy-start(s32[1,128]{1,0:T(1,128)} %param.11) | copy-start | bytes 1540
  119.5 8.3 %all-to-all-start.3 = ((bf16[2,16,8,1,128]{4,1,3,0,2:T(8,128)(2,1)}), bf16[2,16,8,1,128]{4,1,3,0,2:T(8,128)(2,1)S(1)}, u32[]{:S(2)}, u32[]{:S(2)}) async-start(bf16[2,16,8,1,128]{4,1,3,0,2:T(8,128)(2,1)} %copy.76), calls=%async_computation.4 | async-start | bytes 131072 | tf_op jit(solution)/shard_map/all_to_all | solution.py:97
  122.9 39.6 %reduce-scatter.5.cloned.1.call-start = ((), (), s32[]{:S(2)}) async-start(), calls=%async_computation.9 | async-start | bytes 655360 | tf_op jit(solution)/shard_map/reduce_scatter | solution.py:87
  127.8 10.9 %copy-start.3 = (bf16[2,8,16,128,32]{3,4,1,2,0:T(8,128)(2,1)S(1)}, bf16[2,8,16,128,32]{3,4,1,2,0:T(8,128)(2,1)}, u32[]{:S(2)}) copy-start(bf16[2,8,16,128,32]{3,4,1,2,0:T(8,128)(2,1)} %copy-done.1) | copy-start | bytes 6291460
  128.1 13.5 %copy-start.5 = (f32[1,128,256]{2,1,0:T(8,128)}, f32[1,128,256]{2,1,0:T(8,128)S(1)}, u32[]{:S(2)}) copy-start(f32[1,128,256]{2,1,0:T(8,128)S(1)} %fusion.10) | copy-start | bytes 393220
Sparse Core Ops, SparseCore 0:
  60.2 21.5 reduce-scatter.2
  144.3 18.1 reduce-scatter.4
where the time goes:
time: 181 us; the launch traced here: 180 us
  waiting for transfers between devices  74.6 us (41%)
  blocking collectives  39 us (22%)
  matrix products  21.5 us (12%)
  between operations  14.5 us (8%)
  starting transfers between devices  12.6 us (7%)
  local copies, waits for them, and re-layouts  12.5 us (7%)
  other arithmetic  5.39 us (3%)
    reduce_scatter x2, waiting for transfers between devices, forward_sum(): lax.psum_scatter(partial_value.astype(jnp.bfloat16), 'rcv', scatter_dimen...  39.5 us
    all_to_all x1, waiting for transfers between devices, body(): lax.all_to_all(reflection, 'shot', split_axis=1, concat_axis=3, tiled=True)  25.4 us
    all_gather x1, blocking collectives, focal_rows(): return lax.all_gather(pieces, 'rcv', axis=3, tiled=True)  16.1 us
    all_to_all x2, blocking collectives, spectrum_layout(): lax.all_to_all(spectra, 'shot', split_axis=1, concat_axis=2, tiled=True)  14.6 us
    dot_general x8, matrix products, product_term(): jnp.einsum('fdau,fpd->fapu', left_op, right_op, preferred_element_type=jn...  12.9 us
    all_to_all x2, waiting for transfers between devices, time_layout(): lax.all_to_all(spectra.astype(jnp.bfloat16), 'shot', split_axis=2, concat...  9.71 us
    all_to_all x1, blocking collectives, time_layout(): lax.all_to_all(spectra.astype(jnp.bfloat16), 'shot', split_axis=2, concat...  8.29 us
    all_to_all x2, starting transfers between devices, time_layout(): lax.all_to_all(spectra.astype(jnp.bfloat16), 'shot', split_axis=2, concat...  6.99 us
  transfers between devices with their start and end apart: 5, of which 5 were waited for; matrix products, arithmetic and copies ran while one was open for 1% of the time, Pallas kernels for 0%

commit v1 on v0

v1 whole, which is shorter than its diff:
```python
import functools
import math

import jax
import jax.numpy as jnp
import numpy as np
from jax import lax
from jax.experimental import pallas as pl
from jax.experimental.pallas import tpu as pltpu
from jax.sharding import PartitionSpec as P

NT = 256
NF = 128
TAPS = 64
KSHIFT = 64
LANES = 128
GROUP = 8
NG = NF // GROUP

F32 = jnp.float32
BF16 = jnp.bfloat16
NN = (((1,), (0,)), ((), ()))
NT_DIMS = (((1,), (1,)), ((), ()))


def make_tables(source_local):
    sample = np.arange(NT)
    bins = np.arange(NF)
    angles = 2.0 * np.pi / NT * (bins[:, None] * sample[None, :] % NT)
    forward = np.concatenate([np.cos(angles), -np.sin(angles)], axis=0)
    weights = np.where(bins == 0, 1.0, 2.0) / NT
    inverse = (forward * np.concatenate([weights, weights])[:, None]).T
    tap = np.arange(TAPS, dtype=np.float64)
    fraction = np.arange(KSHIFT) * (TAPS / (4.0 * KSHIFT))
    offset = tap[None, :] - 0.375 * TAPS - fraction[:, None]
    window = 0.5 - 0.5 * np.cos(2.0 * np.pi * (tap + 0.5) / TAPS)
    tap_spec = forward[:, :TAPS] @ (np.sinc(offset) * window[None, :]).T
    tap_high = jnp.asarray(tap_spec, F32).astype(BF16)
    tap_low = (jnp.asarray(tap_spec, F32) - tap_high.astype(F32)).astype(BF16)
    width = source_local * GROUP
    source_of = np.arange(width) // GROUP
    blocks = LANES // source_local
    pick = (source_of[:, None] == np.arange(source_local)[None, :]).astype(np.float64)
    gather = np.tile(pick, (1, blocks))
    spread = np.zeros((blocks, LANES, width))
    for block in range(blocks):
        spread[block, block * source_local : (block + 1) * source_local] = pick.T
    return dict(
        forward=jnp.asarray(forward, F32).astype(BF16),
        inverse=jnp.asarray(inverse, F32).astype(BF16),
        taps=jnp.concatenate([tap_high, tap_low], axis=1),
        gather=jnp.asarray(gather, F32).astype(BF16),
        spread=jnp.asarray(spread, F32).astype(BF16),
    )


def mm(left, right, dims=NN):
    return lax.dot_general(left, right, dims, preferred_element_type=F32)


def interleave(first, second):
    width = first.shape[-1]
    pair = jnp.stack(
        [first.reshape(NG, GROUP, width), second.reshape(NG, GROUP, width)], axis=1
    )
    return pair.reshape(NG, 2 * GROUP, width)


def same_bin(rows, lanes):
    row = lax.broadcasted_iota(jnp.int32, (rows, lanes), 0)
    lane = lax.broadcasted_iota(jnp.int32, (rows, lanes), 1)
    return (row % GROUP) == (lane % GROUP)


def store_vector(vector_ref, slot, first, second):
    first_re, first_im = first[:NF], first[NF:]
    second_re, second_im = second[:NF], second[NF:]
    receivers = first.shape[-1]
    re = interleave(first_re, second_re)
    im = interleave(first_im, second_im)
    vector_ref[:, 0, slot, :, :receivers] = re.astype(BF16)
    vector_ref[:, 0, slot, :, receivers:] = (-im).astype(BF16)
    vector_ref[:, 1, slot, :, :receivers] = im.astype(BF16)
    vector_ref[:, 1, slot, :, receivers:] = re.astype(BF16)


def apply_matrix(matrix_ref, vector_ref, gather, store):
    pairs = vector_ref.shape[2]
    rows = 2 * pairs * 2 * GROUP
    width = matrix_ref.shape[1] * matrix_ref.shape[2]
    diagonal = same_bin(rows, width)
    block_of = lax.broadcasted_iota(jnp.int32, (pairs, GROUP, LANES), 2) // (LANES // 4)

    def one(group):
        vector = vector_ref[group].reshape(rows, vector_ref.shape[-1])
        matrix = matrix_ref[group].reshape(width, matrix_ref.shape[-1])
        full = mm(vector, matrix, NT_DIMS)
        kept = jnp.where(diagonal, full, 0.0).astype(BF16)
        spread = mm(kept, gather).reshape(2, pairs, 2, GROUP, LANES)
        low = jnp.where(block_of == 0, spread[0, :, 0], spread[0, :, 1])
        high = jnp.where(block_of == 2, spread[1, :, 0], spread[1, :, 1])
        return jnp.where(block_of < 2, low, high)

    for couple in range(NG // 2):
        both = jnp.concatenate([one(2 * couple), one(2 * couple + 1)], axis=1)
        store(couple * 2 * GROUP, both.astype(BF16))


def build_kernel(
    gain, index_ref, traces_ref, shift_ref, deconv_ref, focal_ref, onset_ref,
    forward_ref, taps_ref, gather_ref, matrix_ref, sum_ref, vector_ref,
):
    sources, receivers = shift_ref.shape
    pairs = focal_ref.shape[0] // 2
    forward = forward_ref[...]
    taps = taps_ref[...]
    deconv = deconv_ref[...]
    deconv_high = deconv.astype(BF16)
    deconv_low = (deconv - deconv_high.astype(F32)).astype(BF16)
    head = forward[:, :TAPS]
    wave = (mm(head, deconv_high, NT_DIMS) + mm(head, deconv_low, NT_DIMS)) * gain
    kinds = lax.broadcasted_iota(jnp.int32, (KSHIFT, receivers), 0)

    for couple in range(sources // 2):
        signals = traces_ref[2 * couple : 2 * couple + 2].reshape(2 * receivers, NT)
        raw = mm(forward, signals, NT_DIMS)
        hot = jnp.concatenate(
            [
                (kinds == shift_ref[2 * couple + half : 2 * couple + half + 1, :]).astype(F32)
                for half in range(2)
            ],
            axis=1,
        ).astype(BF16)
        delay = mm(taps, jnp.concatenate([hot, hot], axis=0))
        parts = []
        for half in range(2):
            lanes = slice(half * receivers, (half + 1) * receivers)
            raw_re, raw_im = raw[:NF, lanes], raw[NF:, lanes]
            delay_re, delay_im = delay[:NF, lanes], delay[NF:, lanes]
            column = slice(2 * couple + half, 2 * couple + half + 1)
            wave_re, wave_im = wave[:NF, column], wave[NF:, column]
            first_re = raw_re * delay_re - raw_im * delay_im
            first_im = raw_re * delay_im + raw_im * delay_re
            parts.append(
                (
                    first_re * wave_re - first_im * wave_im,
                    first_re * wave_im + first_im * wave_re,
                )
            )
        matrix_ref[:, couple, :, :receivers] = interleave(parts[0][0], parts[1][0]).astype(BF16)
        matrix_ref[:, couple, :, receivers:] = interleave(parts[0][1], parts[1][1]).astype(BF16)

    for pair in range(pairs):
        first = mm(forward, focal_ref[2 * pair], NT_DIMS)
        second = mm(forward, focal_ref[2 * pair + 1], NT_DIMS)
        store_vector(vector_ref, pair, first, second)

    def store(row, value):
        for pair in range(pairs):
            sum_ref[pair * NF + row : pair * NF + row + 2 * GROUP, :] = value[pair]

    apply_matrix(matrix_ref, vector_ref, gather_ref[...], store)
    rcv_index = index_ref[1]
    own = onset_ref[...].astype(F32)
    own = jnp.concatenate([own[0:1], own[1:2]] * 2, axis=1)
    own = jnp.broadcast_to(own, (2 * GROUP, LANES))
    row = lax.broadcasted_iota(jnp.int32, own.shape, 0)
    lane = lax.broadcasted_iota(jnp.int32, own.shape, 1)
    here = (row == rcv_index // 2) & (lane // (LANES // 2) == rcv_index % 2)
    sum_ref[pairs * NF :, :] = jnp.where(here, own, 0.0).astype(BF16)


def split_halves(first, second):
    lane = lax.broadcasted_iota(jnp.int32, first.shape, 1)
    low = lane < LANES // 2
    re = jnp.where(low, first, pltpu.roll(second, LANES // 2, 1))
    im = jnp.where(low, pltpu.roll(first, LANES // 2, 1), second)
    return jnp.concatenate([re, im], axis=0)


def mute(signal, onset):
    sample = lax.broadcasted_iota(jnp.int32, signal.shape, 0)
    folded = jnp.minimum(sample, NT - sample).astype(F32)
    return jnp.where(folded < onset, signal, 0.0)


def adjoint_kernel(
    index_ref, mine_ref, other_ref, matrix_ref, forward_ref, inverse_ref, spread_ref,
    keep_ref, send_ref, field_ref, vector_ref,
):
    shot_index = index_ref[0]
    rcv_index = index_ref[1]
    core = shot_index % 2
    chip = shot_index // 2
    pairs = keep_ref.shape[0]
    receivers = matrix_ref.shape[-1] // 2
    sources = 2 * matrix_ref.shape[1]
    width = sources * GROUP
    forward = forward_ref[...]
    inverse = inverse_ref[...]
    onsets = mine_ref[pairs * NF :, :].astype(F32) + other_ref[pairs * NF :, :].astype(F32)
    diagonal = same_bin(NF, width)
    owned = jnp.zeros((NT, LANES), F32)

    for couple in range(pairs // 2):
        rows = slice(2 * couple * NF, 2 * (couple + 1) * NF)
        total = mine_ref[rows, :].astype(F32) + other_ref[rows, :].astype(F32)
        spectra = split_halves(total[:NF], total[NF:]).astype(BF16)
        signal = mute(mm(inverse, spectra), onsets[couple : couple + 1, :])
        owned = jnp.where(rcv_index // 2 == couple, signal, owned)
        echo = mm(forward, signal.astype(BF16)).astype(BF16)
        for half in range(2):
            slot = (2 * couple + half) ^ chip
            for part in range(2):
                values = echo[part * NF : (part + 1) * NF]
                kept, sent = (
                    jnp.where(diagonal, mm(values, spread_ref[2 * half + which]), 0.0)
                    for which in (core, 1 - core)
                )
                vector_ref[:, part, slot] = interleave(kept, sent).astype(BF16)

    owned = jnp.where(rcv_index % 2 == 1, pltpu.roll(owned, LANES // 2, 1), owned)
    flipped = jnp.transpose(owned)[: LANES // 2]
    field_ref[...] = flipped.reshape(field_ref.shape)

    def one(group):
        vector = vector_ref[group].reshape(2 * pairs * 2 * GROUP, width)
        matrix = matrix_ref[group].reshape(width, 2 * receivers)
        full = mm(vector, matrix).reshape(2, pairs, 2, GROUP, 2 * receivers)
        re = full[0, ..., :receivers] + full[1, ..., receivers:]
        im = full[1, ..., :receivers] - full[0, ..., receivers:]
        return re, im

    for couple in range(NG // 2):
        even = one(2 * couple)
        odd = one(2 * couple + 1)
        for part in range(2):
            both = jnp.concatenate([even[part], odd[part]], axis=2).astype(BF16)
            row = part * NF + couple * 2 * GROUP
            keep_ref[:, row : row + 2 * GROUP, :] = both[:, 0]
            send_ref[:, row : row + 2 * GROUP, :] = both[:, 1]


def downgoing_kernel(index_ref, *refs):
    parts = refs[:-6]
    focal_ref, onset_ref, forward_ref, inverse_ref, field_ref, plus_ref = refs[-6:]
    total = parts[0][...].astype(F32)
    for part in parts[1:]:
        total = total + part[...].astype(F32)
    onset = onset_ref[...].astype(F32)
    signal = mute(mm(inverse_ref[...], total.astype(BF16)), onset)
    field = focal_ref[0].astype(F32) + jnp.transpose(signal)
    field_ref[0] = field
    plus_ref[...] = mm(forward_ref[...], field.astype(BF16), NT_DIMS).astype(BF16)


def second_kernel(index_ref, near_ref, far_ref, matrix_ref, gather_ref, sum_ref, vector_ref):
    shot_index = index_ref[0]
    rcv_index = index_ref[1]
    core = shot_index % 2
    chip = shot_index // 2
    pairs = near_ref.shape[0]
    for distance in range(pairs):
        slot = (chip ^ distance) ^ rcv_index
        near = near_ref[distance].astype(F32)
        far = far_ref[distance].astype(F32)
        store_vector(
            vector_ref, slot, jnp.where(core == 0, near, far), jnp.where(core == 0, far, near)
        )

    def store(row, value):
        sum_ref[:, row : row + 2 * GROUP, :] = value

    apply_matrix(matrix_ref, vector_ref, gather_ref[...], store)


def final_kernel(*refs):
    parts = refs[:-3]
    onset_ref, inverse_ref, field_ref = refs[-3:]
    total = parts[0][...].astype(F32)
    for part in parts[1:]:
        total = total + part[...].astype(F32)
    spectra = split_halves(total, total).astype(BF16)
    onset = onset_ref[...].astype(F32)
    onset = jnp.concatenate([onset[0:1], onset[1:2]] * 2, axis=1)
    signal = mute(mm(inverse_ref[...], spectra), onset)
    field_ref[...] = jnp.transpose(signal)[: LANES // 2].reshape(field_ref.shape)


def vmem(count):
    return [pl.BlockSpec(memory_space=pltpu.VMEM) for _ in range(count)]


def smem():
    return [pl.BlockSpec(memory_space=pltpu.SMEM)]


def call(kernel, name, out_shape, in_specs, scratch=()):
    many = isinstance(out_shape, (tuple, list))
    return pl.pallas_call(
        kernel,
        name=name,
        out_shape=out_shape,
        in_specs=in_specs,
        out_specs=vmem(len(out_shape)) if many else vmem(1)[0],
        scratch_shapes=list(scratch),
        compiler_params=pltpu.CompilerParams(vmem_limit_bytes=40 << 20),
    )


def exchange(value, axis, distance):
    count = lax.axis_size(axis)
    return lax.ppermute(value, axis, [(place, place ^ distance) for place in range(count)])


def add_rounded(left, right):
    return (left.astype(F32) + right.astype(F32)).astype(BF16)


def body(traces, shift_index, deconv, focal_start, onset_source, onset_receiver):
    shot_count = lax.axis_size("shot")
    rcv_count = lax.axis_size("rcv")
    sources, receivers, _ = traces.shape
    focal_total = focal_start.shape[0]
    pairs = focal_total // 2
    assert onset_source.shape[0] == 2 and pairs == rcv_count
    assert focal_total == shot_count and 4 * sources == LANES and receivers == LANES
    gain = 1.0 / math.sqrt(NT * receivers * rcv_count)
    tables = make_tables(sources)
    index = jnp.stack([lax.axis_index("shot"), lax.axis_index("rcv")]).astype(jnp.int32)
    shape = jax.ShapeDtypeStruct
    vector = pltpu.VMEM((NG, 2, pairs, 2 * GROUP, 2 * receivers), BF16)

    matrix, partial = call(
        functools.partial(build_kernel, gain),
        "build",
        (
            shape((NG, sources // 2, 2 * GROUP, 2 * receivers), BF16),
            shape((pairs * NF + 2 * GROUP, LANES), BF16),
        ),
        smem() + vmem(8),
        [vector],
    )(
        index, traces, shift_index, deconv, focal_start, onset_source,
        tables["forward"], tables["taps"], tables["gather"],
    )

    distance = 1
    mine, other = partial, exchange(partial, "rcv", 1)
    while 2 * distance < rcv_count:
        distance *= 2
        mine = add_rounded(mine, other)
        other = exchange(mine, "rcv", distance)

    keep, send, upgoing_first = call(
        adjoint_kernel,
        "adjoint",
        (
            shape((pairs, 2 * NF, receivers), BF16),
            shape((pairs, 2 * NF, receivers), BF16),
            shape((2, sources, NT), F32),
        ),
        smem() + vmem(6),
        [pltpu.VMEM((NG, 2, pairs, 2 * GROUP, sources * GROUP), BF16)],
    )(index, mine, other, matrix, tables["forward"], tables["inverse"], tables["spread"])

    keep = add_rounded(keep, exchange(send, "shot", 1))
    parts = [keep[0]]
    for distance in range(1, pairs):
        parts.append(exchange(keep[distance], "shot", 2 * distance))

    downgoing, plus = pl.pallas_call(
        downgoing_kernel,
        name="downgoing",
        out_shape=(shape((1, receivers, NT), F32), shape((2 * NF, receivers), BF16)),
        grid_spec=pltpu.PrefetchScalarGridSpec(
            num_scalar_prefetch=1,
            grid=(1,),
            in_specs=[pl.BlockSpec((2 * NF, receivers), lambda i, s: (0, 0)) for _ in parts]
            + [
                pl.BlockSpec((1, receivers, NT), lambda i, s: (s[0], 0, 0)),
                pl.BlockSpec((1, receivers), lambda i, s: (0, 0)),
                pl.BlockSpec((2 * NF, NT), lambda i, s: (0, 0)),
                pl.BlockSpec((NT, 2 * NF), lambda i, s: (0, 0)),
            ],
            out_specs=[
                pl.BlockSpec((1, receivers, NT), lambda i, s: (0, 0, 0)),
                pl.BlockSpec((2 * NF, receivers), lambda i, s: (0, 0)),
            ],
        ),
    )(index, *parts, focal_start, onset_receiver, tables["forward"], tables["inverse"])

    near = [plus]
    for distance in range(1, pairs):
        near.append(exchange(plus, "shot", 2 * distance))
    near = jnp.stack(near)
    far = exchange(near, "shot", 1)

    second = call(
        second_kernel,
        "second",
        shape((pairs, NF, LANES), BF16),
        smem() + vmem(4),
        [vector],
    )(index, near, far, matrix, tables["gather"])

    parts = [second[0]]
    for distance in range(1, rcv_count):
        parts.append(exchange(second[distance], "rcv", distance))
    upgoing_second = call(
        final_kernel, "final", shape((2, sources, NT), F32), vmem(len(parts) + 2)
    )(*parts, onset_source, tables["inverse"])
    return (upgoing_first, downgoing, upgoing_second)


def solution(mesh):
    placed = (
        P("shot", "rcv", None),
        P("shot", "rcv"),
        P("shot", None),
        P(None, "rcv", None),
        P("rcv", "shot"),
        P("shot", "rcv"),
    )
    return jax.shard_map(
        body,
        mesh=mesh,
        in_specs=placed,
        out_specs=(P("rcv", "shot", None), P("shot", "rcv", None), P("rcv", "shot", None)),
        check_vma=False,
    )
```

time: 181 us -> 67.5 us (0.37)
  waiting for transfers between devices: 74.6 us -> 23.1 us
  blocking collectives: 39 us -> 0 us
  matrix products: 21.5 us -> 0 us
  Pallas kernels: 0 us -> 16 us
  between operations: 14.5 us -> 0.72 us
  starting transfers between devices: 12.6 us -> 17.4 us
  other arithmetic: 5.39 us -> 1.06 us
  local copies, waits for them, and re-layouts: 12.5 us -> 8.65 us
    reduce_scatter x2 -> x0, waiting for transfers between devices: 39.5 us -> none  [forward_sum(): lax.psum_scatter(partial_value.astype(jnp.bfloat16), 'rcv', scatter_dimen...]
    all_to_all x3 -> x0, waiting for transfers between devices: 35.1 us -> none  [the longest x1 25.4 us: body(): lax.all_to_all(reflection, 'shot', split_axis=1, concat_axis=3, tiled=True)]
    ppermute x0 -> x13, waiting for transfers between devices: none -> 23.1 us  [exchange(): lax.ppermute(value, axis, [(place, place ^ distance) for place in range(c...]
    all_to_all x3 -> x0, blocking collectives: 22.9 us -> none  [the longest x2 14.6 us: spectrum_layout(): lax.all_to_all(spectra, 'shot', split_axis=1, concat_axis=2, tiled=True)]
    dot_general x24 -> x0, matrix products: 21.5 us -> none  [the longest x8 12.9 us: product_term(): jnp.einsum('fdau,fpd->fapu', left_op, right_op, preferred_element_type=jn...]
    ppermute x0 -> x13, starting transfers between devices: none -> 17.4 us  [exchange(): lax.ppermute(value, axis, [(place, place ^ distance) for place in range(c...]
    all_gather x1 -> x0, blocking collectives: 16.1 us -> none  [focal_rows(): return lax.all_gather(pieces, 'rcv', axis=3, tiled=True)]
    pallas_call x0 -> x5, Pallas kernels: none -> 16 us  [the longest x1 5.55 us: body(): call(functools.partial(build_kernel, gain), 'build', (shape((NG, sources...]
  transfers between devices with their start and end apart: 5 -> 13, of which waited for: 5 -> 12; matrix products, arithmetic and copies ran while one was open for 1% -> 0% of each run, Pallas kernels for 0% -> 0%
where the time goes in v1:
time: 67.5 us; the launch traced here: 67 us
  waiting for transfers between devices  23.1 us (34%)
  starting transfers between devices  17.4 us (26%)
  Pallas kernels  16 us (24%)
  local copies, waits for them, and re-layouts  8.65 us (13%)
  other arithmetic  1.06 us (2%)
  between operations  0.72 us (1%)
    ppermute x13, waiting for transfers between devices, exchange(): lax.ppermute(value, axis, [(place, place ^ distance) for place in range(c...  23.1 us
    ppermute x13, starting transfers between devices, exchange(): lax.ppermute(value, axis, [(place, place ^ distance) for place in range(c...  17.4 us
    unnamed x38, local copies, waits for them, and re-layouts  7.99 us
    pallas_call x1, Pallas kernels, body(): call(functools.partial(build_kernel, gain), 'build', (shape((NG, sources...  5.55 us
    pallas_call x1, Pallas kernels, body(): call(second_kernel, 'second', shape((pairs, NF, LANES), BF16), smem() + v...  3.78 us
    pallas_call x1, Pallas kernels, body(): pl.pallas_call(downgoing_kernel, name='downgoing', out_shape=(shape((1, r...  3.04 us
    pallas_call x1, Pallas kernels, body(): call(adjoint_kernel, 'adjoint', (shape((pairs, 2 * NF, receivers), BF16),...  2.67 us
  transfers between devices with their start and end apart: 13, of which 12 were waited for; matrix products, arithmetic and copies ran while one was open for 0% of the time, Pallas kernels for 0%

profile of v1, /device:TPU:0, one launch (start us, length us, event | category | flops | bytes accessed | tf_op | source)
XLA Modules:
  0.0 67.0 jit_solution(1241545425006440484)
XLA Ops:
  0.6 0.1 pad_add_fusion.index_ref
  0.7 0.0 copy-start
  0.7 1.6 %copy-done = bf16[32,128,256]{2,1,0:T(8,128)(2,1)S(1)} copy-done((bf16[32,128,256]{2,1,0:T(8,128)(2,1)S(1)}, bf16[32,128,256]{2,1,0:T(8,128)(2,1)}, u32[]{:S(2)}) %copy-start) | copy-done | bytes 2097176
  2.3 0.0 copy-start.1
  2.3 1.0 %copy-done.1 = bf16[8,128,256]{2,1,0:T(8,128)(2,1)S(1)} copy-done((bf16[8,128,256]{2,1,0:T(8,128)(2,1)S(1)}, bf16[8,128,256]{2,1,0:T(8,128)(2,1)}, u32[]{:S(2)}) %copy-start.1) | copy-done | bytes 524312
  3.3 0.0 copy-start.2
  3.3 0.9 %copy-done.2 = bf16[256,256]{1,0:T(8,128)(2,1)S(1)} copy-done((bf16[256,256]{1,0:T(8,128)(2,1)S(1)}, bf16[256,256]{1,0:T(8,128)(2,1)}, u32[]{:S(2)}) %copy-start.2) | copy-done | bytes 131096
  4.2 0.0 copy-start.7
  4.3 0.8 %copy-done.7 = bf16[256,128]{1,0:T(8,128)(2,1)S(1)} copy-done((bf16[256,128]{1,0:T(8,128)(2,1)S(1)}, bf16[256,128]{1,0:T(8,128)(2,1)}, u32[]{:S(2)}) %copy-start.7) | copy-done | bytes 65560
  5.1 0.0 copy-start.9
  5.1 0.8 %copy-done.9 = bf16[256,128]{1,0:T(8,128)(2,1)S(1)} copy-done((bf16[256,128]{1,0:T(8,128)(2,1)S(1)}, bf16[256,128]{1,0:T(8,128)(2,1)}, u32[]{:S(2)}) %copy-start.9) | copy-done | bytes 65560
  5.9 0.0 copy-start.10
  5.9 0.7 %copy-done.10 = s32[32,128]{1,0:T(8,128)S(1)} copy-done((s32[32,128]{1,0:T(8,128)S(1)}, s32[32,128]{1,0:T(8,128)}, u32[]{:S(2)}) %copy-start.10) | copy-done | bytes 16408
  6.6 0.0 copy-start.11
  6.6 0.7 %copy-done.11 = f32[32,64]{1,0:T(8,128)S(1)} copy-done((f32[32,64]{1,0:T(8,128)S(1)}, f32[32,64]{1,0:T(8,128)}, u32[]{:S(2)}) %copy-start.11) | copy-done | bytes 8216
  7.4 0.0 copy-start.14
  7.4 0.7 %copy-done.14 = s32[2,32]{1,0:T(2,128)S(1)} copy-done((s32[2,32]{1,0:T(2,128)S(1)}, s32[2,32]{1,0:T(2,128)}, u32[]{:S(2)}) %copy-start.14) | copy-done | bytes 280
  8.0 0.0 copy-start.12
  8.0 0.0 copy-start.3
  8.1 5.5 %build.1 = (bf16[16,16,16,256]{3,2,1,0:T(8,128)(2,1)S(1)}, bf16[528,128]{1,0:T(8,128)(2,1)S(1)}) custom-call(s32[2]{0:T(128)S(1)} %pad_add_fusion.index_ref, bf16[32,128,256]{2,1,0:T(8,128)(2,1)S(1)} %copy-done, s32[32,128]{1,0:T(8,128)S(1)} %copy-done.10, f32[32,64]{1,0:T(8,128)S(1)} %copy-done.11, bf16[8,128,256]{2,1,0:T(8,128)(2,1)S(1)} %copy-done.1, ...), custom_call_target="tpu_custom_call" | custom-call | tf_op jit(solution)/shard_map/build/pallas_call | solution.py:334
  13.6 3.1 %collective-permute-start = (bf16[528,128]{1,0:T(8,128)(2,1)S(1)}, bf16[528,128]{1,0:T(8,128)(2,1)S(1)}, u32[]{:S(2)}, u32[]{:S(2)}) collective-permute-start(bf16[528,128]{1,0:T(8,128)(2,1)S(1)} %get-tuple-element.10), channel_id=1, source_target_pairs={{0,1},{1,0},{2,3},{3,2},{4,5},{5,4},{6,7},{7,6},{8,9},{9,8},{10,11... | collective-permute-start | bytes 405512 | tf_op jit(solution)/shard_map/ppermute | solution.py:313
  16.7 3.6 %collective-permute-done = bf16[528,128]{1,0:T(8,128)(2,1)S(1)} collective-permute-done((bf16[528,128]{1,0:T(8,128)(2,1)S(1)}, bf16[528,128]{1,0:T(8,128)(2,1)S(1)}, u32[]{:S(2)}, u32[]{:S(2)}) %collective-permute-start) | collective-permute-done | bytes 135200 | tf_op jit(solution)/shard_map/ppermute | solution.py:313
  20.3 2.8 %collective-permute-start.1 = (bf16[528,128]{1,0:T(8,128)(2,1)S(1)}, bf16[528,128]{1,0:T(8,128)(2,1)S(1)}, u32[]{:S(2)}, u32[]{:S(2)}) collective-permute-start(bf16[528,128]{1,0:T(8,128)(2,1)S(1)} %add_convert_fusion.1.mine_ref), channel_id=1, source_target_pairs={{0,2},{1,3},{2,0},{3,1},{4,6},{5,7},{6,4},{7,5},{8,10},{9,11},{10,... | collective-permute-start | bytes 405512 | tf_op jit(solution)/shard_map/ppermute | solution.py:313
  23.1 5.8 %collective-permute-done.1.other_ref = bf16[528,128]{1,0:T(8,128)(2,1)S(1)} collective-permute-done((bf16[528,128]{1,0:T(8,128)(2,1)S(1)}, bf16[528,128]{1,0:T(8,128)(2,1)S(1)}, u32[]{:S(2)}, u32[]{:S(2)}) %collective-permute-start.1) | collective-permute-done | bytes 135200 | tf_op jit(solution)/shard_map/ppermute | solution.py:313
  29.0 0.0 copy-done.3
  29.0 0.0 copy-done.4
  29.0 0.0 copy-done.6
  29.0 2.7 %adjoint.1 = (bf16[4,256,128]{2,1,0:T(8,128)(2,1)S(1)}, bf16[4,256,128]{2,1,0:T(8,128)(2,1)S(1)}, f32[2,32,256]{2,1,0:T(8,128)}) custom-call(s32[2]{0:T(128)S(1)} %pad_add_fusion.index_ref, bf16[528,128]{1,0:T(8,128)(2,1)S(1)} %add_convert_fusion.1.mine_ref, bf16[528,128]{1,0:T(8,128)(2,1)S(1)} %collective-permute-done.1.other_ref, ...), custom_call_target="tpu_custom_call" | custom-call | tf_op jit(solution)/shard_map/adjoint/pallas_call | solution.py:355
  31.6 0.0 copy-done.12
  31.6 0.0 collective-permute-start.2
  31.7 1.5 %collective-permute-done.2 = bf16[4,256,128]{2,1,0:T(8,128)(2,1)S(1)} collective-permute-done((bf16[4,256,128]{2,1,0:T(8,128)(2,1)S(1)}, bf16[4,256,128]{2,1,0:T(8,128)(2,1)S(1)}, u32[]{:S(2)}, u32[]{:S(2)}) %collective-permute-start.2) | collective-permute-done | bytes 262176 | tf_op jit(solution)/shard_map/ppermute | solution.py:313
  33.2 0.1 add_convert_fusion
  33.3 0.6 slice_bitcast_fusion
  33.9 2.3 %collective-permute-start.5 = (bf16[256,128]{1,0:T(8,128)(2,1)S(1)}, bf16[256,128]{1,0:T(8,128)(2,1)S(1)}, u32[]{:S(2)}, u32[]{:S(2)}) collective-permute-start(bf16[256,128]{1,0:T(8,128)(2,1)S(1)} %get-tuple-element.17), channel_id=1, source_target_pairs={{0,24},{4,28},{8,16},{12,20},{16,8},{20,12},{24,0},{28,4},{1,25},{... | collective-permute-start | bytes 196616 | tf_op jit(solution)/shard_map/ppermute | solution.py:313
  36.2 0.5 collective-permute-start.4
  36.7 0.7 %collective-permute-start.3 = (bf16[256,128]{1,0:T(8,128)(2,1)S(1)}, bf16[256,128]{1,0:T(8,128)(2,1)S(1)}, u32[]{:S(2)}, u32[]{:S(2)}) collective-permute-start(bf16[256,128]{1,0:T(8,128)(2,1)S(1)} %get-tuple-element.19), channel_id=1, source_target_pairs={{0,8},{4,12},{8,0},{12,4},{16,24},{20,28},{24,16},{28,20},{1,9},{5... | collective-permute-start | bytes 196616 | tf_op jit(solution)/shard_map/ppermute | solution.py:313
  37.4 1.7 %collective-permute-done.5.refs_3_ = bf16[256,128]{1,0:T(8,128)(2,1)S(1)} collective-permute-done((bf16[256,128]{1,0:T(8,128)(2,1)S(1)}, bf16[256,128]{1,0:T(8,128)(2,1)S(1)}, u32[]{:S(2)}, u32[]{:S(2)}) %collective-permute-start.5) | collective-permute-done | bytes 65568 | tf_op jit(solution)/shard_map/ppermute | solution.py:313
  39.1 1.4 %collective-permute-done.4.refs_2_ = bf16[256,128]{1,0:T(8,128)(2,1)S(1)} collective-permute-done((bf16[256,128]{1,0:T(8,128)(2,1)S(1)}, bf16[256,128]{1,0:T(8,128)(2,1)S(1)}, u32[]{:S(2)}, u32[]{:S(2)}) %collective-permute-start.4) | collective-permute-done | bytes 65568 | tf_op jit(solution)/shard_map/ppermute | solution.py:313
  40.5 0.5 collective-permute-done.3.refs_1_
  41.0 0.0 copy-done.16
  41.0 0.1 copy-done.17
  41.1 0.5 copy-done.18
  41.6 3.0 %downgoing.1 = (f32[1,128,256]{2,1,0:T(8,128)}, bf16[256,128]{1,0:T(8,128)(2,1)}) custom-call(s32[2]{0:T(128)} %copy-done.12, bf16[256,128]{1,0:T(8,128)(2,1)} %get-tuple-element.20.refs_0_, bf16[256,128]{1,0:T(8,128)(2,1)} %copy-done.18, bf16[256,128]{1,0:T(8,128)(2,1)} %copy-done.17, bf16[256,128]{1,0:T(8,128)(2,1)} %copy-done.16, ...), custom_call_target="tpu_custom_call" | custom-call | tf_op jit(solution)/shard_map/downgoing/pallas_call | solution.py:372
  44.6 1.5 %collective-permute-start.8 = (bf16[256,128]{1,0:T(8,128)(2,1)}, bf16[256,128]{1,0:T(8,128)(2,1)S(1)}, u32[]{:S(2)}, u32[]{:S(2)}) collective-permute-start(bf16[256,128]{1,0:T(8,128)(2,1)} %get-tuple-element.16), channel_id=1, source_target_pairs={{0,24},{4,28},{8,16},{12,20},{16,8},{20,12},{24,0},{28,4},{1,25},{... | collective-permute-start | bytes 196616 | tf_op jit(solution)/shard_map/ppermute | solution.py:313
  46.1 0.7 %collective-permute-start.7 = (bf16[256,128]{1,0:T(8,128)(2,1)}, bf16[256,128]{1,0:T(8,128)(2,1)S(1)}, u32[]{:S(2)}, u32[]{:S(2)}) collective-permute-start(bf16[256,128]{1,0:T(8,128)(2,1)} %get-tuple-element.16), channel_id=1, source_target_pairs={{0,16},{4,20},{8,24},{12,28},{16,0},{20,4},{24,8},{28,12},{1,17},{... | collective-permute-start | bytes 196616 | tf_op jit(solution)/shard_map/ppermute | solution.py:313
  46.9 1.3 %collective-permute-start.6 = (bf16[256,128]{1,0:T(8,128)(2,1)}, bf16[256,128]{1,0:T(8,128)(2,1)S(1)}, u32[]{:S(2)}, u32[]{:S(2)}) collective-permute-start(bf16[256,128]{1,0:T(8,128)(2,1)} %get-tuple-element.16), channel_id=1, source_target_pairs={{0,8},{4,12},{8,0},{12,4},{16,24},{20,28},{24,16},{28,20},{1,9},{5... | collective-permute-start | bytes 196616 | tf_op jit(solution)/shard_map/ppermute | solution.py:313
  48.1 2.1 %collective-permute-done.8 = bf16[256,128]{1,0:T(8,128)(2,1)S(1)} collective-permute-done((bf16[256,128]{1,0:T(8,128)(2,1)}, bf16[256,128]{1,0:T(8,128)(2,1)S(1)}, u32[]{:S(2)}, u32[]{:S(2)}) %collective-permute-start.8) | collective-permute-done | bytes 65568 | tf_op jit(solution)/shard_map/ppermute | solution.py:313
  50.2 0.7 %collective-permute-done.7 = bf16[256,128]{1,0:T(8,128)(2,1)S(1)} collective-permute-done((bf16[256,128]{1,0:T(8,128)(2,1)}, bf16[256,128]{1,0:T(8,128)(2,1)S(1)}, u32[]{:S(2)}, u32[]{:S(2)}) %collective-permute-start.7) | collective-permute-done | bytes 65568 | tf_op jit(solution)/shard_map/ppermute | solution.py:313
  50.9 0.4 collective-permute-done.6
  51.4 0.9 %pad_maximum_fusion.near_ref = bf16[4,256,128]{2,1,0:T(8,128)(2,1)S(1)} fusion(bf16[1,256,128]{2,1,0:T(8,128)(2,1)S(1)} %bitcast.23, bf16[1,256,128]{2,1,0:T(8,128)(2,1)S(1)} %bitcast.24, bf16[1,256,128]{2,1,0:T(8,128)(2,1)S(1)} %bitcast.25, bf16[1,256,128]{2,1,0:T(8,128)(2,1)} %bitcast.22), kind=kLoop, calls=%fused_computation.2 | loop fusion | flops 393216 | bytes 524288 | tf_op jit(solution)/shard_map/stack | solution.py:396
  52.2 0.1 collective-permute-start.9
  52.3 1.5 %collective-permute-done.9.far_ref = bf16[4,256,128]{2,1,0:T(8,128)(2,1)S(1)} collective-permute-done((bf16[4,256,128]{2,1,0:T(8,128)(2,1)S(1)}, bf16[4,256,128]{2,1,0:T(8,128)(2,1)S(1)}, u32[]{:S(2)}, u32[]{:S(2)}) %collective-permute-start.9) | collective-permute-done | bytes 262176 | tf_op jit(solution)/shard_map/ppermute | solution.py:313
  53.8 0.0 copy-done.8
  53.8 0.0 copy-done.13
  53.8 3.8 %second.1 = bf16[4,128,128]{2,1,0:T(8,128)(2,1)S(1)} custom-call(s32[2]{0:T(128)S(1)} %copy-done.13, bf16[4,256,128]{2,1,0:T(8,128)(2,1)S(1)} %pad_maximum_fusion.near_ref, bf16[4,256,128]{2,1,0:T(8,128)(2,1)S(1)} %collective-permute-done.9.far_ref, bf16[16,16,16,256]{3,2,1,0:T(8,128)(2,1)S(1)} %get-tuple-element.11.matrix_ref, bf16[256,128]{1,0:T(8,128)(2,1)S(1)} %copy-done.8), custom_call_target="tpu_custom_call" | custom-call | tf_op jit(solution)/shard_map/second/pallas_call | solution.py:399
  57.6 3.6 %collective-permute-start.12 = (bf16[128,128]{1,0:T(8,128)(2,1)S(1)}, bf16[128,128]{1,0:T(8,128)(2,1)S(1)}, u32[]{:S(2)}, u32[]{:S(2)}) collective-permute-start(bf16[128,128]{1,0:T(8,128)(2,1)S(1)} %get-tuple-element.21), channel_id=1, source_target_pairs={{0,3},{1,2},{2,1},{3,0},{4,7},{5,6},{6,5},{7,4},{8,11},{9,10},{10,... | collective-permute-start | bytes 98312 | tf_op jit(solution)/shard_map/ppermute | solution.py:313
  61.2 0.0 collective-permute-start.11
  61.2 0.9 %collective-permute-start.10 = (bf16[128,128]{1,0:T(8,128)(2,1)S(1)}, bf16[128,128]{1,0:T(8,128)(2,1)S(1)}, u32[]{:S(2)}, u32[]{:S(2)}) collective-permute-start(bf16[128,128]{1,0:T(8,128)(2,1)S(1)} %get-tuple-element.23), channel_id=1, source_target_pairs={{0,1},{1,0},{2,3},{3,2},{4,5},{5,4},{6,7},{7,6},{8,9},{9,8},{10,11... | collective-permute-start | bytes 98312 | tf_op jit(solution)/shard_map/ppermute | solution.py:313
  62.1 1.3 %collective-permute-done.12.refs_3_ = bf16[128,128]{1,0:T(8,128)(2,1)S(1)} collective-permute-done((bf16[128,128]{1,0:T(8,128)(2,1)S(1)}, bf16[128,128]{1,0:T(8,128)(2,1)S(1)}, u32[]{:S(2)}, u32[]{:S(2)}) %collective-permute-start.12) | collective-permute-done | bytes 32800 | tf_op jit(solution)/shard_map/ppermute | solution.py:313
  63.4 2.6 %collective-permute-done.11.refs_2_ = bf16[128,128]{1,0:T(8,128)(2,1)S(1)} collective-permute-done((bf16[128,128]{1,0:T(8,128)(2,1)S(1)}, bf16[128,128]{1,0:T(8,128)(2,1)S(1)}, u32[]{:S(2)}, u32[]{:S(2)}) %collective-permute-start.11) | collective-permute-done | bytes 32800 | tf_op jit(solution)/shard_map/ppermute | solution.py:313
  66.0 0.0 collective-permute-done.10.refs_1_
  66.0 0.0 copy-done.5
  66.0 0.0 copy-done.15
  66.0 0.9 %final.1 = f32[2,32,256]{2,1,0:T(8,128)} custom-call(bf16[128,128]{1,0:T(8,128)(2,1)S(1)} %get-tuple-element.24.refs_0_, bf16[128,128]{1,0:T(8,128)(2,1)S(1)} %collective-permute-done.10.refs_1_, bf16[128,128]{1,0:T(8,128)(2,1)S(1)} %collective-permute-done.11.refs_2_, bf16[128,128]{1,0:T(8,128)(2,1)S(1)} %collective-permute-done.12.refs_3_, ...), custom_call_target="tpu_custom_call" | custom-call | tf_op jit(solution)/shard_map/final/pallas_call | solution.py:410
  (11 shorter events, 0.1 us)
Async XLA Ops:
  0.7 1.6 %copy-start = (bf16[32,128,256]{2,1,0:T(8,128)(2,1)S(1)}, bf16[32,128,256]{2,1,0:T(8,128)(2,1)}, u32[]{:S(2)}) copy-start(bf16[32,128,256]{2,1,0:T(8,128)(2,1)} %traces_ref.1) | copy-start | bytes 6291460
  2.3 1.0 %copy-start.1 = (bf16[8,128,256]{2,1,0:T(8,128)(2,1)S(1)}, bf16[8,128,256]{2,1,0:T(8,128)(2,1)}, u32[]{:S(2)}) copy-start(bf16[8,128,256]{2,1,0:T(8,128)(2,1)} %refs_4_.2) | copy-start | bytes 1572868
  3.3 0.9 %copy-start.2 = (bf16[256,256]{1,0:T(8,128)(2,1)S(1)}, bf16[256,256]{1,0:T(8,128)(2,1)}, u32[]{:S(2)}) copy-start(bf16[256,256]{1,0:T(8,128)(2,1)} %constant.26.forward_ref.refs_6_) | copy-start | bytes 393220
  4.2 0.8 %copy-start.7 = (bf16[256,128]{1,0:T(8,128)(2,1)S(1)}, bf16[256,128]{1,0:T(8,128)(2,1)}, u32[]{:S(2)}) copy-start(bf16[256,128]{1,0:T(8,128)(2,1)} %constant.32.gather_ref) | copy-start | bytes 196612
  5.1 0.8 %copy-start.9 = (bf16[256,128]{1,0:T(8,128)(2,1)S(1)}, bf16[256,128]{1,0:T(8,128)(2,1)}, u32[]{:S(2)}) copy-start(bf16[256,128]{1,0:T(8,128)(2,1)} %constant.31.taps_ref) | copy-start | bytes 196612
  5.9 0.7 %copy-start.10 = (s32[32,128]{1,0:T(8,128)S(1)}, s32[32,128]{1,0:T(8,128)}, u32[]{:S(2)}) copy-start(s32[32,128]{1,0:T(8,128)} %shift_ref.1) | copy-start | bytes 49156
  6.6 0.7 %copy-start.11 = (f32[32,64]{1,0:T(8,128)S(1)}, f32[32,64]{1,0:T(8,128)}, u32[]{:S(2)}) copy-start(f32[32,64]{1,0:T(8,128)} %deconv_ref.1) | copy-start | bytes 24580
  7.4 0.7 %copy-start.14 = (s32[2,32]{1,0:T(2,128)S(1)}, s32[2,32]{1,0:T(2,128)}, u32[]{:S(2)}) copy-start(s32[2,32]{1,0:T(2,128)} %refs_4_.3) | copy-start | bytes 772
  8.0 23.6 %copy-start.12 = (s32[2]{0:T(128)}, s32[2]{0:T(128)S(1)}, u32[]{:S(2)}) copy-start(s32[2]{0:T(128)S(1)} %pad_add_fusion.index_ref) | copy-start | bytes 28
  8.0 20.9 %copy-start.3 = (bf16[256,256]{1,0:T(8,128)(2,1)S(1)}, bf16[256,256]{1,0:T(8,128)(2,1)}, u32[]{:S(2)}) copy-start(bf16[256,256]{1,0:T(8,128)(2,1)} %constant.26.forward_ref.refs_6_) | copy-start | bytes 393220
  8.0 20.9 %copy-start.4 = (bf16[256,256]{1,0:T(8,128)(2,1)S(1)}, bf16[256,256]{1,0:T(8,128)(2,1)}, u32[]{:S(2)}) copy-start(bf16[256,256]{1,0:T(8,128)(2,1)} %constant.33.inverse_ref.refs_7_.refs_5_) | copy-start | bytes 393220
  8.1 20.9 %copy-start.6 = (bf16[4,128,256]{2,1,0:T(8,128)(2,1)S(1)}, bf16[4,128,256]{2,1,0:T(8,128)(2,1)}, u32[]{:S(2)}) copy-start(bf16[4,128,256]{2,1,0:T(8,128)(2,1)} %constant.34.spread_ref) | copy-start | bytes 786436
  13.6 6.7 %collective-permute-start = (bf16[528,128]{1,0:T(8,128)(2,1)S(1)}, bf16[528,128]{1,0:T(8,128)(2,1)S(1)}, u32[]{:S(2)}, u32[]{:S(2)}) collective-permute-start(bf16[528,128]{1,0:T(8,128)(2,1)S(1)} %get-tuple-element.10), channel_id=1, source_target_pairs={{0,1},{1,0},{2,3},{3,2},{4,5},{5,4},{6,7},{7,6},{8,9},{9,8},{10,11... | collective-permute-start | bytes 405512 | tf_op jit(solution)/shard_map/ppermute | solution.py:313
  20.3 8.6 %collective-permute-start.1 = (bf16[528,128]{1,0:T(8,128)(2,1)S(1)}, bf16[528,128]{1,0:T(8,128)(2,1)S(1)}, u32[]{:S(2)}, u32[]{:S(2)}) collective-permute-start(bf16[528,128]{1,0:T(8,128)(2,1)S(1)} %add_convert_fusion.1.mine_ref), channel_id=1, source_target_pairs={{0,2},{1,3},{2,0},{3,1},{4,6},{5,7},{6,4},{7,5},{8,10},{9,11},{10,... | collective-permute-start | bytes 405512 | tf_op jit(solution)/shard_map/ppermute | solution.py:313
  31.6 22.2 %copy-start.8 = (bf16[256,128]{1,0:T(8,128)(2,1)S(1)}, bf16[256,128]{1,0:T(8,128)(2,1)}, u32[]{:S(2)}) copy-start(bf16[256,128]{1,0:T(8,128)(2,1)} %constant.32.gather_ref) | copy-start | bytes 196612
  31.6 22.2 %copy-start.13 = (s32[2]{0:T(128)S(1)}, s32[2]{0:T(128)}, u32[]{:S(2)}) copy-start(s32[2]{0:T(128)} %copy-done.12) | copy-start | bytes 28
  31.6 1.5 %collective-permute-start.2 = (bf16[4,256,128]{2,1,0:T(8,128)(2,1)S(1)}, bf16[4,256,128]{2,1,0:T(8,128)(2,1)S(1)}, u32[]{:S(2)}, u32[]{:S(2)}) collective-permute-start(bf16[4,256,128]{2,1,0:T(8,128)(2,1)S(1)} %get-tuple-element.14), channel_id=1, source_target_pairs={{0,4},{4,0},{8,12},{12,8},{16,20},{20,16},{24,28},{28,24},{1,5},{5... | collective-permute-start | bytes 786440 | tf_op jit(solution)/shard_map/ppermute | solution.py:313
  33.9 5.2 %collective-permute-start.5 = (bf16[256,128]{1,0:T(8,128)(2,1)S(1)}, bf16[256,128]{1,0:T(8,128)(2,1)S(1)}, u32[]{:S(2)}, u32[]{:S(2)}) collective-permute-start(bf16[256,128]{1,0:T(8,128)(2,1)S(1)} %get-tuple-element.17), channel_id=1, source_target_pairs={{0,24},{4,28},{8,16},{12,20},{16,8},{20,12},{24,0},{28,4},{1,25},{... | collective-permute-start | bytes 196616 | tf_op jit(solution)/shard_map/ppermute | solution.py:313
  36.2 4.3 %collective-permute-start.4 = (bf16[256,128]{1,0:T(8,128)(2,1)S(1)}, bf16[256,128]{1,0:T(8,128)(2,1)S(1)}, u32[]{:S(2)}, u32[]{:S(2)}) collective-permute-start(bf16[256,128]{1,0:T(8,128)(2,1)S(1)} %get-tuple-element.18), channel_id=1, source_target_pairs={{0,16},{4,20},{8,24},{12,28},{16,0},{20,4},{24,8},{28,12},{1,17},{... | collective-permute-start | bytes 196616 | tf_op jit(solution)/shard_map/ppermute | solution.py:313
  36.7 4.3 %collective-permute-start.3 = (bf16[256,128]{1,0:T(8,128)(2,1)S(1)}, bf16[256,128]{1,0:T(8,128)(2,1)S(1)}, u32[]{:S(2)}, u32[]{:S(2)}) collective-permute-start(bf16[256,128]{1,0:T(8,128)(2,1)S(1)} %get-tuple-element.19), channel_id=1, source_target_pairs={{0,8},{4,12},{8,0},{12,4},{16,24},{20,28},{24,16},{28,20},{1,9},{5... | collective-permute-start | bytes 196616 | tf_op jit(solution)/shard_map/ppermute | solution.py:313
  39.1 1.9 %copy-start.16 = (bf16[256,128]{1,0:T(8,128)(2,1)}, bf16[256,128]{1,0:T(8,128)(2,1)S(1)}, u32[]{:S(2)}) copy-start(bf16[256,128]{1,0:T(8,128)(2,1)S(1)} %collective-permute-done.5.refs_3_) | copy-start | bytes 196612
  40.5 0.6 copy-start.17
  41.0 0.6 copy-start.18
  41.6 24.4 %copy-start.5 = (bf16[256,256]{1,0:T(8,128)(2,1)S(1)}, bf16[256,256]{1,0:T(8,128)(2,1)}, u32[]{:S(2)}) copy-start(bf16[256,256]{1,0:T(8,128)(2,1)} %constant.33.inverse_ref.refs_7_.refs_5_) | copy-start | bytes 393220
  41.6 24.4 %copy-start.15 = (s32[2,32]{1,0:T(2,128)S(1)}, s32[2,32]{1,0:T(2,128)}, u32[]{:S(2)}) copy-start(s32[2,32]{1,0:T(2,128)} %refs_4_.3) | copy-start | bytes 772
  44.6 5.6 %collective-permute-start.8 = (bf16[256,128]{1,0:T(8,128)(2,1)}, bf16[256,128]{1,0:T(8,128)(2,1)S(1)}, u32[]{:S(2)}, u32[]{:S(2)}) collective-permute-start(bf16[256,128]{1,0:T(8,128)(2,1)} %get-tuple-element.16), channel_id=1, source_target_pairs={{0,24},{4,28},{8,16},{12,20},{16,8},{20,12},{24,0},{28,4},{1,25},{... | collective-permute-start | bytes 196616 | tf_op jit(solution)/shard_map/ppermute | solution.py:313
  46.1 4.8 %collective-permute-start.7 = (bf16[256,128]{1,0:T(8,128)(2,1)}, bf16[256,128]{1,0:T(8,128)(2,1)S(1)}, u32[]{:S(2)}, u32[]{:S(2)}) collective-permute-start(bf16[256,128]{1,0:T(8,128)(2,1)} %get-tuple-element.16), channel_id=1, source_target_pairs={{0,16},{4,20},{8,24},{12,28},{16,0},{20,4},{24,8},{28,12},{1,17},{... | collective-permute-start | bytes 196616 | tf_op jit(solution)/shard_map/ppermute | solution.py:313
  46.9 4.5 %collective-permute-start.6 = (bf16[256,128]{1,0:T(8,128)(2,1)}, bf16[256,128]{1,0:T(8,128)(2,1)S(1)}, u32[]{:S(2)}, u32[]{:S(2)}) collective-permute-start(bf16[256,128]{1,0:T(8,128)(2,1)} %get-tuple-element.16), channel_id=1, source_target_pairs={{0,8},{4,12},{8,0},{12,4},{16,24},{20,28},{24,16},{28,20},{1,9},{5... | collective-permute-start | bytes 196616 | tf_op jit(solution)/shard_map/ppermute | solution.py:313
  52.2 1.6 %collective-permute-start.9 = (bf16[4,256,128]{2,1,0:T(8,128)(2,1)S(1)}, bf16[4,256,128]{2,1,0:T(8,128)(2,1)S(1)}, u32[]{:S(2)}, u32[]{:S(2)}) collective-permute-start(bf16[4,256,128]{2,1,0:T(8,128)(2,1)S(1)} %pad_maximum_fusion.near_ref), channel_id=1, source_target_pairs={{0,4},{4,0},{8,12},{12,8},{16,20},{20,16},{24,28},{28,24},{1,5},{5... | collective-permute-start | bytes 786440 | tf_op jit(solution)/shard_map/ppermute | solution.py:313
  57.6 5.8 %collective-permute-start.12 = (bf16[128,128]{1,0:T(8,128)(2,1)S(1)}, bf16[128,128]{1,0:T(8,128)(2,1)S(1)}, u32[]{:S(2)}, u32[]{:S(2)}) collective-permute-start(bf16[128,128]{1,0:T(8,128)(2,1)S(1)} %get-tuple-element.21), channel_id=1, source_target_pairs={{0,3},{1,2},{2,1},{3,0},{4,7},{5,6},{6,5},{7,4},{8,11},{9,10},{10,... | collective-permute-start | bytes 98312 | tf_op jit(solution)/shard_map/ppermute | solution.py:313
  61.2 4.8 %collective-permute-start.11 = (bf16[128,128]{1,0:T(8,128)(2,1)S(1)}, bf16[128,128]{1,0:T(8,128)(2,1)S(1)}, u32[]{:S(2)}, u32[]{:S(2)}) collective-permute-start(bf16[128,128]{1,0:T(8,128)(2,1)S(1)} %get-tuple-element.22), channel_id=1, source_target_pairs={{0,2},{1,3},{2,0},{3,1},{4,6},{5,7},{6,4},{7,5},{8,10},{9,11},{10,... | collective-permute-start | bytes 98312 | tf_op jit(solution)/shard_map/ppermute | solution.py:313
  61.2 4.8 %collective-permute-start.10 = (bf16[128,128]{1,0:T(8,128)(2,1)S(1)}, bf16[128,128]{1,0:T(8,128)(2,1)S(1)}, u32[]{:S(2)}, u32[]{:S(2)}) collective-permute-start(bf16[128,128]{1,0:T(8,128)(2,1)S(1)} %get-tuple-element.23), channel_id=1, source_target_pairs={{0,1},{1,0},{2,3},{3,2},{4,5},{5,4},{6,7},{7,6},{8,9},{9,8},{10,11... | collective-permute-start | bytes 98312 | tf_op jit(solution)/shard_map/ppermute | solution.py:313

commit v2 on v1

v2 whole, which is shorter than its diff:
```python
import functools
import math

import jax
import jax.numpy as jnp
import numpy as np
from jax import lax
from jax.experimental import pallas as pl
from jax.experimental.pallas import tpu as pltpu
from jax.sharding import PartitionSpec as P

NT = 256
NF = 128
TAPS = 64
KSHIFT = 64
LANES = 128
GROUP = 8
NG = NF // GROUP

F32 = jnp.float32
BF16 = jnp.bfloat16
NN = (((1,), (0,)), ((), ()))
NT_DIMS = (((1,), (1,)), ((), ()))


def make_tables(source_local):
    sample = np.arange(NT)
    bins = np.arange(NF)
    angles = 2.0 * np.pi / NT * (bins[:, None] * sample[None, :] % NT)
    forward = np.concatenate([np.cos(angles), -np.sin(angles)], axis=0)
    weights = np.where(bins == 0, 1.0, 2.0) / NT
    inverse = (forward * np.concatenate([weights, weights])[:, None]).T
    tap = np.arange(TAPS, dtype=np.float64)
    fraction = np.arange(KSHIFT) * (TAPS / (4.0 * KSHIFT))
    offset = tap[None, :] - 0.375 * TAPS - fraction[:, None]
    window = 0.5 - 0.5 * np.cos(2.0 * np.pi * (tap + 0.5) / TAPS)
    tap_spec = forward[:, :TAPS] @ (np.sinc(offset) * window[None, :]).T
    width = source_local * GROUP
    source_of = np.arange(width) // GROUP
    blocks = LANES // source_local
    pick = (source_of[:, None] == np.arange(source_local)[None, :]).astype(np.float64)
    gather = np.tile(pick, (1, blocks))
    spread = np.zeros((blocks, LANES, width))
    for block in range(blocks):
        spread[block, block * source_local : (block + 1) * source_local] = pick.T
    return dict(
        forward=jnp.asarray(forward, F32).astype(BF16),
        inverse=jnp.asarray(inverse, F32).astype(BF16),
        taps=jnp.asarray(np.tile(tap_spec, (1, LANES // KSHIFT)), F32),
        gather=jnp.asarray(gather, F32).astype(BF16),
        spread=jnp.asarray(spread, F32).astype(BF16),
    )


def mm(left, right, dims=NN):
    return lax.dot_general(left, right, dims, preferred_element_type=F32)


def interleave(first, second):
    width = first.shape[-1]
    pair = jnp.stack(
        [first.reshape(NG, GROUP, width), second.reshape(NG, GROUP, width)], axis=1
    )
    return pair.reshape(NG, 2 * GROUP, width)


def same_bin(rows, lanes):
    row = lax.broadcasted_iota(jnp.int32, (rows, lanes), 0)
    lane = lax.broadcasted_iota(jnp.int32, (rows, lanes), 1)
    return (row % GROUP) == (lane % GROUP)


def store_vector(vector_ref, place, re, im):
    receivers = re.shape[-1]
    vector_ref[:, place, :, :receivers] = interleave(re, im).astype(BF16)
    vector_ref[:, place, :, receivers:] = interleave(-im, re).astype(BF16)


def unpack(spectra_ref):
    receivers = spectra_ref.shape[-1]
    values = spectra_ref[...].astype(F32).reshape(NG, 2, GROUP, receivers)
    return values[:, 0].reshape(NF, receivers), values[:, 1].reshape(NF, receivers)


def apply_matrix(matrix_ref, vector_ref, kept_ref, gather, store):
    pairs = vector_ref.shape[1] // 2
    rows = 2 * pairs * 2 * GROUP
    width = matrix_ref.shape[1] * matrix_ref.shape[2]
    diagonal = same_bin(rows, width)
    block_of = lax.broadcasted_iota(jnp.int32, (pairs, GROUP, LANES), 2) // (LANES // 4)

    for group in range(NG):
        vector = vector_ref[group].reshape(rows, vector_ref.shape[-1])
        matrix = matrix_ref[group].reshape(width, matrix_ref.shape[-1])
        full = mm(vector, matrix, NT_DIMS)
        kept_ref[group * rows : (group + 1) * rows, :] = jnp.where(diagonal, full, 0.0).astype(BF16)

    for couple in range(NG // 2):
        kept = kept_ref[couple * 2 * rows : (couple + 1) * 2 * rows, :]
        spread = mm(kept, gather).reshape(2, pairs, 2, 2, GROUP, LANES)
        both = []
        for one in range(2):
            real = jnp.where(block_of == 0, spread[one, :, 0, 0], spread[one, :, 1, 0])
            imag = jnp.where(block_of == 2, spread[one, :, 0, 1], spread[one, :, 1, 1])
            both.append(jnp.where(block_of < 2, real, imag))
        store(couple * 2 * GROUP, jnp.concatenate(both, axis=1).astype(BF16))


def build_kernel(
    gain, index_ref, traces_hbm, shift_hbm, deconv_hbm, focal_hbm, onset_hbm,
    forward_hbm, taps_hbm, gather_hbm, matrix_ref, sum_ref, own_ref,
    vector_ref, kept_ref, traces_ref, shift_ref, deconv_ref, focal_ref, onset_ref,
    forward_ref, taps_ref, gather_ref, trace_sem, small_sem, delay_ref,
):
    sources, receivers = shift_ref.shape
    pairs = focal_ref.shape[0] // 2
    small = [
        pltpu.make_async_copy(source, target, small_sem.at[place])
        for place, (source, target) in enumerate(
            [
                (forward_hbm, forward_ref),
                (deconv_hbm, deconv_ref),
                (focal_hbm, focal_ref),
                (taps_hbm, taps_ref),
                (shift_hbm, shift_ref),
                (gather_hbm, gather_ref),
                (onset_hbm, onset_ref),
            ]
        )
    ]
    chunks = trace_sem.shape[0]
    step = sources // chunks
    large = [
        pltpu.make_async_copy(
            traces_hbm.at[pl.ds(chunk * step, step)],
            traces_ref.at[pl.ds(chunk * step, step)],
            trace_sem.at[chunk],
        )
        for chunk in range(chunks)
    ]
    for copy in small[:5] + large + small[5:]:
        copy.start()
    small[0].wait()
    small[1].wait()
    forward = forward_ref[...]
    deconv = deconv_ref[...]
    deconv_high = deconv.astype(BF16)
    deconv_low = (deconv - deconv_high.astype(F32)).astype(BF16)
    head = forward_ref[:, :TAPS]
    wave = (mm(head, deconv_high, NT_DIMS) + mm(head, deconv_low, NT_DIMS)) * gain
    wave_high = wave.astype(BF16)
    wave_low = (wave - wave_high.astype(F32)).astype(BF16)
    wave_both = jnp.concatenate([wave_high, wave_low], axis=1)
    small[3].wait()
    taps = taps_ref[...]
    owner = lax.broadcasted_iota(jnp.int32, (2 * sources, 2 * LANES), 0) % sources
    place = lax.broadcasted_iota(jnp.int32, (2 * sources, 2 * LANES), 1) // KSHIFT
    zeros = jnp.zeros((KSHIFT, receivers), F32)
    kinds = lax.broadcasted_iota(jnp.int32, (KSHIFT, receivers), 0)
    for quad in range(sources // 4):
        spread = mm(wave_both, (owner == place + 4 * quad).astype(F32).astype(BF16))
        for couple in range(2):
            lanes = slice(couple * LANES, (couple + 1) * LANES)
            wave_re, wave_im = spread[:NF, lanes], spread[NF:, lanes]
            taps_re, taps_im = taps[:NF], taps[NF:]
            delay_re = taps_re * wave_re - taps_im * wave_im
            delay_im = taps_re * wave_im + taps_im * wave_re
            delay_ref[2 * quad + couple] = jnp.concatenate([delay_re, delay_im], axis=0).astype(BF16)

    small[2].wait()
    own_ref[...] = focal_ref[index_ref[0]]
    for place in range(2 * pairs):
        spectra = mm(forward, focal_ref[place], NT_DIMS)
        store_vector(vector_ref, place, spectra[:NF], spectra[NF:])

    small[4].wait()
    for couple in range(sources // 2):
        if (2 * couple) % step == 0:
            large[2 * couple // step].wait()
        signals = traces_ref[2 * couple : 2 * couple + 2].reshape(2 * receivers, NT)
        raw = mm(forward, signals, NT_DIMS)
        hot = [
            (kinds == shift_ref[2 * couple + half : 2 * couple + half + 1, :]).astype(F32)
            for half in range(2)
        ]
        hot = jnp.concatenate(
            [
                jnp.concatenate([hot[0], zeros], axis=1),
                jnp.concatenate([zeros, hot[1]], axis=1),
            ],
            axis=0,
        ).astype(BF16)
        delay = mm(delay_ref[couple], hot)
        re = raw[:NF] * delay[:NF] - raw[NF:] * delay[NF:]
        im = raw[:NF] * delay[NF:] + raw[NF:] * delay[:NF]
        matrix_ref[:, couple, :, :receivers] = interleave(
            re[:, :receivers], re[:, receivers:]
        ).astype(BF16)
        matrix_ref[:, couple, :, receivers:] = interleave(
            im[:, :receivers], im[:, receivers:]
        ).astype(BF16)

    def store(row, value):
        for pair in range(pairs):
            sum_ref[pair * NF + row : pair * NF + row + 2 * GROUP, :] = value[pair]

    small[5].wait()
    small[6].wait()
    apply_matrix(matrix_ref, vector_ref, kept_ref, gather_ref[...], store)
    rcv_index = index_ref[1]
    own = onset_ref[...].astype(F32)
    own = jnp.concatenate([own[0:1], own[1:2]] * 2, axis=1)
    own = jnp.broadcast_to(own, (2 * GROUP, LANES))
    row = lax.broadcasted_iota(jnp.int32, own.shape, 0)
    lane = lax.broadcasted_iota(jnp.int32, own.shape, 1)
    here = (row == rcv_index // 2) & (lane // (LANES // 2) == rcv_index % 2)
    sum_ref[pairs * NF :, :] = jnp.where(here, own, 0.0).astype(BF16)


def split_halves(first, second):
    lane = lax.broadcasted_iota(jnp.int32, first.shape, 1)
    low = lane < LANES // 2
    re = jnp.where(low, first, pltpu.roll(second, LANES // 2, 1))
    im = jnp.where(low, pltpu.roll(first, LANES // 2, 1), second)
    return jnp.concatenate([re, im], axis=0)


def mute(signal, onset):
    sample = lax.broadcasted_iota(jnp.int32, signal.shape, 0)
    folded = jnp.minimum(sample, NT - sample).astype(F32)
    return jnp.where(folded < onset, signal, 0.0)


def adjoint_kernel(
    index_ref, mine_ref, other_ref, matrix_ref, forward_ref, inverse_ref, spread_ref, *refs
):
    field_ref, vector_ref, echo_ref = refs[-3:]
    pairs = (len(refs) - 3) // 2
    keep_refs, send_refs = refs[:pairs], refs[pairs : 2 * pairs]
    shot_index = index_ref[0]
    rcv_index = index_ref[1]
    core = shot_index % 2
    chip = shot_index // 2
    receivers = matrix_ref.shape[-1] // 2
    sources = 2 * matrix_ref.shape[1]
    width = sources * GROUP
    forward = forward_ref[...]
    inverse = inverse_ref[...]
    onsets = mine_ref[pairs * NF :, :].astype(F32) + other_ref[pairs * NF :, :].astype(F32)
    owned = jnp.zeros((NT, LANES), F32)

    for couple in range(pairs // 2):
        rows = slice(2 * couple * NF, 2 * (couple + 1) * NF)
        total = mine_ref[rows, :].astype(F32) + other_ref[rows, :].astype(F32)
        spectra = split_halves(total[:NF], total[NF:]).astype(BF16)
        signal = mute(mm(inverse, spectra), onsets[couple : couple + 1, :])
        owned = jnp.where(rcv_index // 2 == couple, signal, owned)
        echo_ref[couple] = mm(forward, signal.astype(BF16)).astype(BF16)

    diagonal = same_bin(2 * NF, width)
    for half in range(2):
        table_kept = spread_ref[2 * half + core]
        table_sent = spread_ref[2 * half + 1 - core]
        for couple in range(pairs // 2):
            slot = (2 * couple + half) ^ chip
            values = echo_ref[couple]
            kept = jnp.where(diagonal, mm(values, table_kept), 0.0)
            sent = jnp.where(diagonal, mm(values, table_sent), 0.0)
            for part in range(2):
                rows = slice(part * NF, (part + 1) * NF)
                vector_ref[:, part, slot] = interleave(kept[rows], sent[rows]).astype(BF16)

    owned = jnp.where(rcv_index % 2 == 1, pltpu.roll(owned, LANES // 2, 1), owned)
    flipped = jnp.transpose(owned)[: LANES // 2]
    field_ref[...] = flipped.reshape(field_ref.shape)

    def one(group):
        vector = vector_ref[group].reshape(2 * pairs * 2 * GROUP, width)
        matrix = matrix_ref[group].reshape(width, 2 * receivers)
        full = mm(vector, matrix).reshape(2, pairs, 2, GROUP, 2 * receivers)
        re = full[0, ..., :receivers] + full[1, ..., receivers:]
        im = full[1, ..., :receivers] - full[0, ..., receivers:]
        return re, im

    for couple in range(NG // 2):
        even = one(2 * couple)
        odd = one(2 * couple + 1)
        for part in range(2):
            both = jnp.concatenate([even[part], odd[part]], axis=2).astype(BF16)
            row = part * NF + couple * 2 * GROUP
            for slot in range(pairs):
                keep_refs[slot][row : row + 2 * GROUP, :] = both[slot, 0]
                send_refs[slot][row : row + 2 * GROUP, :] = both[slot, 1]


def downgoing_kernel(*refs):
    parts = refs[:-6]
    focal_ref, onset_ref, forward_ref, inverse_ref, field_ref, plus_ref = refs[-6:]
    total = parts[0][...].astype(F32)
    for part in parts[1:]:
        total = total + part[...].astype(F32)
    onset = onset_ref[...].astype(F32)
    signal = mute(mm(inverse_ref[...], total.astype(BF16)), onset)
    field = focal_ref[...].astype(F32) + jnp.transpose(signal)
    field_ref[0] = field
    spectra = mm(forward_ref[...], field.astype(BF16), NT_DIMS)
    plus_ref[...] = interleave(spectra[:NF], spectra[NF:]).astype(BF16)


def second_kernel(pairs, index_ref, *refs):
    near_refs, far_refs = refs[:pairs], refs[pairs : 2 * pairs]
    matrix_ref, gather_ref = refs[2 * pairs : 2 * pairs + 2]
    sum_refs = refs[2 * pairs + 2 : -2]
    vector_ref, kept_ref = refs[-2:]
    shot_index = index_ref[0]
    rcv_index = index_ref[1]
    core = shot_index % 2
    chip = shot_index // 2
    for distance in range(pairs):
        slot = (chip ^ distance) ^ rcv_index
        store_vector(vector_ref, 2 * slot + core, *unpack(near_refs[distance]))
        store_vector(vector_ref, 2 * slot + 1 - core, *unpack(far_refs[distance]))

    def store(row, value):
        for slot in range(pairs):
            sum_refs[slot][row : row + 2 * GROUP, :] = value[slot]

    apply_matrix(matrix_ref, vector_ref, kept_ref, gather_ref[...], store)


def final_kernel(*refs):
    parts = refs[:-3]
    onset_ref, inverse_ref, field_ref = refs[-3:]
    total = parts[0][...].astype(F32)
    for part in parts[1:]:
        total = total + part[...].astype(F32)
    spectra = split_halves(total, total).astype(BF16)
    onset = onset_ref[...].astype(F32)
    onset = jnp.concatenate([onset[0:1], onset[1:2]] * 2, axis=1)
    signal = mute(mm(inverse_ref[...], spectra), onset)
    field_ref[...] = jnp.transpose(signal)[: LANES // 2].reshape(field_ref.shape)


def vmem(count):
    return [pl.BlockSpec(memory_space=pltpu.VMEM) for _ in range(count)]


def smem():
    return [pl.BlockSpec(memory_space=pltpu.SMEM)]


def hbm(count):
    return [pl.BlockSpec(memory_space=pltpu.HBM) for _ in range(count)]


def call(kernel, name, out_shape, in_specs, scratch=()):
    many = isinstance(out_shape, (tuple, list))
    return pl.pallas_call(
        kernel,
        name=name,
        out_shape=out_shape,
        in_specs=in_specs,
        out_specs=vmem(len(out_shape)) if many else vmem(1)[0],
        scratch_shapes=list(scratch),
        compiler_params=pltpu.CompilerParams(vmem_limit_bytes=40 << 20),
    )


def exchange(value, axis, distance):
    count = lax.axis_size(axis)
    return lax.ppermute(value, axis, [(place, place ^ distance) for place in range(count)])


def add_rounded(left, right):
    return (left.astype(F32) + right.astype(F32)).astype(BF16)


def body(traces, shift_index, deconv, focal_start, onset_source, onset_receiver):
    shot_count = lax.axis_size("shot")
    rcv_count = lax.axis_size("rcv")
    sources, receivers, _ = traces.shape
    focal_total = focal_start.shape[0]
    pairs = focal_total // 2
    assert onset_source.shape[0] == 2 and pairs == rcv_count
    assert focal_total == shot_count and 4 * sources == LANES and receivers == LANES
    gain = 1.0 / math.sqrt(NT * receivers * rcv_count)
    tables = make_tables(sources)
    index = jnp.stack([lax.axis_index("shot"), lax.axis_index("rcv")]).astype(jnp.int32)
    shape = jax.ShapeDtypeStruct
    vector = pltpu.VMEM((NG, 2 * pairs, 2 * GROUP, 2 * receivers), BF16)
    kept = pltpu.VMEM((NG * 2 * pairs * 2 * GROUP, sources * GROUP), BF16)

    def buffer(value):
        return pltpu.VMEM(value.shape, value.dtype)

    inputs = (
        traces, shift_index, deconv, focal_start, onset_source,
        tables["forward"], tables["taps"], tables["gather"],
    )
    matrix, partial, focal_own = call(
        functools.partial(build_kernel, gain),
        "build",
        (
            shape((NG, sources // 2, 2 * GROUP, 2 * receivers), BF16),
            shape((pairs * NF + 2 * GROUP, LANES), BF16),
            shape((receivers, NT), BF16),
        ),
        smem() + hbm(len(inputs)),
        [vector, kept]
        + [buffer(value) for value in inputs]
        + [pltpu.SemaphoreType.DMA((4,)), pltpu.SemaphoreType.DMA((7,))]
        + [pltpu.VMEM((sources // 2, 2 * NF, LANES), BF16)],
    )(index, *inputs)

    distance = 1
    mine, other = partial, exchange(partial, "rcv", 1)
    while 2 * distance < rcv_count:
        distance *= 2
        mine = add_rounded(mine, other)
        other = exchange(mine, "rcv", distance)

    field = shape((2 * NF, receivers), BF16)
    *blocks, upgoing_first = call(
        adjoint_kernel,
        "adjoint",
        [field] * (2 * pairs) + [shape((2, sources, NT), F32)],
        smem() + vmem(6),
        [
            pltpu.VMEM((NG, 2, pairs, 2 * GROUP, sources * GROUP), BF16),
            pltpu.VMEM((pairs // 2, 2 * NF, LANES), BF16),
        ],
    )(index, mine, other, matrix, tables["forward"], tables["inverse"], tables["spread"])

    parts = []
    for distance in reversed(range(pairs)):
        block = add_rounded(blocks[distance], exchange(blocks[pairs + distance], "shot", 1))
        parts.append(exchange(block, "shot", 2 * distance) if distance else block)

    downgoing, plus = call(
        downgoing_kernel,
        "downgoing",
        (
            shape((1, receivers, NT), F32),
            shape((NG, 2 * GROUP, receivers), BF16),
        ),
        vmem(pairs + 4),
    )(*parts, focal_own, onset_receiver, tables["forward"], tables["inverse"])

    near = [plus]
    for distance in range(1, pairs):
        near.append(exchange(plus, "shot", 2 * distance))
    far = [exchange(value, "shot", 1) for value in near]

    parts = call(
        functools.partial(second_kernel, pairs),
        "second",
        [shape((NF, LANES), BF16)] * pairs,
        smem() + vmem(2 * pairs + 2),
        [vector, kept],
    )(index, *near, *far, matrix, tables["gather"])

    parts = [parts[0]] + [
        exchange(parts[distance], "rcv", distance) for distance in range(1, rcv_count)
    ]
    upgoing_second = call(
        final_kernel, "final", shape((2, sources, NT), F32), vmem(len(parts) + 2)
    )(*parts, onset_source, tables["inverse"])
    return (upgoing_first, downgoing, upgoing_second)


def solution(mesh):
    placed = (
        P("shot", "rcv", None),
        P("shot", "rcv"),
        P("shot", None),
        P(None, "rcv", None),
        P("rcv", "shot"),
        P("shot", "rcv"),
    )
    return jax.shard_map(
        body,
        mesh=mesh,
        in_specs=placed,
        out_specs=(P("rcv", "shot", None), P("shot", "rcv", None), P("rcv", "shot", None)),
        check_vma=False,
    )
```

time: 67.5 us -> 61.5 us (0.911)
  Pallas kernels: 16 us -> 11.5 us
  local copies, waits for them, and re-layouts: 8.65 us -> 7.41 us
  starting transfers between devices: 17.4 us -> 18.6 us
  other arithmetic: 1.06 us -> 0.2 us
    pallas_call x3, Pallas kernels: 9.49 us -> 5.14 us  [the longest x1 2.41 us: body(): call(adjoint_kernel, 'adjoint', [field] * (2 * pairs) + [shape((2, source...]
    ppermute x13 -> x19, starting transfers between devices: 17.4 us -> 18.6 us  [exchange(): lax.ppermute(value, axis, [(place, place ^ distance) for place in range(c...]
    another operation x1 -> x0, other arithmetic: 0.87 us -> none  [body(): near = jnp.stack(near)]
    unnamed x38 -> x26, local copies, waits for them, and re-layouts: 7.99 us -> 7.41 us
    ppermute x13 -> x19, waiting for transfers between devices: 23.1 us -> 22.6 us  [exchange(): lax.ppermute(value, axis, [(place, place ^ distance) for place in range(c...]
  transfers between devices with their start and end apart: 13 -> 19, of which waited for: 12 -> 13; matrix products, arithmetic and copies ran while one was open for 0% -> 0% of each run, Pallas kernels for 0% -> 0%
where the time goes in v2:
time: 61.5 us; the launch traced here: 61.1 us
  waiting for transfers between devices  22.6 us (37%)
  starting transfers between devices  18.6 us (30%)
  Pallas kernels  11.5 us (19%)
  local copies, waits for them, and re-layouts  7.41 us (12%)
  between operations  0.72 us (1%)
    ppermute x19, waiting for transfers between devices, exchange(): lax.ppermute(value, axis, [(place, place ^ distance) for place in range(c...  22.6 us
    ppermute x19, starting transfers between devices, exchange(): lax.ppermute(value, axis, [(place, place ^ distance) for place in range(c...  18.6 us
    unnamed x26, local copies, waits for them, and re-layouts  7.41 us
    pallas_call x1, Pallas kernels, body(): call(functools.partial(build_kernel, gain), 'build', (shape((NG, sources...  5.46 us
    pallas_call x1, Pallas kernels, body(): call(adjoint_kernel, 'adjoint', [field] * (2 * pairs) + [shape((2, source...  2.41 us
    pallas_call x1, Pallas kernels, body(): call(functools.partial(second_kernel, pairs), 'second', [shape((NF, LANES...  1.78 us
  transfers between devices with their start and end apart: 19, of which 13 were waited for; matrix products, arithmetic and copies ran while one was open for 0% of the time, Pallas kernels for 0%

profile of v2, /device:TPU:0, one launch (start us, length us, event | category | flops | bytes accessed | tf_op | source)
XLA Modules:
  0.0 61.1 jit_solution(2431368000299075424)
XLA Ops:
  0.6 0.1 pad_add_fusion.index_ref
  0.7 0.0 copy-start
  0.7 1.6 %copy-done = bf16[32,128,256]{2,1,0:T(8,128)(2,1)S(1)} copy-done((bf16[32,128,256]{2,1,0:T(8,128)(2,1)S(1)}, bf16[32,128,256]{2,1,0:T(8,128)(2,1)}, u32[]{:S(2)}) %copy-start) | copy-done | bytes 2097176
  2.3 0.0 copy-start.1
  2.3 0.9 %copy-done.1 = bf16[256,256]{1,0:T(8,128)(2,1)S(1)} copy-done((bf16[256,256]{1,0:T(8,128)(2,1)S(1)}, bf16[256,256]{1,0:T(8,128)(2,1)}, u32[]{:S(2)}) %copy-start.1) | copy-done | bytes 131096
  3.2 0.0 copy-start.4
  3.2 1.0 %copy-done.4 = bf16[8,128,256]{2,1,0:T(8,128)(2,1)S(1)} copy-done((bf16[8,128,256]{2,1,0:T(8,128)(2,1)S(1)}, bf16[8,128,256]{2,1,0:T(8,128)(2,1)}, u32[]{:S(2)}) %copy-start.4) | copy-done | bytes 524312
  4.3 0.8 %copy-done.6 = bf16[256,128]{1,0:T(8,128)(2,1)S(1)} copy-done((bf16[256,128]{1,0:T(8,128)(2,1)S(1)}, bf16[256,128]{1,0:T(8,128)(2,1)}, u32[]{:S(2)}) %copy-start.6) | copy-done | bytes 65560
  5.1 0.9 %copy-done.8 = f32[256,128]{1,0:T(8,128)S(1)} copy-done((f32[256,128]{1,0:T(8,128)S(1)}, f32[256,128]{1,0:T(8,128)}, u32[]{:S(2)}) %copy-start.8) | copy-done | bytes 131096
  6.0 0.0 copy-start.9
  6.0 0.7 %copy-done.9 = s32[32,128]{1,0:T(8,128)S(1)} copy-done((s32[32,128]{1,0:T(8,128)S(1)}, s32[32,128]{1,0:T(8,128)}, u32[]{:S(2)}) %copy-start.9) | copy-done | bytes 16408
  6.7 0.0 copy-start.10
  6.7 0.7 %copy-done.10 = f32[32,64]{1,0:T(8,128)S(1)} copy-done((f32[32,64]{1,0:T(8,128)S(1)}, f32[32,64]{1,0:T(8,128)}, u32[]{:S(2)}) %copy-start.10) | copy-done | bytes 8216
  7.4 0.7 %copy-done.11 = s32[2,32]{1,0:T(2,128)S(1)} copy-done((s32[2,32]{1,0:T(2,128)S(1)}, s32[2,32]{1,0:T(2,128)}, u32[]{:S(2)}) %copy-start.11) | copy-done | bytes 280
  8.1 5.5 %build.1 = (bf16[16,16,16,256]{3,2,1,0:T(8,128)(2,1)S(1)}, bf16[528,128]{1,0:T(8,128)(2,1)S(1)}, bf16[128,256]{1,0:T(8,128)(2,1)S(1)}) custom-call(s32[2]{0:T(128)S(1)} %pad_add_fusion.index_ref, bf16[32,128,256]{2,1,0:T(8,128)(2,1)S(1)} %copy-done, s32[32,128]{1,0:T(8,128)S(1)} %copy-done.9, f32[32,64]{1,0:T(8,128)S(1)} %copy-done.10, ...), custom_call_target="tpu_custom_call" | custom-call | tf_op jit(solution)/shard_map/build/pallas_call | solution.py:400
  13.6 0.0 copy-start.12
  13.6 3.1 %collective-permute-start = (bf16[528,128]{1,0:T(8,128)(2,1)S(1)}, bf16[528,128]{1,0:T(8,128)(2,1)S(1)}, u32[]{:S(2)}, u32[]{:S(2)}) collective-permute-start(bf16[528,128]{1,0:T(8,128)(2,1)S(1)} %get-tuple-element.21), channel_id=1, source_target_pairs={{0,1},{1,0},{2,3},{3,2},{4,5},{5,4},{6,7},{7,6},{8,9},{9,8},{10,11... | collective-permute-start | bytes 405512 | tf_op jit(solution)/shard_map/ppermute | solution.py:371
  16.7 3.6 %collective-permute-done = bf16[528,128]{1,0:T(8,128)(2,1)S(1)} collective-permute-done((bf16[528,128]{1,0:T(8,128)(2,1)S(1)}, bf16[528,128]{1,0:T(8,128)(2,1)S(1)}, u32[]{:S(2)}, u32[]{:S(2)}) %collective-permute-start) | collective-permute-done | bytes 135200 | tf_op jit(solution)/shard_map/ppermute | solution.py:371
  20.3 2.8 %collective-permute-start.1 = (bf16[528,128]{1,0:T(8,128)(2,1)S(1)}, bf16[528,128]{1,0:T(8,128)(2,1)S(1)}, u32[]{:S(2)}, u32[]{:S(2)}) collective-permute-start(bf16[528,128]{1,0:T(8,128)(2,1)S(1)} %add_convert_fusion.mine_ref), channel_id=1, source_target_pairs={{0,2},{1,3},{2,0},{3,1},{4,6},{5,7},{6,4},{7,5},{8,10},{9,11},{10,... | collective-permute-start | bytes 405512 | tf_op jit(solution)/shard_map/ppermute | solution.py:371
  23.1 5.8 %collective-permute-done.1.other_ref = bf16[528,128]{1,0:T(8,128)(2,1)S(1)} collective-permute-done((bf16[528,128]{1,0:T(8,128)(2,1)S(1)}, bf16[528,128]{1,0:T(8,128)(2,1)S(1)}, u32[]{:S(2)}, u32[]{:S(2)}) %collective-permute-start.1) | collective-permute-done | bytes 135200 | tf_op jit(solution)/shard_map/ppermute | solution.py:371
  28.9 0.0 copy-done.2
  28.9 0.0 copy-done.3
  28.9 0.0 copy-done.5
  28.9 0.0 copy-start.7
  29.0 2.4 %adjoint.1 = (bf16[256,128]{1,0:T(8,128)(2,1)S(1)}, bf16[256,128]{1,0:T(8,128)(2,1)S(1)}, bf16[256,128]{1,0:T(8,128)(2,1)S(1)}, bf16[256,128]{1,0:T(8,128)(2,1)S...) custom-call(s32[2]{0:T(128)S(1)} %pad_add_fusion.index_ref, ...), custom_call_target="tpu_custom_call" | custom-call | tf_op jit(solution)/shard_map/adjoint/pallas_call | solution.py:423
  31.4 0.0 collective-permute-start.2
  31.4 0.5 collective-permute-start.4
  31.9 0.0 collective-permute-start.6
  31.9 0.5 collective-permute-start.8
  32.4 0.2 collective-permute-done.2
  32.6 2.4 %collective-permute-start.3 = (bf16[256,128]{1,0:T(8,128)(2,1)S(1)}, bf16[256,128]{1,0:T(8,128)(2,1)S(1)}, u32[]{:S(2)}, u32[]{:S(2)}) collective-permute-start(bf16[256,128]{1,0:T(8,128)(2,1)S(1)} %add_convert_fusion.4), channel_id=1, source_target_pairs={{0,24},{4,28},{8,16},{12,20},{16,8},{20,12},{24,0},{28,4},{1,25},{... | collective-permute-start | bytes 196616 | tf_op jit(solution)/shard_map/ppermute | solution.py:371
  35.0 0.0 collective-permute-done.4
  35.0 0.6 collective-permute-start.5
  35.6 0.0 collective-permute-done.6
  35.6 0.8 %collective-permute-start.7 = (bf16[256,128]{1,0:T(8,128)(2,1)S(1)}, bf16[256,128]{1,0:T(8,128)(2,1)S(1)}, u32[]{:S(2)}, u32[]{:S(2)}) collective-permute-start(bf16[256,128]{1,0:T(8,128)(2,1)S(1)} %add_convert_fusion.2), channel_id=1, source_target_pairs={{0,8},{4,12},{8,0},{12,4},{16,24},{20,28},{24,16},{28,20},{1,9},{5... | collective-permute-start | bytes 196616 | tf_op jit(solution)/shard_map/ppermute | solution.py:371
  36.4 0.0 collective-permute-done.8
  36.4 1.5 %collective-permute-done.3.refs_0_ = bf16[256,128]{1,0:T(8,128)(2,1)S(1)} collective-permute-done((bf16[256,128]{1,0:T(8,128)(2,1)S(1)}, bf16[256,128]{1,0:T(8,128)(2,1)S(1)}, u32[]{:S(2)}, u32[]{:S(2)}) %collective-permute-start.3) | collective-permute-done | bytes 65568 | tf_op jit(solution)/shard_map/ppermute | solution.py:371
  37.9 1.5 %collective-permute-done.5.refs_1_ = bf16[256,128]{1,0:T(8,128)(2,1)S(1)} collective-permute-done((bf16[256,128]{1,0:T(8,128)(2,1)S(1)}, bf16[256,128]{1,0:T(8,128)(2,1)S(1)}, u32[]{:S(2)}, u32[]{:S(2)}) %collective-permute-start.5) | collective-permute-done | bytes 65568 | tf_op jit(solution)/shard_map/ppermute | solution.py:371
  39.4 0.6 collective-permute-done.7.refs_2_
  40.0 0.0 copy-done.12
  40.0 0.9 %downgoing.1 = (f32[1,128,256]{2,1,0:T(8,128)}, bf16[16,16,128]{2,1,0:T(8,128)(2,1)S(1)}) custom-call(bf16[256,128]{1,0:T(8,128)(2,1)S(1)} %collective-permute-done.3.refs_0_, bf16[256,128]{1,0:T(8,128)(2,1)S(1)} %collective-permute-done.5.refs_1_, bf16[256,128]{1,0:T(8,128)(2,1)S(1)} %collective-permute-done.7.refs_2_, ...), custom_call_target="tpu_custom_call" | custom-call | tf_op jit(solution)/shard_map/downgoing/pallas_call | solution.py:439
  40.9 1.5 %collective-permute-start.11 = (bf16[16,16,128]{2,1,0:T(8,128)(2,1)S(1)}, bf16[16,16,128]{2,1,0:T(8,128)(2,1)S(1)}, u32[]{:S(2)}, u32[]{:S(2)}) collective-permute-start(bf16[16,16,128]{2,1,0:T(8,128)(2,1)S(1)} %get-tuple-element.34.refs_0_), channel_id=1, source_target_pairs={{0,24},{4,28},{8,16},{12,20},{16,8},{20,12},{24,0},{28,4},{1,25},{... | collective-permute-start | bytes 196616 | tf_op jit(solution)/shard_map/ppermute | solution.py:371
  42.4 0.7 %collective-permute-start.10 = (bf16[16,16,128]{2,1,0:T(8,128)(2,1)S(1)}, bf16[16,16,128]{2,1,0:T(8,128)(2,1)S(1)}, u32[]{:S(2)}, u32[]{:S(2)}) collective-permute-start(bf16[16,16,128]{2,1,0:T(8,128)(2,1)S(1)} %get-tuple-element.34.refs_0_), channel_id=1, source_target_pairs={{0,16},{4,20},{8,24},{12,28},{16,0},{20,4},{24,8},{28,12},{1,17},{... | collective-permute-start | bytes 196616 | tf_op jit(solution)/shard_map/ppermute | solution.py:371
  43.1 1.3 %collective-permute-start.9 = (bf16[16,16,128]{2,1,0:T(8,128)(2,1)S(1)}, bf16[16,16,128]{2,1,0:T(8,128)(2,1)S(1)}, u32[]{:S(2)}, u32[]{:S(2)}) collective-permute-start(bf16[16,16,128]{2,1,0:T(8,128)(2,1)S(1)} %get-tuple-element.34.refs_0_), channel_id=1, source_target_pairs={{0,8},{4,12},{8,0},{12,4},{16,24},{20,28},{24,16},{28,20},{1,9},{5... | collective-permute-start | bytes 196616 | tf_op jit(solution)/shard_map/ppermute | solution.py:371
  44.4 0.0 collective-permute-start.12
  44.4 1.7 %collective-permute-done.11.refs_3_ = bf16[16,16,128]{2,1,0:T(8,128)(2,1)S(1)} collective-permute-done((bf16[16,16,128]{2,1,0:T(8,128)(2,1)S(1)}, bf16[16,16,128]{2,1,0:T(8,128)(2,1)S(1)}, u32[]{:S(2)}, u32[]{:S(2)}) %collective-permute-start.11) | collective-permute-done | bytes 65568 | tf_op jit(solution)/shard_map/ppermute | solution.py:371
  46.1 0.0 collective-permute-start.15
  46.1 0.7 %collective-permute-done.10.refs_2_ = bf16[16,16,128]{2,1,0:T(8,128)(2,1)S(1)} collective-permute-done((bf16[16,16,128]{2,1,0:T(8,128)(2,1)S(1)}, bf16[16,16,128]{2,1,0:T(8,128)(2,1)S(1)}, u32[]{:S(2)}, u32[]{:S(2)}) %collective-permute-start.10) | collective-permute-done | bytes 65568 | tf_op jit(solution)/shard_map/ppermute | solution.py:371
  46.8 0.0 collective-permute-start.14
  46.8 0.6 collective-permute-done.9.refs_1_
  47.4 0.0 collective-permute-start.13
  47.4 0.0 collective-permute-done.12.refs_4_
  47.4 0.0 collective-permute-done.15.refs_7_
  47.4 0.7 %collective-permute-done.14.refs_6_ = bf16[16,16,128]{2,1,0:T(8,128)(2,1)S(1)} collective-permute-done((bf16[16,16,128]{2,1,0:T(8,128)(2,1)S(1)}, bf16[16,16,128]{2,1,0:T(8,128)(2,1)S(1)}, u32[]{:S(2)}, u32[]{:S(2)}) %collective-permute-start.14) | collective-permute-done | bytes 65568 | tf_op jit(solution)/shard_map/ppermute | solution.py:371
  48.0 0.6 collective-permute-done.13.refs_5_
  48.6 0.0 copy-done.7
  48.6 1.8 %second.1 = (bf16[128,128]{1,0:T(8,128)(2,1)S(1)}, bf16[128,128]{1,0:T(8,128)(2,1)S(1)}, bf16[128,128]{1,0:T(8,128)(2,1)S(1)}, bf16[128,128]{1,0:T(8,128)(2,1)S(1)}) custom-call(s32[2]{0:T(128)S(1)} %pad_add_fusion.index_ref, bf16[16,16,128]{2,1,0:T(8,128)(2,1)S(1)} %get-tuple-element.34.refs_0_, bf16[16,16,128]{2,1,0:T(8,128)(2,1)S(1)} %collective-permute-done.9.refs_1_, ...), custom_call_target="tpu_custom_call" | custom-call | tf_op jit(solution)/shard_map/second/pallas_call | solution.py:454
  50.4 0.6 %collective-permute-start.16 = (bf16[128,128]{1,0:T(8,128)(2,1)S(1)}, bf16[128,128]{1,0:T(8,128)(2,1)S(1)}, u32[]{:S(2)}, u32[]{:S(2)}) collective-permute-start(bf16[128,128]{1,0:T(8,128)(2,1)S(1)} %get-tuple-element.36), channel_id=1, source_target_pairs={{0,1},{1,0},{2,3},{3,2},{4,5},{5,4},{6,7},{7,6},{8,9},{9,8},{10,11... | collective-permute-start | bytes 98312 | tf_op jit(solution)/shard_map/ppermute | solution.py:371
  51.0 3.4 %collective-permute-start.17 = (bf16[128,128]{1,0:T(8,128)(2,1)S(1)}, bf16[128,128]{1,0:T(8,128)(2,1)S(1)}, u32[]{:S(2)}, u32[]{:S(2)}) collective-permute-start(bf16[128,128]{1,0:T(8,128)(2,1)S(1)} %get-tuple-element.37), channel_id=1, source_target_pairs={{0,2},{1,3},{2,0},{3,1},{4,6},{5,7},{6,4},{7,5},{8,10},{9,11},{10,... | collective-permute-start | bytes 98312 | tf_op jit(solution)/shard_map/ppermute | solution.py:371
  54.4 0.4 collective-permute-start.18
  54.9 0.0 collective-permute-done.16.refs_1_
  54.9 1.4 %collective-permute-done.17.refs_2_ = bf16[128,128]{1,0:T(8,128)(2,1)S(1)} collective-permute-done((bf16[128,128]{1,0:T(8,128)(2,1)S(1)}, bf16[128,128]{1,0:T(8,128)(2,1)S(1)}, u32[]{:S(2)}, u32[]{:S(2)}) %collective-permute-start.17) | collective-permute-done | bytes 32800 | tf_op jit(solution)/shard_map/ppermute | solution.py:371
  56.3 3.8 %collective-permute-done.18.refs_3_ = bf16[128,128]{1,0:T(8,128)(2,1)S(1)} collective-permute-done((bf16[128,128]{1,0:T(8,128)(2,1)S(1)}, bf16[128,128]{1,0:T(8,128)(2,1)S(1)}, u32[]{:S(2)}, u32[]{:S(2)}) %collective-permute-start.18) | collective-permute-done | bytes 32800 | tf_op jit(solution)/shard_map/ppermute | solution.py:371
  60.1 0.9 %final.1 = f32[2,32,256]{2,1,0:T(8,128)} custom-call(bf16[128,128]{1,0:T(8,128)(2,1)S(1)} %get-tuple-element.35.refs_0_, bf16[128,128]{1,0:T(8,128)(2,1)S(1)} %collective-permute-done.16.refs_1_, bf16[128,128]{1,0:T(8,128)(2,1)S(1)} %collective-permute-done.17.refs_2_, bf16[128,128]{1,0:T(8,128)(2,1)S(1)} %collective-permute-done.18.refs_3_, ...), custom_call_target="tpu_custom_call" | custom-call | tf_op jit(solution)/shard_map/final/pallas_call | solution.py:465
  (11 shorter events, 0.1 us)
Async XLA Ops:
  0.7 1.6 %copy-start = (bf16[32,128,256]{2,1,0:T(8,128)(2,1)S(1)}, bf16[32,128,256]{2,1,0:T(8,128)(2,1)}, u32[]{:S(2)}) copy-start(bf16[32,128,256]{2,1,0:T(8,128)(2,1)} %traces_hbm.1) | copy-start | bytes 6291460
  2.3 0.9 %copy-start.1 = (bf16[256,256]{1,0:T(8,128)(2,1)S(1)}, bf16[256,256]{1,0:T(8,128)(2,1)}, u32[]{:S(2)}) copy-start(bf16[256,256]{1,0:T(8,128)(2,1)} %constant.26.forward_hbm.forward_ref.refs_6_) | copy-start | bytes 393220
  3.2 1.0 %copy-start.4 = (bf16[8,128,256]{2,1,0:T(8,128)(2,1)S(1)}, bf16[8,128,256]{2,1,0:T(8,128)(2,1)}, u32[]{:S(2)}) copy-start(bf16[8,128,256]{2,1,0:T(8,128)(2,1)} %focal_hbm.1) | copy-start | bytes 1572868
  4.2 0.8 %copy-start.6 = (bf16[256,128]{1,0:T(8,128)(2,1)S(1)}, bf16[256,128]{1,0:T(8,128)(2,1)}, u32[]{:S(2)}) copy-start(bf16[256,128]{1,0:T(8,128)(2,1)} %constant.27.gather_hbm.refs_9_) | copy-start | bytes 196612
  5.1 0.9 %copy-start.8 = (f32[256,128]{1,0:T(8,128)S(1)}, f32[256,128]{1,0:T(8,128)}, u32[]{:S(2)}) copy-start(f32[256,128]{1,0:T(8,128)} %constant.21.clone.taps_hbm) | copy-start | bytes 393220
  6.0 0.7 %copy-start.9 = (s32[32,128]{1,0:T(8,128)S(1)}, s32[32,128]{1,0:T(8,128)}, u32[]{:S(2)}) copy-start(s32[32,128]{1,0:T(8,128)} %shift_hbm.1) | copy-start | bytes 49156
  6.7 0.7 %copy-start.10 = (f32[32,64]{1,0:T(8,128)S(1)}, f32[32,64]{1,0:T(8,128)}, u32[]{:S(2)}) copy-start(f32[32,64]{1,0:T(8,128)} %deconv_hbm.1) | copy-start | bytes 24580
  7.4 0.7 %copy-start.11 = (s32[2,32]{1,0:T(2,128)S(1)}, s32[2,32]{1,0:T(2,128)}, u32[]{:S(2)}) copy-start(s32[2,32]{1,0:T(2,128)} %refs_4_.1) | copy-start | bytes 772
  8.1 20.8 %copy-start.2 = (bf16[256,256]{1,0:T(8,128)(2,1)S(1)}, bf16[256,256]{1,0:T(8,128)(2,1)}, u32[]{:S(2)}) copy-start(bf16[256,256]{1,0:T(8,128)(2,1)} %constant.26.forward_hbm.forward_ref.refs_6_) | copy-start | bytes 393220
  8.1 20.8 %copy-start.3 = (bf16[256,256]{1,0:T(8,128)(2,1)S(1)}, bf16[256,256]{1,0:T(8,128)(2,1)}, u32[]{:S(2)}) copy-start(bf16[256,256]{1,0:T(8,128)(2,1)} %constant.28.inverse_ref.refs_7_.refs_5_) | copy-start | bytes 393220
  8.1 20.8 %copy-start.5 = (bf16[4,128,256]{2,1,0:T(8,128)(2,1)S(1)}, bf16[4,128,256]{2,1,0:T(8,128)(2,1)}, u32[]{:S(2)}) copy-start(bf16[4,128,256]{2,1,0:T(8,128)(2,1)} %constant.29.spread_ref) | copy-start | bytes 786436
  13.6 26.4 %copy-start.12 = (s32[1,128]{1,0:T(1,128)S(1)}, s32[1,128]{1,0:T(1,128)}, u32[]{:S(2)}) copy-start(s32[1,128]{1,0:T(1,128)} %refs_5_.1) | copy-start | bytes 1540
  13.6 6.7 %collective-permute-start = (bf16[528,128]{1,0:T(8,128)(2,1)S(1)}, bf16[528,128]{1,0:T(8,128)(2,1)S(1)}, u32[]{:S(2)}, u32[]{:S(2)}) collective-permute-start(bf16[528,128]{1,0:T(8,128)(2,1)S(1)} %get-tuple-element.21), channel_id=1, source_target_pairs={{0,1},{1,0},{2,3},{3,2},{4,5},{5,4},{6,7},{7,6},{8,9},{9,8},{10,11... | collective-permute-start | bytes 405512 | tf_op jit(solution)/shard_map/ppermute | solution.py:371
  20.3 8.6 %collective-permute-start.1 = (bf16[528,128]{1,0:T(8,128)(2,1)S(1)}, bf16[528,128]{1,0:T(8,128)(2,1)S(1)}, u32[]{:S(2)}, u32[]{:S(2)}) collective-permute-start(bf16[528,128]{1,0:T(8,128)(2,1)S(1)} %add_convert_fusion.mine_ref), channel_id=1, source_target_pairs={{0,2},{1,3},{2,0},{3,1},{4,6},{5,7},{6,4},{7,5},{8,10},{9,11},{10,... | collective-permute-start | bytes 405512 | tf_op jit(solution)/shard_map/ppermute | solution.py:371
  28.9 19.7 %copy-start.7 = (bf16[256,128]{1,0:T(8,128)(2,1)S(1)}, bf16[256,128]{1,0:T(8,128)(2,1)}, u32[]{:S(2)}) copy-start(bf16[256,128]{1,0:T(8,128)(2,1)} %constant.27.gather_hbm.refs_9_) | copy-start | bytes 196612
  31.4 1.3 %collective-permute-start.2 = (bf16[256,128]{1,0:T(8,128)(2,1)S(1)}, bf16[256,128]{1,0:T(8,128)(2,1)S(1)}, u32[]{:S(2)}, u32[]{:S(2)}) collective-permute-start(bf16[256,128]{1,0:T(8,128)(2,1)S(1)} %get-tuple-element.25), channel_id=1, source_target_pairs={{0,4},{4,0},{8,12},{12,8},{16,20},{20,16},{24,28},{28,24},{1,5},{5... | collective-permute-start | bytes 196616 | tf_op jit(solution)/shard_map/ppermute | solution.py:371
  31.4 3.6 %collective-permute-start.4 = (bf16[256,128]{1,0:T(8,128)(2,1)S(1)}, bf16[256,128]{1,0:T(8,128)(2,1)S(1)}, u32[]{:S(2)}, u32[]{:S(2)}) collective-permute-start(bf16[256,128]{1,0:T(8,128)(2,1)S(1)} %get-tuple-element.27), channel_id=1, source_target_pairs={{0,4},{4,0},{8,12},{12,8},{16,20},{20,16},{24,28},{28,24},{1,5},{5... | collective-permute-start | bytes 196616 | tf_op jit(solution)/shard_map/ppermute | solution.py:371
  31.9 3.7 %collective-permute-start.6 = (bf16[256,128]{1,0:T(8,128)(2,1)S(1)}, bf16[256,128]{1,0:T(8,128)(2,1)S(1)}, u32[]{:S(2)}, u32[]{:S(2)}) collective-permute-start(bf16[256,128]{1,0:T(8,128)(2,1)S(1)} %get-tuple-element.29), channel_id=1, source_target_pairs={{0,4},{4,0},{8,12},{12,8},{16,20},{20,16},{24,28},{28,24},{1,5},{5... | collective-permute-start | bytes 196616 | tf_op jit(solution)/shard_map/ppermute | solution.py:371
  31.9 4.5 %collective-permute-start.8 = (bf16[256,128]{1,0:T(8,128)(2,1)S(1)}, bf16[256,128]{1,0:T(8,128)(2,1)S(1)}, u32[]{:S(2)}, u32[]{:S(2)}) collective-permute-start(bf16[256,128]{1,0:T(8,128)(2,1)S(1)} %get-tuple-element.31), channel_id=1, source_target_pairs={{0,4},{4,0},{8,12},{12,8},{16,20},{20,16},{24,28},{28,24},{1,5},{5... | collective-permute-start | bytes 196616 | tf_op jit(solution)/shard_map/ppermute | solution.py:371
  32.6 5.3 %collective-permute-start.3 = (bf16[256,128]{1,0:T(8,128)(2,1)S(1)}, bf16[256,128]{1,0:T(8,128)(2,1)S(1)}, u32[]{:S(2)}, u32[]{:S(2)}) collective-permute-start(bf16[256,128]{1,0:T(8,128)(2,1)S(1)} %add_convert_fusion.4), channel_id=1, source_target_pairs={{0,24},{4,28},{8,16},{12,20},{16,8},{20,12},{24,0},{28,4},{1,25},{... | collective-permute-start | bytes 196616 | tf_op jit(solution)/shard_map/ppermute | solution.py:371
  35.0 4.3 %collective-permute-start.5 = (bf16[256,128]{1,0:T(8,128)(2,1)S(1)}, bf16[256,128]{1,0:T(8,128)(2,1)S(1)}, u32[]{:S(2)}, u32[]{:S(2)}) collective-permute-start(bf16[256,128]{1,0:T(8,128)(2,1)S(1)} %add_convert_fusion.3), channel_id=1, source_target_pairs={{0,16},{4,20},{8,24},{12,28},{16,0},{20,4},{24,8},{28,12},{1,17},{... | collective-permute-start | bytes 196616 | tf_op jit(solution)/shard_map/ppermute | solution.py:371
  35.6 4.3 %collective-permute-start.7 = (bf16[256,128]{1,0:T(8,128)(2,1)S(1)}, bf16[256,128]{1,0:T(8,128)(2,1)S(1)}, u32[]{:S(2)}, u32[]{:S(2)}) collective-permute-start(bf16[256,128]{1,0:T(8,128)(2,1)S(1)} %add_convert_fusion.2), channel_id=1, source_target_pairs={{0,8},{4,12},{8,0},{12,4},{16,24},{20,28},{24,16},{28,20},{1,9},{5... | collective-permute-start | bytes 196616 | tf_op jit(solution)/shard_map/ppermute | solution.py:371
  40.9 5.2 %collective-permute-start.11 = (bf16[16,16,128]{2,1,0:T(8,128)(2,1)S(1)}, bf16[16,16,128]{2,1,0:T(8,128)(2,1)S(1)}, u32[]{:S(2)}, u32[]{:S(2)}) collective-permute-start(bf16[16,16,128]{2,1,0:T(8,128)(2,1)S(1)} %get-tuple-element.34.refs_0_), channel_id=1, source_target_pairs={{0,24},{4,28},{8,16},{12,20},{16,8},{20,12},{24,0},{28,4},{1,25},{... | collective-permute-start | bytes 196616 | tf_op jit(solution)/shard_map/ppermute | solution.py:371
  42.4 4.4 %collective-permute-start.10 = (bf16[16,16,128]{2,1,0:T(8,128)(2,1)S(1)}, bf16[16,16,128]{2,1,0:T(8,128)(2,1)S(1)}, u32[]{:S(2)}, u32[]{:S(2)}) collective-permute-start(bf16[16,16,128]{2,1,0:T(8,128)(2,1)S(1)} %get-tuple-element.34.refs_0_), channel_id=1, source_target_pairs={{0,16},{4,20},{8,24},{12,28},{16,0},{20,4},{24,8},{28,12},{1,17},{... | collective-permute-start | bytes 196616 | tf_op jit(solution)/shard_map/ppermute | solution.py:371
  43.1 4.3 %collective-permute-start.9 = (bf16[16,16,128]{2,1,0:T(8,128)(2,1)S(1)}, bf16[16,16,128]{2,1,0:T(8,128)(2,1)S(1)}, u32[]{:S(2)}, u32[]{:S(2)}) collective-permute-start(bf16[16,16,128]{2,1,0:T(8,128)(2,1)S(1)} %get-tuple-element.34.refs_0_), channel_id=1, source_target_pairs={{0,8},{4,12},{8,0},{12,4},{16,24},{20,28},{24,16},{28,20},{1,9},{5... | collective-permute-start | bytes 196616 | tf_op jit(solution)/shard_map/ppermute | solution.py:371
  44.4 3.0 %collective-permute-start.12 = (bf16[16,16,128]{2,1,0:T(8,128)(2,1)S(1)}, bf16[16,16,128]{2,1,0:T(8,128)(2,1)S(1)}, u32[]{:S(2)}, u32[]{:S(2)}) collective-permute-start(bf16[16,16,128]{2,1,0:T(8,128)(2,1)S(1)} %get-tuple-element.34.refs_0_), channel_id=1, source_target_pairs={{0,4},{4,0},{8,12},{12,8},{16,20},{20,16},{24,28},{28,24},{1,5},{5... | collective-permute-start | bytes 196616 | tf_op jit(solution)/shard_map/ppermute | solution.py:371
  46.1 1.3 %collective-permute-start.15 = (bf16[16,16,128]{2,1,0:T(8,128)(2,1)S(1)}, bf16[16,16,128]{2,1,0:T(8,128)(2,1)S(1)}, u32[]{:S(2)}, u32[]{:S(2)}) collective-permute-start(bf16[16,16,128]{2,1,0:T(8,128)(2,1)S(1)} %collective-permute-done.11.refs_3_), channel_id=1, source_target_pairs={{0,4},{4,0},{8,12},{12,8},{16,20},{20,16},{24,28},{28,24},{1,5},{5... | collective-permute-start | bytes 196616 | tf_op jit(solution)/shard_map/ppermute | solution.py:371
  46.8 1.3 %collective-permute-start.14 = (bf16[16,16,128]{2,1,0:T(8,128)(2,1)S(1)}, bf16[16,16,128]{2,1,0:T(8,128)(2,1)S(1)}, u32[]{:S(2)}, u32[]{:S(2)}) collective-permute-start(bf16[16,16,128]{2,1,0:T(8,128)(2,1)S(1)} %collective-permute-done.10.refs_2_), channel_id=1, source_target_pairs={{0,4},{4,0},{8,12},{12,8},{16,20},{20,16},{24,28},{28,24},{1,5},{5... | collective-permute-start | bytes 196616 | tf_op jit(solution)/shard_map/ppermute | solution.py:371
  47.4 1.3 %collective-permute-start.13 = (bf16[16,16,128]{2,1,0:T(8,128)(2,1)S(1)}, bf16[16,16,128]{2,1,0:T(8,128)(2,1)S(1)}, u32[]{:S(2)}, u32[]{:S(2)}) collective-permute-start(bf16[16,16,128]{2,1,0:T(8,128)(2,1)S(1)} %collective-permute-done.9.refs_1_), channel_id=1, source_target_pairs={{0,4},{4,0},{8,12},{12,8},{16,20},{20,16},{24,28},{28,24},{1,5},{5... | collective-permute-start | bytes 196616 | tf_op jit(solution)/shard_map/ppermute | solution.py:371
  50.4 4.5 %collective-permute-start.16 = (bf16[128,128]{1,0:T(8,128)(2,1)S(1)}, bf16[128,128]{1,0:T(8,128)(2,1)S(1)}, u32[]{:S(2)}, u32[]{:S(2)}) collective-permute-start(bf16[128,128]{1,0:T(8,128)(2,1)S(1)} %get-tuple-element.36), channel_id=1, source_target_pairs={{0,1},{1,0},{2,3},{3,2},{4,5},{5,4},{6,7},{7,6},{8,9},{9,8},{10,11... | collective-permute-start | bytes 98312 | tf_op jit(solution)/shard_map/ppermute | solution.py:371
  51.0 5.3 %collective-permute-start.17 = (bf16[128,128]{1,0:T(8,128)(2,1)S(1)}, bf16[128,128]{1,0:T(8,128)(2,1)S(1)}, u32[]{:S(2)}, u32[]{:S(2)}) collective-permute-start(bf16[128,128]{1,0:T(8,128)(2,1)S(1)} %get-tuple-element.37), channel_id=1, source_target_pairs={{0,2},{1,3},{2,0},{3,1},{4,6},{5,7},{6,4},{7,5},{8,10},{9,11},{10,... | collective-permute-start | bytes 98312 | tf_op jit(solution)/shard_map/ppermute | solution.py:371
  54.4 5.7 %collective-permute-start.18 = (bf16[128,128]{1,0:T(8,128)(2,1)S(1)}, bf16[128,128]{1,0:T(8,128)(2,1)S(1)}, u32[]{:S(2)}, u32[]{:S(2)}) collective-permute-start(bf16[128,128]{1,0:T(8,128)(2,1)S(1)} %get-tuple-element.38), channel_id=1, source_target_pairs={{0,3},{1,2},{2,1},{3,0},{4,7},{5,6},{6,5},{7,4},{8,11},{9,10},{10,... | collective-permute-start | bytes 98312 | tf_op jit(solution)/shard_map/ppermute | solution.py:371

commit v3 on v2

--- a/solution.py
+++ b/solution.py
@@ -410,7 +410,7 @@
         + [buffer(value) for value in inputs]
         + [pltpu.SemaphoreType.DMA((4,)), pltpu.SemaphoreType.DMA((7,))]
         + [pltpu.VMEM((sources // 2, 2 * NF, LANES), BF16)],
-    )(index, *inputs)
+    )(index, *[pltpu.with_memory_space_constraint(value, pltpu.HBM) for value in inputs])
 
     distance = 1
     mine, other = partial, exchange(partial, "rcv", 1)

time: 61.5 us -> 54.1 us (0.88)
  local copies, waits for them, and re-layouts: 7.41 us -> 0.04 us
    unnamed x26 -> x12, local copies, waits for them, and re-layouts: 7.41 us -> 0.04 us
where the time goes in v3:
time: 54.1 us; the launch traced here: 54 us
  waiting for transfers between devices  22.6 us (42%)
  starting transfers between devices  18.6 us (34%)
  Pallas kernels  11.8 us (22%)
  between operations  0.74 us (1%)
    ppermute x19, waiting for transfers between devices, exchange(): lax.ppermute(value, axis, [(place, place ^ distance) for place in range(c...  22.6 us
    ppermute x19, starting transfers between devices, exchange(): lax.ppermute(value, axis, [(place, place ^ distance) for place in range(c...  18.6 us
    pallas_call x1, Pallas kernels, body(): call(functools.partial(build_kernel, gain), 'build', (shape((NG, sources...  5.72 us
    pallas_call x1, Pallas kernels, body(): call(adjoint_kernel, 'adjoint', [field] * (2 * pairs) + [shape((2, source...  2.41 us
    pallas_call x1, Pallas kernels, body(): call(functools.partial(second_kernel, pairs), 'second', [shape((NF, LANES...  1.78 us
  transfers between devices with their start and end apart: 19, of which 13 were waited for; matrix products, arithmetic and copies ran while one was open for 0% of the time, Pallas kernels for 0%

profile of v3, /device:TPU:0, one launch (start us, length us, event | category | flops | bytes accessed | tf_op | source)
XLA Modules:
  0.0 54.0 jit_solution(2061784059627952049)
XLA Ops:
  0.6 0.0 copy-start
  0.6 0.0 copy-start.1
  0.7 0.0 copy-start.2
  0.7 0.1 pad_add_fusion.index_ref
  0.7 5.7 %build.1 = (bf16[16,16,16,256]{3,2,1,0:T(8,128)(2,1)S(1)}, bf16[528,128]{1,0:T(8,128)(2,1)S(1)}, bf16[128,256]{1,0:T(8,128)(2,1)S(1)}) custom-call(s32[2]{0:T(128)S(1)} %pad_add_fusion.index_ref, bf16[32,128,256]{2,1,0:T(8,128)(2,1)} %traces_hbm.1, s32[32,128]{1,0:T(8,128)} %shift_hbm.1, f32[32,64]{1,0:T(8,128)} %deconv_hbm.1, ...), custom_call_target="tpu_custom_call" | custom-call | tf_op jit(solution)/shard_map/build/pallas_call | solution.py:400
  6.5 0.0 copy-start.5
  6.5 3.1 %collective-permute-start = (bf16[528,128]{1,0:T(8,128)(2,1)S(1)}, bf16[528,128]{1,0:T(8,128)(2,1)S(1)}, u32[]{:S(2)}, u32[]{:S(2)}) collective-permute-start(bf16[528,128]{1,0:T(8,128)(2,1)S(1)} %get-tuple-element.21), channel_id=1, source_target_pairs={{0,1},{1,0},{2,3},{3,2},{4,5},{5,4},{6,7},{7,6},{8,9},{9,8},{10,11... | collective-permute-start | bytes 405512 | tf_op jit(solution)/shard_map/ppermute | solution.py:371
  9.6 3.6 %collective-permute-done = bf16[528,128]{1,0:T(8,128)(2,1)S(1)} collective-permute-done((bf16[528,128]{1,0:T(8,128)(2,1)S(1)}, bf16[528,128]{1,0:T(8,128)(2,1)S(1)}, u32[]{:S(2)}, u32[]{:S(2)}) %collective-permute-start) | collective-permute-done | bytes 135200 | tf_op jit(solution)/shard_map/ppermute | solution.py:371
  13.2 2.8 %collective-permute-start.1 = (bf16[528,128]{1,0:T(8,128)(2,1)S(1)}, bf16[528,128]{1,0:T(8,128)(2,1)S(1)}, u32[]{:S(2)}, u32[]{:S(2)}) collective-permute-start(bf16[528,128]{1,0:T(8,128)(2,1)S(1)} %add_convert_fusion.mine_ref), channel_id=1, source_target_pairs={{0,2},{1,3},{2,0},{3,1},{4,6},{5,7},{6,4},{7,5},{8,10},{9,11},{10,... | collective-permute-start | bytes 405512 | tf_op jit(solution)/shard_map/ppermute | solution.py:371
  16.0 5.8 %collective-permute-done.1.other_ref = bf16[528,128]{1,0:T(8,128)(2,1)S(1)} collective-permute-done((bf16[528,128]{1,0:T(8,128)(2,1)S(1)}, bf16[528,128]{1,0:T(8,128)(2,1)S(1)}, u32[]{:S(2)}, u32[]{:S(2)}) %collective-permute-start.1) | collective-permute-done | bytes 135200 | tf_op jit(solution)/shard_map/ppermute | solution.py:371
  21.8 0.0 copy-done
  21.8 0.0 copy-done.1
  21.8 0.0 copy-done.2
  21.8 0.0 copy-start.3
  21.9 2.4 %adjoint.1 = (bf16[256,128]{1,0:T(8,128)(2,1)S(1)}, bf16[256,128]{1,0:T(8,128)(2,1)S(1)}, bf16[256,128]{1,0:T(8,128)(2,1)S(1)}, bf16[256,128]{1,0:T(8,128)(2,1)S...) custom-call(s32[2]{0:T(128)S(1)} %pad_add_fusion.index_ref, ...), custom_call_target="tpu_custom_call" | custom-call | tf_op jit(solution)/shard_map/adjoint/pallas_call | solution.py:423
  24.3 0.0 copy-start.4
  24.3 0.0 collective-permute-start.2
  24.3 0.5 collective-permute-start.4
  24.8 0.0 collective-permute-start.6
  24.8 0.5 collective-permute-start.8
  25.3 0.2 collective-permute-done.2
  25.5 2.4 %collective-permute-start.3 = (bf16[256,128]{1,0:T(8,128)(2,1)S(1)}, bf16[256,128]{1,0:T(8,128)(2,1)S(1)}, u32[]{:S(2)}, u32[]{:S(2)}) collective-permute-start(bf16[256,128]{1,0:T(8,128)(2,1)S(1)} %add_convert_fusion.4), channel_id=1, source_target_pairs={{0,24},{4,28},{8,16},{12,20},{16,8},{20,12},{24,0},{28,4},{1,25},{... | collective-permute-start | bytes 196616 | tf_op jit(solution)/shard_map/ppermute | solution.py:371
  27.9 0.0 collective-permute-done.4
  27.9 0.6 %collective-permute-start.5 = (bf16[256,128]{1,0:T(8,128)(2,1)S(1)}, bf16[256,128]{1,0:T(8,128)(2,1)S(1)}, u32[]{:S(2)}, u32[]{:S(2)}) collective-permute-start(bf16[256,128]{1,0:T(8,128)(2,1)S(1)} %add_convert_fusion.3), channel_id=1, source_target_pairs={{0,16},{4,20},{8,24},{12,28},{16,0},{20,4},{24,8},{28,12},{1,17},{... | collective-permute-start | bytes 196616 | tf_op jit(solution)/shard_map/ppermute | solution.py:371
  28.5 0.0 collective-permute-done.6
  28.5 0.7 %collective-permute-start.7 = (bf16[256,128]{1,0:T(8,128)(2,1)S(1)}, bf16[256,128]{1,0:T(8,128)(2,1)S(1)}, u32[]{:S(2)}, u32[]{:S(2)}) collective-permute-start(bf16[256,128]{1,0:T(8,128)(2,1)S(1)} %add_convert_fusion.2), channel_id=1, source_target_pairs={{0,8},{4,12},{8,0},{12,4},{16,24},{20,28},{24,16},{28,20},{1,9},{5... | collective-permute-start | bytes 196616 | tf_op jit(solution)/shard_map/ppermute | solution.py:371
  29.3 0.0 collective-permute-done.8
  29.3 1.5 %collective-permute-done.3.refs_0_ = bf16[256,128]{1,0:T(8,128)(2,1)S(1)} collective-permute-done((bf16[256,128]{1,0:T(8,128)(2,1)S(1)}, bf16[256,128]{1,0:T(8,128)(2,1)S(1)}, u32[]{:S(2)}, u32[]{:S(2)}) %collective-permute-start.3) | collective-permute-done | bytes 65568 | tf_op jit(solution)/shard_map/ppermute | solution.py:371
  30.8 1.5 %collective-permute-done.5.refs_1_ = bf16[256,128]{1,0:T(8,128)(2,1)S(1)} collective-permute-done((bf16[256,128]{1,0:T(8,128)(2,1)S(1)}, bf16[256,128]{1,0:T(8,128)(2,1)S(1)}, u32[]{:S(2)}, u32[]{:S(2)}) %collective-permute-start.5) | collective-permute-done | bytes 65568 | tf_op jit(solution)/shard_map/ppermute | solution.py:371
  32.3 0.6 %collective-permute-done.7.refs_2_ = bf16[256,128]{1,0:T(8,128)(2,1)S(1)} collective-permute-done((bf16[256,128]{1,0:T(8,128)(2,1)S(1)}, bf16[256,128]{1,0:T(8,128)(2,1)S(1)}, u32[]{:S(2)}, u32[]{:S(2)}) %collective-permute-start.7) | collective-permute-done | bytes 65568 | tf_op jit(solution)/shard_map/ppermute | solution.py:371
  32.9 0.0 copy-done.5
  32.9 0.9 %downgoing.1 = (f32[1,128,256]{2,1,0:T(8,128)}, bf16[16,16,128]{2,1,0:T(8,128)(2,1)S(1)}) custom-call(bf16[256,128]{1,0:T(8,128)(2,1)S(1)} %collective-permute-done.3.refs_0_, bf16[256,128]{1,0:T(8,128)(2,1)S(1)} %collective-permute-done.5.refs_1_, bf16[256,128]{1,0:T(8,128)(2,1)S(1)} %collective-permute-done.7.refs_2_, ...), custom_call_target="tpu_custom_call" | custom-call | tf_op jit(solution)/shard_map/downgoing/pallas_call | solution.py:439
  33.8 1.5 %collective-permute-start.11 = (bf16[16,16,128]{2,1,0:T(8,128)(2,1)S(1)}, bf16[16,16,128]{2,1,0:T(8,128)(2,1)S(1)}, u32[]{:S(2)}, u32[]{:S(2)}) collective-permute-start(bf16[16,16,128]{2,1,0:T(8,128)(2,1)S(1)} %get-tuple-element.34.refs_0_), channel_id=1, source_target_pairs={{0,24},{4,28},{8,16},{12,20},{16,8},{20,12},{24,0},{28,4},{1,25},{... | collective-permute-start | bytes 196616 | tf_op jit(solution)/shard_map/ppermute | solution.py:371
  35.3 0.7 %collective-permute-start.10 = (bf16[16,16,128]{2,1,0:T(8,128)(2,1)S(1)}, bf16[16,16,128]{2,1,0:T(8,128)(2,1)S(1)}, u32[]{:S(2)}, u32[]{:S(2)}) collective-permute-start(bf16[16,16,128]{2,1,0:T(8,128)(2,1)S(1)} %get-tuple-element.34.refs_0_), channel_id=1, source_target_pairs={{0,16},{4,20},{8,24},{12,28},{16,0},{20,4},{24,8},{28,12},{1,17},{... | collective-permute-start | bytes 196616 | tf_op jit(solution)/shard_map/ppermute | solution.py:371
  36.0 1.3 %collective-permute-start.9 = (bf16[16,16,128]{2,1,0:T(8,128)(2,1)S(1)}, bf16[16,16,128]{2,1,0:T(8,128)(2,1)S(1)}, u32[]{:S(2)}, u32[]{:S(2)}) collective-permute-start(bf16[16,16,128]{2,1,0:T(8,128)(2,1)S(1)} %get-tuple-element.34.refs_0_), channel_id=1, source_target_pairs={{0,8},{4,12},{8,0},{12,4},{16,24},{20,28},{24,16},{28,20},{1,9},{5... | collective-permute-start | bytes 196616 | tf_op jit(solution)/shard_map/ppermute | solution.py:371
  37.3 0.0 collective-permute-start.12
  37.3 1.7 %collective-permute-done.11.refs_3_ = bf16[16,16,128]{2,1,0:T(8,128)(2,1)S(1)} collective-permute-done((bf16[16,16,128]{2,1,0:T(8,128)(2,1)S(1)}, bf16[16,16,128]{2,1,0:T(8,128)(2,1)S(1)}, u32[]{:S(2)}, u32[]{:S(2)}) %collective-permute-start.11) | collective-permute-done | bytes 65568 | tf_op jit(solution)/shard_map/ppermute | solution.py:371
  39.0 0.0 collective-permute-start.15
  39.0 0.7 %collective-permute-done.10.refs_2_ = bf16[16,16,128]{2,1,0:T(8,128)(2,1)S(1)} collective-permute-done((bf16[16,16,128]{2,1,0:T(8,128)(2,1)S(1)}, bf16[16,16,128]{2,1,0:T(8,128)(2,1)S(1)}, u32[]{:S(2)}, u32[]{:S(2)}) %collective-permute-start.10) | collective-permute-done | bytes 65568 | tf_op jit(solution)/shard_map/ppermute | solution.py:371
  39.7 0.0 collective-permute-start.14
  39.7 0.6 %collective-permute-done.9.refs_1_ = bf16[16,16,128]{2,1,0:T(8,128)(2,1)S(1)} collective-permute-done((bf16[16,16,128]{2,1,0:T(8,128)(2,1)S(1)}, bf16[16,16,128]{2,1,0:T(8,128)(2,1)S(1)}, u32[]{:S(2)}, u32[]{:S(2)}) %collective-permute-start.9) | collective-permute-done | bytes 65568 | tf_op jit(solution)/shard_map/ppermute | solution.py:371
  40.3 0.0 collective-permute-start.13
  40.3 0.0 collective-permute-done.12.refs_4_
  40.3 0.0 collective-permute-done.15.refs_7_
  40.3 0.7 %collective-permute-done.14.refs_6_ = bf16[16,16,128]{2,1,0:T(8,128)(2,1)S(1)} collective-permute-done((bf16[16,16,128]{2,1,0:T(8,128)(2,1)S(1)}, bf16[16,16,128]{2,1,0:T(8,128)(2,1)S(1)}, u32[]{:S(2)}, u32[]{:S(2)}) %collective-permute-start.14) | collective-permute-done | bytes 65568 | tf_op jit(solution)/shard_map/ppermute | solution.py:371
  40.9 0.6 %collective-permute-done.13.refs_5_ = bf16[16,16,128]{2,1,0:T(8,128)(2,1)S(1)} collective-permute-done((bf16[16,16,128]{2,1,0:T(8,128)(2,1)S(1)}, bf16[16,16,128]{2,1,0:T(8,128)(2,1)S(1)}, u32[]{:S(2)}, u32[]{:S(2)}) %collective-permute-start.13) | collective-permute-done | bytes 65568 | tf_op jit(solution)/shard_map/ppermute | solution.py:371
  41.5 0.0 copy-done.3
  41.5 1.8 %second.1 = (bf16[128,128]{1,0:T(8,128)(2,1)S(1)}, bf16[128,128]{1,0:T(8,128)(2,1)S(1)}, bf16[128,128]{1,0:T(8,128)(2,1)S(1)}, bf16[128,128]{1,0:T(8,128)(2,1)S(1)}) custom-call(s32[2]{0:T(128)S(1)} %pad_add_fusion.index_ref, bf16[16,16,128]{2,1,0:T(8,128)(2,1)S(1)} %get-tuple-element.34.refs_0_, bf16[16,16,128]{2,1,0:T(8,128)(2,1)S(1)} %collective-permute-done.9.refs_1_, ...), custom_call_target="tpu_custom_call" | custom-call | tf_op jit(solution)/shard_map/second/pallas_call | solution.py:454
  43.3 0.6 %collective-permute-start.16 = (bf16[128,128]{1,0:T(8,128)(2,1)S(1)}, bf16[128,128]{1,0:T(8,128)(2,1)S(1)}, u32[]{:S(2)}, u32[]{:S(2)}) collective-permute-start(bf16[128,128]{1,0:T(8,128)(2,1)S(1)} %get-tuple-element.36), channel_id=1, source_target_pairs={{0,1},{1,0},{2,3},{3,2},{4,5},{5,4},{6,7},{7,6},{8,9},{9,8},{10,11... | collective-permute-start | bytes 98312 | tf_op jit(solution)/shard_map/ppermute | solution.py:371
  43.9 3.4 %collective-permute-start.17 = (bf16[128,128]{1,0:T(8,128)(2,1)S(1)}, bf16[128,128]{1,0:T(8,128)(2,1)S(1)}, u32[]{:S(2)}, u32[]{:S(2)}) collective-permute-start(bf16[128,128]{1,0:T(8,128)(2,1)S(1)} %get-tuple-element.37), channel_id=1, source_target_pairs={{0,2},{1,3},{2,0},{3,1},{4,6},{5,7},{6,4},{7,5},{8,10},{9,11},{10,... | collective-permute-start | bytes 98312 | tf_op jit(solution)/shard_map/ppermute | solution.py:371
  47.3 0.4 collective-permute-start.18
  47.8 0.0 collective-permute-done.16.refs_1_
  47.8 1.4 %collective-permute-done.17.refs_2_ = bf16[128,128]{1,0:T(8,128)(2,1)S(1)} collective-permute-done((bf16[128,128]{1,0:T(8,128)(2,1)S(1)}, bf16[128,128]{1,0:T(8,128)(2,1)S(1)}, u32[]{:S(2)}, u32[]{:S(2)}) %collective-permute-start.17) | collective-permute-done | bytes 32800 | tf_op jit(solution)/shard_map/ppermute | solution.py:371
  49.2 3.8 %collective-permute-done.18.refs_3_ = bf16[128,128]{1,0:T(8,128)(2,1)S(1)} collective-permute-done((bf16[128,128]{1,0:T(8,128)(2,1)S(1)}, bf16[128,128]{1,0:T(8,128)(2,1)S(1)}, u32[]{:S(2)}, u32[]{:S(2)}) %collective-permute-start.18) | collective-permute-done | bytes 32800 | tf_op jit(solution)/shard_map/ppermute | solution.py:371
  53.0 0.0 copy-done.4
  53.0 0.9 %final.1 = f32[2,32,256]{2,1,0:T(8,128)} custom-call(bf16[128,128]{1,0:T(8,128)(2,1)S(1)} %get-tuple-element.35.refs_0_, bf16[128,128]{1,0:T(8,128)(2,1)S(1)} %collective-permute-done.16.refs_1_, bf16[128,128]{1,0:T(8,128)(2,1)S(1)} %collective-permute-done.17.refs_2_, bf16[128,128]{1,0:T(8,128)(2,1)S(1)} %collective-permute-done.18.refs_3_, ...), custom_call_target="tpu_custom_call" | custom-call | tf_op jit(solution)/shard_map/final/pallas_call | solution.py:465
  (5 shorter events, 0.1 us)
Async XLA Ops:
  0.6 21.2 %copy-start = (bf16[256,256]{1,0:T(8,128)(2,1)S(1)}, bf16[256,256]{1,0:T(8,128)(2,1)}, u32[]{:S(2)}) copy-start(bf16[256,256]{1,0:T(8,128)(2,1)} %constant.26.forward_hbm.forward_ref.refs_6_) | copy-start | bytes 393220
  0.6 21.2 %copy-start.1 = (bf16[256,256]{1,0:T(8,128)(2,1)S(1)}, bf16[256,256]{1,0:T(8,128)(2,1)}, u32[]{:S(2)}) copy-start(bf16[256,256]{1,0:T(8,128)(2,1)} %constant.28.inverse_ref.refs_7_.refs_5_) | copy-start | bytes 393220
  0.7 21.2 %copy-start.2 = (bf16[4,128,256]{2,1,0:T(8,128)(2,1)S(1)}, bf16[4,128,256]{2,1,0:T(8,128)(2,1)}, u32[]{:S(2)}) copy-start(bf16[4,128,256]{2,1,0:T(8,128)(2,1)} %constant.29.spread_ref) | copy-start | bytes 786436
  6.5 26.4 %copy-start.5 = (s32[1,128]{1,0:T(1,128)S(1)}, s32[1,128]{1,0:T(1,128)}, u32[]{:S(2)}) copy-start(s32[1,128]{1,0:T(1,128)} %refs_5_.1) | copy-start | bytes 1540
  6.5 6.7 %collective-permute-start = (bf16[528,128]{1,0:T(8,128)(2,1)S(1)}, bf16[528,128]{1,0:T(8,128)(2,1)S(1)}, u32[]{:S(2)}, u32[]{:S(2)}) collective-permute-start(bf16[528,128]{1,0:T(8,128)(2,1)S(1)} %get-tuple-element.21), channel_id=1, source_target_pairs={{0,1},{1,0},{2,3},{3,2},{4,5},{5,4},{6,7},{7,6},{8,9},{9,8},{10,11... | collective-permute-start | bytes 405512 | tf_op jit(solution)/shard_map/ppermute | solution.py:371
  13.2 8.6 %collective-permute-start.1 = (bf16[528,128]{1,0:T(8,128)(2,1)S(1)}, bf16[528,128]{1,0:T(8,128)(2,1)S(1)}, u32[]{:S(2)}, u32[]{:S(2)}) collective-permute-start(bf16[528,128]{1,0:T(8,128)(2,1)S(1)} %add_convert_fusion.mine_ref), channel_id=1, source_target_pairs={{0,2},{1,3},{2,0},{3,1},{4,6},{5,7},{6,4},{7,5},{8,10},{9,11},{10,... | collective-permute-start | bytes 405512 | tf_op jit(solution)/shard_map/ppermute | solution.py:371
  21.8 19.7 %copy-start.3 = (bf16[256,128]{1,0:T(8,128)(2,1)S(1)}, bf16[256,128]{1,0:T(8,128)(2,1)}, u32[]{:S(2)}) copy-start(bf16[256,128]{1,0:T(8,128)(2,1)} %constant.27.gather_hbm.refs_9_) | copy-start | bytes 196612
  24.3 28.8 %copy-start.4 = (s32[2,32]{1,0:T(2,128)S(1)}, s32[2,32]{1,0:T(2,128)}, u32[]{:S(2)}) copy-start(s32[2,32]{1,0:T(2,128)} %refs_4_.1) | copy-start | bytes 772
  24.3 1.3 %collective-permute-start.2 = (bf16[256,128]{1,0:T(8,128)(2,1)S(1)}, bf16[256,128]{1,0:T(8,128)(2,1)S(1)}, u32[]{:S(2)}, u32[]{:S(2)}) collective-permute-start(bf16[256,128]{1,0:T(8,128)(2,1)S(1)} %get-tuple-element.25), channel_id=1, source_target_pairs={{0,4},{4,0},{8,12},{12,8},{16,20},{20,16},{24,28},{28,24},{1,5},{5... | collective-permute-start | bytes 196616 | tf_op jit(solution)/shard_map/ppermute | solution.py:371
  24.3 3.6 %collective-permute-start.4 = (bf16[256,128]{1,0:T(8,128)(2,1)S(1)}, bf16[256,128]{1,0:T(8,128)(2,1)S(1)}, u32[]{:S(2)}, u32[]{:S(2)}) collective-permute-start(bf16[256,128]{1,0:T(8,128)(2,1)S(1)} %get-tuple-element.27), channel_id=1, source_target_pairs={{0,4},{4,0},{8,12},{12,8},{16,20},{20,16},{24,28},{28,24},{1,5},{5... | collective-permute-start | bytes 196616 | tf_op jit(solution)/shard_map/ppermute | solution.py:371
  24.8 3.7 %collective-permute-start.6 = (bf16[256,128]{1,0:T(8,128)(2,1)S(1)}, bf16[256,128]{1,0:T(8,128)(2,1)S(1)}, u32[]{:S(2)}, u32[]{:S(2)}) collective-permute-start(bf16[256,128]{1,0:T(8,128)(2,1)S(1)} %get-tuple-element.29), channel_id=1, source_target_pairs={{0,4},{4,0},{8,12},{12,8},{16,20},{20,16},{24,28},{28,24},{1,5},{5... | collective-permute-start | bytes 196616 | tf_op jit(solution)/shard_map/ppermute | solution.py:371
  24.8 4.5 %collective-permute-start.8 = (bf16[256,128]{1,0:T(8,128)(2,1)S(1)}, bf16[256,128]{1,0:T(8,128)(2,1)S(1)}, u32[]{:S(2)}, u32[]{:S(2)}) collective-permute-start(bf16[256,128]{1,0:T(8,128)(2,1)S(1)} %get-tuple-element.31), channel_id=1, source_target_pairs={{0,4},{4,0},{8,12},{12,8},{16,20},{20,16},{24,28},{28,24},{1,5},{5... | collective-permute-start | bytes 196616 | tf_op jit(solution)/shard_map/ppermute | solution.py:371
  25.5 5.3 %collective-permute-start.3 = (bf16[256,128]{1,0:T(8,128)(2,1)S(1)}, bf16[256,128]{1,0:T(8,128)(2,1)S(1)}, u32[]{:S(2)}, u32[]{:S(2)}) collective-permute-start(bf16[256,128]{1,0:T(8,128)(2,1)S(1)} %add_convert_fusion.4), channel_id=1, source_target_pairs={{0,24},{4,28},{8,16},{12,20},{16,8},{20,12},{24,0},{28,4},{1,25},{... | collective-permute-start | bytes 196616 | tf_op jit(solution)/shard_map/ppermute | solution.py:371
  27.9 4.3 %collective-permute-start.5 = (bf16[256,128]{1,0:T(8,128)(2,1)S(1)}, bf16[256,128]{1,0:T(8,128)(2,1)S(1)}, u32[]{:S(2)}, u32[]{:S(2)}) collective-permute-start(bf16[256,128]{1,0:T(8,128)(2,1)S(1)} %add_convert_fusion.3), channel_id=1, source_target_pairs={{0,16},{4,20},{8,24},{12,28},{16,0},{20,4},{24,8},{28,12},{1,17},{... | collective-permute-start | bytes 196616 | tf_op jit(solution)/shard_map/ppermute | solution.py:371
  28.5 4.3 %collective-permute-start.7 = (bf16[256,128]{1,0:T(8,128)(2,1)S(1)}, bf16[256,128]{1,0:T(8,128)(2,1)S(1)}, u32[]{:S(2)}, u32[]{:S(2)}) collective-permute-start(bf16[256,128]{1,0:T(8,128)(2,1)S(1)} %add_convert_fusion.2), channel_id=1, source_target_pairs={{0,8},{4,12},{8,0},{12,4},{16,24},{20,28},{24,16},{28,20},{1,9},{5... | collective-permute-start | bytes 196616 | tf_op jit(solution)/shard_map/ppermute | solution.py:371
  33.8 5.2 %collective-permute-start.11 = (bf16[16,16,128]{2,1,0:T(8,128)(2,1)S(1)}, bf16[16,16,128]{2,1,0:T(8,128)(2,1)S(1)}, u32[]{:S(2)}, u32[]{:S(2)}) collective-permute-start(bf16[16,16,128]{2,1,0:T(8,128)(2,1)S(1)} %get-tuple-element.34.refs_0_), channel_id=1, source_target_pairs={{0,24},{4,28},{8,16},{12,20},{16,8},{20,12},{24,0},{28,4},{1,25},{... | collective-permute-start | bytes 196616 | tf_op jit(solution)/shard_map/ppermute | solution.py:371
  35.3 4.4 %collective-permute-start.10 = (bf16[16,16,128]{2,1,0:T(8,128)(2,1)S(1)}, bf16[16,16,128]{2,1,0:T(8,128)(2,1)S(1)}, u32[]{:S(2)}, u32[]{:S(2)}) collective-permute-start(bf16[16,16,128]{2,1,0:T(8,128)(2,1)S(1)} %get-tuple-element.34.refs_0_), channel_id=1, source_target_pairs={{0,16},{4,20},{8,24},{12,28},{16,0},{20,4},{24,8},{28,12},{1,17},{... | collective-permute-start | bytes 196616 | tf_op jit(solution)/shard_map/ppermute | solution.py:371
  36.0 4.3 %collective-permute-start.9 = (bf16[16,16,128]{2,1,0:T(8,128)(2,1)S(1)}, bf16[16,16,128]{2,1,0:T(8,128)(2,1)S(1)}, u32[]{:S(2)}, u32[]{:S(2)}) collective-permute-start(bf16[16,16,128]{2,1,0:T(8,128)(2,1)S(1)} %get-tuple-element.34.refs_0_), channel_id=1, source_target_pairs={{0,8},{4,12},{8,0},{12,4},{16,24},{20,28},{24,16},{28,20},{1,9},{5... | collective-permute-start | bytes 196616 | tf_op jit(solution)/shard_map/ppermute | solution.py:371
  37.3 3.0 %collective-permute-start.12 = (bf16[16,16,128]{2,1,0:T(8,128)(2,1)S(1)}, bf16[16,16,128]{2,1,0:T(8,128)(2,1)S(1)}, u32[]{:S(2)}, u32[]{:S(2)}) collective-permute-start(bf16[16,16,128]{2,1,0:T(8,128)(2,1)S(1)} %get-tuple-element.34.refs_0_), channel_id=1, source_target_pairs={{0,4},{4,0},{8,12},{12,8},{16,20},{20,16},{24,28},{28,24},{1,5},{5... | collective-permute-start | bytes 196616 | tf_op jit(solution)/shard_map/ppermute | solution.py:371
  39.0 1.3 %collective-permute-start.15 = (bf16[16,16,128]{2,1,0:T(8,128)(2,1)S(1)}, bf16[16,16,128]{2,1,0:T(8,128)(2,1)S(1)}, u32[]{:S(2)}, u32[]{:S(2)}) collective-permute-start(bf16[16,16,128]{2,1,0:T(8,128)(2,1)S(1)} %collective-permute-done.11.refs_3_), channel_id=1, source_target_pairs={{0,4},{4,0},{8,12},{12,8},{16,20},{20,16},{24,28},{28,24},{1,5},{5... | collective-permute-start | bytes 196616 | tf_op jit(solution)/shard_map/ppermute | solution.py:371
  39.7 1.3 %collective-permute-start.14 = (bf16[16,16,128]{2,1,0:T(8,128)(2,1)S(1)}, bf16[16,16,128]{2,1,0:T(8,128)(2,1)S(1)}, u32[]{:S(2)}, u32[]{:S(2)}) collective-permute-start(bf16[16,16,128]{2,1,0:T(8,128)(2,1)S(1)} %collective-permute-done.10.refs_2_), channel_id=1, source_target_pairs={{0,4},{4,0},{8,12},{12,8},{16,20},{20,16},{24,28},{28,24},{1,5},{5... | collective-permute-start | bytes 196616 | tf_op jit(solution)/shard_map/ppermute | solution.py:371
  40.3 1.3 %collective-permute-start.13 = (bf16[16,16,128]{2,1,0:T(8,128)(2,1)S(1)}, bf16[16,16,128]{2,1,0:T(8,128)(2,1)S(1)}, u32[]{:S(2)}, u32[]{:S(2)}) collective-permute-start(bf16[16,16,128]{2,1,0:T(8,128)(2,1)S(1)} %collective-permute-done.9.refs_1_), channel_id=1, source_target_pairs={{0,4},{4,0},{8,12},{12,8},{16,20},{20,16},{24,28},{28,24},{1,5},{5... | collective-permute-start | bytes 196616 | tf_op jit(solution)/shard_map/ppermute | solution.py:371
  43.3 4.5 %collective-permute-start.16 = (bf16[128,128]{1,0:T(8,128)(2,1)S(1)}, bf16[128,128]{1,0:T(8,128)(2,1)S(1)}, u32[]{:S(2)}, u32[]{:S(2)}) collective-permute-start(bf16[128,128]{1,0:T(8,128)(2,1)S(1)} %get-tuple-element.36), channel_id=1, source_target_pairs={{0,1},{1,0},{2,3},{3,2},{4,5},{5,4},{6,7},{7,6},{8,9},{9,8},{10,11... | collective-permute-start | bytes 98312 | tf_op jit(solution)/shard_map/ppermute | solution.py:371
  43.9 5.3 %collective-permute-start.17 = (bf16[128,128]{1,0:T(8,128)(2,1)S(1)}, bf16[128,128]{1,0:T(8,128)(2,1)S(1)}, u32[]{:S(2)}, u32[]{:S(2)}) collective-permute-start(bf16[128,128]{1,0:T(8,128)(2,1)S(1)} %get-tuple-element.37), channel_id=1, source_target_pairs={{0,2},{1,3},{2,0},{3,1},{4,6},{5,7},{6,4},{7,5},{8,10},{9,11},{10,... | collective-permute-start | bytes 98312 | tf_op jit(solution)/shard_map/ppermute | solution.py:371
  47.3 5.7 %collective-permute-start.18 = (bf16[128,128]{1,0:T(8,128)(2,1)S(1)}, bf16[128,128]{1,0:T(8,128)(2,1)S(1)}, u32[]{:S(2)}, u32[]{:S(2)}) collective-permute-start(bf16[128,128]{1,0:T(8,128)(2,1)S(1)} %get-tuple-element.38), channel_id=1, source_target_pairs={{0,3},{1,2},{2,1},{3,0},{4,7},{5,6},{6,5},{7,4},{8,11},{9,10},{10,... | collective-permute-start | bytes 98312 | tf_op jit(solution)/shard_map/ppermute | solution.py:371

commit v4 on v3

v4 whole, which is shorter than its diff:
```python
import functools
import math

import jax
import jax.numpy as jnp
import numpy as np
from jax import lax
from jax.experimental import pallas as pl
from jax.experimental.pallas import tpu as pltpu
from jax.sharding import PartitionSpec as P

NT = 256
NF = 128
TAPS = 64
KSHIFT = 64
LANES = 128
GROUP = 8
NG = NF // GROUP

F32 = jnp.float32
BF16 = jnp.bfloat16
NN = (((1,), (0,)), ((), ()))
NT_DIMS = (((1,), (1,)), ((), ()))


def make_tables(source_local):
    sample = np.arange(NT)
    bins = np.arange(NF)
    angles = 2.0 * np.pi / NT * (bins[:, None] * sample[None, :] % NT)
    forward = np.concatenate([np.cos(angles), -np.sin(angles)], axis=0)
    weights = np.where(bins == 0, 1.0, 2.0) / NT
    inverse = (forward * np.concatenate([weights, weights])[:, None]).T
    tap = np.arange(TAPS, dtype=np.float64)
    fraction = np.arange(KSHIFT) * (TAPS / (4.0 * KSHIFT))
    offset = tap[None, :] - 0.375 * TAPS - fraction[:, None]
    window = 0.5 - 0.5 * np.cos(2.0 * np.pi * (tap + 0.5) / TAPS)
    tap_spec = forward[:, :TAPS] @ (np.sinc(offset) * window[None, :]).T
    return dict(
        forward=jnp.asarray(forward, F32).astype(BF16),
        inverse=jnp.asarray(inverse, F32).astype(BF16),
        taps=jnp.asarray(np.tile(tap_spec, (1, LANES // KSHIFT)), F32),
        gather=gather_table(source_local),
        gather_half=gather_table(source_local // 2),
        spread=spread_table(source_local // 2),
    )


def gather_table(sources):
    source_of = np.arange(sources * GROUP) // GROUP
    pick = source_of[:, None] == np.arange(sources)[None, :]
    return jnp.asarray(np.tile(pick, (1, LANES // sources)), F32).astype(BF16)


def spread_table(sources):
    pick = (np.arange(sources * GROUP)[None, :] // GROUP == np.arange(sources)[:, None]).astype(
        np.float32
    )
    blocks = LANES // sources
    table = np.zeros((2, blocks // 2, blocks, sources, 2, sources * GROUP), np.float32)
    for core in range(2):
        for pair in range(blocks // 2):
            table[core, pair, 2 * pair + core, :, 0] = pick
            table[core, pair, 2 * pair + 1 - core, :, 1] = pick
    table = table.reshape(2, blocks // 2, LANES, 2 * sources * GROUP)
    return jnp.asarray(table, F32).astype(BF16)


def mm(left, right, dims=NN):
    return lax.dot_general(left, right, dims, preferred_element_type=F32)


def interleave(first, second):
    width = first.shape[-1]
    pair = jnp.stack(
        [first.reshape(NG, GROUP, width), second.reshape(NG, GROUP, width)], axis=1
    )
    return pair.reshape(NG, 2 * GROUP, width)


def same_bin(rows, lanes):
    row = lax.broadcasted_iota(jnp.int32, (rows, lanes), 0)
    lane = lax.broadcasted_iota(jnp.int32, (rows, lanes), 1)
    return (row % GROUP) == (lane % GROUP)


def store_vector(vector_ref, place, re, im):
    receivers = re.shape[-1]
    vector_ref[:, place, :, :receivers] = interleave(re, im).astype(BF16)
    vector_ref[:, place, :, receivers:] = interleave(-im, re).astype(BF16)


def unpack(spectra_ref):
    receivers = spectra_ref.shape[-1]
    values = spectra_ref[...].astype(F32).reshape(NG, 2, GROUP, receivers)
    return values[:, 0].reshape(NF, receivers), values[:, 1].reshape(NF, receivers)


def apply_matrix(matrix_refs, vector_ref, kept_ref, gather, store):
    fields = vector_ref.shape[1]
    rows = fields * 2 * GROUP
    half = matrix_refs[0].shape[1] * matrix_refs[0].shape[2]
    width = half * len(matrix_refs)
    blocks = LANES // (width // GROUP)
    members = blocks // 2
    sets = fields // members
    diagonal = same_bin(rows, width)
    block_of = lax.broadcasted_iota(jnp.int32, (sets, GROUP, LANES), 2) // (LANES // blocks)

    for group in range(NG):
        vector = vector_ref[group].reshape(rows, vector_ref.shape[-1])
        matrix = [ref[group].reshape(half, ref.shape[-1]) for ref in matrix_refs]
        matrix = matrix[0] if len(matrix) == 1 else jnp.concatenate(matrix, axis=0)
        full = mm(vector, matrix, NT_DIMS)
        kept_ref[group * rows : (group + 1) * rows, :] = jnp.where(diagonal, full, 0.0).astype(BF16)

    for couple in range(NG // 2):
        kept = kept_ref[couple * 2 * rows : (couple + 1) * 2 * rows, :]
        spread = mm(kept, gather).reshape(2, sets, members, 2, GROUP, LANES)
        both = []
        for one in range(2):
            value = spread[one, :, 0, 0]
            for block in range(1, blocks):
                term = spread[one, :, block % members, block // members]
                value = jnp.where(block_of == block, term, value)
            both.append(value)
        store(couple * 2 * GROUP, jnp.concatenate(both, axis=1).astype(BF16))


def make_delays(first, count, forward_ref, deconv_ref, taps_ref, gain, delay_ref):
    deconv = deconv_ref[...]
    sources = deconv.shape[0]
    deconv_high = deconv.astype(BF16)
    deconv_low = (deconv - deconv_high.astype(F32)).astype(BF16)
    head = forward_ref[:, :TAPS]
    wave = (mm(head, deconv_high, NT_DIMS) + mm(head, deconv_low, NT_DIMS)) * gain
    wave_high = wave.astype(BF16)
    wave_low = (wave - wave_high.astype(F32)).astype(BF16)
    wave_both = jnp.concatenate([wave_high, wave_low], axis=1)
    taps = taps_ref[...]
    taps_re, taps_im = taps[:NF], taps[NF:]
    owner = lax.broadcasted_iota(jnp.int32, (2 * sources, 2 * LANES), 0) % sources
    place = lax.broadcasted_iota(jnp.int32, (2 * sources, 2 * LANES), 1) // KSHIFT
    for quad in range(count // 4):
        spread = mm(wave_both, (owner == place + (first + 4 * quad)).astype(F32).astype(BF16))
        for couple in range(2):
            lanes = slice(couple * LANES, (couple + 1) * LANES)
            wave_re, wave_im = spread[:NF, lanes], spread[NF:, lanes]
            delay_re = taps_re * wave_re - taps_im * wave_im
            delay_im = taps_re * wave_im + taps_im * wave_re
            delay_ref[2 * quad + couple] = jnp.concatenate([delay_re, delay_im], axis=0).astype(BF16)


def make_matrix(first, couple, forward, traces_ref, shift_ref, delay_ref, matrix_ref):
    receivers = shift_ref.shape[1]
    source = first + 2 * couple
    zeros = jnp.zeros((KSHIFT, receivers), F32)
    kinds = lax.broadcasted_iota(jnp.int32, (KSHIFT, receivers), 0)
    signals = traces_ref[2 * couple : 2 * couple + 2].reshape(2 * receivers, NT)
    raw = mm(forward, signals, NT_DIMS)
    hot = [
        (kinds == shift_ref[source + half : source + half + 1, :]).astype(F32)
        for half in range(2)
    ]
    hot = jnp.concatenate(
        [jnp.concatenate([hot[0], zeros], axis=1), jnp.concatenate([zeros, hot[1]], axis=1)],
        axis=0,
    ).astype(BF16)
    delay = mm(delay_ref[couple], hot)
    re = raw[:NF] * delay[:NF] - raw[NF:] * delay[NF:]
    im = raw[:NF] * delay[NF:] + raw[NF:] * delay[:NF]
    matrix_ref[:, couple, :, :receivers] = interleave(
        re[:, :receivers], re[:, receivers:]
    ).astype(BF16)
    matrix_ref[:, couple, :, receivers:] = interleave(
        im[:, :receivers], im[:, receivers:]
    ).astype(BF16)


def make_sums(first, rcv_index, matrix_ref, vector_ref, kept_ref, gather, onset_ref, sum_ref):
    half = 2 * matrix_ref.shape[1]
    sets = vector_ref.shape[1] // (LANES // half // 2)

    def store(row, value):
        for one in range(sets):
            sum_ref[one * NF + row : one * NF + row + 2 * GROUP, :] = value[one]

    apply_matrix([matrix_ref], vector_ref, kept_ref, gather, store)
    own = onset_ref[...].astype(F32)[:, first : first + half]
    turns = LANES // (2 * half)
    own = jnp.concatenate([own[0:1], own[1:2]] * turns, axis=1)
    own = jnp.broadcast_to(own, (2 * GROUP, LANES))
    row = lax.broadcasted_iota(jnp.int32, own.shape, 0)
    lane = lax.broadcasted_iota(jnp.int32, own.shape, 1)
    here = (row == rcv_index // turns) & (lane // (2 * half) == rcv_index % turns)
    sum_ref[sets * NF :, :] = jnp.where(here, own, 0.0).astype(BF16)


def first_kernel(
    gain, index_ref, traces_hbm, shift_hbm, deconv_hbm, focal_hbm, onset_hbm,
    forward_hbm, taps_hbm, gather_hbm, matrix_ref, sum_ref, own_ref, vector_ref,
    kept_ref, traces_ref, shift_ref, deconv_ref, focal_ref, onset_ref,
    forward_ref, taps_ref, gather_ref, trace_sem, small_sem, delay_ref,
):
    half = traces_ref.shape[0]
    fields = focal_ref.shape[0]
    small = [
        pltpu.make_async_copy(source, target, small_sem.at[place])
        for place, (source, target) in enumerate(
            [
                (forward_hbm, forward_ref),
                (deconv_hbm, deconv_ref),
                (taps_hbm, taps_ref),
                (focal_hbm, focal_ref),
                (shift_hbm, shift_ref),
                (gather_hbm, gather_ref),
                (onset_hbm, onset_ref),
            ]
        )
    ]
    chunks = trace_sem.shape[0]
    step = half // chunks
    large = [
        pltpu.make_async_copy(
            traces_hbm.at[pl.ds(chunk * step, step)],
            traces_ref.at[pl.ds(chunk * step, step)],
            trace_sem.at[chunk],
        )
        for chunk in range(chunks)
    ]
    for copy in small[:5] + large + small[5:]:
        copy.start()
    for copy in small[:3]:
        copy.wait()
    make_delays(0, half, forward_ref, deconv_ref, taps_ref, gain, delay_ref)
    forward = forward_ref[...]
    small[3].wait()
    own_ref[...] = focal_ref[index_ref[0]]
    for place in range(fields):
        spectra = mm(forward, focal_ref[place], NT_DIMS)
        store_vector(vector_ref, place, spectra[:NF], spectra[NF:])
    small[4].wait()
    for couple in range(half // 2):
        if (2 * couple) % step == 0:
            large[2 * couple // step].wait()
        make_matrix(0, couple, forward, traces_ref, shift_ref, delay_ref, matrix_ref)
    small[5].wait()
    small[6].wait()
    make_sums(
        0, index_ref[1], matrix_ref, vector_ref, kept_ref, gather_ref[...], onset_ref, sum_ref
    )


def rest_kernel(
    gain, index_ref, traces_ref, shift_ref, deconv_ref, onset_ref, forward_ref, taps_ref,
    gather_ref, vector_ref, matrix_ref, sum_ref, kept_ref, delay_ref,
):
    half = traces_ref.shape[0] // 2
    make_delays(half, half, forward_ref, deconv_ref, taps_ref, gain, delay_ref)
    forward = forward_ref[...]
    upper = traces_ref.at[pl.ds(half, half)]
    for couple in range(half // 2):
        make_matrix(half, couple, forward, upper, shift_ref, delay_ref, matrix_ref)
    make_sums(
        half, index_ref[1], matrix_ref, vector_ref, kept_ref, gather_ref[...], onset_ref, sum_ref
    )


def split_halves(first, second):
    lane = lax.broadcasted_iota(jnp.int32, first.shape, 1)
    low = lane < LANES // 2
    re = jnp.where(low, first, pltpu.roll(second, LANES // 2, 1))
    im = jnp.where(low, pltpu.roll(first, LANES // 2, 1), second)
    return jnp.concatenate([re, im], axis=0)


def mute(signal, onset):
    sample = lax.broadcasted_iota(jnp.int32, signal.shape, 0)
    folded = jnp.minimum(sample, NT - sample).astype(F32)
    return jnp.where(folded < onset, signal, 0.0)


def mute_half(index_ref, mine_ref, other_ref, forward, inverse, spread_ref, vector_ref):
    shot_index = index_ref[0]
    rcv_index = index_ref[1]
    core = shot_index % 2
    chip = shot_index // 2
    width = vector_ref.shape[-1]
    half = width // GROUP
    blocks = LANES // half
    sets = (mine_ref.shape[0] - 2 * GROUP) // NF
    turns = blocks // 2
    onsets = mine_ref[sets * NF :, :].astype(F32) + other_ref[sets * NF :, :].astype(F32)
    owned = jnp.zeros((NT, LANES), F32)
    diagonal = same_bin(2 * NF, 2 * width)
    for couple in range(sets // 2):
        rows = slice(2 * couple * NF, 2 * (couple + 1) * NF)
        total = mine_ref[rows, :].astype(F32) + other_ref[rows, :].astype(F32)
        spectra = split_halves(total[:NF], total[NF:]).astype(BF16)
        signal = mute(mm(inverse, spectra), onsets[couple : couple + 1, :])
        owned = jnp.where(rcv_index // turns == couple, signal, owned)
        echo = mm(forward, signal.astype(BF16)).astype(BF16)
        for pair in range(blocks // 2):
            slot = (couple * (blocks // 2) + pair) ^ chip
            wide = jnp.where(diagonal, mm(echo, spread_ref[core, pair]), 0.0)
            for part in range(2):
                rows = slice(part * NF, (part + 1) * NF)
                vector_ref[:, part, slot] = interleave(
                    wide[rows, :width], wide[rows, width:]
                ).astype(BF16)
    turn = (turns - rcv_index % turns) % turns
    owned = pltpu.roll(owned, turn * (2 * half), 1)
    return jnp.transpose(owned)[: 2 * half].reshape(2, half, NT)


def mute_kernel(
    index_ref, mine_ref, other_ref, forward_ref, inverse_ref, spread_ref, vector_ref, field_ref
):
    field_ref[...] = mute_half(
        index_ref, mine_ref, other_ref, forward_ref[...], inverse_ref[...], spread_ref, vector_ref
    )


def adjoint_kernel(
    index_ref, mine_ref, other_ref, forward_ref, inverse_ref, spread_ref,
    lower_ref, field_half_ref, first_ref, rest_ref, *refs
):
    field_ref, upper_ref = refs[-2:]
    pairs = (len(refs) - 2) // 2
    keep_refs, send_refs = refs[:pairs], refs[pairs : 2 * pairs]
    receivers = first_ref.shape[-1] // 2
    width = lower_ref.shape[-1]
    half = width // GROUP
    field_ref[:, :half] = field_half_ref[...]
    field_ref[:, half:] = mute_half(
        index_ref, mine_ref, other_ref, forward_ref[...], inverse_ref[...], spread_ref, upper_ref
    )

    def one(group):
        rows = 2 * pairs * 2 * GROUP
        vector = jnp.concatenate(
            [ref[group].reshape(rows, width) for ref in (lower_ref, upper_ref)], axis=1
        )
        matrix = jnp.concatenate(
            [ref[group].reshape(width, 2 * receivers) for ref in (first_ref, rest_ref)], axis=0
        )
        full = mm(vector, matrix).reshape(2, pairs, 2, GROUP, 2 * receivers)
        re = full[0, ..., :receivers] + full[1, ..., receivers:]
        im = full[1, ..., :receivers] - full[0, ..., receivers:]
        return re, im

    for couple in range(NG // 2):
        even = one(2 * couple)
        odd = one(2 * couple + 1)
        for part in range(2):
            both = jnp.concatenate([even[part], odd[part]], axis=2).astype(BF16)
            row = part * NF + couple * 2 * GROUP
            for slot in range(pairs):
                keep_refs[slot][row : row + 2 * GROUP, :] = both[slot, 0]
                send_refs[slot][row : row + 2 * GROUP, :] = both[slot, 1]


def downgoing_kernel(*refs):
    parts = refs[:-6]
    focal_ref, onset_ref, forward_ref, inverse_ref, field_ref, plus_ref = refs[-6:]
    total = parts[0][...].astype(F32)
    for part in parts[1:]:
        total = total + part[...].astype(F32)
    onset = onset_ref[...].astype(F32)
    signal = mute(mm(inverse_ref[...], total.astype(BF16)), onset)
    field = focal_ref[...].astype(F32) + jnp.transpose(signal)
    field_ref[0] = field
    spectra = mm(forward_ref[...], field.astype(BF16), NT_DIMS)
    plus_ref[...] = interleave(spectra[:NF], spectra[NF:]).astype(BF16)


def second_kernel(pairs, index_ref, *refs):
    near_refs, far_refs = refs[:pairs], refs[pairs : 2 * pairs]
    first_ref, rest_ref, gather_ref = refs[2 * pairs : 2 * pairs + 3]
    sum_refs = refs[2 * pairs + 3 : -2]
    vector_ref, kept_ref = refs[-2:]
    shot_index = index_ref[0]
    rcv_index = index_ref[1]
    core = shot_index % 2
    chip = shot_index // 2
    for distance in range(pairs):
        slot = (chip ^ distance) ^ rcv_index
        store_vector(vector_ref, 2 * slot + core, *unpack(near_refs[distance]))
        store_vector(vector_ref, 2 * slot + 1 - core, *unpack(far_refs[distance]))

    def store(row, value):
        for slot in range(pairs):
            sum_refs[slot][row : row + 2 * GROUP, :] = value[slot]

    apply_matrix([first_ref, rest_ref], vector_ref, kept_ref, gather_ref[...], store)


def final_kernel(*refs):
    parts = refs[:-3]
    onset_ref, inverse_ref, field_ref = refs[-3:]
    total = parts[0][...].astype(F32)
    for part in parts[1:]:
        total = total + part[...].astype(F32)
    spectra = split_halves(total, total).astype(BF16)
    onset = onset_ref[...].astype(F32)
    onset = jnp.concatenate([onset[0:1], onset[1:2]] * 2, axis=1)
    signal = mute(mm(inverse_ref[...], spectra), onset)
    field_ref[...] = jnp.transpose(signal)[: LANES // 2].reshape(field_ref.shape)


def vmem(count):
    return [pl.BlockSpec(memory_space=pltpu.VMEM) for _ in range(count)]


def smem():
    return [pl.BlockSpec(memory_space=pltpu.SMEM)]


def hbm(count):
    return [pl.BlockSpec(memory_space=pltpu.HBM) for _ in range(count)]


def call(kernel, name, out_shape, in_specs, scratch=(), work=1.0e9):
    many = isinstance(out_shape, (tuple, list))
    return pl.pallas_call(
        kernel,
        name=name,
        out_shape=out_shape,
        in_specs=in_specs,
        out_specs=vmem(len(out_shape)) if many else vmem(1)[0],
        scratch_shapes=list(scratch),
        compiler_params=pltpu.CompilerParams(vmem_limit_bytes=40 << 20),
        cost_estimate=pl.CostEstimate(flops=int(work), bytes_accessed=1 << 20, transcendentals=0),
    )


def exchange(value, axis, distance):
    count = lax.axis_size(axis)
    return lax.ppermute(value, axis, [(place, place ^ distance) for place in range(count)])


def add_rounded(left, right):
    return (left.astype(F32) + right.astype(F32)).astype(BF16)


def body(traces, shift_index, deconv, focal_start, onset_source, onset_receiver):
    shot_count = lax.axis_size("shot")
    rcv_count = lax.axis_size("rcv")
    sources, receivers, _ = traces.shape
    focal_total = focal_start.shape[0]
    pairs = focal_total // 2
    assert onset_source.shape[0] == 2 and pairs == rcv_count
    assert focal_total == shot_count and 4 * sources == LANES and receivers == LANES
    gain = 1.0 / math.sqrt(NT * receivers * rcv_count)
    tables = make_tables(sources)
    index = jnp.stack([lax.axis_index("shot"), lax.axis_index("rcv")]).astype(jnp.int32)
    shape = jax.ShapeDtypeStruct
    half = sources // 2
    sets = focal_total // (LANES // half // 2)
    vector = shape((NG, focal_total, 2 * GROUP, 2 * receivers), BF16)
    half_matrix = shape((NG, half // 2, 2 * GROUP, 2 * receivers), BF16)
    half_sums = shape((sets * NF + 2 * GROUP, LANES), BF16)
    half_kept = pltpu.VMEM((NG * focal_total * 2 * GROUP, half * GROUP), BF16)
    half_delays = pltpu.VMEM((half // 2, 2 * NF, LANES), BF16)
    assert sets % 2 == 0 and rcv_count <= 2 * GROUP * (LANES // half // 2)

    def buffer(value):
        return pltpu.VMEM(value.shape, value.dtype)

    inputs = (
        traces, shift_index, deconv, focal_start, onset_source,
        tables["forward"], tables["taps"], tables["gather_half"],
    )
    first, first_sum, focal_own, start = call(
        functools.partial(first_kernel, gain),
        "first",
        (half_matrix, half_sums, shape((receivers, NT), BF16), vector),
        smem() + hbm(len(inputs)),
        [half_kept, pltpu.VMEM((half, receivers, NT), BF16)]
        + [buffer(value) for value in inputs[1:]]
        + [pltpu.SemaphoreType.DMA((2,)), pltpu.SemaphoreType.DMA((7,)), half_delays],
        work=4.0e9,
    )(index, *[pltpu.with_memory_space_constraint(value, pltpu.HBM) for value in inputs])
    rest, rest_sum = call(
        functools.partial(rest_kernel, gain),
        "rest",
        (half_matrix, half_sums),
        smem() + vmem(8),
        [half_kept, half_delays],
        work=3.0e9,
    )(
        index, traces, shift_index, deconv, onset_source,
        tables["forward"], tables["taps"], tables["gather_half"], start,
    )

    mine = [first_sum, rest_sum]
    other = [exchange(value, "rcv", 1) for value in mine]
    distance = 1
    while 2 * distance < rcv_count:
        distance *= 2
        mine = [add_rounded(left, right) for left, right in zip(mine, other)]
        other = [exchange(value, "rcv", distance) for value in mine]

    echo = shape((NG, 2, pairs, 2 * GROUP, half * GROUP), BF16)
    shared = (tables["forward"], tables["inverse"], tables["spread"])
    lower, field_half = call(
        mute_kernel,
        "mute",
        (echo, shape((2, half, NT), F32)),
        smem() + vmem(5),
        work=1.0e9,
    )(index, mine[0], other[0], *shared)

    field = shape((2 * NF, receivers), BF16)
    *blocks, upgoing_first = call(
        adjoint_kernel,
        "adjoint",
        [field] * (2 * pairs) + [shape((2, sources, NT), F32)],
        smem() + vmem(9),
        [buffer(echo)],
        work=2.0e9,
    )(index, mine[1], other[1], *shared, lower, field_half, first, rest)

    parts = []
    for distance in reversed(range(pairs)):
        block = add_rounded(blocks[distance], exchange(blocks[pairs + distance], "shot", 1))
        parts.append(exchange(block, "shot", 2 * distance) if distance else block)

    downgoing, plus = call(
        downgoing_kernel,
        "downgoing",
        (
            shape((1, receivers, NT), F32),
            shape((NG, 2 * GROUP, receivers), BF16),
        ),
        vmem(pairs + 4),
    )(*parts, focal_own, onset_receiver, tables["forward"], tables["inverse"])

    near = [plus]
    for distance in range(1, pairs):
        near.append(exchange(plus, "shot", 2 * distance))
    far = [exchange(value, "shot", 1) for value in near]

    parts = call(
        functools.partial(second_kernel, pairs),
        "second",
        [shape((NF, LANES), BF16)] * pairs,
        smem() + vmem(2 * pairs + 3),
        [buffer(vector), pltpu.VMEM((NG * focal_total * 2 * GROUP, sources * GROUP), BF16)],
    )(index, *near, *far, first, rest, tables["gather"])

    parts = [parts[0]] + [
        exchange(parts[distance], "rcv", distance) for distance in range(1, rcv_count)
    ]
    upgoing_second = call(
        final_kernel, "final", shape((2, sources, NT), F32), vmem(len(parts) + 2)
    )(*parts, onset_source, tables["inverse"])
    return (upgoing_first, downgoing, upgoing_second)


def solution(mesh):
    placed = (
        P("shot", "rcv", None),
        P("shot", "rcv"),
        P("shot", None),
        P(None, "rcv", None),
        P("rcv", "shot"),
        P("shot", "rcv"),
    )
    return jax.shard_map(
        body,
        mesh=mesh,
        in_specs=placed,
        out_specs=(P("rcv", "shot", None), P("shot", "rcv", None), P("rcv", "shot", None)),
        check_vma=False,
    )
```

time: 54.1 us -> 52.1 us (0.963)
  waiting for transfers between devices: 22.6 us -> 16 us
  starting transfers between devices: 18.6 us -> 21.2 us
  Pallas kernels: 11.8 us -> 13.7 us
    ppermute x19 -> x21, waiting for transfers between devices: 22.6 us -> 16 us  [exchange(): lax.ppermute(value, axis, [(place, place ^ distance) for place in range(c...]
    ppermute x19 -> x21, starting transfers between devices: 18.6 us -> 21.2 us  [exchange(): lax.ppermute(value, axis, [(place, place ^ distance) for place in range(c...]
    pallas_call x1 -> x3, Pallas kernels: 5.72 us -> 7.84 us  [the longest x1 4.34 us: body(): call(functools.partial(first_kernel, gain), 'first', (half_matrix, half_s...]
  transfers between devices with their start and end apart: 19 -> 21, of which waited for: 13 -> 13; matrix products, arithmetic and copies ran while one was open for 0% -> 0% of each run, Pallas kernels for 0% -> 7%
where the time goes in v4:
time: 52.1 us; the launch traced here: 52 us
  starting transfers between devices  21.2 us (41%)
  waiting for transfers between devices  16 us (31%)
  Pallas kernels  13.7 us (26%)
  between operations  0.81 us (2%)
    ppermute x21, starting transfers between devices, exchange(): lax.ppermute(value, axis, [(place, place ^ distance) for place in range(c...  21.2 us
    ppermute x21, waiting for transfers between devices, exchange(): lax.ppermute(value, axis, [(place, place ^ distance) for place in range(c...  16 us
    pallas_call x1, Pallas kernels, body(): call(functools.partial(first_kernel, gain), 'first', (half_matrix, half_s...  4.34 us
    pallas_call x1, Pallas kernels, body(): call(functools.partial(rest_kernel, gain), 'rest', (half_matrix, half_sum...  2.28 us
    pallas_call x1, Pallas kernels, body(): call(adjoint_kernel, 'adjoint', [field] * (2 * pairs) + [shape((2, source...  2.23 us
    pallas_call x1, Pallas kernels, body(): call(functools.partial(second_kernel, pairs), 'second', [shape((NF, LANES...  1.78 us
    pallas_call x1, Pallas kernels, body(): call(mute_kernel, 'mute', (echo, shape((2, half, NT), F32)), smem() + vme...  1.22 us
  transfers between devices with their start and end apart: 21, of which 13 were waited for; matrix products, arithmetic and copies ran while one was open for 0% of the time, Pallas kernels for 7%

profile of v4, /device:TPU:0, one launch (start us, length us, event | category | flops | bytes accessed | tf_op | source)
XLA Modules:
  0.0 52.0 jit_solution(9484554842857791216)
XLA Ops:
  0.6 0.1 pad_add_fusion.index_ref
  0.7 0.0 copy-start.7
  0.7 0.0 copy-start.8
  0.7 0.0 copy-start.10
  0.8 4.3 %first.1 = (bf16[16,8,16,256]{3,2,1,0:T(8,128)(2,1)S(1)}, bf16[272,128]{1,0:T(8,128)(2,1)S(1)}, bf16[128,256]{1,0:T(8,128)(2,1)S(1)}, bf16[16,8,16,256]{3,2,1,0:T(8,128)(2,1)S(1)}) custom-call(s32[2]{0:T(128)S(1)} %pad_add_fusion.index_ref, bf16[32,128,256]{2,1,0:T(8,128)(2,1)} %traces_ref.1, s32[32,128]{1,0:T(8,128)} %shift_ref.1, f32[32,64]{1,0:T(8,128)} %deconv_ref.1, ...), custom_call_target="tpu_custom_call" | custom-call | flops 4000000000 | bytes 1048576 | tf_op jit(solution)/shard_map/first/pallas_call | solution.py:473
  5.1 3.1 %collective-permute-start.2 = (bf16[272,128]{1,0:T(8,128)(2,1)S(1)}, bf16[272,128]{1,0:T(8,128)(2,1)S(1)}, u32[]{:S(2)}, u32[]{:S(2)}) collective-permute-start(bf16[272,128]{1,0:T(8,128)(2,1)S(1)} %get-tuple-element.28), channel_id=1, source_target_pairs={{0,1},{1,0},{2,3},{3,2},{4,5},{5,4},{6,7},{7,6},{8,9},{9,8},{10,11... | collective-permute-start | bytes 208904 | tf_op jit(solution)/shard_map/ppermute | solution.py:438
  8.2 0.0 copy-done
  8.2 0.0 copy-done.1
  8.2 0.0 copy-done.2
  8.2 0.0 copy-done.3
  8.2 0.0 copy-done.7
  8.2 0.0 copy-done.8
  8.2 0.0 copy-start.5
  8.3 0.0 copy-start.6
  8.3 2.3 %rest.1 = (bf16[16,8,16,256]{3,2,1,0:T(8,128)(2,1)S(1)}, bf16[272,128]{1,0:T(8,128)(2,1)S(1)}) custom-call(s32[2]{0:T(128)S(1)} %pad_add_fusion.index_ref, bf16[32,128,256]{2,1,0:T(8,128)(2,1)S(1)} %copy-done, s32[32,128]{1,0:T(8,128)S(1)} %copy-done.1, f32[32,64]{1,0:T(8,128)S(1)} %copy-done.2, s32[2,32]{1,0:T(2,128)S(1)} %copy-done.3, ...), custom_call_target="tpu_custom_call" | custom-call | flops 3000000000 | bytes 1048576 | tf_op jit(solution)/shard_map/rest/pallas_call | solution.py:483
  10.6 0.1 collective-permute-start
  10.7 0.0 collective-permute-done.2
  10.7 3.1 %collective-permute-start.3 = (bf16[272,128]{1,0:T(8,128)(2,1)S(1)}, bf16[272,128]{1,0:T(8,128)(2,1)S(1)}, u32[]{:S(2)}, u32[]{:S(2)}) collective-permute-start(bf16[272,128]{1,0:T(8,128)(2,1)S(1)} %add_convert_fusion.mine_ref), channel_id=1, source_target_pairs={{0,2},{1,3},{2,0},{3,1},{4,6},{5,7},{6,4},{7,5},{8,10},{9,11},{10,... | collective-permute-start | bytes 208904 | tf_op jit(solution)/shard_map/ppermute | solution.py:438
  13.8 1.6 %collective-permute-done = bf16[272,128]{1,0:T(8,128)(2,1)S(1)} collective-permute-done((bf16[272,128]{1,0:T(8,128)(2,1)S(1)}, bf16[272,128]{1,0:T(8,128)(2,1)S(1)}, u32[]{:S(2)}, u32[]{:S(2)}) %collective-permute-start) | collective-permute-done | bytes 69664 | tf_op jit(solution)/shard_map/ppermute | solution.py:438
  15.4 2.3 %collective-permute-start.1 = (bf16[272,128]{1,0:T(8,128)(2,1)S(1)}, bf16[272,128]{1,0:T(8,128)(2,1)S(1)}, u32[]{:S(2)}, u32[]{:S(2)}) collective-permute-start(bf16[272,128]{1,0:T(8,128)(2,1)S(1)} %add_convert_fusion.1.mine_ref), channel_id=1, source_target_pairs={{0,2},{1,3},{2,0},{3,1},{4,6},{5,7},{6,4},{7,5},{8,10},{9,11},{10,... | collective-permute-start | bytes 208904 | tf_op jit(solution)/shard_map/ppermute | solution.py:438
  17.7 0.0 collective-permute-done.3.other_ref
  17.7 0.0 copy-done.6
  17.7 1.2 %mute.1 = (bf16[16,2,4,16,128]{4,3,2,1,0:T(8,128)(2,1)S(1)}, f32[2,16,256]{2,1,0:T(8,128)S(1)}) custom-call(s32[2]{0:T(128)S(1)} %pad_add_fusion.index_ref, bf16[272,128]{1,0:T(8,128)(2,1)S(1)} %add_convert_fusion.mine_ref, bf16[272,128]{1,0:T(8,128)(2,1)S(1)} %collective-permute-done.3.other_ref, bf16[256,256]{1,0:T(8,128)(2,1)S(1)} %copy-done.7, ...), custom_call_target="tpu_custom_call" | custom-call | flops 1000000000 | bytes 1048576 | tf_op jit(solution)/shard_map/mute/pallas_call | solution.py:505
  18.9 1.9 %collective-permute-done.1.other_ref = bf16[272,128]{1,0:T(8,128)(2,1)S(1)} collective-permute-done((bf16[272,128]{1,0:T(8,128)(2,1)S(1)}, bf16[272,128]{1,0:T(8,128)(2,1)S(1)}, u32[]{:S(2)}, u32[]{:S(2)}) %collective-permute-start.1) | collective-permute-done | bytes 69664 | tf_op jit(solution)/shard_map/ppermute | solution.py:438
  20.8 2.2 %adjoint.1 = (bf16[256,128]{1,0:T(8,128)(2,1)S(1)}, bf16[256,128]{1,0:T(8,128)(2,1)S(1)}, bf16[256,128]{1,0:T(8,128)(2,1)S(1)}, bf16[256,128]{1,0:T(8,128)(2,1)S...) custom-call(s32[2]{0:T(128)S(1)} %pad_add_fusion.index_ref, ...), custom_call_target="tpu_custom_call" | custom-call | flops 2000000000 | bytes 1048576 | tf_op jit(solution)/shard_map/adjoint/pallas_call | solution.py:514
  23.0 0.0 collective-permute-start.4
  23.0 0.5 collective-permute-start.6
  23.6 0.0 collective-permute-start.8
  23.6 0.5 collective-permute-start.10
  24.1 0.2 collective-permute-done.4
  24.3 2.6 %collective-permute-start.5 = (bf16[256,128]{1,0:T(8,128)(2,1)S(1)}, bf16[256,128]{1,0:T(8,128)(2,1)S(1)}, u32[]{:S(2)}, u32[]{:S(2)}) collective-permute-start(bf16[256,128]{1,0:T(8,128)(2,1)S(1)} %add_convert_fusion.5), channel_id=1, source_target_pairs={{0,24},{4,28},{8,16},{12,20},{16,8},{20,12},{24,0},{28,4},{1,25},{... | collective-permute-start | bytes 196616 | tf_op jit(solution)/shard_map/ppermute | solution.py:438
  26.9 0.0 collective-permute-done.6
  26.9 0.0 copy-start.9
  26.9 0.6 %collective-permute-start.7 = (bf16[256,128]{1,0:T(8,128)(2,1)S(1)}, bf16[256,128]{1,0:T(8,128)(2,1)S(1)}, u32[]{:S(2)}, u32[]{:S(2)}) collective-permute-start(bf16[256,128]{1,0:T(8,128)(2,1)S(1)} %add_convert_fusion.4), channel_id=1, source_target_pairs={{0,16},{4,20},{8,24},{12,28},{16,0},{20,4},{24,8},{28,12},{1,17},{... | collective-permute-start | bytes 196616 | tf_op jit(solution)/shard_map/ppermute | solution.py:438
  27.5 0.0 collective-permute-done.8
  27.5 0.6 %collective-permute-start.9 = (bf16[256,128]{1,0:T(8,128)(2,1)S(1)}, bf16[256,128]{1,0:T(8,128)(2,1)S(1)}, u32[]{:S(2)}, u32[]{:S(2)}) collective-permute-start(bf16[256,128]{1,0:T(8,128)(2,1)S(1)} %add_convert_fusion.3), channel_id=1, source_target_pairs={{0,8},{4,12},{8,0},{12,4},{16,24},{20,28},{24,16},{28,20},{1,9},{5... | collective-permute-start | bytes 196616 | tf_op jit(solution)/shard_map/ppermute | solution.py:438
  28.1 0.0 collective-permute-done.10
  28.1 1.5 %collective-permute-done.5.refs_0_ = bf16[256,128]{1,0:T(8,128)(2,1)S(1)} collective-permute-done((bf16[256,128]{1,0:T(8,128)(2,1)S(1)}, bf16[256,128]{1,0:T(8,128)(2,1)S(1)}, u32[]{:S(2)}, u32[]{:S(2)}) %collective-permute-start.5) | collective-permute-done | bytes 65568 | tf_op jit(solution)/shard_map/ppermute | solution.py:438
  29.6 1.7 %collective-permute-done.7.refs_1_ = bf16[256,128]{1,0:T(8,128)(2,1)S(1)} collective-permute-done((bf16[256,128]{1,0:T(8,128)(2,1)S(1)}, bf16[256,128]{1,0:T(8,128)(2,1)S(1)}, u32[]{:S(2)}, u32[]{:S(2)}) %collective-permute-start.7) | collective-permute-done | bytes 65568 | tf_op jit(solution)/shard_map/ppermute | solution.py:438
  31.3 0.6 %collective-permute-done.9.refs_2_ = bf16[256,128]{1,0:T(8,128)(2,1)S(1)} collective-permute-done((bf16[256,128]{1,0:T(8,128)(2,1)S(1)}, bf16[256,128]{1,0:T(8,128)(2,1)S(1)}, u32[]{:S(2)}, u32[]{:S(2)}) %collective-permute-start.9) | collective-permute-done | bytes 65568 | tf_op jit(solution)/shard_map/ppermute | solution.py:438
  31.9 0.9 %downgoing.1 = (f32[1,128,256]{2,1,0:T(8,128)}, bf16[16,16,128]{2,1,0:T(8,128)(2,1)S(1)}) custom-call(bf16[256,128]{1,0:T(8,128)(2,1)S(1)} %collective-permute-done.5.refs_0_, bf16[256,128]{1,0:T(8,128)(2,1)S(1)} %collective-permute-done.7.refs_1_, bf16[256,128]{1,0:T(8,128)(2,1)S(1)} %collective-permute-done.9.refs_2_, ...), custom_call_target="tpu_custom_call" | custom-call | flops 1000000000 | bytes 1048576 | tf_op jit(solution)/shard_map/downgoing/pallas_call | solution.py:528
  32.8 1.5 %collective-permute-start.13 = (bf16[16,16,128]{2,1,0:T(8,128)(2,1)S(1)}, bf16[16,16,128]{2,1,0:T(8,128)(2,1)S(1)}, u32[]{:S(2)}, u32[]{:S(2)}) collective-permute-start(bf16[16,16,128]{2,1,0:T(8,128)(2,1)S(1)} %get-tuple-element.44.refs_0_), channel_id=1, source_target_pairs={{0,24},{4,28},{8,16},{12,20},{16,8},{20,12},{24,0},{28,4},{1,25},{... | collective-permute-start | bytes 196616 | tf_op jit(solution)/shard_map/ppermute | solution.py:438
  34.3 0.6 %collective-permute-start.12 = (bf16[16,16,128]{2,1,0:T(8,128)(2,1)S(1)}, bf16[16,16,128]{2,1,0:T(8,128)(2,1)S(1)}, u32[]{:S(2)}, u32[]{:S(2)}) collective-permute-start(bf16[16,16,128]{2,1,0:T(8,128)(2,1)S(1)} %get-tuple-element.44.refs_0_), channel_id=1, source_target_pairs={{0,16},{4,20},{8,24},{12,28},{16,0},{20,4},{24,8},{28,12},{1,17},{... | collective-permute-start | bytes 196616 | tf_op jit(solution)/shard_map/ppermute | solution.py:438
  34.9 1.4 %collective-permute-start.11 = (bf16[16,16,128]{2,1,0:T(8,128)(2,1)S(1)}, bf16[16,16,128]{2,1,0:T(8,128)(2,1)S(1)}, u32[]{:S(2)}, u32[]{:S(2)}) collective-permute-start(bf16[16,16,128]{2,1,0:T(8,128)(2,1)S(1)} %get-tuple-element.44.refs_0_), channel_id=1, source_target_pairs={{0,8},{4,12},{8,0},{12,4},{16,24},{20,28},{24,16},{28,20},{1,9},{5... | collective-permute-start | bytes 196616 | tf_op jit(solution)/shard_map/ppermute | solution.py:438
  36.3 0.0 collective-permute-start.14
  36.3 1.7 %collective-permute-done.13.refs_3_ = bf16[16,16,128]{2,1,0:T(8,128)(2,1)S(1)} collective-permute-done((bf16[16,16,128]{2,1,0:T(8,128)(2,1)S(1)}, bf16[16,16,128]{2,1,0:T(8,128)(2,1)S(1)}, u32[]{:S(2)}, u32[]{:S(2)}) %collective-permute-start.13) | collective-permute-done | bytes 65568 | tf_op jit(solution)/shard_map/ppermute | solution.py:438
  38.0 0.0 collective-permute-start.17
  38.0 0.7 %collective-permute-done.12.refs_2_ = bf16[16,16,128]{2,1,0:T(8,128)(2,1)S(1)} collective-permute-done((bf16[16,16,128]{2,1,0:T(8,128)(2,1)S(1)}, bf16[16,16,128]{2,1,0:T(8,128)(2,1)S(1)}, u32[]{:S(2)}, u32[]{:S(2)}) %collective-permute-start.12) | collective-permute-done | bytes 65568 | tf_op jit(solution)/shard_map/ppermute | solution.py:438
  38.7 0.0 collective-permute-start.16
  38.7 0.5 collective-permute-done.11.refs_1_
  39.2 0.0 collective-permute-start.15
  39.2 0.0 collective-permute-done.14.refs_4_
  39.2 0.0 collective-permute-done.17.refs_7_
  39.2 0.7 %collective-permute-done.16.refs_6_ = bf16[16,16,128]{2,1,0:T(8,128)(2,1)S(1)} collective-permute-done((bf16[16,16,128]{2,1,0:T(8,128)(2,1)S(1)}, bf16[16,16,128]{2,1,0:T(8,128)(2,1)S(1)}, u32[]{:S(2)}, u32[]{:S(2)}) %collective-permute-start.16) | collective-permute-done | bytes 65568 | tf_op jit(solution)/shard_map/ppermute | solution.py:438
  39.9 0.5 collective-permute-done.15.refs_5_
  40.4 0.0 copy-done.9
  40.4 1.8 %second.1 = (bf16[128,128]{1,0:T(8,128)(2,1)S(1)}, bf16[128,128]{1,0:T(8,128)(2,1)S(1)}, bf16[128,128]{1,0:T(8,128)(2,1)S(1)}, bf16[128,128]{1,0:T(8,128)(2,1)S(1)}) custom-call(s32[2]{0:T(128)S(1)} %pad_add_fusion.index_ref, bf16[16,16,128]{2,1,0:T(8,128)(2,1)S(1)} %get-tuple-element.44.refs_0_, bf16[16,16,128]{2,1,0:T(8,128)(2,1)S(1)} %collective-permute-done.11.refs_1_, ...), custom_call_target="tpu_custom_call" | custom-call | flops 1000000000 | bytes 1048576 | tf_op jit(solution)/shard_map/second/pallas_call | solution.py:543
  42.2 0.1 collective-permute-start.18
  42.3 3.0 %collective-permute-start.19 = (bf16[128,128]{1,0:T(8,128)(2,1)S(1)}, bf16[128,128]{1,0:T(8,128)(2,1)S(1)}, u32[]{:S(2)}, u32[]{:S(2)}) collective-permute-start(bf16[128,128]{1,0:T(8,128)(2,1)S(1)} %get-tuple-element.47), channel_id=1, source_target_pairs={{0,2},{1,3},{2,0},{3,1},{4,6},{5,7},{6,4},{7,5},{8,10},{9,11},{10,... | collective-permute-start | bytes 98312 | tf_op jit(solution)/shard_map/ppermute | solution.py:438
  45.3 1.3 %collective-permute-start.20 = (bf16[128,128]{1,0:T(8,128)(2,1)S(1)}, bf16[128,128]{1,0:T(8,128)(2,1)S(1)}, u32[]{:S(2)}, u32[]{:S(2)}) collective-permute-start(bf16[128,128]{1,0:T(8,128)(2,1)S(1)} %get-tuple-element.48), channel_id=1, source_target_pairs={{0,3},{1,2},{2,1},{3,0},{4,7},{5,6},{6,5},{7,4},{8,11},{9,10},{10,... | collective-permute-start | bytes 98312 | tf_op jit(solution)/shard_map/ppermute | solution.py:438
  46.7 0.0 collective-permute-done.18.refs_1_
  46.7 0.9 %collective-permute-done.19.refs_2_ = bf16[128,128]{1,0:T(8,128)(2,1)S(1)} collective-permute-done((bf16[128,128]{1,0:T(8,128)(2,1)S(1)}, bf16[128,128]{1,0:T(8,128)(2,1)S(1)}, u32[]{:S(2)}, u32[]{:S(2)}) %collective-permute-start.19) | collective-permute-done | bytes 32800 | tf_op jit(solution)/shard_map/ppermute | solution.py:438
  47.5 3.5 %collective-permute-done.20.refs_3_ = bf16[128,128]{1,0:T(8,128)(2,1)S(1)} collective-permute-done((bf16[128,128]{1,0:T(8,128)(2,1)S(1)}, bf16[128,128]{1,0:T(8,128)(2,1)S(1)}, u32[]{:S(2)}, u32[]{:S(2)}) %collective-permute-start.20) | collective-permute-done | bytes 32800 | tf_op jit(solution)/shard_map/ppermute | solution.py:438
  51.0 0.9 %final.1 = f32[2,32,256]{2,1,0:T(8,128)} custom-call(bf16[128,128]{1,0:T(8,128)(2,1)S(1)} %get-tuple-element.45.refs_0_, bf16[128,128]{1,0:T(8,128)(2,1)S(1)} %collective-permute-done.18.refs_1_, bf16[128,128]{1,0:T(8,128)(2,1)S(1)} %collective-permute-done.19.refs_2_, bf16[128,128]{1,0:T(8,128)(2,1)S(1)} %collective-permute-done.20.refs_3_, ...), custom_call_target="tpu_custom_call" | custom-call | flops 1000000000 | bytes 1048576 | tf_op jit(solution)/shard_map/final/pallas_call | solution.py:554
  (14 shorter events, 0.1 us)
Async XLA Ops:
  0.7 7.5 %copy-start = (bf16[32,128,256]{2,1,0:T(8,128)(2,1)S(1)}, bf16[32,128,256]{2,1,0:T(8,128)(2,1)}, u32[]{:S(2)}) copy-start(bf16[32,128,256]{2,1,0:T(8,128)(2,1)} %traces_ref.1) | copy-start | bytes 6291460
  0.7 7.5 %copy-start.1 = (s32[32,128]{1,0:T(8,128)S(1)}, s32[32,128]{1,0:T(8,128)}, u32[]{:S(2)}) copy-start(s32[32,128]{1,0:T(8,128)} %shift_ref.1) | copy-start | bytes 49156
  0.7 7.5 %copy-start.2 = (f32[32,64]{1,0:T(8,128)S(1)}, f32[32,64]{1,0:T(8,128)}, u32[]{:S(2)}) copy-start(f32[32,64]{1,0:T(8,128)} %deconv_ref.1) | copy-start | bytes 24580
  0.7 7.5 %copy-start.3 = (s32[2,32]{1,0:T(2,128)S(1)}, s32[2,32]{1,0:T(2,128)}, u32[]{:S(2)}) copy-start(s32[2,32]{1,0:T(2,128)} %refs_4_.1) | copy-start | bytes 772
  0.7 7.5 %copy-start.7 = (bf16[256,256]{1,0:T(8,128)(2,1)S(1)}, bf16[256,256]{1,0:T(8,128)(2,1)}, u32[]{:S(2)}) copy-start(bf16[256,256]{1,0:T(8,128)(2,1)} %constant.29.forward_hbm.forward_ref.refs_6_) | copy-start | bytes 393220
  0.7 7.5 %copy-start.8 = (f32[256,128]{1,0:T(8,128)S(1)}, f32[256,128]{1,0:T(8,128)}, u32[]{:S(2)}) copy-start(f32[256,128]{1,0:T(8,128)} %constant.23.clone.taps_hbm.taps_ref) | copy-start | bytes 393220
  0.7 7.5 %copy-start.10 = (bf16[128,128]{1,0:T(8,128)(2,1)S(1)}, bf16[128,128]{1,0:T(8,128)(2,1)}, u32[]{:S(2)}) copy-start(bf16[128,128]{1,0:T(8,128)(2,1)} %constant.30.gather_hbm.gather_ref) | copy-start | bytes 98308
  5.1 5.6 %collective-permute-start.2 = (bf16[272,128]{1,0:T(8,128)(2,1)S(1)}, bf16[272,128]{1,0:T(8,128)(2,1)S(1)}, u32[]{:S(2)}, u32[]{:S(2)}) collective-permute-start(bf16[272,128]{1,0:T(8,128)(2,1)S(1)} %get-tuple-element.28), channel_id=1, source_target_pairs={{0,1},{1,0},{2,3},{3,2},{4,5},{5,4},{6,7},{7,6},{8,9},{9,8},{10,11... | collective-permute-start | bytes 208904 | tf_op jit(solution)/shard_map/ppermute | solution.py:438
  8.2 9.4 %copy-start.5 = (bf16[2,4,128,256]{3,2,1,0:T(8,128)(2,1)S(1)}, bf16[2,4,128,256]{3,2,1,0:T(8,128)(2,1)}, u32[]{:S(2)}) copy-start(bf16[2,4,128,256]{3,2,1,0:T(8,128)(2,1)} %constant.32.spread_ref) | copy-start | bytes 1572868
  8.3 9.4 %copy-start.6 = (bf16[256,256]{1,0:T(8,128)(2,1)S(1)}, bf16[256,256]{1,0:T(8,128)(2,1)}, u32[]{:S(2)}) copy-start(bf16[256,256]{1,0:T(8,128)(2,1)} %constant.31.inverse_ref.refs_7_.refs_5_) | copy-start | bytes 393220
  10.6 4.8 %collective-permute-start = (bf16[272,128]{1,0:T(8,128)(2,1)S(1)}, bf16[272,128]{1,0:T(8,128)(2,1)S(1)}, u32[]{:S(2)}, u32[]{:S(2)}) collective-permute-start(bf16[272,128]{1,0:T(8,128)(2,1)S(1)} %get-tuple-element.27), channel_id=1, source_target_pairs={{0,1},{1,0},{2,3},{3,2},{4,5},{5,4},{6,7},{7,6},{8,9},{9,8},{10,11... | collective-permute-start | bytes 208904 | tf_op jit(solution)/shard_map/ppermute | solution.py:438
  10.7 7.0 %collective-permute-start.3 = (bf16[272,128]{1,0:T(8,128)(2,1)S(1)}, bf16[272,128]{1,0:T(8,128)(2,1)S(1)}, u32[]{:S(2)}, u32[]{:S(2)}) collective-permute-start(bf16[272,128]{1,0:T(8,128)(2,1)S(1)} %add_convert_fusion.mine_ref), channel_id=1, source_target_pairs={{0,2},{1,3},{2,0},{3,1},{4,6},{5,7},{6,4},{7,5},{8,10},{9,11},{10,... | collective-permute-start | bytes 208904 | tf_op jit(solution)/shard_map/ppermute | solution.py:438
  15.4 5.4 %collective-permute-start.1 = (bf16[272,128]{1,0:T(8,128)(2,1)S(1)}, bf16[272,128]{1,0:T(8,128)(2,1)S(1)}, u32[]{:S(2)}, u32[]{:S(2)}) collective-permute-start(bf16[272,128]{1,0:T(8,128)(2,1)S(1)} %add_convert_fusion.1.mine_ref), channel_id=1, source_target_pairs={{0,2},{1,3},{2,0},{3,1},{4,6},{5,7},{6,4},{7,5},{8,10},{9,11},{10,... | collective-permute-start | bytes 208904 | tf_op jit(solution)/shard_map/ppermute | solution.py:438
  20.8 11.0 %copy-start.4 = (s32[1,128]{1,0:T(1,128)S(1)}, s32[1,128]{1,0:T(1,128)}, u32[]{:S(2)}) copy-start(s32[1,128]{1,0:T(1,128)} %refs_5_.1) | copy-start | bytes 1540
  23.0 1.3 %collective-permute-start.4 = (bf16[256,128]{1,0:T(8,128)(2,1)S(1)}, bf16[256,128]{1,0:T(8,128)(2,1)S(1)}, u32[]{:S(2)}, u32[]{:S(2)}) collective-permute-start(bf16[256,128]{1,0:T(8,128)(2,1)S(1)} %get-tuple-element.35), channel_id=1, source_target_pairs={{0,4},{4,0},{8,12},{12,8},{16,20},{20,16},{24,28},{28,24},{1,5},{5... | collective-permute-start | bytes 196616 | tf_op jit(solution)/shard_map/ppermute | solution.py:438
  23.0 3.8 %collective-permute-start.6 = (bf16[256,128]{1,0:T(8,128)(2,1)S(1)}, bf16[256,128]{1,0:T(8,128)(2,1)S(1)}, u32[]{:S(2)}, u32[]{:S(2)}) collective-permute-start(bf16[256,128]{1,0:T(8,128)(2,1)S(1)} %get-tuple-element.37), channel_id=1, source_target_pairs={{0,4},{4,0},{8,12},{12,8},{16,20},{20,16},{24,28},{28,24},{1,5},{5... | collective-permute-start | bytes 196616 | tf_op jit(solution)/shard_map/ppermute | solution.py:438
  23.6 3.9 %collective-permute-start.8 = (bf16[256,128]{1,0:T(8,128)(2,1)S(1)}, bf16[256,128]{1,0:T(8,128)(2,1)S(1)}, u32[]{:S(2)}, u32[]{:S(2)}) collective-permute-start(bf16[256,128]{1,0:T(8,128)(2,1)S(1)} %get-tuple-element.39), channel_id=1, source_target_pairs={{0,4},{4,0},{8,12},{12,8},{16,20},{20,16},{24,28},{28,24},{1,5},{5... | collective-permute-start | bytes 196616 | tf_op jit(solution)/shard_map/ppermute | solution.py:438
  23.6 4.5 %collective-permute-start.10 = (bf16[256,128]{1,0:T(8,128)(2,1)S(1)}, bf16[256,128]{1,0:T(8,128)(2,1)S(1)}, u32[]{:S(2)}, u32[]{:S(2)}) collective-permute-start(bf16[256,128]{1,0:T(8,128)(2,1)S(1)} %get-tuple-element.41), channel_id=1, source_target_pairs={{0,4},{4,0},{8,12},{12,8},{16,20},{20,16},{24,28},{28,24},{1,5},{5... | collective-permute-start | bytes 196616 | tf_op jit(solution)/shard_map/ppermute | solution.py:438
  24.3 5.2 %collective-permute-start.5 = (bf16[256,128]{1,0:T(8,128)(2,1)S(1)}, bf16[256,128]{1,0:T(8,128)(2,1)S(1)}, u32[]{:S(2)}, u32[]{:S(2)}) collective-permute-start(bf16[256,128]{1,0:T(8,128)(2,1)S(1)} %add_convert_fusion.5), channel_id=1, source_target_pairs={{0,24},{4,28},{8,16},{12,20},{16,8},{20,12},{24,0},{28,4},{1,25},{... | collective-permute-start | bytes 196616 | tf_op jit(solution)/shard_map/ppermute | solution.py:438
  26.9 13.5 %copy-start.9 = (bf16[256,128]{1,0:T(8,128)(2,1)S(1)}, bf16[256,128]{1,0:T(8,128)(2,1)}, u32[]{:S(2)}) copy-start(bf16[256,128]{1,0:T(8,128)(2,1)} %constant.33.refs_10_) | copy-start | bytes 196612
  26.9 4.3 %collective-permute-start.7 = (bf16[256,128]{1,0:T(8,128)(2,1)S(1)}, bf16[256,128]{1,0:T(8,128)(2,1)S(1)}, u32[]{:S(2)}, u32[]{:S(2)}) collective-permute-start(bf16[256,128]{1,0:T(8,128)(2,1)S(1)} %add_convert_fusion.4), channel_id=1, source_target_pairs={{0,16},{4,20},{8,24},{12,28},{16,0},{20,4},{24,8},{28,12},{1,17},{... | collective-permute-start | bytes 196616 | tf_op jit(solution)/shard_map/ppermute | solution.py:438
  27.5 4.3 %collective-permute-start.9 = (bf16[256,128]{1,0:T(8,128)(2,1)S(1)}, bf16[256,128]{1,0:T(8,128)(2,1)S(1)}, u32[]{:S(2)}, u32[]{:S(2)}) collective-permute-start(bf16[256,128]{1,0:T(8,128)(2,1)S(1)} %add_convert_fusion.3), channel_id=1, source_target_pairs={{0,8},{4,12},{8,0},{12,4},{16,24},{20,28},{24,16},{28,20},{1,9},{5... | collective-permute-start | bytes 196616 | tf_op jit(solution)/shard_map/ppermute | solution.py:438
  32.8 5.2 %collective-permute-start.13 = (bf16[16,16,128]{2,1,0:T(8,128)(2,1)S(1)}, bf16[16,16,128]{2,1,0:T(8,128)(2,1)S(1)}, u32[]{:S(2)}, u32[]{:S(2)}) collective-permute-start(bf16[16,16,128]{2,1,0:T(8,128)(2,1)S(1)} %get-tuple-element.44.refs_0_), channel_id=1, source_target_pairs={{0,24},{4,28},{8,16},{12,20},{16,8},{20,12},{24,0},{28,4},{1,25},{... | collective-permute-start | bytes 196616 | tf_op jit(solution)/shard_map/ppermute | solution.py:438
  34.3 4.4 %collective-permute-start.12 = (bf16[16,16,128]{2,1,0:T(8,128)(2,1)S(1)}, bf16[16,16,128]{2,1,0:T(8,128)(2,1)S(1)}, u32[]{:S(2)}, u32[]{:S(2)}) collective-permute-start(bf16[16,16,128]{2,1,0:T(8,128)(2,1)S(1)} %get-tuple-element.44.refs_0_), channel_id=1, source_target_pairs={{0,16},{4,20},{8,24},{12,28},{16,0},{20,4},{24,8},{28,12},{1,17},{... | collective-permute-start | bytes 196616 | tf_op jit(solution)/shard_map/ppermute | solution.py:438
  34.9 4.3 %collective-permute-start.11 = (bf16[16,16,128]{2,1,0:T(8,128)(2,1)S(1)}, bf16[16,16,128]{2,1,0:T(8,128)(2,1)S(1)}, u32[]{:S(2)}, u32[]{:S(2)}) collective-permute-start(bf16[16,16,128]{2,1,0:T(8,128)(2,1)S(1)} %get-tuple-element.44.refs_0_), channel_id=1, source_target_pairs={{0,8},{4,12},{8,0},{12,4},{16,24},{20,28},{24,16},{28,20},{1,9},{5... | collective-permute-start | bytes 196616 | tf_op jit(solution)/shard_map/ppermute | solution.py:438
  36.3 2.9 %collective-permute-start.14 = (bf16[16,16,128]{2,1,0:T(8,128)(2,1)S(1)}, bf16[16,16,128]{2,1,0:T(8,128)(2,1)S(1)}, u32[]{:S(2)}, u32[]{:S(2)}) collective-permute-start(bf16[16,16,128]{2,1,0:T(8,128)(2,1)S(1)} %get-tuple-element.44.refs_0_), channel_id=1, source_target_pairs={{0,4},{4,0},{8,12},{12,8},{16,20},{20,16},{24,28},{28,24},{1,5},{5... | collective-permute-start | bytes 196616 | tf_op jit(solution)/shard_map/ppermute | solution.py:438
  38.0 1.3 %collective-permute-start.17 = (bf16[16,16,128]{2,1,0:T(8,128)(2,1)S(1)}, bf16[16,16,128]{2,1,0:T(8,128)(2,1)S(1)}, u32[]{:S(2)}, u32[]{:S(2)}) collective-permute-start(bf16[16,16,128]{2,1,0:T(8,128)(2,1)S(1)} %collective-permute-done.13.refs_3_), channel_id=1, source_target_pairs={{0,4},{4,0},{8,12},{12,8},{16,20},{20,16},{24,28},{28,24},{1,5},{5... | collective-permute-start | bytes 196616 | tf_op jit(solution)/shard_map/ppermute | solution.py:438
  38.7 1.3 %collective-permute-start.16 = (bf16[16,16,128]{2,1,0:T(8,128)(2,1)S(1)}, bf16[16,16,128]{2,1,0:T(8,128)(2,1)S(1)}, u32[]{:S(2)}, u32[]{:S(2)}) collective-permute-start(bf16[16,16,128]{2,1,0:T(8,128)(2,1)S(1)} %collective-permute-done.12.refs_2_), channel_id=1, source_target_pairs={{0,4},{4,0},{8,12},{12,8},{16,20},{20,16},{24,28},{28,24},{1,5},{5... | collective-permute-start | bytes 196616 | tf_op jit(solution)/shard_map/ppermute | solution.py:438
  39.2 1.3 %collective-permute-start.15 = (bf16[16,16,128]{2,1,0:T(8,128)(2,1)S(1)}, bf16[16,16,128]{2,1,0:T(8,128)(2,1)S(1)}, u32[]{:S(2)}, u32[]{:S(2)}) collective-permute-start(bf16[16,16,128]{2,1,0:T(8,128)(2,1)S(1)} %collective-permute-done.11.refs_1_), channel_id=1, source_target_pairs={{0,4},{4,0},{8,12},{12,8},{16,20},{20,16},{24,28},{28,24},{1,5},{5... | collective-permute-start | bytes 196616 | tf_op jit(solution)/shard_map/ppermute | solution.py:438
  42.2 4.5 %collective-permute-start.18 = (bf16[128,128]{1,0:T(8,128)(2,1)S(1)}, bf16[128,128]{1,0:T(8,128)(2,1)S(1)}, u32[]{:S(2)}, u32[]{:S(2)}) collective-permute-start(bf16[128,128]{1,0:T(8,128)(2,1)S(1)} %get-tuple-element.46), channel_id=1, source_target_pairs={{0,1},{1,0},{2,3},{3,2},{4,5},{5,4},{6,7},{7,6},{8,9},{9,8},{10,11... | collective-permute-start | bytes 98312 | tf_op jit(solution)/shard_map/ppermute | solution.py:438
  42.3 5.3 %collective-permute-start.19 = (bf16[128,128]{1,0:T(8,128)(2,1)S(1)}, bf16[128,128]{1,0:T(8,128)(2,1)S(1)}, u32[]{:S(2)}, u32[]{:S(2)}) collective-permute-start(bf16[128,128]{1,0:T(8,128)(2,1)S(1)} %get-tuple-element.47), channel_id=1, source_target_pairs={{0,2},{1,3},{2,0},{3,1},{4,6},{5,7},{6,4},{7,5},{8,10},{9,11},{10,... | collective-permute-start | bytes 98312 | tf_op jit(solution)/shard_map/ppermute | solution.py:438
  45.3 5.7 %collective-permute-start.20 = (bf16[128,128]{1,0:T(8,128)(2,1)S(1)}, bf16[128,128]{1,0:T(8,128)(2,1)S(1)}, u32[]{:S(2)}, u32[]{:S(2)}) collective-permute-start(bf16[128,128]{1,0:T(8,128)(2,1)S(1)} %get-tuple-element.48), channel_id=1, source_target_pairs={{0,3},{1,2},{2,1},{3,0},{4,7},{5,6},{6,5},{7,4},{8,11},{9,10},{10,... | collective-permute-start | bytes 98312 | tf_op jit(solution)/shard_map/ppermute | solution.py:438

commit v5 on v4

--- a/solution.py
+++ b/solution.py
@@ -198,8 +198,8 @@
 def first_kernel(
     gain, index_ref, traces_hbm, shift_hbm, deconv_hbm, focal_hbm, onset_hbm,
     forward_hbm, taps_hbm, gather_hbm, matrix_ref, sum_ref, own_ref, vector_ref,
-    kept_ref, traces_ref, shift_ref, deconv_ref, focal_ref, onset_ref,
-    forward_ref, taps_ref, gather_ref, trace_sem, small_sem, delay_ref,
+    upper_ref, shift_ref, deconv_ref, onset_ref, forward_ref, taps_ref, gather_ref,
+    kept_ref, traces_ref, focal_ref, large_sem, small_sem, delay_ref,
 ):
     half = traces_ref.shape[0]
     fields = focal_ref.shape[0]
@@ -210,56 +210,60 @@
                 (forward_hbm, forward_ref),
                 (deconv_hbm, deconv_ref),
                 (taps_hbm, taps_ref),
-                (focal_hbm, focal_ref),
                 (shift_hbm, shift_ref),
                 (gather_hbm, gather_ref),
                 (onset_hbm, onset_ref),
             ]
         )
     ]
-    chunks = trace_sem.shape[0]
-    step = half // chunks
+    step = half // 4
+    fields_step = fields // 2
+    ranges = [(focal_hbm, focal_ref, piece * fields_step, 0, fields_step) for piece in range(2)]
+    ranges += [(traces_hbm, traces_ref, piece * step, 0, step) for piece in range(4)]
+    ranges += [(traces_hbm, upper_ref, piece * 2 * step, half, 2 * step) for piece in range(2)]
     large = [
         pltpu.make_async_copy(
-            traces_hbm.at[pl.ds(chunk * step, step)],
-            traces_ref.at[pl.ds(chunk * step, step)],
-            trace_sem.at[chunk],
+            source.at[pl.ds(offset + start, count)],
+            target.at[pl.ds(start, count)],
+            large_sem.at[place],
         )
-        for chunk in range(chunks)
+        for place, (source, target, start, offset, count) in enumerate(ranges)
     ]
-    for copy in small[:5] + large + small[5:]:
+    for copy in small[:4] + large[:6] + small[4:] + large[6:]:
         copy.start()
     for copy in small[:3]:
         copy.wait()
     make_delays(0, half, forward_ref, deconv_ref, taps_ref, gain, delay_ref)
     forward = forward_ref[...]
-    small[3].wait()
-    own_ref[...] = focal_ref[index_ref[0]]
     for place in range(fields):
+        if place % fields_step == 0:
+            large[place // fields_step].wait()
         spectra = mm(forward, focal_ref[place], NT_DIMS)
         store_vector(vector_ref, place, spectra[:NF], spectra[NF:])
-    small[4].wait()
+    own_ref[...] = focal_ref[index_ref[0]]
+    small[3].wait()
     for couple in range(half // 2):
         if (2 * couple) % step == 0:
-            large[2 * couple // step].wait()
+            large[2 + 2 * couple // step].wait()
         make_matrix(0, couple, forward, traces_ref, shift_ref, delay_ref, matrix_ref)
+    small[4].wait()
     small[5].wait()
-    small[6].wait()
     make_sums(
         0, index_ref[1], matrix_ref, vector_ref, kept_ref, gather_ref[...], onset_ref, sum_ref
     )
+    large[6].wait()
+    large[7].wait()
 
 
 def rest_kernel(
     gain, index_ref, traces_ref, shift_ref, deconv_ref, onset_ref, forward_ref, taps_ref,
     gather_ref, vector_ref, matrix_ref, sum_ref, kept_ref, delay_ref,
 ):
-    half = traces_ref.shape[0] // 2
+    half = traces_ref.shape[0]
     make_delays(half, half, forward_ref, deconv_ref, taps_ref, gain, delay_ref)
     forward = forward_ref[...]
-    upper = traces_ref.at[pl.ds(half, half)]
     for couple in range(half // 2):
-        make_matrix(half, couple, forward, upper, shift_ref, delay_ref, matrix_ref)
+        make_matrix(half, couple, forward, traces_ref, shift_ref, delay_ref, matrix_ref)
     make_sums(
         half, index_ref[1], matrix_ref, vector_ref, kept_ref, gather_ref[...], onset_ref, sum_ref
     )
@@ -324,9 +328,8 @@
     index_ref, mine_ref, other_ref, forward_ref, inverse_ref, spread_ref,
     lower_ref, field_half_ref, first_ref, rest_ref, *refs
 ):
-    field_ref, upper_ref = refs[-2:]
-    pairs = (len(refs) - 2) // 2
-    keep_refs, send_refs = refs[:pairs], refs[pairs : 2 * pairs]
+    keep_ref, far_ref, send_ref, field_hbm, upper_ref, field_ref, field_sem = refs
+    pairs = keep_ref.shape[0]
     receivers = first_ref.shape[-1] // 2
     width = lower_ref.shape[-1]
     half = width // GROUP
@@ -334,6 +337,8 @@
     field_ref[:, half:] = mute_half(
         index_ref, mine_ref, other_ref, forward_ref[...], inverse_ref[...], spread_ref, upper_ref
     )
+    copy = pltpu.make_async_copy(field_ref, field_hbm, field_sem)
+    copy.start()
 
     def one(group):
         rows = 2 * pairs * 2 * GROUP
@@ -354,9 +359,10 @@
         for part in range(2):
             both = jnp.concatenate([even[part], odd[part]], axis=2).astype(BF16)
             row = part * NF + couple * 2 * GROUP
-            for slot in range(pairs):
-                keep_refs[slot][row : row + 2 * GROUP, :] = both[slot, 0]
-                send_refs[slot][row : row + 2 * GROUP, :] = both[slot, 1]
+            keep_ref[:, row : row + 2 * GROUP, :] = both[:, 0]
+            far_ref[row : row + 2 * GROUP, :] = both[pairs - 1, 1]
+            send_ref[:, row : row + 2 * GROUP, :] = both[: pairs - 1, 1]
+    copy.wait()
 
 
 def downgoing_kernel(*refs):
@@ -368,16 +374,18 @@
     onset = onset_ref[...].astype(F32)
     signal = mute(mm(inverse_ref[...], total.astype(BF16)), onset)
     field = focal_ref[...].astype(F32) + jnp.transpose(signal)
-    field_ref[0] = field
+    field_ref[...] = field
     spectra = mm(forward_ref[...], field.astype(BF16), NT_DIMS)
     plus_ref[...] = interleave(spectra[:NF], spectra[NF:]).astype(BF16)
 
 
 def second_kernel(pairs, index_ref, *refs):
     near_refs, far_refs = refs[:pairs], refs[pairs : 2 * pairs]
-    first_ref, rest_ref, gather_ref = refs[2 * pairs : 2 * pairs + 3]
-    sum_refs = refs[2 * pairs + 3 : -2]
-    vector_ref, kept_ref = refs[-2:]
+    first_ref, rest_ref, gather_ref, field_ref, field_hbm = refs[2 * pairs : 2 * pairs + 5]
+    sum_refs = refs[2 * pairs + 5 : -3]
+    vector_ref, kept_ref, field_sem = refs[-3:]
+    copy = pltpu.make_async_copy(field_ref, field_hbm.at[0], field_sem)
+    copy.start()
     shot_index = index_ref[0]
     rcv_index = index_ref[1]
     core = shot_index % 2
@@ -392,6 +400,7 @@
             sum_refs[slot][row : row + 2 * GROUP, :] = value[slot]
 
     apply_matrix([first_ref, rest_ref], vector_ref, kept_ref, gather_ref[...], store)
+    copy.wait()
 
 
 def final_kernel(*refs):
@@ -419,14 +428,16 @@
     return [pl.BlockSpec(memory_space=pltpu.HBM) for _ in range(count)]
 
 
-def call(kernel, name, out_shape, in_specs, scratch=(), work=1.0e9):
-    many = isinstance(out_shape, (tuple, list))
+def call(kernel, name, out_shape, in_specs, scratch=(), work=1.0e9, out_specs=None):
+    if out_specs is None:
+        many = isinstance(out_shape, (tuple, list))
+        out_specs = vmem(len(out_shape)) if many else vmem(1)[0]
     return pl.pallas_call(
         kernel,
         name=name,
         out_shape=out_shape,
         in_specs=in_specs,
-        out_specs=vmem(len(out_shape)) if many else vmem(1)[0],
+        out_specs=out_specs,
         scratch_shapes=list(scratch),
         compiler_params=pltpu.CompilerParams(vmem_limit_bytes=40 << 20),
         cost_estimate=pl.CostEstimate(flops=int(work), bytes_accessed=1 << 20, transcendentals=0),
@@ -470,16 +481,30 @@
         traces, shift_index, deconv, focal_start, onset_source,
         tables["forward"], tables["taps"], tables["gather_half"],
     )
-    first, first_sum, focal_own, start = call(
+    small = (shift_index, deconv, onset_source) + inputs[5:]
+    first, first_sum, focal_own, start, upper, *loaded = call(
         functools.partial(first_kernel, gain),
         "first",
-        (half_matrix, half_sums, shape((receivers, NT), BF16), vector),
+        [
+            half_matrix,
+            half_sums,
+            shape((receivers, NT), BF16),
+            vector,
+            shape((half, receivers, NT), BF16),
+        ]
+        + [shape(value.shape, value.dtype) for value in small],
         smem() + hbm(len(inputs)),
-        [half_kept, pltpu.VMEM((half, receivers, NT), BF16)]
-        + [buffer(value) for value in inputs[1:]]
-        + [pltpu.SemaphoreType.DMA((2,)), pltpu.SemaphoreType.DMA((7,)), half_delays],
+        [
+            half_kept,
+            pltpu.VMEM((half, receivers, NT), BF16),
+            buffer(focal_start),
+            pltpu.SemaphoreType.DMA((8,)),
+            pltpu.SemaphoreType.DMA((6,)),
+            half_delays,
+        ],
         work=4.0e9,
     )(index, *[pltpu.with_memory_space_constraint(value, pltpu.HBM) for value in inputs])
+    forward = loaded[3]
     rest, rest_sum = call(
         functools.partial(rest_kernel, gain),
         "rest",
@@ -487,10 +512,7 @@
         smem() + vmem(8),
         [half_kept, half_delays],
         work=3.0e9,
-    )(
-        index, traces, shift_index, deconv, onset_source,
-        tables["forward"], tables["taps"], tables["gather_half"], start,
-    )
+    )(index, upper, *loaded, start)
 
     mine = [first_sum, rest_sum]
     other = [exchange(value, "rcv", 1) for value in mine]
@@ -501,7 +523,7 @@
         other = [exchange(value, "rcv", distance) for value in mine]
 
     echo = shape((NG, 2, pairs, 2 * GROUP, half * GROUP), BF16)
-    shared = (tables["forward"], tables["inverse"], tables["spread"])
+    shared = (forward, tables["inverse"], tables["spread"])
     lower, field_half = call(
         mute_kernel,
         "mute",
@@ -510,50 +532,62 @@
         work=1.0e9,
     )(index, mine[0], other[0], *shared)
 
-    field = shape((2 * NF, receivers), BF16)
-    *blocks, upgoing_first = call(
+    keep, far, send, upgoing_first = call(
         adjoint_kernel,
         "adjoint",
-        [field] * (2 * pairs) + [shape((2, sources, NT), F32)],
+        [
+            shape((pairs, 2 * NF, receivers), BF16),
+            shape((2 * NF, receivers), BF16),
+            shape((pairs - 1, 2 * NF, receivers), BF16),
+            shape((2, sources, NT), F32),
+        ],
         smem() + vmem(9),
-        [buffer(echo)],
+        [buffer(echo), pltpu.VMEM((2, sources, NT), F32), pltpu.SemaphoreType.DMA(())],
         work=2.0e9,
+        out_specs=vmem(3) + hbm(1),
     )(index, mine[1], other[1], *shared, lower, field_half, first, rest)
 
-    parts = []
-    for distance in reversed(range(pairs)):
-        block = add_rounded(blocks[distance], exchange(blocks[pairs + distance], "shot", 1))
+    far = exchange(far, "shot", 1)
+    near = exchange(send, "shot", 1)
+    parts = [exchange(add_rounded(keep[pairs - 1], far), "shot", 2 * (pairs - 1))]
+    for distance in reversed(range(pairs - 1)):
+        block = add_rounded(keep[distance], near[distance])
         parts.append(exchange(block, "shot", 2 * distance) if distance else block)
 
     downgoing, plus = call(
         downgoing_kernel,
         "downgoing",
         (
-            shape((1, receivers, NT), F32),
+            shape((receivers, NT), F32),
             shape((NG, 2 * GROUP, receivers), BF16),
         ),
         vmem(pairs + 4),
-    )(*parts, focal_own, onset_receiver, tables["forward"], tables["inverse"])
+    )(*parts, focal_own, onset_receiver, forward, tables["inverse"])
 
     near = [plus]
     for distance in range(1, pairs):
         near.append(exchange(plus, "shot", 2 * distance))
     far = [exchange(value, "shot", 1) for value in near]
 
-    parts = call(
+    downgoing, *parts = call(
         functools.partial(second_kernel, pairs),
         "second",
-        [shape((NF, LANES), BF16)] * pairs,
-        smem() + vmem(2 * pairs + 3),
-        [buffer(vector), pltpu.VMEM((NG * focal_total * 2 * GROUP, sources * GROUP), BF16)],
-    )(index, *near, *far, first, rest, tables["gather"])
-
-    parts = [parts[0]] + [
-        exchange(parts[distance], "rcv", distance) for distance in range(1, rcv_count)
-    ]
+        [shape((1, receivers, NT), F32)] + [shape((NF, LANES), BF16)] * pairs,
+        smem() + vmem(2 * pairs + 4),
+        [
+            buffer(vector),
+            pltpu.VMEM((NG * focal_total * 2 * GROUP, sources * GROUP), BF16),
+            pltpu.SemaphoreType.DMA(()),
+        ],
+        out_specs=hbm(1) + vmem(pairs),
+    )(index, *near, *far, first, rest, tables["gather"], downgoing)
+
+    parts = [
+        exchange(parts[distance], "rcv", distance) for distance in reversed(range(1, rcv_count))
+    ] + [parts[0]]
     upgoing_second = call(
         final_kernel, "final", shape((2, sources, NT), F32), vmem(len(parts) + 2)
-    )(*parts, onset_source, tables["inverse"])
+    )(*parts, loaded[2], tables["inverse"])
     return (upgoing_first, downgoing, upgoing_second)
 
 

time: 52.1 us -> 52.2 us (level)
  Pallas kernels: 13.7 us -> 14.4 us
    pallas_call x4, Pallas kernels: 9.29 us -> 9.93 us  [the longest x1 5.02 us: body(): call(functools.partial(first_kernel, gain), 'first', [half_matrix, half_s...]
    ppermute x21 -> x19, starting transfers between devices: 21.2 us -> 20.9 us  [exchange(): lax.ppermute(value, axis, [(place, place ^ distance) for place in range(c...]
    ppermute x21 -> x19, waiting for transfers between devices: 16 us -> 15.7 us  [exchange(): lax.ppermute(value, axis, [(place, place ^ distance) for place in range(c...]
  transfers between devices with their start and end apart: 21 -> 19, of which waited for: 13 -> 13; matrix products, arithmetic and copies ran while one was open for 0% -> 0% of each run, Pallas kernels for 7% -> 7%
where the time goes in v5:
time: 52.2 us; the launch traced here: 52 us
  starting transfers between devices  20.9 us (40%)
  waiting for transfers between devices  15.7 us (30%)
  Pallas kernels  14.4 us (28%)
  between operations  0.74 us (1%)
    ppermute x19, starting transfers between devices, exchange(): lax.ppermute(value, axis, [(place, place ^ distance) for place in range(c...  20.9 us
    ppermute x19, waiting for transfers between devices, exchange(): lax.ppermute(value, axis, [(place, place ^ distance) for place in range(c...  15.7 us
    pallas_call x1, Pallas kernels, body(): call(functools.partial(first_kernel, gain), 'first', [half_matrix, half_s...  5.02 us
    pallas_call x1, Pallas kernels, body(): call(functools.partial(rest_kernel, gain), 'rest', (half_matrix, half_sum...  2.3 us
    pallas_call x1, Pallas kernels, body(): call(adjoint_kernel, 'adjoint', [shape((pairs, 2 * NF, receivers), BF16),...  2.24 us
    pallas_call x1, Pallas kernels, body(): call(functools.partial(second_kernel, pairs), 'second', [shape((1, receiv...  2.21 us
    pallas_call x1, Pallas kernels, body(): call(mute_kernel, 'mute', (echo, shape((2, half, NT), F32)), smem() + vme...  1.22 us
  transfers between devices with their start and end apart: 19, of which 13 were waited for; matrix products, arithmetic and copies ran while one was open for 0% of the time, Pallas kernels for 7%

profile of v5, /device:TPU:0, one launch (start us, length us, event | category | flops | bytes accessed | tf_op | source)
XLA Modules:
  0.0 52.0 jit_solution(4441663430979442940)
XLA Ops:
  0.6 0.1 pad_add_fusion.index_ref
  0.7 5.0 %first.1 = (bf16[16,8,16,256]{3,2,1,0:T(8,128)(2,1)S(1)}, bf16[272,128]{1,0:T(8,128)(2,1)S(1)}, bf16[128,256]{1,0:T(8,128)(2,1)S(1)}, bf16[16,8,16,256]{3,2,1,0:...) custom-call(s32[2]{0:T(128)S(1)} %pad_add_fusion.index_ref, ...), custom_call_target="tpu_custom_call" | custom-call | flops 4000000000 | bytes 1048576 | tf_op jit(solution)/shard_map/first/pallas_call | solution.py:485
  5.7 3.1 %collective-permute-start.2 = (bf16[272,128]{1,0:T(8,128)(2,1)S(1)}, bf16[272,128]{1,0:T(8,128)(2,1)S(1)}, u32[]{:S(2)}, u32[]{:S(2)}) collective-permute-start(bf16[272,128]{1,0:T(8,128)(2,1)S(1)} %get-tuple-element.38), channel_id=1, source_target_pairs={{0,1},{1,0},{2,3},{3,2},{4,5},{5,4},{6,7},{7,6},{8,9},{9,8},{10,11... | collective-permute-start | bytes 208904 | tf_op jit(solution)/shard_map/ppermute | solution.py:449
  8.8 0.0 copy-start.1
  8.8 0.0 copy-start.2
  8.8 2.3 %rest.1 = (bf16[16,8,16,256]{3,2,1,0:T(8,128)(2,1)S(1)}, bf16[272,128]{1,0:T(8,128)(2,1)S(1)}) custom-call(s32[2]{0:T(128)S(1)} %pad_add_fusion.index_ref, bf16[16,128,256]{2,1,0:T(8,128)(2,1)S(1)} %get-tuple-element.29.traces_ref, s32[32,128]{1,0:T(8,128)S(1)} %get-tuple-element.30.shift_ref, f32[32,64]{1,0:T(8,128)S(1)} %get-tuple-element.31.deconv_ref, ...), custom_call_target="tpu_custom_call" | custom-call | flops 3000000000 | bytes 1048576 | tf_op jit(solution)/shard_map/rest/pallas_call | solution.py:508
  11.1 0.1 collective-permute-start
  11.2 0.0 collective-permute-done.2
  11.3 3.1 %collective-permute-start.3 = (bf16[272,128]{1,0:T(8,128)(2,1)S(1)}, bf16[272,128]{1,0:T(8,128)(2,1)S(1)}, u32[]{:S(2)}, u32[]{:S(2)}) collective-permute-start(bf16[272,128]{1,0:T(8,128)(2,1)S(1)} %add_convert_fusion.mine_ref), channel_id=1, source_target_pairs={{0,2},{1,3},{2,0},{3,1},{4,6},{5,7},{6,4},{7,5},{8,10},{9,11},{10,... | collective-permute-start | bytes 208904 | tf_op jit(solution)/shard_map/ppermute | solution.py:449
  14.3 1.6 %collective-permute-done = bf16[272,128]{1,0:T(8,128)(2,1)S(1)} collective-permute-done((bf16[272,128]{1,0:T(8,128)(2,1)S(1)}, bf16[272,128]{1,0:T(8,128)(2,1)S(1)}, u32[]{:S(2)}, u32[]{:S(2)}) %collective-permute-start) | collective-permute-done | bytes 69664 | tf_op jit(solution)/shard_map/ppermute | solution.py:449
  16.0 2.3 %collective-permute-start.1 = (bf16[272,128]{1,0:T(8,128)(2,1)S(1)}, bf16[272,128]{1,0:T(8,128)(2,1)S(1)}, u32[]{:S(2)}, u32[]{:S(2)}) collective-permute-start(bf16[272,128]{1,0:T(8,128)(2,1)S(1)} %add_convert_fusion.1.mine_ref), channel_id=1, source_target_pairs={{0,2},{1,3},{2,0},{3,1},{4,6},{5,7},{6,4},{7,5},{8,10},{9,11},{10,... | collective-permute-start | bytes 208904 | tf_op jit(solution)/shard_map/ppermute | solution.py:449
  18.3 0.0 collective-permute-done.3.other_ref
  18.3 0.0 copy-done.1
  18.3 0.0 copy-done.2
  18.3 1.2 %mute.1 = (bf16[16,2,4,16,128]{4,3,2,1,0:T(8,128)(2,1)S(1)}, f32[2,16,256]{2,1,0:T(8,128)S(1)}) custom-call(s32[2]{0:T(128)S(1)} %pad_add_fusion.index_ref, bf16[272,128]{1,0:T(8,128)(2,1)S(1)} %add_convert_fusion.mine_ref, bf16[272,128]{1,0:T(8,128)(2,1)S(1)} %collective-permute-done.3.other_ref, ...), custom_call_target="tpu_custom_call" | custom-call | flops 1000000000 | bytes 1048576 | tf_op jit(solution)/shard_map/mute/pallas_call | solution.py:527
  19.5 1.9 %collective-permute-done.1.other_ref = bf16[272,128]{1,0:T(8,128)(2,1)S(1)} collective-permute-done((bf16[272,128]{1,0:T(8,128)(2,1)S(1)}, bf16[272,128]{1,0:T(8,128)(2,1)S(1)}, u32[]{:S(2)}, u32[]{:S(2)}) %collective-permute-start.1) | collective-permute-done | bytes 69664 | tf_op jit(solution)/shard_map/ppermute | solution.py:449
  21.4 0.0 copy-start
  21.4 2.2 %adjoint.1 = (bf16[4,256,128]{2,1,0:T(8,128)(2,1)S(1)}, bf16[256,128]{1,0:T(8,128)(2,1)S(1)}, bf16[3,256,128]{2,1,0:T(8,128)(2,1)S(1)}, f32[2,32,256]{2,1,0:T(8,128)}) custom-call(s32[2]{0:T(128)S(1)} %pad_add_fusion.index_ref, bf16[272,128]{1,0:T(8,128)(2,1)S(1)} %add_convert_fusion.1.mine_ref, bf16[272,128]{1,0:T(8,128)(2,1)S(1)} %collective-permute-done.1.other_ref, ...), custom_call_target="tpu_custom_call" | custom-call | flops 2000000000 | bytes 1048576 | tf_op jit(solution)/shard_map/adjoint/pallas_call | solution.py:535
  23.6 0.1 collective-permute-start.4
  23.7 0.5 collective-permute-start.6
  24.2 0.7 %collective-permute-done.4 = bf16[256,128]{1,0:T(8,128)(2,1)S(1)} collective-permute-done((bf16[256,128]{1,0:T(8,128)(2,1)S(1)}, bf16[256,128]{1,0:T(8,128)(2,1)S(1)}, u32[]{:S(2)}, u32[]{:S(2)}) %collective-permute-start.4) | collective-permute-done | bytes 65568 | tf_op jit(solution)/shard_map/ppermute | solution.py:449
  25.0 0.0 copy-start.3
  25.0 2.6 %collective-permute-start.5 = (bf16[256,128]{1,0:T(8,128)(2,1)S(1)}, bf16[256,128]{1,0:T(8,128)(2,1)S(1)}, u32[]{:S(2)}, u32[]{:S(2)}) collective-permute-start(bf16[256,128]{1,0:T(8,128)(2,1)S(1)} %fusion), channel_id=1, source_target_pairs={{0,24},{4,28},{8,16},{12,20},{16,8},{20,12},{24,0},{28,4},{1,25},{... | collective-permute-start | bytes 196616 | tf_op jit(solution)/shard_map/ppermute | solution.py:449
  27.6 0.0 collective-permute-done.6
  27.6 0.1 fusion.3
  27.6 0.6 %collective-permute-start.8 = (bf16[256,128]{1,0:T(8,128)(2,1)S(1)}, bf16[256,128]{1,0:T(8,128)(2,1)S(1)}, u32[]{:S(2)}, u32[]{:S(2)}) collective-permute-start(bf16[256,128]{1,0:T(8,128)(2,1)S(1)} %get-tuple-element.56), channel_id=1, source_target_pairs={{0,8},{4,12},{8,0},{12,4},{16,24},{20,28},{24,16},{28,20},{1,9},{5... | collective-permute-start | bytes 196616 | tf_op jit(solution)/shard_map/ppermute | solution.py:449
  28.2 0.5 collective-permute-start.7
  28.7 1.8 %collective-permute-done.5.refs_0_ = bf16[256,128]{1,0:T(8,128)(2,1)S(1)} collective-permute-done((bf16[256,128]{1,0:T(8,128)(2,1)S(1)}, bf16[256,128]{1,0:T(8,128)(2,1)S(1)}, u32[]{:S(2)}, u32[]{:S(2)}) %collective-permute-start.5) | collective-permute-done | bytes 65568 | tf_op jit(solution)/shard_map/ppermute | solution.py:449
  30.4 1.5 %collective-permute-done.8.refs_2_ = bf16[256,128]{1,0:T(8,128)(2,1)S(1)} collective-permute-done((bf16[256,128]{1,0:T(8,128)(2,1)S(1)}, bf16[256,128]{1,0:T(8,128)(2,1)S(1)}, u32[]{:S(2)}, u32[]{:S(2)}) %collective-permute-start.8) | collective-permute-done | bytes 65568 | tf_op jit(solution)/shard_map/ppermute | solution.py:449
  32.0 0.5 %collective-permute-done.7.refs_1_ = bf16[256,128]{1,0:T(8,128)(2,1)S(1)} collective-permute-done((bf16[256,128]{1,0:T(8,128)(2,1)S(1)}, bf16[256,128]{1,0:T(8,128)(2,1)S(1)}, u32[]{:S(2)}, u32[]{:S(2)}) %collective-permute-start.7) | collective-permute-done | bytes 65568 | tf_op jit(solution)/shard_map/ppermute | solution.py:449
  32.5 0.0 copy-done
  32.5 0.5 downgoing.1
  33.0 1.6 %collective-permute-start.11 = (bf16[16,16,128]{2,1,0:T(8,128)(2,1)S(1)}, bf16[16,16,128]{2,1,0:T(8,128)(2,1)S(1)}, u32[]{:S(2)}, u32[]{:S(2)}) collective-permute-start(bf16[16,16,128]{2,1,0:T(8,128)(2,1)S(1)} %get-tuple-element.48.refs_0_), channel_id=1, source_target_pairs={{0,24},{4,28},{8,16},{12,20},{16,8},{20,12},{24,0},{28,4},{1,25},{... | collective-permute-start | bytes 196616 | tf_op jit(solution)/shard_map/ppermute | solution.py:449
  34.6 1.4 %collective-permute-start.10 = (bf16[16,16,128]{2,1,0:T(8,128)(2,1)S(1)}, bf16[16,16,128]{2,1,0:T(8,128)(2,1)S(1)}, u32[]{:S(2)}, u32[]{:S(2)}) collective-permute-start(bf16[16,16,128]{2,1,0:T(8,128)(2,1)S(1)} %get-tuple-element.48.refs_0_), channel_id=1, source_target_pairs={{0,16},{4,20},{8,24},{12,28},{16,0},{20,4},{24,8},{28,12},{1,17},{... | collective-permute-start | bytes 196616 | tf_op jit(solution)/shard_map/ppermute | solution.py:449
  36.0 0.5 %collective-permute-start.9 = (bf16[16,16,128]{2,1,0:T(8,128)(2,1)S(1)}, bf16[16,16,128]{2,1,0:T(8,128)(2,1)S(1)}, u32[]{:S(2)}, u32[]{:S(2)}) collective-permute-start(bf16[16,16,128]{2,1,0:T(8,128)(2,1)S(1)} %get-tuple-element.48.refs_0_), channel_id=1, source_target_pairs={{0,8},{4,12},{8,0},{12,4},{16,24},{20,28},{24,16},{28,20},{1,9},{5... | collective-permute-start | bytes 196616 | tf_op jit(solution)/shard_map/ppermute | solution.py:449
  36.5 0.0 collective-permute-start.12
  36.5 2.4 %collective-permute-done.11.refs_3_ = bf16[16,16,128]{2,1,0:T(8,128)(2,1)S(1)} collective-permute-done((bf16[16,16,128]{2,1,0:T(8,128)(2,1)S(1)}, bf16[16,16,128]{2,1,0:T(8,128)(2,1)S(1)}, u32[]{:S(2)}, u32[]{:S(2)}) %collective-permute-start.11) | collective-permute-done | bytes 65568 | tf_op jit(solution)/shard_map/ppermute | solution.py:449
  38.9 0.0 collective-permute-start.15
  38.9 0.3 collective-permute-done.10.refs_2_
  39.2 0.2 collective-permute-start.14
  39.4 0.8 %collective-permute-done.9.refs_1_ = bf16[16,16,128]{2,1,0:T(8,128)(2,1)S(1)} collective-permute-done((bf16[16,16,128]{2,1,0:T(8,128)(2,1)S(1)}, bf16[16,16,128]{2,1,0:T(8,128)(2,1)S(1)}, u32[]{:S(2)}, u32[]{:S(2)}) %collective-permute-start.9) | collective-permute-done | bytes 65568 | tf_op jit(solution)/shard_map/ppermute | solution.py:449
  40.3 0.0 collective-permute-start.13
  40.3 0.0 collective-permute-done.12.refs_4_
  40.3 0.0 collective-permute-done.15.refs_7_
  40.3 0.2 collective-permute-done.14.refs_6_
  40.5 1.0 %collective-permute-done.13.refs_5_ = bf16[16,16,128]{2,1,0:T(8,128)(2,1)S(1)} collective-permute-done((bf16[16,16,128]{2,1,0:T(8,128)(2,1)S(1)}, bf16[16,16,128]{2,1,0:T(8,128)(2,1)S(1)}, u32[]{:S(2)}, u32[]{:S(2)}) %collective-permute-start.13) | collective-permute-done | bytes 65568 | tf_op jit(solution)/shard_map/ppermute | solution.py:449
  41.5 0.0 copy-done.3
  41.5 2.2 %second.1 = (f32[1,128,256]{2,1,0:T(8,128)}, bf16[128,128]{1,0:T(8,128)(2,1)S(1)}, bf16[128,128]{1,0:T(8,128)(2,1)S(1)}, bf16[128,128]{1,0:T(8,128)(2,1)S(1)}, bf16[128,128]{1,0:T(8,128)(2,1)S(1)}) custom-call(s32[2]{0:T(128)S(1)} %pad_add_fusion.index_ref, bf16[16,16,128]{2,1,0:T(8,128)(2,1)S(1)} %get-tuple-element.48.refs_0_, ...), custom_call_target="tpu_custom_call" | custom-call | flops 1000000000 | bytes 1048576 | tf_op jit(solution)/shard_map/second/pallas_call | solution.py:572
  43.7 2.5 %collective-permute-start.16 = (bf16[128,128]{1,0:T(8,128)(2,1)S(1)}, bf16[128,128]{1,0:T(8,128)(2,1)S(1)}, u32[]{:S(2)}, u32[]{:S(2)}) collective-permute-start(bf16[128,128]{1,0:T(8,128)(2,1)S(1)} %get-tuple-element.51), channel_id=1, source_target_pairs={{0,3},{1,2},{2,1},{3,0},{4,7},{5,6},{6,5},{7,4},{8,11},{9,10},{10,... | collective-permute-start | bytes 98312 | tf_op jit(solution)/shard_map/ppermute | solution.py:449
  46.3 0.0 collective-permute-start.17
  46.3 1.9 %collective-permute-start.18 = (bf16[128,128]{1,0:T(8,128)(2,1)S(1)}, bf16[128,128]{1,0:T(8,128)(2,1)S(1)}, u32[]{:S(2)}, u32[]{:S(2)}) collective-permute-start(bf16[128,128]{1,0:T(8,128)(2,1)S(1)} %get-tuple-element.53), channel_id=1, source_target_pairs={{0,1},{1,0},{2,3},{3,2},{4,5},{5,4},{6,7},{7,6},{8,9},{9,8},{10,11... | collective-permute-start | bytes 98312 | tf_op jit(solution)/shard_map/ppermute | solution.py:449
  48.2 1.7 %collective-permute-done.16.refs_0_ = bf16[128,128]{1,0:T(8,128)(2,1)S(1)} collective-permute-done((bf16[128,128]{1,0:T(8,128)(2,1)S(1)}, bf16[128,128]{1,0:T(8,128)(2,1)S(1)}, u32[]{:S(2)}, u32[]{:S(2)}) %collective-permute-start.16) | collective-permute-done | bytes 32800 | tf_op jit(solution)/shard_map/ppermute | solution.py:449
  49.8 1.2 %collective-permute-done.17.refs_1_ = bf16[128,128]{1,0:T(8,128)(2,1)S(1)} collective-permute-done((bf16[128,128]{1,0:T(8,128)(2,1)S(1)}, bf16[128,128]{1,0:T(8,128)(2,1)S(1)}, u32[]{:S(2)}, u32[]{:S(2)}) %collective-permute-start.17) | collective-permute-done | bytes 32800 | tf_op jit(solution)/shard_map/ppermute | solution.py:449
  51.1 0.0 collective-permute-done.18.refs_2_
  51.1 0.9 %final.1 = f32[2,32,256]{2,1,0:T(8,128)} custom-call(bf16[128,128]{1,0:T(8,128)(2,1)S(1)} %collective-permute-done.16.refs_0_, bf16[128,128]{1,0:T(8,128)(2,1)S(1)} %collective-permute-done.17.refs_1_, bf16[128,128]{1,0:T(8,128)(2,1)S(1)} %collective-permute-done.18.refs_2_, bf16[128,128]{1,0:T(8,128)(2,1)S(1)} %get-tuple-element.54.refs_3_, ...), custom_call_target="tpu_custom_call" | custom-call | flops 1000000000 | bytes 1048576 | tf_op jit(solution)/shard_map/final/pallas_call | solution.py:588
  (3 shorter events, 0.1 us)
Async XLA Ops:
  5.7 5.5 %collective-permute-start.2 = (bf16[272,128]{1,0:T(8,128)(2,1)S(1)}, bf16[272,128]{1,0:T(8,128)(2,1)S(1)}, u32[]{:S(2)}, u32[]{:S(2)}) collective-permute-start(bf16[272,128]{1,0:T(8,128)(2,1)S(1)} %get-tuple-element.38), channel_id=1, source_target_pairs={{0,1},{1,0},{2,3},{3,2},{4,5},{5,4},{6,7},{7,6},{8,9},{9,8},{10,11... | collective-permute-start | bytes 208904 | tf_op jit(solution)/shard_map/ppermute | solution.py:449
  8.8 9.5 %copy-start.1 = (bf16[2,4,128,256]{3,2,1,0:T(8,128)(2,1)S(1)}, bf16[2,4,128,256]{3,2,1,0:T(8,128)(2,1)}, u32[]{:S(2)}) copy-start(bf16[2,4,128,256]{3,2,1,0:T(8,128)(2,1)} %constant.32.spread_ref) | copy-start | bytes 1572868
  8.8 9.5 %copy-start.2 = (bf16[256,256]{1,0:T(8,128)(2,1)S(1)}, bf16[256,256]{1,0:T(8,128)(2,1)}, u32[]{:S(2)}) copy-start(bf16[256,256]{1,0:T(8,128)(2,1)} %constant.31.inverse_ref.refs_7_.refs_5_) | copy-start | bytes 393220
  11.1 4.8 %collective-permute-start = (bf16[272,128]{1,0:T(8,128)(2,1)S(1)}, bf16[272,128]{1,0:T(8,128)(2,1)S(1)}, u32[]{:S(2)}, u32[]{:S(2)}) collective-permute-start(bf16[272,128]{1,0:T(8,128)(2,1)S(1)} %get-tuple-element.37), channel_id=1, source_target_pairs={{0,1},{1,0},{2,3},{3,2},{4,5},{5,4},{6,7},{7,6},{8,9},{9,8},{10,11... | collective-permute-start | bytes 208904 | tf_op jit(solution)/shard_map/ppermute | solution.py:449
  11.3 7.0 %collective-permute-start.3 = (bf16[272,128]{1,0:T(8,128)(2,1)S(1)}, bf16[272,128]{1,0:T(8,128)(2,1)S(1)}, u32[]{:S(2)}, u32[]{:S(2)}) collective-permute-start(bf16[272,128]{1,0:T(8,128)(2,1)S(1)} %add_convert_fusion.mine_ref), channel_id=1, source_target_pairs={{0,2},{1,3},{2,0},{3,1},{4,6},{5,7},{6,4},{7,5},{8,10},{9,11},{10,... | collective-permute-start | bytes 208904 | tf_op jit(solution)/shard_map/ppermute | solution.py:449
  16.0 5.4 %collective-permute-start.1 = (bf16[272,128]{1,0:T(8,128)(2,1)S(1)}, bf16[272,128]{1,0:T(8,128)(2,1)S(1)}, u32[]{:S(2)}, u32[]{:S(2)}) collective-permute-start(bf16[272,128]{1,0:T(8,128)(2,1)S(1)} %add_convert_fusion.1.mine_ref), channel_id=1, source_target_pairs={{0,2},{1,3},{2,0},{3,1},{4,6},{5,7},{6,4},{7,5},{8,10},{9,11},{10,... | collective-permute-start | bytes 208904 | tf_op jit(solution)/shard_map/ppermute | solution.py:449
  21.4 11.1 %copy-start = (s32[1,128]{1,0:T(1,128)S(1)}, s32[1,128]{1,0:T(1,128)}, u32[]{:S(2)}) copy-start(s32[1,128]{1,0:T(1,128)} %refs_5_.1) | copy-start | bytes 1540
  23.6 1.3 %collective-permute-start.4 = (bf16[256,128]{1,0:T(8,128)(2,1)S(1)}, bf16[256,128]{1,0:T(8,128)(2,1)S(1)}, u32[]{:S(2)}, u32[]{:S(2)}) collective-permute-start(bf16[256,128]{1,0:T(8,128)(2,1)S(1)} %get-tuple-element.45), channel_id=1, source_target_pairs={{0,4},{4,0},{8,12},{12,8},{16,20},{20,16},{24,28},{28,24},{1,5},{5... | collective-permute-start | bytes 196616 | tf_op jit(solution)/shard_map/ppermute | solution.py:449
  23.7 3.8 %collective-permute-start.6 = (bf16[3,256,128]{2,1,0:T(8,128)(2,1)S(1)}, bf16[3,256,128]{2,1,0:T(8,128)(2,1)S(1)}, u32[]{:S(2)}, u32[]{:S(2)}) collective-permute-start(bf16[3,256,128]{2,1,0:T(8,128)(2,1)S(1)} %get-tuple-element.46), channel_id=1, source_target_pairs={{0,4},{4,0},{8,12},{12,8},{16,20},{20,16},{24,28},{28,24},{1,5},{5... | collective-permute-start | bytes 589832 | tf_op jit(solution)/shard_map/ppermute | solution.py:449
  25.0 16.5 %copy-start.3 = (bf16[256,128]{1,0:T(8,128)(2,1)S(1)}, bf16[256,128]{1,0:T(8,128)(2,1)}, u32[]{:S(2)}) copy-start(bf16[256,128]{1,0:T(8,128)(2,1)} %constant.33.refs_10_) | copy-start | bytes 196612
  25.0 5.4 %collective-permute-start.5 = (bf16[256,128]{1,0:T(8,128)(2,1)S(1)}, bf16[256,128]{1,0:T(8,128)(2,1)S(1)}, u32[]{:S(2)}, u32[]{:S(2)}) collective-permute-start(bf16[256,128]{1,0:T(8,128)(2,1)S(1)} %fusion), channel_id=1, source_target_pairs={{0,24},{4,28},{8,16},{12,20},{16,8},{20,12},{24,0},{28,4},{1,25},{... | collective-permute-start | bytes 196616 | tf_op jit(solution)/shard_map/ppermute | solution.py:449
  27.6 4.3 %collective-permute-start.8 = (bf16[256,128]{1,0:T(8,128)(2,1)S(1)}, bf16[256,128]{1,0:T(8,128)(2,1)S(1)}, u32[]{:S(2)}, u32[]{:S(2)}) collective-permute-start(bf16[256,128]{1,0:T(8,128)(2,1)S(1)} %get-tuple-element.56), channel_id=1, source_target_pairs={{0,8},{4,12},{8,0},{12,4},{16,24},{20,28},{24,16},{28,20},{1,9},{5... | collective-permute-start | bytes 196616 | tf_op jit(solution)/shard_map/ppermute | solution.py:449
  28.2 4.3 %collective-permute-start.7 = (bf16[256,128]{1,0:T(8,128)(2,1)S(1)}, bf16[256,128]{1,0:T(8,128)(2,1)S(1)}, u32[]{:S(2)}, u32[]{:S(2)}) collective-permute-start(bf16[256,128]{1,0:T(8,128)(2,1)S(1)} %get-tuple-element.57), channel_id=1, source_target_pairs={{0,16},{4,20},{8,24},{12,28},{16,0},{20,4},{24,8},{28,12},{1,17},{... | collective-permute-start | bytes 196616 | tf_op jit(solution)/shard_map/ppermute | solution.py:449
  33.0 5.9 %collective-permute-start.11 = (bf16[16,16,128]{2,1,0:T(8,128)(2,1)S(1)}, bf16[16,16,128]{2,1,0:T(8,128)(2,1)S(1)}, u32[]{:S(2)}, u32[]{:S(2)}) collective-permute-start(bf16[16,16,128]{2,1,0:T(8,128)(2,1)S(1)} %get-tuple-element.48.refs_0_), channel_id=1, source_target_pairs={{0,24},{4,28},{8,16},{12,20},{16,8},{20,12},{24,0},{28,4},{1,25},{... | collective-permute-start | bytes 196616 | tf_op jit(solution)/shard_map/ppermute | solution.py:449
  34.6 4.6 %collective-permute-start.10 = (bf16[16,16,128]{2,1,0:T(8,128)(2,1)S(1)}, bf16[16,16,128]{2,1,0:T(8,128)(2,1)S(1)}, u32[]{:S(2)}, u32[]{:S(2)}) collective-permute-start(bf16[16,16,128]{2,1,0:T(8,128)(2,1)S(1)} %get-tuple-element.48.refs_0_), channel_id=1, source_target_pairs={{0,16},{4,20},{8,24},{12,28},{16,0},{20,4},{24,8},{28,12},{1,17},{... | collective-permute-start | bytes 196616 | tf_op jit(solution)/shard_map/ppermute | solution.py:449
  36.0 4.3 %collective-permute-start.9 = (bf16[16,16,128]{2,1,0:T(8,128)(2,1)S(1)}, bf16[16,16,128]{2,1,0:T(8,128)(2,1)S(1)}, u32[]{:S(2)}, u32[]{:S(2)}) collective-permute-start(bf16[16,16,128]{2,1,0:T(8,128)(2,1)S(1)} %get-tuple-element.48.refs_0_), channel_id=1, source_target_pairs={{0,8},{4,12},{8,0},{12,4},{16,24},{20,28},{24,16},{28,20},{1,9},{5... | collective-permute-start | bytes 196616 | tf_op jit(solution)/shard_map/ppermute | solution.py:449
  36.5 3.7 %collective-permute-start.12 = (bf16[16,16,128]{2,1,0:T(8,128)(2,1)S(1)}, bf16[16,16,128]{2,1,0:T(8,128)(2,1)S(1)}, u32[]{:S(2)}, u32[]{:S(2)}) collective-permute-start(bf16[16,16,128]{2,1,0:T(8,128)(2,1)S(1)} %get-tuple-element.48.refs_0_), channel_id=1, source_target_pairs={{0,4},{4,0},{8,12},{12,8},{16,20},{20,16},{24,28},{28,24},{1,5},{5... | collective-permute-start | bytes 196616 | tf_op jit(solution)/shard_map/ppermute | solution.py:449
  38.9 1.4 %collective-permute-start.15 = (bf16[16,16,128]{2,1,0:T(8,128)(2,1)S(1)}, bf16[16,16,128]{2,1,0:T(8,128)(2,1)S(1)}, u32[]{:S(2)}, u32[]{:S(2)}) collective-permute-start(bf16[16,16,128]{2,1,0:T(8,128)(2,1)S(1)} %collective-permute-done.11.refs_3_), channel_id=1, source_target_pairs={{0,4},{4,0},{8,12},{12,8},{16,20},{20,16},{24,28},{28,24},{1,5},{5... | collective-permute-start | bytes 196616 | tf_op jit(solution)/shard_map/ppermute | solution.py:449
  39.2 1.3 %collective-permute-start.14 = (bf16[16,16,128]{2,1,0:T(8,128)(2,1)S(1)}, bf16[16,16,128]{2,1,0:T(8,128)(2,1)S(1)}, u32[]{:S(2)}, u32[]{:S(2)}) collective-permute-start(bf16[16,16,128]{2,1,0:T(8,128)(2,1)S(1)} %collective-permute-done.10.refs_2_), channel_id=1, source_target_pairs={{0,4},{4,0},{8,12},{12,8},{16,20},{20,16},{24,28},{28,24},{1,5},{5... | collective-permute-start | bytes 196616 | tf_op jit(solution)/shard_map/ppermute | solution.py:449
  40.3 1.3 %collective-permute-start.13 = (bf16[16,16,128]{2,1,0:T(8,128)(2,1)S(1)}, bf16[16,16,128]{2,1,0:T(8,128)(2,1)S(1)}, u32[]{:S(2)}, u32[]{:S(2)}) collective-permute-start(bf16[16,16,128]{2,1,0:T(8,128)(2,1)S(1)} %collective-permute-done.9.refs_1_), channel_id=1, source_target_pairs={{0,4},{4,0},{8,12},{12,8},{16,20},{20,16},{24,28},{28,24},{1,5},{5... | collective-permute-start | bytes 196616 | tf_op jit(solution)/shard_map/ppermute | solution.py:449
  43.7 6.1 %collective-permute-start.16 = (bf16[128,128]{1,0:T(8,128)(2,1)S(1)}, bf16[128,128]{1,0:T(8,128)(2,1)S(1)}, u32[]{:S(2)}, u32[]{:S(2)}) collective-permute-start(bf16[128,128]{1,0:T(8,128)(2,1)S(1)} %get-tuple-element.51), channel_id=1, source_target_pairs={{0,3},{1,2},{2,1},{3,0},{4,7},{5,6},{6,5},{7,4},{8,11},{9,10},{10,... | collective-permute-start | bytes 98312 | tf_op jit(solution)/shard_map/ppermute | solution.py:449
  46.3 4.8 %collective-permute-start.17 = (bf16[128,128]{1,0:T(8,128)(2,1)S(1)}, bf16[128,128]{1,0:T(8,128)(2,1)S(1)}, u32[]{:S(2)}, u32[]{:S(2)}) collective-permute-start(bf16[128,128]{1,0:T(8,128)(2,1)S(1)} %get-tuple-element.52), channel_id=1, source_target_pairs={{0,2},{1,3},{2,0},{3,1},{4,6},{5,7},{6,4},{7,5},{8,10},{9,11},{10,... | collective-permute-start | bytes 98312 | tf_op jit(solution)/shard_map/ppermute | solution.py:449
  46.3 4.8 %collective-permute-start.18 = (bf16[128,128]{1,0:T(8,128)(2,1)S(1)}, bf16[128,128]{1,0:T(8,128)(2,1)S(1)}, u32[]{:S(2)}, u32[]{:S(2)}) collective-permute-start(bf16[128,128]{1,0:T(8,128)(2,1)S(1)} %get-tuple-element.53), channel_id=1, source_target_pairs={{0,1},{1,0},{2,3},{3,2},{4,5},{5,4},{6,7},{7,6},{8,9},{9,8},{10,11... | collective-permute-start | bytes 98312 | tf_op jit(solution)/shard_map/ppermute | solution.py:449

commit v6 on v5

--- a/solution.py
+++ b/solution.py
@@ -198,7 +198,7 @@
 def first_kernel(
     gain, index_ref, traces_hbm, shift_hbm, deconv_hbm, focal_hbm, onset_hbm,
     forward_hbm, taps_hbm, gather_hbm, matrix_ref, sum_ref, own_ref, vector_ref,
-    upper_ref, shift_ref, deconv_ref, onset_ref, forward_ref, taps_ref, gather_ref,
+    shift_ref, deconv_ref, onset_ref, forward_ref, taps_ref, gather_ref,
     kept_ref, traces_ref, focal_ref, large_sem, small_sem, delay_ref,
 ):
     half = traces_ref.shape[0]
@@ -216,54 +216,39 @@
             ]
         )
     ]
-    step = half // 4
-    fields_step = fields // 2
-    ranges = [(focal_hbm, focal_ref, piece * fields_step, 0, fields_step) for piece in range(2)]
-    ranges += [(traces_hbm, traces_ref, piece * step, 0, step) for piece in range(4)]
-    ranges += [(traces_hbm, upper_ref, piece * 2 * step, half, 2 * step) for piece in range(2)]
     large = [
-        pltpu.make_async_copy(
-            source.at[pl.ds(offset + start, count)],
-            target.at[pl.ds(start, count)],
-            large_sem.at[place],
-        )
-        for place, (source, target, start, offset, count) in enumerate(ranges)
+        pltpu.make_async_copy(focal_hbm, focal_ref, large_sem.at[0]),
+        pltpu.make_async_copy(traces_hbm.at[pl.ds(0, half)], traces_ref, large_sem.at[1]),
     ]
-    for copy in small[:4] + large[:6] + small[4:] + large[6:]:
+    for copy in small[:3] + large + small[3:]:
         copy.start()
-    for copy in small[:3]:
+    for copy in small[:3] + large[:1]:
         copy.wait()
     make_delays(0, half, forward_ref, deconv_ref, taps_ref, gain, delay_ref)
     forward = forward_ref[...]
     for place in range(fields):
-        if place % fields_step == 0:
-            large[place // fields_step].wait()
         spectra = mm(forward, focal_ref[place], NT_DIMS)
         store_vector(vector_ref, place, spectra[:NF], spectra[NF:])
     own_ref[...] = focal_ref[index_ref[0]]
-    small[3].wait()
+    for copy in small[3:] + large[1:]:
+        copy.wait()
     for couple in range(half // 2):
-        if (2 * couple) % step == 0:
-            large[2 + 2 * couple // step].wait()
         make_matrix(0, couple, forward, traces_ref, shift_ref, delay_ref, matrix_ref)
-    small[4].wait()
-    small[5].wait()
     make_sums(
         0, index_ref[1], matrix_ref, vector_ref, kept_ref, gather_ref[...], onset_ref, sum_ref
     )
-    large[6].wait()
-    large[7].wait()
 
 
 def rest_kernel(
     gain, index_ref, traces_ref, shift_ref, deconv_ref, onset_ref, forward_ref, taps_ref,
     gather_ref, vector_ref, matrix_ref, sum_ref, kept_ref, delay_ref,
 ):
-    half = traces_ref.shape[0]
+    half = traces_ref.shape[0] // 2
     make_delays(half, half, forward_ref, deconv_ref, taps_ref, gain, delay_ref)
     forward = forward_ref[...]
+    upper = traces_ref.at[pl.ds(half, half)]
     for couple in range(half // 2):
-        make_matrix(half, couple, forward, traces_ref, shift_ref, delay_ref, matrix_ref)
+        make_matrix(half, couple, forward, upper, shift_ref, delay_ref, matrix_ref)
     make_sums(
         half, index_ref[1], matrix_ref, vector_ref, kept_ref, gather_ref[...], onset_ref, sum_ref
     )
@@ -328,7 +313,7 @@
     index_ref, mine_ref, other_ref, forward_ref, inverse_ref, spread_ref,
     lower_ref, field_half_ref, first_ref, rest_ref, *refs
 ):
-    keep_ref, far_ref, send_ref, field_hbm, upper_ref, field_ref, field_sem = refs
+    keep_ref, far_ref, send_ref, field_ref, upper_ref = refs
     pairs = keep_ref.shape[0]
     receivers = first_ref.shape[-1] // 2
     width = lower_ref.shape[-1]
@@ -337,8 +322,6 @@
     field_ref[:, half:] = mute_half(
         index_ref, mine_ref, other_ref, forward_ref[...], inverse_ref[...], spread_ref, upper_ref
     )
-    copy = pltpu.make_async_copy(field_ref, field_hbm, field_sem)
-    copy.start()
 
     def one(group):
         rows = 2 * pairs * 2 * GROUP
@@ -362,7 +345,6 @@
             keep_ref[:, row : row + 2 * GROUP, :] = both[:, 0]
             far_ref[row : row + 2 * GROUP, :] = both[pairs - 1, 1]
             send_ref[:, row : row + 2 * GROUP, :] = both[: pairs - 1, 1]
-    copy.wait()
 
 
 def downgoing_kernel(*refs):
@@ -374,18 +356,16 @@
     onset = onset_ref[...].astype(F32)
     signal = mute(mm(inverse_ref[...], total.astype(BF16)), onset)
     field = focal_ref[...].astype(F32) + jnp.transpose(signal)
-    field_ref[...] = field
+    field_ref[0] = field
     spectra = mm(forward_ref[...], field.astype(BF16), NT_DIMS)
     plus_ref[...] = interleave(spectra[:NF], spectra[NF:]).astype(BF16)
 
 
 def second_kernel(pairs, index_ref, *refs):
     near_refs, far_refs = refs[:pairs], refs[pairs : 2 * pairs]
-    first_ref, rest_ref, gather_ref, field_ref, field_hbm = refs[2 * pairs : 2 * pairs + 5]
-    sum_refs = refs[2 * pairs + 5 : -3]
-    vector_ref, kept_ref, field_sem = refs[-3:]
-    copy = pltpu.make_async_copy(field_ref, field_hbm.at[0], field_sem)
-    copy.start()
+    first_ref, rest_ref, gather_ref = refs[2 * pairs : 2 * pairs + 3]
+    sum_refs = refs[2 * pairs + 3 : -2]
+    vector_ref, kept_ref = refs[-2:]
     shot_index = index_ref[0]
     rcv_index = index_ref[1]
     core = shot_index % 2
@@ -400,7 +380,6 @@
             sum_refs[slot][row : row + 2 * GROUP, :] = value[slot]
 
     apply_matrix([first_ref, rest_ref], vector_ref, kept_ref, gather_ref[...], store)
-    copy.wait()
 
 
 def final_kernel(*refs):
@@ -414,6 +393,10 @@
     onset = jnp.concatenate([onset[0:1], onset[1:2]] * 2, axis=1)
     signal = mute(mm(inverse_ref[...], spectra), onset)
     field_ref[...] = jnp.transpose(signal)[: LANES // 2].reshape(field_ref.shape)
+
+
+def emit_kernel(field_ref, out_ref):
+    out_ref[...] = field_ref[...]
 
 
 def vmem(count):
@@ -442,6 +425,12 @@
         compiler_params=pltpu.CompilerParams(vmem_limit_bytes=40 << 20),
         cost_estimate=pl.CostEstimate(flops=int(work), bytes_accessed=1 << 20, transcendentals=0),
     )
+
+
+def emit(field):
+    return call(
+        emit_kernel, "emit", jax.ShapeDtypeStruct(field.shape, field.dtype), vmem(1), work=0.3e9
+    )(field)
 
 
 def exchange(value, axis, distance):
@@ -482,7 +471,7 @@
         tables["forward"], tables["taps"], tables["gather_half"],
     )
     small = (shift_index, deconv, onset_source) + inputs[5:]
-    first, first_sum, focal_own, start, upper, *loaded = call(
+    first, first_sum, focal_own, start, *loaded = call(
         functools.partial(first_kernel, gain),
         "first",
         [
@@ -490,7 +479,6 @@
             half_sums,
             shape((receivers, NT), BF16),
             vector,
-            shape((half, receivers, NT), BF16),
         ]
         + [shape(value.shape, value.dtype) for value in small],
         smem() + hbm(len(inputs)),
@@ -498,7 +486,7 @@
             half_kept,
             pltpu.VMEM((half, receivers, NT), BF16),
             buffer(focal_start),
-            pltpu.SemaphoreType.DMA((8,)),
+            pltpu.SemaphoreType.DMA((2,)),
             pltpu.SemaphoreType.DMA((6,)),
             half_delays,
         ],
@@ -512,7 +500,7 @@
         smem() + vmem(8),
         [half_kept, half_delays],
         work=3.0e9,
-    )(index, upper, *loaded, start)
+    )(index, traces, *loaded, start)
 
     mine = [first_sum, rest_sum]
     other = [exchange(value, "rcv", 1) for value in mine]
@@ -542,9 +530,8 @@
             shape((2, sources, NT), F32),
         ],
         smem() + vmem(9),
-        [buffer(echo), pltpu.VMEM((2, sources, NT), F32), pltpu.SemaphoreType.DMA(())],
+        [buffer(echo)],
         work=2.0e9,
-        out_specs=vmem(3) + hbm(1),
     )(index, mine[1], other[1], *shared, lower, field_half, first, rest)
 
     far = exchange(far, "shot", 1)
@@ -558,7 +545,7 @@
         downgoing_kernel,
         "downgoing",
         (
-            shape((receivers, NT), F32),
+            shape((1, receivers, NT), F32),
             shape((NG, 2 * GROUP, receivers), BF16),
         ),
         vmem(pairs + 4),
@@ -569,18 +556,16 @@
         near.append(exchange(plus, "shot", 2 * distance))
     far = [exchange(value, "shot", 1) for value in near]
 
-    downgoing, *parts = call(
+    parts = call(
         functools.partial(second_kernel, pairs),
         "second",
-        [shape((1, receivers, NT), F32)] + [shape((NF, LANES), BF16)] * pairs,
-        smem() + vmem(2 * pairs + 4),
+        [shape((NF, LANES), BF16)] * pairs,
+        smem() + vmem(2 * pairs + 3),
         [
             buffer(vector),
             pltpu.VMEM((NG * focal_total * 2 * GROUP, sources * GROUP), BF16),
-            pltpu.SemaphoreType.DMA(()),
         ],
-        out_specs=hbm(1) + vmem(pairs),
-    )(index, *near, *far, first, rest, tables["gather"], downgoing)
+    )(index, *near, *far, first, rest, tables["gather"])
 
     parts = [
         exchange(parts[distance], "rcv", distance) for distance in reversed(range(1, rcv_count))
@@ -588,7 +573,7 @@
     upgoing_second = call(
         final_kernel, "final", shape((2, sources, NT), F32), vmem(len(parts) + 2)
     )(*parts, loaded[2], tables["inverse"])
-    return (upgoing_first, downgoing, upgoing_second)
+    return (emit(upgoing_first), emit(downgoing), upgoing_second)
 
 
 def solution(mesh):

time: 52.2 us -> 50.2 us (0.962)
  waiting for transfers between devices: 15.7 us -> 14.4 us
  Pallas kernels: 14.4 us -> 13.7 us
    ppermute x19, waiting for transfers between devices: 15.7 us -> 14.4 us  [exchange(): lax.ppermute(value, axis, [(place, place ^ distance) for place in range(c...]
    pallas_call x1, Pallas kernels: 5.02 us -> 4.06 us  [body(): call(functools.partial(first_kernel, gain), 'first', [half_matrix, half_s...]
    pallas_call x2 -> x4, Pallas kernels: 2.68 us -> 3.54 us  [the longest x1 1.78 us: body(): call(functools.partial(second_kernel, pairs), 'second', [shape((NF, LANES...]
    pallas_call x1, Pallas kernels: 2.24 us -> 1.67 us  [body(): call(adjoint_kernel, 'adjoint', [shape((pairs, 2 * NF, receivers), BF16),...]
  transfers between devices with their start and end apart: 19 -> 19, of which waited for: 13 -> 13; matrix products, arithmetic and copies ran while one was open for 0% -> 0% of each run, Pallas kernels for 7% -> 10%
where the time goes in v6:
time: 50.2 us; the launch traced here: 50 us
  starting transfers between devices  20.9 us (42%)
  waiting for transfers between devices  14.4 us (29%)
  Pallas kernels  13.7 us (27%)
  between operations  0.74 us (1%)
    ppermute x19, starting transfers between devices, exchange(): lax.ppermute(value, axis, [(place, place ^ distance) for place in range(c...  20.9 us
    ppermute x19, waiting for transfers between devices, exchange(): lax.ppermute(value, axis, [(place, place ^ distance) for place in range(c...  14.4 us
    pallas_call x1, Pallas kernels, body(): call(functools.partial(first_kernel, gain), 'first', [half_matrix, half_s...  4.06 us
    pallas_call x1, Pallas kernels, body(): call(functools.partial(rest_kernel, gain), 'rest', (half_matrix, half_sum...  2.29 us
    pallas_call x1, Pallas kernels, body(): call(functools.partial(second_kernel, pairs), 'second', [shape((NF, LANES...  1.78 us
    pallas_call x1, Pallas kernels, body(): call(adjoint_kernel, 'adjoint', [shape((pairs, 2 * NF, receivers), BF16),...  1.67 us
    pallas_call x2, Pallas kernels, emit(): call(emit_kernel, 'emit', jax.ShapeDtypeStruct(field.shape, field.dtype),...  1.3 us
    pallas_call x1, Pallas kernels, body(): call(mute_kernel, 'mute', (echo, shape((2, half, NT), F32)), smem() + vme...  1.22 us
  transfers between devices with their start and end apart: 19, of which 13 were waited for; matrix products, arithmetic and copies ran while one was open for 0% of the time, Pallas kernels for 10%

profile of v6, /device:TPU:0, one launch (start us, length us, event | category | flops | bytes accessed | tf_op | source)
XLA Modules:
  0.0 50.0 jit_solution(3712757993489447109)
XLA Ops:
  0.6 0.1 pad_add_fusion.index_ref
  0.7 0.0 copy-start
  0.7 4.1 %first.1 = (bf16[16,8,16,256]{3,2,1,0:T(8,128)(2,1)S(1)}, bf16[272,128]{1,0:T(8,128)(2,1)S(1)}, bf16[128,256]{1,0:T(8,128)(2,1)S(1)}, bf16[16,8,16,256]{3,2,1,0:...) custom-call(s32[2]{0:T(128)S(1)} %pad_add_fusion.index_ref, ...), custom_call_target="tpu_custom_call" | custom-call | flops 4000000000 | bytes 1048576 | tf_op jit(solution)/shard_map/first/pallas_call | solution.py:474
  4.8 3.1 %collective-permute-start.2 = (bf16[272,128]{1,0:T(8,128)(2,1)S(1)}, bf16[272,128]{1,0:T(8,128)(2,1)S(1)}, u32[]{:S(2)}, u32[]{:S(2)}) collective-permute-start(bf16[272,128]{1,0:T(8,128)(2,1)S(1)} %get-tuple-element.35), channel_id=1, source_target_pairs={{0,1},{1,0},{2,3},{3,2},{4,5},{5,4},{6,7},{7,6},{8,9},{9,8},{10,11... | collective-permute-start | bytes 208904 | tf_op jit(solution)/shard_map/ppermute | solution.py:438
  7.9 0.0 copy-done
  7.9 0.0 copy-start.2
  7.9 0.0 copy-start.3
  7.9 2.3 %rest.1 = (bf16[16,8,16,256]{3,2,1,0:T(8,128)(2,1)S(1)}, bf16[272,128]{1,0:T(8,128)(2,1)S(1)}) custom-call(s32[2]{0:T(128)S(1)} %pad_add_fusion.index_ref, bf16[32,128,256]{2,1,0:T(8,128)(2,1)S(1)} %copy-done, s32[32,128]{1,0:T(8,128)S(1)} %get-tuple-element.27.shift_ref, f32[32,64]{1,0:T(8,128)S(1)} %get-tuple-element.28.deconv_ref, ...), custom_call_target="tpu_custom_call" | custom-call | flops 3000000000 | bytes 1048576 | tf_op jit(solution)/shard_map/rest/pallas_call | solution.py:496
  10.2 0.1 collective-permute-start
  10.3 0.0 collective-permute-done.2
  10.3 3.1 %collective-permute-start.3 = (bf16[272,128]{1,0:T(8,128)(2,1)S(1)}, bf16[272,128]{1,0:T(8,128)(2,1)S(1)}, u32[]{:S(2)}, u32[]{:S(2)}) collective-permute-start(bf16[272,128]{1,0:T(8,128)(2,1)S(1)} %add_convert_fusion.mine_ref), channel_id=1, source_target_pairs={{0,2},{1,3},{2,0},{3,1},{4,6},{5,7},{6,4},{7,5},{8,10},{9,11},{10,... | collective-permute-start | bytes 208904 | tf_op jit(solution)/shard_map/ppermute | solution.py:438
  13.4 1.6 %collective-permute-done = bf16[272,128]{1,0:T(8,128)(2,1)S(1)} collective-permute-done((bf16[272,128]{1,0:T(8,128)(2,1)S(1)}, bf16[272,128]{1,0:T(8,128)(2,1)S(1)}, u32[]{:S(2)}, u32[]{:S(2)}) %collective-permute-start) | collective-permute-done | bytes 69664 | tf_op jit(solution)/shard_map/ppermute | solution.py:438
  15.0 2.3 %collective-permute-start.1 = (bf16[272,128]{1,0:T(8,128)(2,1)S(1)}, bf16[272,128]{1,0:T(8,128)(2,1)S(1)}, u32[]{:S(2)}, u32[]{:S(2)}) collective-permute-start(bf16[272,128]{1,0:T(8,128)(2,1)S(1)} %add_convert_fusion.1.mine_ref), channel_id=1, source_target_pairs={{0,2},{1,3},{2,0},{3,1},{4,6},{5,7},{6,4},{7,5},{8,10},{9,11},{10,... | collective-permute-start | bytes 208904 | tf_op jit(solution)/shard_map/ppermute | solution.py:438
  17.3 0.0 collective-permute-done.3.other_ref
  17.3 0.0 copy-done.2
  17.3 0.0 copy-done.3
  17.3 1.2 %mute.1 = (bf16[16,2,4,16,128]{4,3,2,1,0:T(8,128)(2,1)S(1)}, f32[2,16,256]{2,1,0:T(8,128)S(1)}) custom-call(s32[2]{0:T(128)S(1)} %pad_add_fusion.index_ref, bf16[272,128]{1,0:T(8,128)(2,1)S(1)} %add_convert_fusion.mine_ref, bf16[272,128]{1,0:T(8,128)(2,1)S(1)} %collective-permute-done.3.other_ref, ...), custom_call_target="tpu_custom_call" | custom-call | flops 1000000000 | bytes 1048576 | tf_op jit(solution)/shard_map/mute/pallas_call | solution.py:515
  18.6 1.9 %collective-permute-done.1.other_ref = bf16[272,128]{1,0:T(8,128)(2,1)S(1)} collective-permute-done((bf16[272,128]{1,0:T(8,128)(2,1)S(1)}, bf16[272,128]{1,0:T(8,128)(2,1)S(1)}, u32[]{:S(2)}, u32[]{:S(2)}) %collective-permute-start.1) | collective-permute-done | bytes 69664 | tf_op jit(solution)/shard_map/ppermute | solution.py:438
  20.4 0.0 copy-start.1
  20.4 1.7 %adjoint.1 = (bf16[4,256,128]{2,1,0:T(8,128)(2,1)S(1)}, bf16[256,128]{1,0:T(8,128)(2,1)S(1)}, bf16[3,256,128]{2,1,0:T(8,128)(2,1)S(1)}, f32[2,32,256]{2,1,0:T(8,128)S(1)}) custom-call(s32[2]{0:T(128)S(1)} %pad_add_fusion.index_ref, bf16[272,128]{1,0:T(8,128)(2,1)S(1)} %add_convert_fusion.1.mine_ref, bf16[272,128]{1,0:T(8,128)(2,1)S(1)} %collective-permute-done.1.other_ref, ...), custom_call_target="tpu_custom_call" | custom-call | flops 2000000000 | bytes 1048576 | tf_op jit(solution)/shard_map/adjoint/pallas_call | solution.py:523
  22.1 0.1 collective-permute-start.4
  22.2 0.5 collective-permute-start.6
  22.7 0.7 %collective-permute-done.4 = bf16[256,128]{1,0:T(8,128)(2,1)S(1)} collective-permute-done((bf16[256,128]{1,0:T(8,128)(2,1)S(1)}, bf16[256,128]{1,0:T(8,128)(2,1)S(1)}, u32[]{:S(2)}, u32[]{:S(2)}) %collective-permute-start.4) | collective-permute-done | bytes 65568 | tf_op jit(solution)/shard_map/ppermute | solution.py:438
  23.5 0.0 copy-start.4
  23.5 2.6 %collective-permute-start.5 = (bf16[256,128]{1,0:T(8,128)(2,1)S(1)}, bf16[256,128]{1,0:T(8,128)(2,1)S(1)}, u32[]{:S(2)}, u32[]{:S(2)}) collective-permute-start(bf16[256,128]{1,0:T(8,128)(2,1)S(1)} %fusion), channel_id=1, source_target_pairs={{0,24},{4,28},{8,16},{12,20},{16,8},{20,12},{24,0},{28,4},{1,25},{... | collective-permute-start | bytes 196616 | tf_op jit(solution)/shard_map/ppermute | solution.py:438
  26.0 0.0 collective-permute-done.6
  26.0 0.1 fusion.3
  26.1 0.6 %collective-permute-start.8 = (bf16[256,128]{1,0:T(8,128)(2,1)S(1)}, bf16[256,128]{1,0:T(8,128)(2,1)S(1)}, u32[]{:S(2)}, u32[]{:S(2)}) collective-permute-start(bf16[256,128]{1,0:T(8,128)(2,1)S(1)} %get-tuple-element.52), channel_id=1, source_target_pairs={{0,8},{4,12},{8,0},{12,4},{16,24},{20,28},{24,16},{28,20},{1,9},{5... | collective-permute-start | bytes 196616 | tf_op jit(solution)/shard_map/ppermute | solution.py:438
  26.7 0.5 collective-permute-start.7
  27.2 1.7 %collective-permute-done.5.refs_0_ = bf16[256,128]{1,0:T(8,128)(2,1)S(1)} collective-permute-done((bf16[256,128]{1,0:T(8,128)(2,1)S(1)}, bf16[256,128]{1,0:T(8,128)(2,1)S(1)}, u32[]{:S(2)}, u32[]{:S(2)}) %collective-permute-start.5) | collective-permute-done | bytes 65568 | tf_op jit(solution)/shard_map/ppermute | solution.py:438
  28.9 1.5 %collective-permute-done.8.refs_2_ = bf16[256,128]{1,0:T(8,128)(2,1)S(1)} collective-permute-done((bf16[256,128]{1,0:T(8,128)(2,1)S(1)}, bf16[256,128]{1,0:T(8,128)(2,1)S(1)}, u32[]{:S(2)}, u32[]{:S(2)}) %collective-permute-start.8) | collective-permute-done | bytes 65568 | tf_op jit(solution)/shard_map/ppermute | solution.py:438
  30.4 0.5 %collective-permute-done.7.refs_1_ = bf16[256,128]{1,0:T(8,128)(2,1)S(1)} collective-permute-done((bf16[256,128]{1,0:T(8,128)(2,1)S(1)}, bf16[256,128]{1,0:T(8,128)(2,1)S(1)}, u32[]{:S(2)}, u32[]{:S(2)}) %collective-permute-start.7) | collective-permute-done | bytes 65568 | tf_op jit(solution)/shard_map/ppermute | solution.py:438
  31.0 0.0 copy-done.1
  31.0 0.5 downgoing.1
  31.4 1.6 %collective-permute-start.11 = (bf16[16,16,128]{2,1,0:T(8,128)(2,1)S(1)}, bf16[16,16,128]{2,1,0:T(8,128)(2,1)S(1)}, u32[]{:S(2)}, u32[]{:S(2)}) collective-permute-start(bf16[16,16,128]{2,1,0:T(8,128)(2,1)S(1)} %get-tuple-element.46.refs_0_), channel_id=1, source_target_pairs={{0,24},{4,28},{8,16},{12,20},{16,8},{20,12},{24,0},{28,4},{1,25},{... | collective-permute-start | bytes 196616 | tf_op jit(solution)/shard_map/ppermute | solution.py:438
  33.0 1.4 %collective-permute-start.10 = (bf16[16,16,128]{2,1,0:T(8,128)(2,1)S(1)}, bf16[16,16,128]{2,1,0:T(8,128)(2,1)S(1)}, u32[]{:S(2)}, u32[]{:S(2)}) collective-permute-start(bf16[16,16,128]{2,1,0:T(8,128)(2,1)S(1)} %get-tuple-element.46.refs_0_), channel_id=1, source_target_pairs={{0,16},{4,20},{8,24},{12,28},{16,0},{20,4},{24,8},{28,12},{1,17},{... | collective-permute-start | bytes 196616 | tf_op jit(solution)/shard_map/ppermute | solution.py:438
  34.5 0.5 %collective-permute-start.9 = (bf16[16,16,128]{2,1,0:T(8,128)(2,1)S(1)}, bf16[16,16,128]{2,1,0:T(8,128)(2,1)S(1)}, u32[]{:S(2)}, u32[]{:S(2)}) collective-permute-start(bf16[16,16,128]{2,1,0:T(8,128)(2,1)S(1)} %get-tuple-element.46.refs_0_), channel_id=1, source_target_pairs={{0,8},{4,12},{8,0},{12,4},{16,24},{20,28},{24,16},{28,20},{1,9},{5... | collective-permute-start | bytes 196616 | tf_op jit(solution)/shard_map/ppermute | solution.py:438
  35.0 0.0 collective-permute-start.12
  35.0 2.4 %collective-permute-done.11.refs_3_ = bf16[16,16,128]{2,1,0:T(8,128)(2,1)S(1)} collective-permute-done((bf16[16,16,128]{2,1,0:T(8,128)(2,1)S(1)}, bf16[16,16,128]{2,1,0:T(8,128)(2,1)S(1)}, u32[]{:S(2)}, u32[]{:S(2)}) %collective-permute-start.11) | collective-permute-done | bytes 65568 | tf_op jit(solution)/shard_map/ppermute | solution.py:438
  37.4 0.0 collective-permute-start.15
  37.4 0.3 collective-permute-done.10.refs_2_
  37.7 0.2 collective-permute-start.14
  37.9 0.8 %collective-permute-done.9.refs_1_ = bf16[16,16,128]{2,1,0:T(8,128)(2,1)S(1)} collective-permute-done((bf16[16,16,128]{2,1,0:T(8,128)(2,1)S(1)}, bf16[16,16,128]{2,1,0:T(8,128)(2,1)S(1)}, u32[]{:S(2)}, u32[]{:S(2)}) %collective-permute-start.9) | collective-permute-done | bytes 65568 | tf_op jit(solution)/shard_map/ppermute | solution.py:438
  38.7 0.0 collective-permute-start.13
  38.7 0.0 collective-permute-done.12.refs_4_
  38.7 0.0 collective-permute-done.15.refs_7_
  38.7 0.2 collective-permute-done.14.refs_6_
  38.9 1.0 %collective-permute-done.13.refs_5_ = bf16[16,16,128]{2,1,0:T(8,128)(2,1)S(1)} collective-permute-done((bf16[16,16,128]{2,1,0:T(8,128)(2,1)S(1)}, bf16[16,16,128]{2,1,0:T(8,128)(2,1)S(1)}, u32[]{:S(2)}, u32[]{:S(2)}) %collective-permute-start.13) | collective-permute-done | bytes 65568 | tf_op jit(solution)/shard_map/ppermute | solution.py:438
  40.0 0.0 copy-done.4
  40.0 1.8 %second.1 = (bf16[128,128]{1,0:T(8,128)(2,1)S(1)}, bf16[128,128]{1,0:T(8,128)(2,1)S(1)}, bf16[128,128]{1,0:T(8,128)(2,1)S(1)}, bf16[128,128]{1,0:T(8,128)(2,1)S(1)}) custom-call(s32[2]{0:T(128)S(1)} %pad_add_fusion.index_ref, bf16[16,16,128]{2,1,0:T(8,128)(2,1)S(1)} %get-tuple-element.46.refs_0_, bf16[16,16,128]{2,1,0:T(8,128)(2,1)S(1)} %collective-permute-done.9.refs_1_, ...), custom_call_target="tpu_custom_call" | custom-call | flops 1000000000 | bytes 1048576 | tf_op jit(solution)/shard_map/second/pallas_call | solution.py:559
  41.8 2.5 %collective-permute-start.16 = (bf16[128,128]{1,0:T(8,128)(2,1)S(1)}, bf16[128,128]{1,0:T(8,128)(2,1)S(1)}, u32[]{:S(2)}, u32[]{:S(2)}) collective-permute-start(bf16[128,128]{1,0:T(8,128)(2,1)S(1)} %get-tuple-element.47), channel_id=1, source_target_pairs={{0,3},{1,2},{2,1},{3,0},{4,7},{5,6},{6,5},{7,4},{8,11},{9,10},{10,... | collective-permute-start | bytes 98312 | tf_op jit(solution)/shard_map/ppermute | solution.py:438
  44.3 0.0 collective-permute-start.17
  44.3 1.9 %collective-permute-start.18 = (bf16[128,128]{1,0:T(8,128)(2,1)S(1)}, bf16[128,128]{1,0:T(8,128)(2,1)S(1)}, u32[]{:S(2)}, u32[]{:S(2)}) collective-permute-start(bf16[128,128]{1,0:T(8,128)(2,1)S(1)} %get-tuple-element.49), channel_id=1, source_target_pairs={{0,1},{1,0},{2,3},{3,2},{4,5},{5,4},{6,7},{7,6},{8,9},{9,8},{10,11... | collective-permute-start | bytes 98312 | tf_op jit(solution)/shard_map/ppermute | solution.py:438
  46.2 0.6 %emit.2 = f32[2,32,256]{2,1,0:T(8,128)} custom-call(f32[2,32,256]{2,1,0:T(8,128)S(1)} %get-tuple-element.40.field_ref), custom_call_target="tpu_custom_call" | custom-call | flops 300000000 | bytes 1048576 | tf_op jit(solution)/shard_map/emit/pallas_call | solution.py:431
  46.9 0.7 %emit.3 = f32[1,128,256]{2,1,0:T(8,128)} custom-call(f32[1,128,256]{2,1,0:T(8,128)S(1)} %get-tuple-element.45.field_ref), custom_call_target="tpu_custom_call" | custom-call | flops 300000000 | bytes 1048576 | tf_op jit(solution)/shard_map/emit/pallas_call | solution.py:431
  47.5 0.3 collective-permute-done.16.refs_0_
  47.9 1.2 %collective-permute-done.17.refs_1_ = bf16[128,128]{1,0:T(8,128)(2,1)S(1)} collective-permute-done((bf16[128,128]{1,0:T(8,128)(2,1)S(1)}, bf16[128,128]{1,0:T(8,128)(2,1)S(1)}, u32[]{:S(2)}, u32[]{:S(2)}) %collective-permute-start.17) | collective-permute-done | bytes 32800 | tf_op jit(solution)/shard_map/ppermute | solution.py:438
  49.1 0.0 collective-permute-done.18.refs_2_
  49.1 0.9 %final.1 = f32[2,32,256]{2,1,0:T(8,128)} custom-call(bf16[128,128]{1,0:T(8,128)(2,1)S(1)} %collective-permute-done.16.refs_0_, bf16[128,128]{1,0:T(8,128)(2,1)S(1)} %collective-permute-done.17.refs_1_, bf16[128,128]{1,0:T(8,128)(2,1)S(1)} %collective-permute-done.18.refs_2_, bf16[128,128]{1,0:T(8,128)(2,1)S(1)} %get-tuple-element.50.refs_3_, ...), custom_call_target="tpu_custom_call" | custom-call | flops 1000000000 | bytes 1048576 | tf_op jit(solution)/shard_map/final/pallas_call | solution.py:573
  (3 shorter events, 0.1 us)
Async XLA Ops:
  0.7 7.2 %copy-start = (bf16[32,128,256]{2,1,0:T(8,128)(2,1)S(1)}, bf16[32,128,256]{2,1,0:T(8,128)(2,1)}, u32[]{:S(2)}) copy-start(bf16[32,128,256]{2,1,0:T(8,128)(2,1)} %traces_ref.1) | copy-start | bytes 6291460
  4.8 5.5 %collective-permute-start.2 = (bf16[272,128]{1,0:T(8,128)(2,1)S(1)}, bf16[272,128]{1,0:T(8,128)(2,1)S(1)}, u32[]{:S(2)}, u32[]{:S(2)}) collective-permute-start(bf16[272,128]{1,0:T(8,128)(2,1)S(1)} %get-tuple-element.35), channel_id=1, source_target_pairs={{0,1},{1,0},{2,3},{3,2},{4,5},{5,4},{6,7},{7,6},{8,9},{9,8},{10,11... | collective-permute-start | bytes 208904 | tf_op jit(solution)/shard_map/ppermute | solution.py:438
  7.9 9.4 %copy-start.2 = (bf16[2,4,128,256]{3,2,1,0:T(8,128)(2,1)S(1)}, bf16[2,4,128,256]{3,2,1,0:T(8,128)(2,1)}, u32[]{:S(2)}) copy-start(bf16[2,4,128,256]{3,2,1,0:T(8,128)(2,1)} %constant.32.spread_ref) | copy-start | bytes 1572868
  7.9 9.4 %copy-start.3 = (bf16[256,256]{1,0:T(8,128)(2,1)S(1)}, bf16[256,256]{1,0:T(8,128)(2,1)}, u32[]{:S(2)}) copy-start(bf16[256,256]{1,0:T(8,128)(2,1)} %constant.31.inverse_ref.refs_7_.refs_5_) | copy-start | bytes 393220
  10.2 4.8 %collective-permute-start = (bf16[272,128]{1,0:T(8,128)(2,1)S(1)}, bf16[272,128]{1,0:T(8,128)(2,1)S(1)}, u32[]{:S(2)}, u32[]{:S(2)}) collective-permute-start(bf16[272,128]{1,0:T(8,128)(2,1)S(1)} %get-tuple-element.34), channel_id=1, source_target_pairs={{0,1},{1,0},{2,3},{3,2},{4,5},{5,4},{6,7},{7,6},{8,9},{9,8},{10,11... | collective-permute-start | bytes 208904 | tf_op jit(solution)/shard_map/ppermute | solution.py:438
  10.3 7.0 %collective-permute-start.3 = (bf16[272,128]{1,0:T(8,128)(2,1)S(1)}, bf16[272,128]{1,0:T(8,128)(2,1)S(1)}, u32[]{:S(2)}, u32[]{:S(2)}) collective-permute-start(bf16[272,128]{1,0:T(8,128)(2,1)S(1)} %add_convert_fusion.mine_ref), channel_id=1, source_target_pairs={{0,2},{1,3},{2,0},{3,1},{4,6},{5,7},{6,4},{7,5},{8,10},{9,11},{10,... | collective-permute-start | bytes 208904 | tf_op jit(solution)/shard_map/ppermute | solution.py:438
  15.0 5.4 %collective-permute-start.1 = (bf16[272,128]{1,0:T(8,128)(2,1)S(1)}, bf16[272,128]{1,0:T(8,128)(2,1)S(1)}, u32[]{:S(2)}, u32[]{:S(2)}) collective-permute-start(bf16[272,128]{1,0:T(8,128)(2,1)S(1)} %add_convert_fusion.1.mine_ref), channel_id=1, source_target_pairs={{0,2},{1,3},{2,0},{3,1},{4,6},{5,7},{6,4},{7,5},{8,10},{9,11},{10,... | collective-permute-start | bytes 208904 | tf_op jit(solution)/shard_map/ppermute | solution.py:438
  20.4 10.5 %copy-start.1 = (s32[1,128]{1,0:T(1,128)S(1)}, s32[1,128]{1,0:T(1,128)}, u32[]{:S(2)}) copy-start(s32[1,128]{1,0:T(1,128)} %refs_5_.1) | copy-start | bytes 1540
  22.1 1.3 %collective-permute-start.4 = (bf16[256,128]{1,0:T(8,128)(2,1)S(1)}, bf16[256,128]{1,0:T(8,128)(2,1)S(1)}, u32[]{:S(2)}, u32[]{:S(2)}) collective-permute-start(bf16[256,128]{1,0:T(8,128)(2,1)S(1)} %get-tuple-element.42), channel_id=1, source_target_pairs={{0,4},{4,0},{8,12},{12,8},{16,20},{20,16},{24,28},{28,24},{1,5},{5... | collective-permute-start | bytes 196616 | tf_op jit(solution)/shard_map/ppermute | solution.py:438
  22.2 3.8 %collective-permute-start.6 = (bf16[3,256,128]{2,1,0:T(8,128)(2,1)S(1)}, bf16[3,256,128]{2,1,0:T(8,128)(2,1)S(1)}, u32[]{:S(2)}, u32[]{:S(2)}) collective-permute-start(bf16[3,256,128]{2,1,0:T(8,128)(2,1)S(1)} %get-tuple-element.43), channel_id=1, source_target_pairs={{0,4},{4,0},{8,12},{12,8},{16,20},{20,16},{24,28},{28,24},{1,5},{5... | collective-permute-start | bytes 589832 | tf_op jit(solution)/shard_map/ppermute | solution.py:438
  23.5 16.5 %copy-start.4 = (bf16[256,128]{1,0:T(8,128)(2,1)S(1)}, bf16[256,128]{1,0:T(8,128)(2,1)}, u32[]{:S(2)}) copy-start(bf16[256,128]{1,0:T(8,128)(2,1)} %constant.33.refs_10_) | copy-start | bytes 196612
  23.5 5.4 %collective-permute-start.5 = (bf16[256,128]{1,0:T(8,128)(2,1)S(1)}, bf16[256,128]{1,0:T(8,128)(2,1)S(1)}, u32[]{:S(2)}, u32[]{:S(2)}) collective-permute-start(bf16[256,128]{1,0:T(8,128)(2,1)S(1)} %fusion), channel_id=1, source_target_pairs={{0,24},{4,28},{8,16},{12,20},{16,8},{20,12},{24,0},{28,4},{1,25},{... | collective-permute-start | bytes 196616 | tf_op jit(solution)/shard_map/ppermute | solution.py:438
  26.1 4.3 %collective-permute-start.8 = (bf16[256,128]{1,0:T(8,128)(2,1)S(1)}, bf16[256,128]{1,0:T(8,128)(2,1)S(1)}, u32[]{:S(2)}, u32[]{:S(2)}) collective-permute-start(bf16[256,128]{1,0:T(8,128)(2,1)S(1)} %get-tuple-element.52), channel_id=1, source_target_pairs={{0,8},{4,12},{8,0},{12,4},{16,24},{20,28},{24,16},{28,20},{1,9},{5... | collective-permute-start | bytes 196616 | tf_op jit(solution)/shard_map/ppermute | solution.py:438
  26.7 4.3 %collective-permute-start.7 = (bf16[256,128]{1,0:T(8,128)(2,1)S(1)}, bf16[256,128]{1,0:T(8,128)(2,1)S(1)}, u32[]{:S(2)}, u32[]{:S(2)}) collective-permute-start(bf16[256,128]{1,0:T(8,128)(2,1)S(1)} %get-tuple-element.53), channel_id=1, source_target_pairs={{0,16},{4,20},{8,24},{12,28},{16,0},{20,4},{24,8},{28,12},{1,17},{... | collective-permute-start | bytes 196616 | tf_op jit(solution)/shard_map/ppermute | solution.py:438
  31.4 5.9 %collective-permute-start.11 = (bf16[16,16,128]{2,1,0:T(8,128)(2,1)S(1)}, bf16[16,16,128]{2,1,0:T(8,128)(2,1)S(1)}, u32[]{:S(2)}, u32[]{:S(2)}) collective-permute-start(bf16[16,16,128]{2,1,0:T(8,128)(2,1)S(1)} %get-tuple-element.46.refs_0_), channel_id=1, source_target_pairs={{0,24},{4,28},{8,16},{12,20},{16,8},{20,12},{24,0},{28,4},{1,25},{... | collective-permute-start | bytes 196616 | tf_op jit(solution)/shard_map/ppermute | solution.py:438
  33.0 4.6 %collective-permute-start.10 = (bf16[16,16,128]{2,1,0:T(8,128)(2,1)S(1)}, bf16[16,16,128]{2,1,0:T(8,128)(2,1)S(1)}, u32[]{:S(2)}, u32[]{:S(2)}) collective-permute-start(bf16[16,16,128]{2,1,0:T(8,128)(2,1)S(1)} %get-tuple-element.46.refs_0_), channel_id=1, source_target_pairs={{0,16},{4,20},{8,24},{12,28},{16,0},{20,4},{24,8},{28,12},{1,17},{... | collective-permute-start | bytes 196616 | tf_op jit(solution)/shard_map/ppermute | solution.py:438
  34.5 4.3 %collective-permute-start.9 = (bf16[16,16,128]{2,1,0:T(8,128)(2,1)S(1)}, bf16[16,16,128]{2,1,0:T(8,128)(2,1)S(1)}, u32[]{:S(2)}, u32[]{:S(2)}) collective-permute-start(bf16[16,16,128]{2,1,0:T(8,128)(2,1)S(1)} %get-tuple-element.46.refs_0_), channel_id=1, source_target_pairs={{0,8},{4,12},{8,0},{12,4},{16,24},{20,28},{24,16},{28,20},{1,9},{5... | collective-permute-start | bytes 196616 | tf_op jit(solution)/shard_map/ppermute | solution.py:438
  35.0 3.7 %collective-permute-start.12 = (bf16[16,16,128]{2,1,0:T(8,128)(2,1)S(1)}, bf16[16,16,128]{2,1,0:T(8,128)(2,1)S(1)}, u32[]{:S(2)}, u32[]{:S(2)}) collective-permute-start(bf16[16,16,128]{2,1,0:T(8,128)(2,1)S(1)} %get-tuple-element.46.refs_0_), channel_id=1, source_target_pairs={{0,4},{4,0},{8,12},{12,8},{16,20},{20,16},{24,28},{28,24},{1,5},{5... | collective-permute-start | bytes 196616 | tf_op jit(solution)/shard_map/ppermute | solution.py:438
  37.4 1.4 %collective-permute-start.15 = (bf16[16,16,128]{2,1,0:T(8,128)(2,1)S(1)}, bf16[16,16,128]{2,1,0:T(8,128)(2,1)S(1)}, u32[]{:S(2)}, u32[]{:S(2)}) collective-permute-start(bf16[16,16,128]{2,1,0:T(8,128)(2,1)S(1)} %collective-permute-done.11.refs_3_), channel_id=1, source_target_pairs={{0,4},{4,0},{8,12},{12,8},{16,20},{20,16},{24,28},{28,24},{1,5},{5... | collective-permute-start | bytes 196616 | tf_op jit(solution)/shard_map/ppermute | solution.py:438
  37.7 1.3 %collective-permute-start.14 = (bf16[16,16,128]{2,1,0:T(8,128)(2,1)S(1)}, bf16[16,16,128]{2,1,0:T(8,128)(2,1)S(1)}, u32[]{:S(2)}, u32[]{:S(2)}) collective-permute-start(bf16[16,16,128]{2,1,0:T(8,128)(2,1)S(1)} %collective-permute-done.10.refs_2_), channel_id=1, source_target_pairs={{0,4},{4,0},{8,12},{12,8},{16,20},{20,16},{24,28},{28,24},{1,5},{5... | collective-permute-start | bytes 196616 | tf_op jit(solution)/shard_map/ppermute | solution.py:438
  38.7 1.3 %collective-permute-start.13 = (bf16[16,16,128]{2,1,0:T(8,128)(2,1)S(1)}, bf16[16,16,128]{2,1,0:T(8,128)(2,1)S(1)}, u32[]{:S(2)}, u32[]{:S(2)}) collective-permute-start(bf16[16,16,128]{2,1,0:T(8,128)(2,1)S(1)} %collective-permute-done.9.refs_1_), channel_id=1, source_target_pairs={{0,4},{4,0},{8,12},{12,8},{16,20},{20,16},{24,28},{28,24},{1,5},{5... | collective-permute-start | bytes 196616 | tf_op jit(solution)/shard_map/ppermute | solution.py:438
  41.8 6.1 %collective-permute-start.16 = (bf16[128,128]{1,0:T(8,128)(2,1)S(1)}, bf16[128,128]{1,0:T(8,128)(2,1)S(1)}, u32[]{:S(2)}, u32[]{:S(2)}) collective-permute-start(bf16[128,128]{1,0:T(8,128)(2,1)S(1)} %get-tuple-element.47), channel_id=1, source_target_pairs={{0,3},{1,2},{2,1},{3,0},{4,7},{5,6},{6,5},{7,4},{8,11},{9,10},{10,... | collective-permute-start | bytes 98312 | tf_op jit(solution)/shard_map/ppermute | solution.py:438
  44.3 4.8 %collective-permute-start.17 = (bf16[128,128]{1,0:T(8,128)(2,1)S(1)}, bf16[128,128]{1,0:T(8,128)(2,1)S(1)}, u32[]{:S(2)}, u32[]{:S(2)}) collective-permute-start(bf16[128,128]{1,0:T(8,128)(2,1)S(1)} %get-tuple-element.48), channel_id=1, source_target_pairs={{0,2},{1,3},{2,0},{3,1},{4,6},{5,7},{6,4},{7,5},{8,10},{9,11},{10,... | collective-permute-start | bytes 98312 | tf_op jit(solution)/shard_map/ppermute | solution.py:438
  44.3 4.8 %collective-permute-start.18 = (bf16[128,128]{1,0:T(8,128)(2,1)S(1)}, bf16[128,128]{1,0:T(8,128)(2,1)S(1)}, u32[]{:S(2)}, u32[]{:S(2)}) collective-permute-start(bf16[128,128]{1,0:T(8,128)(2,1)S(1)} %get-tuple-element.49), channel_id=1, source_target_pairs={{0,1},{1,0},{2,3},{3,2},{4,5},{5,4},{6,7},{7,6},{8,9},{9,8},{10,11... | collective-permute-start | bytes 98312 | tf_op jit(solution)/shard_map/ppermute | solution.py:438

commit v7 on v6

--- a/solution.py
+++ b/solution.py
@@ -196,7 +196,7 @@
 
 
 def first_kernel(
-    gain, index_ref, traces_hbm, shift_hbm, deconv_hbm, focal_hbm, onset_hbm,
+    gain, traces_hbm, shift_hbm, deconv_hbm, focal_hbm, onset_hbm,
     forward_hbm, taps_hbm, gather_hbm, matrix_ref, sum_ref, own_ref, vector_ref,
     shift_ref, deconv_ref, onset_ref, forward_ref, taps_ref, gather_ref,
     kept_ref, traces_ref, focal_ref, large_sem, small_sem, delay_ref,
@@ -229,18 +229,18 @@
     for place in range(fields):
         spectra = mm(forward, focal_ref[place], NT_DIMS)
         store_vector(vector_ref, place, spectra[:NF], spectra[NF:])
-    own_ref[...] = focal_ref[index_ref[0]]
+    own_ref[...] = focal_ref[lax.axis_index("shot")]
     for copy in small[3:] + large[1:]:
         copy.wait()
     for couple in range(half // 2):
         make_matrix(0, couple, forward, traces_ref, shift_ref, delay_ref, matrix_ref)
     make_sums(
-        0, index_ref[1], matrix_ref, vector_ref, kept_ref, gather_ref[...], onset_ref, sum_ref
+        0, lax.axis_index("rcv"), matrix_ref, vector_ref, kept_ref, gather_ref[...], onset_ref, sum_ref
     )
 
 
 def rest_kernel(
-    gain, index_ref, traces_ref, shift_ref, deconv_ref, onset_ref, forward_ref, taps_ref,
+    gain, traces_ref, shift_ref, deconv_ref, onset_ref, forward_ref, taps_ref,
     gather_ref, vector_ref, matrix_ref, sum_ref, kept_ref, delay_ref,
 ):
     half = traces_ref.shape[0] // 2
@@ -250,7 +250,7 @@
     for couple in range(half // 2):
         make_matrix(half, couple, forward, upper, shift_ref, delay_ref, matrix_ref)
     make_sums(
-        half, index_ref[1], matrix_ref, vector_ref, kept_ref, gather_ref[...], onset_ref, sum_ref
+        half, lax.axis_index("rcv"), matrix_ref, vector_ref, kept_ref, gather_ref[...], onset_ref, sum_ref
     )
 
 
@@ -268,9 +268,9 @@
     return jnp.where(folded < onset, signal, 0.0)
 
 
-def mute_half(index_ref, mine_ref, other_ref, forward, inverse, spread_ref, vector_ref):
-    shot_index = index_ref[0]
-    rcv_index = index_ref[1]
+def mute_half(mine_ref, other_ref, forward, inverse, spread_ref, vector_ref):
+    shot_index = lax.axis_index("shot")
+    rcv_index = lax.axis_index("rcv")
     core = shot_index % 2
     chip = shot_index // 2
     width = vector_ref.shape[-1]
@@ -302,15 +302,15 @@
 
 
 def mute_kernel(
-    index_ref, mine_ref, other_ref, forward_ref, inverse_ref, spread_ref, vector_ref, field_ref
+    mine_ref, other_ref, forward_ref, inverse_ref, spread_ref, vector_ref, field_ref
 ):
     field_ref[...] = mute_half(
-        index_ref, mine_ref, other_ref, forward_ref[...], inverse_ref[...], spread_ref, vector_ref
+        mine_ref, other_ref, forward_ref[...], inverse_ref[...], spread_ref, vector_ref
     )
 
 
 def adjoint_kernel(
-    index_ref, mine_ref, other_ref, forward_ref, inverse_ref, spread_ref,
+    mine_ref, other_ref, forward_ref, inverse_ref, spread_ref,
     lower_ref, field_half_ref, first_ref, rest_ref, *refs
 ):
     keep_ref, far_ref, send_ref, field_ref, upper_ref = refs
@@ -320,7 +320,7 @@
     half = width // GROUP
     field_ref[:, :half] = field_half_ref[...]
     field_ref[:, half:] = mute_half(
-        index_ref, mine_ref, other_ref, forward_ref[...], inverse_ref[...], spread_ref, upper_ref
+        mine_ref, other_ref, forward_ref[...], inverse_ref[...], spread_ref, upper_ref
     )
 
     def one(group):
@@ -361,13 +361,13 @@
     plus_ref[...] = interleave(spectra[:NF], spectra[NF:]).astype(BF16)
 
 
-def second_kernel(pairs, index_ref, *refs):
+def second_kernel(pairs, *refs):
     near_refs, far_refs = refs[:pairs], refs[pairs : 2 * pairs]
     first_ref, rest_ref, gather_ref = refs[2 * pairs : 2 * pairs + 3]
     sum_refs = refs[2 * pairs + 3 : -2]
     vector_ref, kept_ref = refs[-2:]
-    shot_index = index_ref[0]
-    rcv_index = index_ref[1]
+    shot_index = lax.axis_index("shot")
+    rcv_index = lax.axis_index("rcv")
     core = shot_index % 2
     chip = shot_index // 2
     for distance in range(pairs):
@@ -401,10 +401,6 @@
 
 def vmem(count):
     return [pl.BlockSpec(memory_space=pltpu.VMEM) for _ in range(count)]
-
-
-def smem():
-    return [pl.BlockSpec(memory_space=pltpu.SMEM)]
 
 
 def hbm(count):
@@ -452,7 +448,6 @@
     assert focal_total == shot_count and 4 * sources == LANES and receivers == LANES
     gain = 1.0 / math.sqrt(NT * receivers * rcv_count)
     tables = make_tables(sources)
-    index = jnp.stack([lax.axis_index("shot"), lax.axis_index("rcv")]).astype(jnp.int32)
     shape = jax.ShapeDtypeStruct
     half = sources // 2
     sets = focal_total // (LANES // half // 2)
@@ -481,7 +476,7 @@
             vector,
         ]
         + [shape(value.shape, value.dtype) for value in small],
-        smem() + hbm(len(inputs)),
+        hbm(len(inputs)),
         [
             half_kept,
             pltpu.VMEM((half, receivers, NT), BF16),
@@ -491,16 +486,16 @@
             half_delays,
         ],
         work=4.0e9,
-    )(index, *[pltpu.with_memory_space_constraint(value, pltpu.HBM) for value in inputs])
+    )(*[pltpu.with_memory_space_constraint(value, pltpu.HBM) for value in inputs])
     forward = loaded[3]
     rest, rest_sum = call(
         functools.partial(rest_kernel, gain),
         "rest",
         (half_matrix, half_sums),
-        smem() + vmem(8),
+        vmem(8),
         [half_kept, half_delays],
         work=3.0e9,
-    )(index, traces, *loaded, start)
+    )(traces, *loaded, start)
 
     mine = [first_sum, rest_sum]
     other = [exchange(value, "rcv", 1) for value in mine]
@@ -516,9 +511,9 @@
         mute_kernel,
         "mute",
         (echo, shape((2, half, NT), F32)),
-        smem() + vmem(5),
+        vmem(5),
         work=1.0e9,
-    )(index, mine[0], other[0], *shared)
+    )(mine[0], other[0], *shared)
 
     keep, far, send, upgoing_first = call(
         adjoint_kernel,
@@ -529,10 +524,10 @@
             shape((pairs - 1, 2 * NF, receivers), BF16),
             shape((2, sources, NT), F32),
         ],
-        smem() + vmem(9),
+        vmem(9),
         [buffer(echo)],
         work=2.0e9,
-    )(index, mine[1], other[1], *shared, lower, field_half, first, rest)
+    )(mine[1], other[1], *shared, lower, field_half, first, rest)
 
     far = exchange(far, "shot", 1)
     near = exchange(send, "shot", 1)
@@ -560,12 +555,12 @@
         functools.partial(second_kernel, pairs),
         "second",
         [shape((NF, LANES), BF16)] * pairs,
-        smem() + vmem(2 * pairs + 3),
+        vmem(2 * pairs + 3),
         [
             buffer(vector),
             pltpu.VMEM((NG * focal_total * 2 * GROUP, sources * GROUP), BF16),
         ],
-    )(index, *near, *far, first, rest, tables["gather"])
+    )(*near, *far, first, rest, tables["gather"])
 
     parts = [
         exchange(parts[distance], "rcv", distance) for distance in reversed(range(1, rcv_count))

time: 50.2 us -> 48.1 us (0.958)
  Pallas kernels: 13.7 us -> 11.1 us
    pallas_call x1, Pallas kernels: 1.67 us -> 1.13 us  [body(): call(adjoint_kernel, 'adjoint', [shape((pairs, 2 * NF, receivers), BF16),...]
    pallas_call x1, Pallas kernels: 1.22 us -> 0.69 us  [body(): call(mute_kernel, 'mute', (echo, shape((2, half, NT), F32)), vmem(5), wor...]
    pallas_call x1, Pallas kernels: 1.78 us -> 1.25 us  [body(): call(functools.partial(second_kernel, pairs), 'second', [shape((NF, LANES...]
    pallas_call x1, Pallas kernels: 2.29 us -> 1.78 us  [body(): call(functools.partial(rest_kernel, gain), 'rest', (half_matrix, half_sum...]
  transfers between devices with their start and end apart: 19 -> 19, of which waited for: 13 -> 14; matrix products, arithmetic and copies ran while one was open for 0% -> 0% of each run, Pallas kernels for 10% -> 8%
where the time goes in v7:
time: 48.1 us; the launch traced here: 47.9 us
  starting transfers between devices  21 us (44%)
  waiting for transfers between devices  14.9 us (31%)
  Pallas kernels  11.1 us (23%)
  between operations  0.75 us (2%)
    ppermute x19, starting transfers between devices, exchange(): lax.ppermute(value, axis, [(place, place ^ distance) for place in range(c...  21 us
    ppermute x19, waiting for transfers between devices, exchange(): lax.ppermute(value, axis, [(place, place ^ distance) for place in range(c...  14.9 us
    pallas_call x1, Pallas kernels, body(): call(functools.partial(first_kernel, gain), 'first', [half_matrix, half_s...  3.6 us
    pallas_call x1, Pallas kernels, body(): call(functools.partial(rest_kernel, gain), 'rest', (half_matrix, half_sum...  1.78 us
    pallas_call x2, Pallas kernels, emit(): call(emit_kernel, 'emit', jax.ShapeDtypeStruct(field.shape, field.dtype),...  1.3 us
    pallas_call x1, Pallas kernels, body(): call(functools.partial(second_kernel, pairs), 'second', [shape((NF, LANES...  1.25 us
    pallas_call x1, Pallas kernels, body(): call(adjoint_kernel, 'adjoint', [shape((pairs, 2 * NF, receivers), BF16),...  1.13 us
  transfers between devices with their start and end apart: 19, of which 14 were waited for; matrix products, arithmetic and copies ran while one was open for 0% of the time, Pallas kernels for 8%

profile of v7, /device:TPU:0, one launch (start us, length us, event | category | flops | bytes accessed | tf_op | source)
XLA Modules:
  0.0 47.9 jit_solution(9216810047219312070)
XLA Ops:
  0.6 0.0 copy-start
  0.6 3.6 %first.1 = (bf16[16,8,16,256]{3,2,1,0:T(8,128)(2,1)S(1)}, bf16[272,128]{1,0:T(8,128)(2,1)S(1)}, bf16[128,256]{1,0:T(8,128)(2,1)S(1)}, bf16[16,8,16,256]{3,2,1,0:...) custom-call(bf16[32,128,256]{2,1,0:T(8,128)(2,1)} %traces_ref.1, ...), custom_call_target="tpu_custom_call" | custom-call | flops 4000000000 | bytes 1048576 | tf_op jit(solution)/shard_map/first/pallas_call | solution.py:469
  4.3 3.1 %collective-permute-start.2 = (bf16[272,128]{1,0:T(8,128)(2,1)S(1)}, bf16[272,128]{1,0:T(8,128)(2,1)S(1)}, u32[]{:S(2)}, u32[]{:S(2)}) collective-permute-start(bf16[272,128]{1,0:T(8,128)(2,1)S(1)} %get-tuple-element.35), channel_id=1, source_target_pairs={{0,1},{1,0},{2,3},{3,2},{4,5},{5,4},{6,7},{7,6},{8,9},{9,8},{10,11... | collective-permute-start | bytes 208904 | tf_op jit(solution)/shard_map/ppermute | solution.py:434
  7.3 0.0 copy-done
  7.3 0.0 copy-start.2
  7.3 0.0 copy-start.3
  7.3 1.8 %rest.1 = (bf16[16,8,16,256]{3,2,1,0:T(8,128)(2,1)S(1)}, bf16[272,128]{1,0:T(8,128)(2,1)S(1)}) custom-call(bf16[32,128,256]{2,1,0:T(8,128)(2,1)S(1)} %copy-done, s32[32,128]{1,0:T(8,128)S(1)} %get-tuple-element.27.shift_ref, f32[32,64]{1,0:T(8,128)S(1)} %get-tuple-element.28.deconv_ref, s32[2,32]{1,0:T(2,128)S(1)} %get-tuple-element.29.onset_ref.refs_4_, ...), custom_call_target="tpu_custom_call" | custom-call | flops 3000000000 | bytes 1048576 | tf_op jit(solution)/shard_map/rest/pallas_call | solution.py:491
  9.1 0.1 collective-permute-start
  9.2 0.4 collective-permute-done.2
  9.6 3.1 %collective-permute-start.3 = (bf16[272,128]{1,0:T(8,128)(2,1)S(1)}, bf16[272,128]{1,0:T(8,128)(2,1)S(1)}, u32[]{:S(2)}, u32[]{:S(2)}) collective-permute-start(bf16[272,128]{1,0:T(8,128)(2,1)S(1)} %add_convert_fusion.mine_ref), channel_id=1, source_target_pairs={{0,2},{1,3},{2,0},{3,1},{4,6},{5,7},{6,4},{7,5},{8,10},{9,11},{10,... | collective-permute-start | bytes 208904 | tf_op jit(solution)/shard_map/ppermute | solution.py:434
  12.7 1.2 %collective-permute-done = bf16[272,128]{1,0:T(8,128)(2,1)S(1)} collective-permute-done((bf16[272,128]{1,0:T(8,128)(2,1)S(1)}, bf16[272,128]{1,0:T(8,128)(2,1)S(1)}, u32[]{:S(2)}, u32[]{:S(2)}) %collective-permute-start) | collective-permute-done | bytes 69664 | tf_op jit(solution)/shard_map/ppermute | solution.py:434
  14.0 2.3 %collective-permute-start.1 = (bf16[272,128]{1,0:T(8,128)(2,1)S(1)}, bf16[272,128]{1,0:T(8,128)(2,1)S(1)}, u32[]{:S(2)}, u32[]{:S(2)}) collective-permute-start(bf16[272,128]{1,0:T(8,128)(2,1)S(1)} %add_convert_fusion.1.mine_ref), channel_id=1, source_target_pairs={{0,2},{1,3},{2,0},{3,1},{4,6},{5,7},{6,4},{7,5},{8,10},{9,11},{10,... | collective-permute-start | bytes 208904 | tf_op jit(solution)/shard_map/ppermute | solution.py:434
  16.3 0.0 collective-permute-done.3.other_ref
  16.3 0.0 copy-done.2
  16.3 0.0 copy-done.3
  16.3 0.7 %mute.1 = (bf16[16,2,4,16,128]{4,3,2,1,0:T(8,128)(2,1)S(1)}, f32[2,16,256]{2,1,0:T(8,128)S(1)}) custom-call(bf16[272,128]{1,0:T(8,128)(2,1)S(1)} %add_convert_fusion.mine_ref, bf16[272,128]{1,0:T(8,128)(2,1)S(1)} %collective-permute-done.3.other_ref, bf16[256,256]{1,0:T(8,128)(2,1)S(1)} %get-tuple-element.30.forward_ref.refs_6_, ...), custom_call_target="tpu_custom_call" | custom-call | flops 1000000000 | bytes 1048576 | tf_op jit(solution)/shard_map/mute/pallas_call | solution.py:510
  17.0 2.8 %collective-permute-done.1.other_ref = bf16[272,128]{1,0:T(8,128)(2,1)S(1)} collective-permute-done((bf16[272,128]{1,0:T(8,128)(2,1)S(1)}, bf16[272,128]{1,0:T(8,128)(2,1)S(1)}, u32[]{:S(2)}, u32[]{:S(2)}) %collective-permute-start.1) | collective-permute-done | bytes 69664 | tf_op jit(solution)/shard_map/ppermute | solution.py:434
  19.8 0.0 copy-start.1
  19.8 1.1 %adjoint.1 = (bf16[4,256,128]{2,1,0:T(8,128)(2,1)S(1)}, bf16[256,128]{1,0:T(8,128)(2,1)S(1)}, bf16[3,256,128]{2,1,0:T(8,128)(2,1)S(1)}, f32[2,32,256]{2,1,0:T(8,128)S(1)}) custom-call(bf16[272,128]{1,0:T(8,128)(2,1)S(1)} %add_convert_fusion.1.mine_ref, bf16[272,128]{1,0:T(8,128)(2,1)S(1)} %collective-permute-done.1.other_ref, ...), custom_call_target="tpu_custom_call" | custom-call | flops 2000000000 | bytes 1048576 | tf_op jit(solution)/shard_map/adjoint/pallas_call | solution.py:518
  21.0 0.1 collective-permute-start.4
  21.0 0.5 %collective-permute-start.6 = (bf16[3,256,128]{2,1,0:T(8,128)(2,1)S(1)}, bf16[3,256,128]{2,1,0:T(8,128)(2,1)S(1)}, u32[]{:S(2)}, u32[]{:S(2)}) collective-permute-start(bf16[3,256,128]{2,1,0:T(8,128)(2,1)S(1)} %get-tuple-element.43), channel_id=1, source_target_pairs={{0,4},{4,0},{8,12},{12,8},{16,20},{20,16},{24,28},{28,24},{1,5},{5... | collective-permute-start | bytes 589832 | tf_op jit(solution)/shard_map/ppermute | solution.py:434
  21.5 0.7 %collective-permute-done.4 = bf16[256,128]{1,0:T(8,128)(2,1)S(1)} collective-permute-done((bf16[256,128]{1,0:T(8,128)(2,1)S(1)}, bf16[256,128]{1,0:T(8,128)(2,1)S(1)}, u32[]{:S(2)}, u32[]{:S(2)}) %collective-permute-start.4) | collective-permute-done | bytes 65568 | tf_op jit(solution)/shard_map/ppermute | solution.py:434
  22.3 0.0 copy-start.4
  22.3 2.5 %collective-permute-start.5 = (bf16[256,128]{1,0:T(8,128)(2,1)S(1)}, bf16[256,128]{1,0:T(8,128)(2,1)S(1)}, u32[]{:S(2)}, u32[]{:S(2)}) collective-permute-start(bf16[256,128]{1,0:T(8,128)(2,1)S(1)} %fusion), channel_id=1, source_target_pairs={{0,24},{4,28},{8,16},{12,20},{16,8},{20,12},{24,0},{28,4},{1,25},{... | collective-permute-start | bytes 196616 | tf_op jit(solution)/shard_map/ppermute | solution.py:434
  24.8 0.0 collective-permute-done.6
  24.8 0.1 fusion.3
  24.9 0.6 %collective-permute-start.8 = (bf16[256,128]{1,0:T(8,128)(2,1)S(1)}, bf16[256,128]{1,0:T(8,128)(2,1)S(1)}, u32[]{:S(2)}, u32[]{:S(2)}) collective-permute-start(bf16[256,128]{1,0:T(8,128)(2,1)S(1)} %get-tuple-element.52), channel_id=1, source_target_pairs={{0,8},{4,12},{8,0},{12,4},{16,24},{20,28},{24,16},{28,20},{1,9},{5... | collective-permute-start | bytes 196616 | tf_op jit(solution)/shard_map/ppermute | solution.py:434
  25.5 0.5 %collective-permute-start.7 = (bf16[256,128]{1,0:T(8,128)(2,1)S(1)}, bf16[256,128]{1,0:T(8,128)(2,1)S(1)}, u32[]{:S(2)}, u32[]{:S(2)}) collective-permute-start(bf16[256,128]{1,0:T(8,128)(2,1)S(1)} %get-tuple-element.53), channel_id=1, source_target_pairs={{0,16},{4,20},{8,24},{12,28},{16,0},{20,4},{24,8},{28,12},{1,17},{... | collective-permute-start | bytes 196616 | tf_op jit(solution)/shard_map/ppermute | solution.py:434
  26.0 1.8 %collective-permute-done.5.refs_0_ = bf16[256,128]{1,0:T(8,128)(2,1)S(1)} collective-permute-done((bf16[256,128]{1,0:T(8,128)(2,1)S(1)}, bf16[256,128]{1,0:T(8,128)(2,1)S(1)}, u32[]{:S(2)}, u32[]{:S(2)}) %collective-permute-start.5) | collective-permute-done | bytes 65568 | tf_op jit(solution)/shard_map/ppermute | solution.py:434
  27.8 1.4 %collective-permute-done.8.refs_2_ = bf16[256,128]{1,0:T(8,128)(2,1)S(1)} collective-permute-done((bf16[256,128]{1,0:T(8,128)(2,1)S(1)}, bf16[256,128]{1,0:T(8,128)(2,1)S(1)}, u32[]{:S(2)}, u32[]{:S(2)}) %collective-permute-start.8) | collective-permute-done | bytes 65568 | tf_op jit(solution)/shard_map/ppermute | solution.py:434
  29.2 0.5 %collective-permute-done.7.refs_1_ = bf16[256,128]{1,0:T(8,128)(2,1)S(1)} collective-permute-done((bf16[256,128]{1,0:T(8,128)(2,1)S(1)}, bf16[256,128]{1,0:T(8,128)(2,1)S(1)}, u32[]{:S(2)}, u32[]{:S(2)}) %collective-permute-start.7) | collective-permute-done | bytes 65568 | tf_op jit(solution)/shard_map/ppermute | solution.py:434
  29.8 0.0 copy-done.1
  29.8 0.5 downgoing.1
  30.2 1.6 %collective-permute-start.11 = (bf16[16,16,128]{2,1,0:T(8,128)(2,1)S(1)}, bf16[16,16,128]{2,1,0:T(8,128)(2,1)S(1)}, u32[]{:S(2)}, u32[]{:S(2)}) collective-permute-start(bf16[16,16,128]{2,1,0:T(8,128)(2,1)S(1)} %get-tuple-element.46.refs_0_), channel_id=1, source_target_pairs={{0,24},{4,28},{8,16},{12,20},{16,8},{20,12},{24,0},{28,4},{1,25},{... | collective-permute-start | bytes 196616 | tf_op jit(solution)/shard_map/ppermute | solution.py:434
  31.8 1.4 %collective-permute-start.10 = (bf16[16,16,128]{2,1,0:T(8,128)(2,1)S(1)}, bf16[16,16,128]{2,1,0:T(8,128)(2,1)S(1)}, u32[]{:S(2)}, u32[]{:S(2)}) collective-permute-start(bf16[16,16,128]{2,1,0:T(8,128)(2,1)S(1)} %get-tuple-element.46.refs_0_), channel_id=1, source_target_pairs={{0,16},{4,20},{8,24},{12,28},{16,0},{20,4},{24,8},{28,12},{1,17},{... | collective-permute-start | bytes 196616 | tf_op jit(solution)/shard_map/ppermute | solution.py:434
  33.2 0.5 %collective-permute-start.9 = (bf16[16,16,128]{2,1,0:T(8,128)(2,1)S(1)}, bf16[16,16,128]{2,1,0:T(8,128)(2,1)S(1)}, u32[]{:S(2)}, u32[]{:S(2)}) collective-permute-start(bf16[16,16,128]{2,1,0:T(8,128)(2,1)S(1)} %get-tuple-element.46.refs_0_), channel_id=1, source_target_pairs={{0,8},{4,12},{8,0},{12,4},{16,24},{20,28},{24,16},{28,20},{1,9},{5... | collective-permute-start | bytes 196616 | tf_op jit(solution)/shard_map/ppermute | solution.py:434
  33.8 0.0 collective-permute-start.12
  33.8 2.4 %collective-permute-done.11.refs_3_ = bf16[16,16,128]{2,1,0:T(8,128)(2,1)S(1)} collective-permute-done((bf16[16,16,128]{2,1,0:T(8,128)(2,1)S(1)}, bf16[16,16,128]{2,1,0:T(8,128)(2,1)S(1)}, u32[]{:S(2)}, u32[]{:S(2)}) %collective-permute-start.11) | collective-permute-done | bytes 65568 | tf_op jit(solution)/shard_map/ppermute | solution.py:434
  36.1 0.0 collective-permute-start.15
  36.2 0.3 collective-permute-done.10.refs_2_
  36.5 0.2 collective-permute-start.14
  36.7 0.8 %collective-permute-done.9.refs_1_ = bf16[16,16,128]{2,1,0:T(8,128)(2,1)S(1)} collective-permute-done((bf16[16,16,128]{2,1,0:T(8,128)(2,1)S(1)}, bf16[16,16,128]{2,1,0:T(8,128)(2,1)S(1)}, u32[]{:S(2)}, u32[]{:S(2)}) %collective-permute-start.9) | collective-permute-done | bytes 65568 | tf_op jit(solution)/shard_map/ppermute | solution.py:434
  37.5 0.0 collective-permute-start.13
  37.5 0.0 collective-permute-done.12.refs_4_
  37.5 0.0 collective-permute-done.15.refs_7_
  37.5 0.2 collective-permute-done.14.refs_6_
  37.7 1.0 %collective-permute-done.13.refs_5_ = bf16[16,16,128]{2,1,0:T(8,128)(2,1)S(1)} collective-permute-done((bf16[16,16,128]{2,1,0:T(8,128)(2,1)S(1)}, bf16[16,16,128]{2,1,0:T(8,128)(2,1)S(1)}, u32[]{:S(2)}, u32[]{:S(2)}) %collective-permute-start.13) | collective-permute-done | bytes 65568 | tf_op jit(solution)/shard_map/ppermute | solution.py:434
  38.8 0.0 copy-done.4
  38.8 1.3 %second.1 = (bf16[128,128]{1,0:T(8,128)(2,1)S(1)}, bf16[128,128]{1,0:T(8,128)(2,1)S(1)}, bf16[128,128]{1,0:T(8,128)(2,1)S(1)}, bf16[128,128]{1,0:T(8,128)(2,1)S(1)}) custom-call(bf16[16,16,128]{2,1,0:T(8,128)(2,1)S(1)} %get-tuple-element.46.refs_0_, bf16[16,16,128]{2,1,0:T(8,128)(2,1)S(1)} %collective-permute-done.9.refs_1_, ...), custom_call_target="tpu_custom_call" | custom-call | flops 1000000000 | bytes 1048576 | tf_op jit(solution)/shard_map/second/pallas_call | solution.py:554
  40.0 2.0 %collective-permute-start.16 = (bf16[128,128]{1,0:T(8,128)(2,1)S(1)}, bf16[128,128]{1,0:T(8,128)(2,1)S(1)}, u32[]{:S(2)}, u32[]{:S(2)}) collective-permute-start(bf16[128,128]{1,0:T(8,128)(2,1)S(1)} %get-tuple-element.47), channel_id=1, source_target_pairs={{0,3},{1,2},{2,1},{3,0},{4,7},{5,6},{6,5},{7,4},{8,11},{9,10},{10,... | collective-permute-start | bytes 98312 | tf_op jit(solution)/shard_map/ppermute | solution.py:434
  42.0 0.0 collective-permute-start.17
  42.0 2.5 %collective-permute-start.18 = (bf16[128,128]{1,0:T(8,128)(2,1)S(1)}, bf16[128,128]{1,0:T(8,128)(2,1)S(1)}, u32[]{:S(2)}, u32[]{:S(2)}) collective-permute-start(bf16[128,128]{1,0:T(8,128)(2,1)S(1)} %get-tuple-element.49), channel_id=1, source_target_pairs={{0,1},{1,0},{2,3},{3,2},{4,5},{5,4},{6,7},{7,6},{8,9},{9,8},{10,11... | collective-permute-start | bytes 98312 | tf_op jit(solution)/shard_map/ppermute | solution.py:434
  44.5 0.6 %emit.2 = f32[2,32,256]{2,1,0:T(8,128)} custom-call(f32[2,32,256]{2,1,0:T(8,128)S(1)} %get-tuple-element.40.field_ref), custom_call_target="tpu_custom_call" | custom-call | flops 300000000 | bytes 1048576 | tf_op jit(solution)/shard_map/emit/pallas_call | solution.py:427
  45.1 0.7 %emit.3 = f32[1,128,256]{2,1,0:T(8,128)} custom-call(f32[1,128,256]{2,1,0:T(8,128)S(1)} %get-tuple-element.45.field_ref), custom_call_target="tpu_custom_call" | custom-call | flops 300000000 | bytes 1048576 | tf_op jit(solution)/shard_map/emit/pallas_call | solution.py:427
  45.8 0.2 collective-permute-done.16.refs_0_
  45.9 1.0 %collective-permute-done.17.refs_1_ = bf16[128,128]{1,0:T(8,128)(2,1)S(1)} collective-permute-done((bf16[128,128]{1,0:T(8,128)(2,1)S(1)}, bf16[128,128]{1,0:T(8,128)(2,1)S(1)}, u32[]{:S(2)}, u32[]{:S(2)}) %collective-permute-start.17) | collective-permute-done | bytes 32800 | tf_op jit(solution)/shard_map/ppermute | solution.py:434
  47.0 0.0 collective-permute-done.18.refs_2_
  47.0 0.9 %final.1 = f32[2,32,256]{2,1,0:T(8,128)} custom-call(bf16[128,128]{1,0:T(8,128)(2,1)S(1)} %collective-permute-done.16.refs_0_, bf16[128,128]{1,0:T(8,128)(2,1)S(1)} %collective-permute-done.17.refs_1_, bf16[128,128]{1,0:T(8,128)(2,1)S(1)} %collective-permute-done.18.refs_2_, bf16[128,128]{1,0:T(8,128)(2,1)S(1)} %get-tuple-element.50.refs_3_, ...), custom_call_target="tpu_custom_call" | custom-call | flops 1000000000 | bytes 1048576 | tf_op jit(solution)/shard_map/final/pallas_call | solution.py:568
  (3 shorter events, 0.1 us)
Async XLA Ops:
  0.6 6.7 %copy-start = (bf16[32,128,256]{2,1,0:T(8,128)(2,1)S(1)}, bf16[32,128,256]{2,1,0:T(8,128)(2,1)}, u32[]{:S(2)}) copy-start(bf16[32,128,256]{2,1,0:T(8,128)(2,1)} %traces_ref.1) | copy-start | bytes 6291460
  4.3 5.4 %collective-permute-start.2 = (bf16[272,128]{1,0:T(8,128)(2,1)S(1)}, bf16[272,128]{1,0:T(8,128)(2,1)S(1)}, u32[]{:S(2)}, u32[]{:S(2)}) collective-permute-start(bf16[272,128]{1,0:T(8,128)(2,1)S(1)} %get-tuple-element.35), channel_id=1, source_target_pairs={{0,1},{1,0},{2,3},{3,2},{4,5},{5,4},{6,7},{7,6},{8,9},{9,8},{10,11... | collective-permute-start | bytes 208904 | tf_op jit(solution)/shard_map/ppermute | solution.py:434
  7.3 8.9 %copy-start.2 = (bf16[2,4,128,256]{3,2,1,0:T(8,128)(2,1)S(1)}, bf16[2,4,128,256]{3,2,1,0:T(8,128)(2,1)}, u32[]{:S(2)}) copy-start(bf16[2,4,128,256]{3,2,1,0:T(8,128)(2,1)} %constant.23.spread_ref) | copy-start | bytes 1572868
  7.3 8.9 %copy-start.3 = (bf16[256,256]{1,0:T(8,128)(2,1)S(1)}, bf16[256,256]{1,0:T(8,128)(2,1)}, u32[]{:S(2)}) copy-start(bf16[256,256]{1,0:T(8,128)(2,1)} %constant.22.inverse_ref.refs_7_.refs_5_) | copy-start | bytes 393220
  9.1 4.8 %collective-permute-start = (bf16[272,128]{1,0:T(8,128)(2,1)S(1)}, bf16[272,128]{1,0:T(8,128)(2,1)S(1)}, u32[]{:S(2)}, u32[]{:S(2)}) collective-permute-start(bf16[272,128]{1,0:T(8,128)(2,1)S(1)} %get-tuple-element.34), channel_id=1, source_target_pairs={{0,1},{1,0},{2,3},{3,2},{4,5},{5,4},{6,7},{7,6},{8,9},{9,8},{10,11... | collective-permute-start | bytes 208904 | tf_op jit(solution)/shard_map/ppermute | solution.py:434
  9.6 6.6 %collective-permute-start.3 = (bf16[272,128]{1,0:T(8,128)(2,1)S(1)}, bf16[272,128]{1,0:T(8,128)(2,1)S(1)}, u32[]{:S(2)}, u32[]{:S(2)}) collective-permute-start(bf16[272,128]{1,0:T(8,128)(2,1)S(1)} %add_convert_fusion.mine_ref), channel_id=1, source_target_pairs={{0,2},{1,3},{2,0},{3,1},{4,6},{5,7},{6,4},{7,5},{8,10},{9,11},{10,... | collective-permute-start | bytes 208904 | tf_op jit(solution)/shard_map/ppermute | solution.py:434
  14.0 5.8 %collective-permute-start.1 = (bf16[272,128]{1,0:T(8,128)(2,1)S(1)}, bf16[272,128]{1,0:T(8,128)(2,1)S(1)}, u32[]{:S(2)}, u32[]{:S(2)}) collective-permute-start(bf16[272,128]{1,0:T(8,128)(2,1)S(1)} %add_convert_fusion.1.mine_ref), channel_id=1, source_target_pairs={{0,2},{1,3},{2,0},{3,1},{4,6},{5,7},{6,4},{7,5},{8,10},{9,11},{10,... | collective-permute-start | bytes 208904 | tf_op jit(solution)/shard_map/ppermute | solution.py:434
  19.8 9.9 %copy-start.1 = (s32[1,128]{1,0:T(1,128)S(1)}, s32[1,128]{1,0:T(1,128)}, u32[]{:S(2)}) copy-start(s32[1,128]{1,0:T(1,128)} %refs_5_.1) | copy-start | bytes 1540
  21.0 1.3 %collective-permute-start.4 = (bf16[256,128]{1,0:T(8,128)(2,1)S(1)}, bf16[256,128]{1,0:T(8,128)(2,1)S(1)}, u32[]{:S(2)}, u32[]{:S(2)}) collective-permute-start(bf16[256,128]{1,0:T(8,128)(2,1)S(1)} %get-tuple-element.42), channel_id=1, source_target_pairs={{0,4},{4,0},{8,12},{12,8},{16,20},{20,16},{24,28},{28,24},{1,5},{5... | collective-permute-start | bytes 196616 | tf_op jit(solution)/shard_map/ppermute | solution.py:434
  21.0 3.8 %collective-permute-start.6 = (bf16[3,256,128]{2,1,0:T(8,128)(2,1)S(1)}, bf16[3,256,128]{2,1,0:T(8,128)(2,1)S(1)}, u32[]{:S(2)}, u32[]{:S(2)}) collective-permute-start(bf16[3,256,128]{2,1,0:T(8,128)(2,1)S(1)} %get-tuple-element.43), channel_id=1, source_target_pairs={{0,4},{4,0},{8,12},{12,8},{16,20},{20,16},{24,28},{28,24},{1,5},{5... | collective-permute-start | bytes 589832 | tf_op jit(solution)/shard_map/ppermute | solution.py:434
  22.3 16.5 %copy-start.4 = (bf16[256,128]{1,0:T(8,128)(2,1)S(1)}, bf16[256,128]{1,0:T(8,128)(2,1)}, u32[]{:S(2)}) copy-start(bf16[256,128]{1,0:T(8,128)(2,1)} %constant.24.refs_10_) | copy-start | bytes 196612
  22.3 5.5 %collective-permute-start.5 = (bf16[256,128]{1,0:T(8,128)(2,1)S(1)}, bf16[256,128]{1,0:T(8,128)(2,1)S(1)}, u32[]{:S(2)}, u32[]{:S(2)}) collective-permute-start(bf16[256,128]{1,0:T(8,128)(2,1)S(1)} %fusion), channel_id=1, source_target_pairs={{0,24},{4,28},{8,16},{12,20},{16,8},{20,12},{24,0},{28,4},{1,25},{... | collective-permute-start | bytes 196616 | tf_op jit(solution)/shard_map/ppermute | solution.py:434
  24.9 4.3 %collective-permute-start.8 = (bf16[256,128]{1,0:T(8,128)(2,1)S(1)}, bf16[256,128]{1,0:T(8,128)(2,1)S(1)}, u32[]{:S(2)}, u32[]{:S(2)}) collective-permute-start(bf16[256,128]{1,0:T(8,128)(2,1)S(1)} %get-tuple-element.52), channel_id=1, source_target_pairs={{0,8},{4,12},{8,0},{12,4},{16,24},{20,28},{24,16},{28,20},{1,9},{5... | collective-permute-start | bytes 196616 | tf_op jit(solution)/shard_map/ppermute | solution.py:434
  25.5 4.3 %collective-permute-start.7 = (bf16[256,128]{1,0:T(8,128)(2,1)S(1)}, bf16[256,128]{1,0:T(8,128)(2,1)S(1)}, u32[]{:S(2)}, u32[]{:S(2)}) collective-permute-start(bf16[256,128]{1,0:T(8,128)(2,1)S(1)} %get-tuple-element.53), channel_id=1, source_target_pairs={{0,16},{4,20},{8,24},{12,28},{16,0},{20,4},{24,8},{28,12},{1,17},{... | collective-permute-start | bytes 196616 | tf_op jit(solution)/shard_map/ppermute | solution.py:434
  30.2 5.9 %collective-permute-start.11 = (bf16[16,16,128]{2,1,0:T(8,128)(2,1)S(1)}, bf16[16,16,128]{2,1,0:T(8,128)(2,1)S(1)}, u32[]{:S(2)}, u32[]{:S(2)}) collective-permute-start(bf16[16,16,128]{2,1,0:T(8,128)(2,1)S(1)} %get-tuple-element.46.refs_0_), channel_id=1, source_target_pairs={{0,24},{4,28},{8,16},{12,20},{16,8},{20,12},{24,0},{28,4},{1,25},{... | collective-permute-start | bytes 196616 | tf_op jit(solution)/shard_map/ppermute | solution.py:434
  31.8 4.7 %collective-permute-start.10 = (bf16[16,16,128]{2,1,0:T(8,128)(2,1)S(1)}, bf16[16,16,128]{2,1,0:T(8,128)(2,1)S(1)}, u32[]{:S(2)}, u32[]{:S(2)}) collective-permute-start(bf16[16,16,128]{2,1,0:T(8,128)(2,1)S(1)} %get-tuple-element.46.refs_0_), channel_id=1, source_target_pairs={{0,16},{4,20},{8,24},{12,28},{16,0},{20,4},{24,8},{28,12},{1,17},{... | collective-permute-start | bytes 196616 | tf_op jit(solution)/shard_map/ppermute | solution.py:434
  33.2 4.3 %collective-permute-start.9 = (bf16[16,16,128]{2,1,0:T(8,128)(2,1)S(1)}, bf16[16,16,128]{2,1,0:T(8,128)(2,1)S(1)}, u32[]{:S(2)}, u32[]{:S(2)}) collective-permute-start(bf16[16,16,128]{2,1,0:T(8,128)(2,1)S(1)} %get-tuple-element.46.refs_0_), channel_id=1, source_target_pairs={{0,8},{4,12},{8,0},{12,4},{16,24},{20,28},{24,16},{28,20},{1,9},{5... | collective-permute-start | bytes 196616 | tf_op jit(solution)/shard_map/ppermute | solution.py:434
  33.8 3.7 %collective-permute-start.12 = (bf16[16,16,128]{2,1,0:T(8,128)(2,1)S(1)}, bf16[16,16,128]{2,1,0:T(8,128)(2,1)S(1)}, u32[]{:S(2)}, u32[]{:S(2)}) collective-permute-start(bf16[16,16,128]{2,1,0:T(8,128)(2,1)S(1)} %get-tuple-element.46.refs_0_), channel_id=1, source_target_pairs={{0,4},{4,0},{8,12},{12,8},{16,20},{20,16},{24,28},{28,24},{1,5},{5... | collective-permute-start | bytes 196616 | tf_op jit(solution)/shard_map/ppermute | solution.py:434
  36.1 1.4 %collective-permute-start.15 = (bf16[16,16,128]{2,1,0:T(8,128)(2,1)S(1)}, bf16[16,16,128]{2,1,0:T(8,128)(2,1)S(1)}, u32[]{:S(2)}, u32[]{:S(2)}) collective-permute-start(bf16[16,16,128]{2,1,0:T(8,128)(2,1)S(1)} %collective-permute-done.11.refs_3_), channel_id=1, source_target_pairs={{0,4},{4,0},{8,12},{12,8},{16,20},{20,16},{24,28},{28,24},{1,5},{5... | collective-permute-start | bytes 196616 | tf_op jit(solution)/shard_map/ppermute | solution.py:434
  36.5 1.3 %collective-permute-start.14 = (bf16[16,16,128]{2,1,0:T(8,128)(2,1)S(1)}, bf16[16,16,128]{2,1,0:T(8,128)(2,1)S(1)}, u32[]{:S(2)}, u32[]{:S(2)}) collective-permute-start(bf16[16,16,128]{2,1,0:T(8,128)(2,1)S(1)} %collective-permute-done.10.refs_2_), channel_id=1, source_target_pairs={{0,4},{4,0},{8,12},{12,8},{16,20},{20,16},{24,28},{28,24},{1,5},{5... | collective-permute-start | bytes 196616 | tf_op jit(solution)/shard_map/ppermute | solution.py:434
  37.5 1.3 %collective-permute-start.13 = (bf16[16,16,128]{2,1,0:T(8,128)(2,1)S(1)}, bf16[16,16,128]{2,1,0:T(8,128)(2,1)S(1)}, u32[]{:S(2)}, u32[]{:S(2)}) collective-permute-start(bf16[16,16,128]{2,1,0:T(8,128)(2,1)S(1)} %collective-permute-done.9.refs_1_), channel_id=1, source_target_pairs={{0,4},{4,0},{8,12},{12,8},{16,20},{20,16},{24,28},{28,24},{1,5},{5... | collective-permute-start | bytes 196616 | tf_op jit(solution)/shard_map/ppermute | solution.py:434
  40.0 5.9 %collective-permute-start.16 = (bf16[128,128]{1,0:T(8,128)(2,1)S(1)}, bf16[128,128]{1,0:T(8,128)(2,1)S(1)}, u32[]{:S(2)}, u32[]{:S(2)}) collective-permute-start(bf16[128,128]{1,0:T(8,128)(2,1)S(1)} %get-tuple-element.47), channel_id=1, source_target_pairs={{0,3},{1,2},{2,1},{3,0},{4,7},{5,6},{6,5},{7,4},{8,11},{9,10},{10,... | collective-permute-start | bytes 98312 | tf_op jit(solution)/shard_map/ppermute | solution.py:434
  42.0 5.0 %collective-permute-start.17 = (bf16[128,128]{1,0:T(8,128)(2,1)S(1)}, bf16[128,128]{1,0:T(8,128)(2,1)S(1)}, u32[]{:S(2)}, u32[]{:S(2)}) collective-permute-start(bf16[128,128]{1,0:T(8,128)(2,1)S(1)} %get-tuple-element.48), channel_id=1, source_target_pairs={{0,2},{1,3},{2,0},{3,1},{4,6},{5,7},{6,4},{7,5},{8,10},{9,11},{10,... | collective-permute-start | bytes 98312 | tf_op jit(solution)/shard_map/ppermute | solution.py:434
  42.0 5.0 %collective-permute-start.18 = (bf16[128,128]{1,0:T(8,128)(2,1)S(1)}, bf16[128,128]{1,0:T(8,128)(2,1)S(1)}, u32[]{:S(2)}, u32[]{:S(2)}) collective-permute-start(bf16[128,128]{1,0:T(8,128)(2,1)S(1)} %get-tuple-element.49), channel_id=1, source_target_pairs={{0,1},{1,0},{2,3},{3,2},{4,5},{5,4},{6,7},{7,6},{8,9},{9,8},{10,11... | collective-permute-start | bytes 98312 | tf_op jit(solution)/shard_map/ppermute | solution.py:434

commit v8 on v7

--- a/solution.py
+++ b/solution.py
@@ -191,8 +191,13 @@
     own = jnp.broadcast_to(own, (2 * GROUP, LANES))
     row = lax.broadcasted_iota(jnp.int32, own.shape, 0)
     lane = lax.broadcasted_iota(jnp.int32, own.shape, 1)
-    here = (row == rcv_index // turns) & (lane // (2 * half) == rcv_index % turns)
-    sum_ref[sets * NF :, :] = jnp.where(here, own, 0.0).astype(BF16)
+    spare = (row == 0) & (lane >= LANES // 2)
+    for one in range(sets):
+        block = turns // 2 + (rcv_index - one * (turns // 2))
+        here = (rcv_index // (turns // 2) == one) & (lane // (2 * half) == block)
+        rows = slice(one * NF, one * NF + 2 * GROUP)
+        value = sum_ref[rows, :].astype(F32)
+        sum_ref[rows, :] = jnp.where(spare, jnp.where(here, own, 0.0), value).astype(BF16)
 
 
 def first_kernel(
@@ -222,10 +227,11 @@
     ]
     for copy in small[:3] + large + small[3:]:
         copy.start()
-    for copy in small[:3] + large[:1]:
+    for copy in small[:3]:
         copy.wait()
     make_delays(0, half, forward_ref, deconv_ref, taps_ref, gain, delay_ref)
     forward = forward_ref[...]
+    large[0].wait()
     for place in range(fields):
         spectra = mm(forward, focal_ref[place], NT_DIMS)
         store_vector(vector_ref, place, spectra[:NF], spectra[NF:])
@@ -276,16 +282,15 @@
     width = vector_ref.shape[-1]
     half = width // GROUP
     blocks = LANES // half
-    sets = (mine_ref.shape[0] - 2 * GROUP) // NF
+    sets = mine_ref.shape[0] // NF
     turns = blocks // 2
-    onsets = mine_ref[sets * NF :, :].astype(F32) + other_ref[sets * NF :, :].astype(F32)
     owned = jnp.zeros((NT, LANES), F32)
     diagonal = same_bin(2 * NF, 2 * width)
     for couple in range(sets // 2):
         rows = slice(2 * couple * NF, 2 * (couple + 1) * NF)
         total = mine_ref[rows, :].astype(F32) + other_ref[rows, :].astype(F32)
-        spectra = split_halves(total[:NF], total[NF:]).astype(BF16)
-        signal = mute(mm(inverse, spectra), onsets[couple : couple + 1, :])
+        spectra = split_halves(total[:NF], total[NF:])
+        signal = mute(mm(inverse, spectra.astype(BF16)), spectra[NF : NF + 1, :])
         owned = jnp.where(rcv_index // turns == couple, signal, owned)
         echo = mm(forward, signal.astype(BF16)).astype(BF16)
         for pair in range(blocks // 2):
@@ -453,10 +458,10 @@
     sets = focal_total // (LANES // half // 2)
     vector = shape((NG, focal_total, 2 * GROUP, 2 * receivers), BF16)
     half_matrix = shape((NG, half // 2, 2 * GROUP, 2 * receivers), BF16)
-    half_sums = shape((sets * NF + 2 * GROUP, LANES), BF16)
+    half_sums = shape((sets * NF, LANES), BF16)
     half_kept = pltpu.VMEM((NG * focal_total * 2 * GROUP, half * GROUP), BF16)
     half_delays = pltpu.VMEM((half // 2, 2 * NF, LANES), BF16)
-    assert sets % 2 == 0 and rcv_count <= 2 * GROUP * (LANES // half // 2)
+    assert sets % 2 == 0 and half * 8 == LANES
 
     def buffer(value):
         return pltpu.VMEM(value.shape, value.dtype)

time: 48.1 us -> 47.7 us (level)
  no operation moved by 1% of the time
where the time goes in v8:
time: 47.7 us; the launch traced here: 47.6 us
  starting transfers between devices  20.9 us (44%)
  waiting for transfers between devices  14.7 us (31%)
  Pallas kernels  11 us (23%)
  between operations  0.75 us (2%)
    ppermute x19, starting transfers between devices, exchange(): lax.ppermute(value, axis, [(place, place ^ distance) for place in range(c...  20.9 us
    ppermute x19, waiting for transfers between devices, exchange(): lax.ppermute(value, axis, [(place, place ^ distance) for place in range(c...  14.7 us
    pallas_call x1, Pallas kernels, body(): call(functools.partial(first_kernel, gain), 'first', [half_matrix, half_s...  3.54 us
    pallas_call x1, Pallas kernels, body(): call(functools.partial(rest_kernel, gain), 'rest', (half_matrix, half_sum...  1.75 us
    pallas_call x2, Pallas kernels, emit(): call(emit_kernel, 'emit', jax.ShapeDtypeStruct(field.shape, field.dtype),...  1.3 us
    pallas_call x1, Pallas kernels, body(): call(functools.partial(second_kernel, pairs), 'second', [shape((NF, LANES...  1.24 us
    pallas_call x1, Pallas kernels, body(): call(adjoint_kernel, 'adjoint', [shape((pairs, 2 * NF, receivers), BF16),...  1.13 us
  transfers between devices with their start and end apart: 19, of which 14 were waited for; matrix products, arithmetic and copies ran while one was open for 0% of the time, Pallas kernels for 8%

profile of v8, /device:TPU:0, one launch (start us, length us, event | category | flops | bytes accessed | tf_op | source)
XLA Modules:
  0.0 47.6 jit_solution(14845945614270461283)
XLA Ops:
  0.6 0.0 copy-start
  0.6 3.5 %first.1 = (bf16[16,8,16,256]{3,2,1,0:T(8,128)(2,1)S(1)}, bf16[256,128]{1,0:T(8,128)(2,1)S(1)}, bf16[128,256]{1,0:T(8,128)(2,1)S(1)}, bf16[16,8,16,256]{3,2,1,0:...) custom-call(bf16[32,128,256]{2,1,0:T(8,128)(2,1)} %traces_ref.1, ...), custom_call_target="tpu_custom_call" | custom-call | flops 4000000000 | bytes 1048576 | tf_op jit(solution)/shard_map/first/pallas_call | solution.py:474
  4.2 3.1 %collective-permute-start.2 = (bf16[256,128]{1,0:T(8,128)(2,1)S(1)}, bf16[256,128]{1,0:T(8,128)(2,1)S(1)}, u32[]{:S(2)}, u32[]{:S(2)}) collective-permute-start(bf16[256,128]{1,0:T(8,128)(2,1)S(1)} %get-tuple-element.35), channel_id=1, source_target_pairs={{0,1},{1,0},{2,3},{3,2},{4,5},{5,4},{6,7},{7,6},{8,9},{9,8},{10,11... | collective-permute-start | bytes 196616 | tf_op jit(solution)/shard_map/ppermute | solution.py:439
  7.3 0.0 copy-done
  7.3 0.0 copy-start.2
  7.3 0.0 copy-start.3
  7.3 1.8 %rest.1 = (bf16[16,8,16,256]{3,2,1,0:T(8,128)(2,1)S(1)}, bf16[256,128]{1,0:T(8,128)(2,1)S(1)}) custom-call(bf16[32,128,256]{2,1,0:T(8,128)(2,1)S(1)} %copy-done, s32[32,128]{1,0:T(8,128)S(1)} %get-tuple-element.27.shift_ref, f32[32,64]{1,0:T(8,128)S(1)} %get-tuple-element.28.deconv_ref, s32[2,32]{1,0:T(2,128)S(1)} %get-tuple-element.29.onset_ref.refs_4_, ...), custom_call_target="tpu_custom_call" | custom-call | flops 3000000000 | bytes 1048576 | tf_op jit(solution)/shard_map/rest/pallas_call | solution.py:496
  9.0 0.1 collective-permute-start
  9.2 0.4 collective-permute-done.2
  9.6 3.1 %collective-permute-start.3 = (bf16[256,128]{1,0:T(8,128)(2,1)S(1)}, bf16[256,128]{1,0:T(8,128)(2,1)S(1)}, u32[]{:S(2)}, u32[]{:S(2)}) collective-permute-start(bf16[256,128]{1,0:T(8,128)(2,1)S(1)} %add_convert_fusion.3.mine_ref), channel_id=1, source_target_pairs={{0,2},{1,3},{2,0},{3,1},{4,6},{5,7},{6,4},{7,5},{8,10},{9,11},{10,... | collective-permute-start | bytes 196616 | tf_op jit(solution)/shard_map/ppermute | solution.py:439
  12.7 1.1 %collective-permute-done = bf16[256,128]{1,0:T(8,128)(2,1)S(1)} collective-permute-done((bf16[256,128]{1,0:T(8,128)(2,1)S(1)}, bf16[256,128]{1,0:T(8,128)(2,1)S(1)}, u32[]{:S(2)}, u32[]{:S(2)}) %collective-permute-start) | collective-permute-done | bytes 65568 | tf_op jit(solution)/shard_map/ppermute | solution.py:439
  13.8 2.3 %collective-permute-start.1 = (bf16[256,128]{1,0:T(8,128)(2,1)S(1)}, bf16[256,128]{1,0:T(8,128)(2,1)S(1)}, u32[]{:S(2)}, u32[]{:S(2)}) collective-permute-start(bf16[256,128]{1,0:T(8,128)(2,1)S(1)} %add_convert_fusion.4.mine_ref), channel_id=1, source_target_pairs={{0,2},{1,3},{2,0},{3,1},{4,6},{5,7},{6,4},{7,5},{8,10},{9,11},{10,... | collective-permute-start | bytes 196616 | tf_op jit(solution)/shard_map/ppermute | solution.py:439
  16.0 0.0 collective-permute-done.3.other_ref
  16.0 0.0 copy-done.2
  16.1 0.0 copy-done.3
  16.1 0.7 %mute.1 = (bf16[16,2,4,16,128]{4,3,2,1,0:T(8,128)(2,1)S(1)}, f32[2,16,256]{2,1,0:T(8,128)S(1)}) custom-call(bf16[256,128]{1,0:T(8,128)(2,1)S(1)} %add_convert_fusion.3.mine_ref, bf16[256,128]{1,0:T(8,128)(2,1)S(1)} %collective-permute-done.3.other_ref, bf16[256,256]{1,0:T(8,128)(2,1)S(1)} %get-tuple-element.30.forward_ref.refs_6_, ...), custom_call_target="tpu_custom_call" | custom-call | flops 1000000000 | bytes 1048576 | tf_op jit(solution)/shard_map/mute/pallas_call | solution.py:515
  16.7 2.9 %collective-permute-done.1.other_ref = bf16[256,128]{1,0:T(8,128)(2,1)S(1)} collective-permute-done((bf16[256,128]{1,0:T(8,128)(2,1)S(1)}, bf16[256,128]{1,0:T(8,128)(2,1)S(1)}, u32[]{:S(2)}, u32[]{:S(2)}) %collective-permute-start.1) | collective-permute-done | bytes 65568 | tf_op jit(solution)/shard_map/ppermute | solution.py:439
  19.6 0.0 copy-start.1
  19.6 1.1 %adjoint.1 = (bf16[4,256,128]{2,1,0:T(8,128)(2,1)S(1)}, bf16[256,128]{1,0:T(8,128)(2,1)S(1)}, bf16[3,256,128]{2,1,0:T(8,128)(2,1)S(1)}, f32[2,32,256]{2,1,0:T(8,128)S(1)}) custom-call(bf16[256,128]{1,0:T(8,128)(2,1)S(1)} %add_convert_fusion.4.mine_ref, bf16[256,128]{1,0:T(8,128)(2,1)S(1)} %collective-permute-done.1.other_ref, ...), custom_call_target="tpu_custom_call" | custom-call | flops 2000000000 | bytes 1048576 | tf_op jit(solution)/shard_map/adjoint/pallas_call | solution.py:523
  20.8 0.1 collective-permute-start.4
  20.8 0.5 %collective-permute-start.6 = (bf16[3,256,128]{2,1,0:T(8,128)(2,1)S(1)}, bf16[3,256,128]{2,1,0:T(8,128)(2,1)S(1)}, u32[]{:S(2)}, u32[]{:S(2)}) collective-permute-start(bf16[3,256,128]{2,1,0:T(8,128)(2,1)S(1)} %get-tuple-element.43), channel_id=1, source_target_pairs={{0,4},{4,0},{8,12},{12,8},{16,20},{20,16},{24,28},{28,24},{1,5},{5... | collective-permute-start | bytes 589832 | tf_op jit(solution)/shard_map/ppermute | solution.py:439
  21.3 0.7 %collective-permute-done.4 = bf16[256,128]{1,0:T(8,128)(2,1)S(1)} collective-permute-done((bf16[256,128]{1,0:T(8,128)(2,1)S(1)}, bf16[256,128]{1,0:T(8,128)(2,1)S(1)}, u32[]{:S(2)}, u32[]{:S(2)}) %collective-permute-start.4) | collective-permute-done | bytes 65568 | tf_op jit(solution)/shard_map/ppermute | solution.py:439
  22.1 0.0 copy-start.4
  22.1 2.5 %collective-permute-start.5 = (bf16[256,128]{1,0:T(8,128)(2,1)S(1)}, bf16[256,128]{1,0:T(8,128)(2,1)S(1)}, u32[]{:S(2)}, u32[]{:S(2)}) collective-permute-start(bf16[256,128]{1,0:T(8,128)(2,1)S(1)} %fusion), channel_id=1, source_target_pairs={{0,24},{4,28},{8,16},{12,20},{16,8},{20,12},{24,0},{28,4},{1,25},{... | collective-permute-start | bytes 196616 | tf_op jit(solution)/shard_map/ppermute | solution.py:439
  24.6 0.0 collective-permute-done.6
  24.6 0.1 fusion.3
  24.7 0.6 %collective-permute-start.8 = (bf16[256,128]{1,0:T(8,128)(2,1)S(1)}, bf16[256,128]{1,0:T(8,128)(2,1)S(1)}, u32[]{:S(2)}, u32[]{:S(2)}) collective-permute-start(bf16[256,128]{1,0:T(8,128)(2,1)S(1)} %get-tuple-element.52), channel_id=1, source_target_pairs={{0,8},{4,12},{8,0},{12,4},{16,24},{20,28},{24,16},{28,20},{1,9},{5... | collective-permute-start | bytes 196616 | tf_op jit(solution)/shard_map/ppermute | solution.py:439
  25.3 0.5 %collective-permute-start.7 = (bf16[256,128]{1,0:T(8,128)(2,1)S(1)}, bf16[256,128]{1,0:T(8,128)(2,1)S(1)}, u32[]{:S(2)}, u32[]{:S(2)}) collective-permute-start(bf16[256,128]{1,0:T(8,128)(2,1)S(1)} %get-tuple-element.53), channel_id=1, source_target_pairs={{0,16},{4,20},{8,24},{12,28},{16,0},{20,4},{24,8},{28,12},{1,17},{... | collective-permute-start | bytes 196616 | tf_op jit(solution)/shard_map/ppermute | solution.py:439
  25.8 1.8 %collective-permute-done.5.refs_0_ = bf16[256,128]{1,0:T(8,128)(2,1)S(1)} collective-permute-done((bf16[256,128]{1,0:T(8,128)(2,1)S(1)}, bf16[256,128]{1,0:T(8,128)(2,1)S(1)}, u32[]{:S(2)}, u32[]{:S(2)}) %collective-permute-start.5) | collective-permute-done | bytes 65568 | tf_op jit(solution)/shard_map/ppermute | solution.py:439
  27.6 1.4 %collective-permute-done.8.refs_2_ = bf16[256,128]{1,0:T(8,128)(2,1)S(1)} collective-permute-done((bf16[256,128]{1,0:T(8,128)(2,1)S(1)}, bf16[256,128]{1,0:T(8,128)(2,1)S(1)}, u32[]{:S(2)}, u32[]{:S(2)}) %collective-permute-start.8) | collective-permute-done | bytes 65568 | tf_op jit(solution)/shard_map/ppermute | solution.py:439
  29.0 0.5 %collective-permute-done.7.refs_1_ = bf16[256,128]{1,0:T(8,128)(2,1)S(1)} collective-permute-done((bf16[256,128]{1,0:T(8,128)(2,1)S(1)}, bf16[256,128]{1,0:T(8,128)(2,1)S(1)}, u32[]{:S(2)}, u32[]{:S(2)}) %collective-permute-start.7) | collective-permute-done | bytes 65568 | tf_op jit(solution)/shard_map/ppermute | solution.py:439
  29.6 0.0 copy-done.1
  29.6 0.5 downgoing.1
  30.0 1.6 %collective-permute-start.11 = (bf16[16,16,128]{2,1,0:T(8,128)(2,1)S(1)}, bf16[16,16,128]{2,1,0:T(8,128)(2,1)S(1)}, u32[]{:S(2)}, u32[]{:S(2)}) collective-permute-start(bf16[16,16,128]{2,1,0:T(8,128)(2,1)S(1)} %get-tuple-element.46.refs_0_), channel_id=1, source_target_pairs={{0,24},{4,28},{8,16},{12,20},{16,8},{20,12},{24,0},{28,4},{1,25},{... | collective-permute-start | bytes 196616 | tf_op jit(solution)/shard_map/ppermute | solution.py:439
  31.6 1.4 %collective-permute-start.10 = (bf16[16,16,128]{2,1,0:T(8,128)(2,1)S(1)}, bf16[16,16,128]{2,1,0:T(8,128)(2,1)S(1)}, u32[]{:S(2)}, u32[]{:S(2)}) collective-permute-start(bf16[16,16,128]{2,1,0:T(8,128)(2,1)S(1)} %get-tuple-element.46.refs_0_), channel_id=1, source_target_pairs={{0,16},{4,20},{8,24},{12,28},{16,0},{20,4},{24,8},{28,12},{1,17},{... | collective-permute-start | bytes 196616 | tf_op jit(solution)/shard_map/ppermute | solution.py:439
  33.0 0.5 %collective-permute-start.9 = (bf16[16,16,128]{2,1,0:T(8,128)(2,1)S(1)}, bf16[16,16,128]{2,1,0:T(8,128)(2,1)S(1)}, u32[]{:S(2)}, u32[]{:S(2)}) collective-permute-start(bf16[16,16,128]{2,1,0:T(8,128)(2,1)S(1)} %get-tuple-element.46.refs_0_), channel_id=1, source_target_pairs={{0,8},{4,12},{8,0},{12,4},{16,24},{20,28},{24,16},{28,20},{1,9},{5... | collective-permute-start | bytes 196616 | tf_op jit(solution)/shard_map/ppermute | solution.py:439
  33.6 0.0 collective-permute-start.12
  33.6 2.4 %collective-permute-done.11.refs_3_ = bf16[16,16,128]{2,1,0:T(8,128)(2,1)S(1)} collective-permute-done((bf16[16,16,128]{2,1,0:T(8,128)(2,1)S(1)}, bf16[16,16,128]{2,1,0:T(8,128)(2,1)S(1)}, u32[]{:S(2)}, u32[]{:S(2)}) %collective-permute-start.11) | collective-permute-done | bytes 65568 | tf_op jit(solution)/shard_map/ppermute | solution.py:439
  36.0 0.0 collective-permute-start.15
  36.0 0.3 collective-permute-done.10.refs_2_
  36.3 0.2 collective-permute-start.14
  36.5 0.8 %collective-permute-done.9.refs_1_ = bf16[16,16,128]{2,1,0:T(8,128)(2,1)S(1)} collective-permute-done((bf16[16,16,128]{2,1,0:T(8,128)(2,1)S(1)}, bf16[16,16,128]{2,1,0:T(8,128)(2,1)S(1)}, u32[]{:S(2)}, u32[]{:S(2)}) %collective-permute-start.9) | collective-permute-done | bytes 65568 | tf_op jit(solution)/shard_map/ppermute | solution.py:439
  37.3 0.0 collective-permute-start.13
  37.3 0.0 collective-permute-done.12.refs_4_
  37.3 0.0 collective-permute-done.15.refs_7_
  37.3 0.2 collective-permute-done.14.refs_6_
  37.5 1.0 %collective-permute-done.13.refs_5_ = bf16[16,16,128]{2,1,0:T(8,128)(2,1)S(1)} collective-permute-done((bf16[16,16,128]{2,1,0:T(8,128)(2,1)S(1)}, bf16[16,16,128]{2,1,0:T(8,128)(2,1)S(1)}, u32[]{:S(2)}, u32[]{:S(2)}) %collective-permute-start.13) | collective-permute-done | bytes 65568 | tf_op jit(solution)/shard_map/ppermute | solution.py:439
  38.6 0.0 copy-done.4
  38.6 1.2 %second.1 = (bf16[128,128]{1,0:T(8,128)(2,1)S(1)}, bf16[128,128]{1,0:T(8,128)(2,1)S(1)}, bf16[128,128]{1,0:T(8,128)(2,1)S(1)}, bf16[128,128]{1,0:T(8,128)(2,1)S(1)}) custom-call(bf16[16,16,128]{2,1,0:T(8,128)(2,1)S(1)} %get-tuple-element.46.refs_0_, bf16[16,16,128]{2,1,0:T(8,128)(2,1)S(1)} %collective-permute-done.9.refs_1_, ...), custom_call_target="tpu_custom_call" | custom-call | flops 1000000000 | bytes 1048576 | tf_op jit(solution)/shard_map/second/pallas_call | solution.py:559
  39.8 1.8 %collective-permute-start.16 = (bf16[128,128]{1,0:T(8,128)(2,1)S(1)}, bf16[128,128]{1,0:T(8,128)(2,1)S(1)}, u32[]{:S(2)}, u32[]{:S(2)}) collective-permute-start(bf16[128,128]{1,0:T(8,128)(2,1)S(1)} %get-tuple-element.47), channel_id=1, source_target_pairs={{0,3},{1,2},{2,1},{3,0},{4,7},{5,6},{6,5},{7,4},{8,11},{9,10},{10,... | collective-permute-start | bytes 98312 | tf_op jit(solution)/shard_map/ppermute | solution.py:439
  41.6 0.0 collective-permute-start.17
  41.6 2.6 %collective-permute-start.18 = (bf16[128,128]{1,0:T(8,128)(2,1)S(1)}, bf16[128,128]{1,0:T(8,128)(2,1)S(1)}, u32[]{:S(2)}, u32[]{:S(2)}) collective-permute-start(bf16[128,128]{1,0:T(8,128)(2,1)S(1)} %get-tuple-element.49), channel_id=1, source_target_pairs={{0,1},{1,0},{2,3},{3,2},{4,5},{5,4},{6,7},{7,6},{8,9},{9,8},{10,11... | collective-permute-start | bytes 98312 | tf_op jit(solution)/shard_map/ppermute | solution.py:439
  44.3 0.6 %emit.2 = f32[2,32,256]{2,1,0:T(8,128)} custom-call(f32[2,32,256]{2,1,0:T(8,128)S(1)} %get-tuple-element.40.field_ref), custom_call_target="tpu_custom_call" | custom-call | flops 300000000 | bytes 1048576 | tf_op jit(solution)/shard_map/emit/pallas_call | solution.py:432
  44.9 0.7 %emit.3 = f32[1,128,256]{2,1,0:T(8,128)} custom-call(f32[1,128,256]{2,1,0:T(8,128)S(1)} %get-tuple-element.45.field_ref), custom_call_target="tpu_custom_call" | custom-call | flops 300000000 | bytes 1048576 | tf_op jit(solution)/shard_map/emit/pallas_call | solution.py:432
  45.6 0.1 collective-permute-done.16.refs_0_
  45.6 1.0 %collective-permute-done.17.refs_1_ = bf16[128,128]{1,0:T(8,128)(2,1)S(1)} collective-permute-done((bf16[128,128]{1,0:T(8,128)(2,1)S(1)}, bf16[128,128]{1,0:T(8,128)(2,1)S(1)}, u32[]{:S(2)}, u32[]{:S(2)}) %collective-permute-start.17) | collective-permute-done | bytes 32800 | tf_op jit(solution)/shard_map/ppermute | solution.py:439
  46.6 0.0 collective-permute-done.18.refs_2_
  46.6 0.9 %final.1 = f32[2,32,256]{2,1,0:T(8,128)} custom-call(bf16[128,128]{1,0:T(8,128)(2,1)S(1)} %collective-permute-done.16.refs_0_, bf16[128,128]{1,0:T(8,128)(2,1)S(1)} %collective-permute-done.17.refs_1_, bf16[128,128]{1,0:T(8,128)(2,1)S(1)} %collective-permute-done.18.refs_2_, bf16[128,128]{1,0:T(8,128)(2,1)S(1)} %get-tuple-element.50.refs_3_, ...), custom_call_target="tpu_custom_call" | custom-call | flops 1000000000 | bytes 1048576 | tf_op jit(solution)/shard_map/final/pallas_call | solution.py:573
  (3 shorter events, 0.1 us)
Async XLA Ops:
  0.6 6.7 %copy-start = (bf16[32,128,256]{2,1,0:T(8,128)(2,1)S(1)}, bf16[32,128,256]{2,1,0:T(8,128)(2,1)}, u32[]{:S(2)}) copy-start(bf16[32,128,256]{2,1,0:T(8,128)(2,1)} %traces_ref.1) | copy-start | bytes 6291460
  4.2 5.3 %collective-permute-start.2 = (bf16[256,128]{1,0:T(8,128)(2,1)S(1)}, bf16[256,128]{1,0:T(8,128)(2,1)S(1)}, u32[]{:S(2)}, u32[]{:S(2)}) collective-permute-start(bf16[256,128]{1,0:T(8,128)(2,1)S(1)} %get-tuple-element.35), channel_id=1, source_target_pairs={{0,1},{1,0},{2,3},{3,2},{4,5},{5,4},{6,7},{7,6},{8,9},{9,8},{10,11... | collective-permute-start | bytes 196616 | tf_op jit(solution)/shard_map/ppermute | solution.py:439
  7.3 8.8 %copy-start.2 = (bf16[2,4,128,256]{3,2,1,0:T(8,128)(2,1)S(1)}, bf16[2,4,128,256]{3,2,1,0:T(8,128)(2,1)}, u32[]{:S(2)}) copy-start(bf16[2,4,128,256]{3,2,1,0:T(8,128)(2,1)} %constant.23.spread_ref) | copy-start | bytes 1572868
  7.3 8.8 %copy-start.3 = (bf16[256,256]{1,0:T(8,128)(2,1)S(1)}, bf16[256,256]{1,0:T(8,128)(2,1)}, u32[]{:S(2)}) copy-start(bf16[256,256]{1,0:T(8,128)(2,1)} %constant.22.inverse_ref.refs_7_.refs_5_) | copy-start | bytes 393220
  9.0 4.7 %collective-permute-start = (bf16[256,128]{1,0:T(8,128)(2,1)S(1)}, bf16[256,128]{1,0:T(8,128)(2,1)S(1)}, u32[]{:S(2)}, u32[]{:S(2)}) collective-permute-start(bf16[256,128]{1,0:T(8,128)(2,1)S(1)} %get-tuple-element.34), channel_id=1, source_target_pairs={{0,1},{1,0},{2,3},{3,2},{4,5},{5,4},{6,7},{7,6},{8,9},{9,8},{10,11... | collective-permute-start | bytes 196616 | tf_op jit(solution)/shard_map/ppermute | solution.py:439
  9.6 6.5 %collective-permute-start.3 = (bf16[256,128]{1,0:T(8,128)(2,1)S(1)}, bf16[256,128]{1,0:T(8,128)(2,1)S(1)}, u32[]{:S(2)}, u32[]{:S(2)}) collective-permute-start(bf16[256,128]{1,0:T(8,128)(2,1)S(1)} %add_convert_fusion.3.mine_ref), channel_id=1, source_target_pairs={{0,2},{1,3},{2,0},{3,1},{4,6},{5,7},{6,4},{7,5},{8,10},{9,11},{10,... | collective-permute-start | bytes 196616 | tf_op jit(solution)/shard_map/ppermute | solution.py:439
  13.8 5.8 %collective-permute-start.1 = (bf16[256,128]{1,0:T(8,128)(2,1)S(1)}, bf16[256,128]{1,0:T(8,128)(2,1)S(1)}, u32[]{:S(2)}, u32[]{:S(2)}) collective-permute-start(bf16[256,128]{1,0:T(8,128)(2,1)S(1)} %add_convert_fusion.4.mine_ref), channel_id=1, source_target_pairs={{0,2},{1,3},{2,0},{3,1},{4,6},{5,7},{6,4},{7,5},{8,10},{9,11},{10,... | collective-permute-start | bytes 196616 | tf_op jit(solution)/shard_map/ppermute | solution.py:439
  19.6 9.9 %copy-start.1 = (s32[1,128]{1,0:T(1,128)S(1)}, s32[1,128]{1,0:T(1,128)}, u32[]{:S(2)}) copy-start(s32[1,128]{1,0:T(1,128)} %refs_5_.1) | copy-start | bytes 1540
  20.8 1.3 %collective-permute-start.4 = (bf16[256,128]{1,0:T(8,128)(2,1)S(1)}, bf16[256,128]{1,0:T(8,128)(2,1)S(1)}, u32[]{:S(2)}, u32[]{:S(2)}) collective-permute-start(bf16[256,128]{1,0:T(8,128)(2,1)S(1)} %get-tuple-element.42), channel_id=1, source_target_pairs={{0,4},{4,0},{8,12},{12,8},{16,20},{20,16},{24,28},{28,24},{1,5},{5... | collective-permute-start | bytes 196616 | tf_op jit(solution)/shard_map/ppermute | solution.py:439
  20.8 3.8 %collective-permute-start.6 = (bf16[3,256,128]{2,1,0:T(8,128)(2,1)S(1)}, bf16[3,256,128]{2,1,0:T(8,128)(2,1)S(1)}, u32[]{:S(2)}, u32[]{:S(2)}) collective-permute-start(bf16[3,256,128]{2,1,0:T(8,128)(2,1)S(1)} %get-tuple-element.43), channel_id=1, source_target_pairs={{0,4},{4,0},{8,12},{12,8},{16,20},{20,16},{24,28},{28,24},{1,5},{5... | collective-permute-start | bytes 589832 | tf_op jit(solution)/shard_map/ppermute | solution.py:439
  22.1 16.5 %copy-start.4 = (bf16[256,128]{1,0:T(8,128)(2,1)S(1)}, bf16[256,128]{1,0:T(8,128)(2,1)}, u32[]{:S(2)}) copy-start(bf16[256,128]{1,0:T(8,128)(2,1)} %constant.24.refs_10_) | copy-start | bytes 196612
  22.1 5.5 %collective-permute-start.5 = (bf16[256,128]{1,0:T(8,128)(2,1)S(1)}, bf16[256,128]{1,0:T(8,128)(2,1)S(1)}, u32[]{:S(2)}, u32[]{:S(2)}) collective-permute-start(bf16[256,128]{1,0:T(8,128)(2,1)S(1)} %fusion), channel_id=1, source_target_pairs={{0,24},{4,28},{8,16},{12,20},{16,8},{20,12},{24,0},{28,4},{1,25},{... | collective-permute-start | bytes 196616 | tf_op jit(solution)/shard_map/ppermute | solution.py:439
  24.7 4.3 %collective-permute-start.8 = (bf16[256,128]{1,0:T(8,128)(2,1)S(1)}, bf16[256,128]{1,0:T(8,128)(2,1)S(1)}, u32[]{:S(2)}, u32[]{:S(2)}) collective-permute-start(bf16[256,128]{1,0:T(8,128)(2,1)S(1)} %get-tuple-element.52), channel_id=1, source_target_pairs={{0,8},{4,12},{8,0},{12,4},{16,24},{20,28},{24,16},{28,20},{1,9},{5... | collective-permute-start | bytes 196616 | tf_op jit(solution)/shard_map/ppermute | solution.py:439
  25.3 4.3 %collective-permute-start.7 = (bf16[256,128]{1,0:T(8,128)(2,1)S(1)}, bf16[256,128]{1,0:T(8,128)(2,1)S(1)}, u32[]{:S(2)}, u32[]{:S(2)}) collective-permute-start(bf16[256,128]{1,0:T(8,128)(2,1)S(1)} %get-tuple-element.53), channel_id=1, source_target_pairs={{0,16},{4,20},{8,24},{12,28},{16,0},{20,4},{24,8},{28,12},{1,17},{... | collective-permute-start | bytes 196616 | tf_op jit(solution)/shard_map/ppermute | solution.py:439
  30.0 5.9 %collective-permute-start.11 = (bf16[16,16,128]{2,1,0:T(8,128)(2,1)S(1)}, bf16[16,16,128]{2,1,0:T(8,128)(2,1)S(1)}, u32[]{:S(2)}, u32[]{:S(2)}) collective-permute-start(bf16[16,16,128]{2,1,0:T(8,128)(2,1)S(1)} %get-tuple-element.46.refs_0_), channel_id=1, source_target_pairs={{0,24},{4,28},{8,16},{12,20},{16,8},{20,12},{24,0},{28,4},{1,25},{... | collective-permute-start | bytes 196616 | tf_op jit(solution)/shard_map/ppermute | solution.py:439
  31.6 4.7 %collective-permute-start.10 = (bf16[16,16,128]{2,1,0:T(8,128)(2,1)S(1)}, bf16[16,16,128]{2,1,0:T(8,128)(2,1)S(1)}, u32[]{:S(2)}, u32[]{:S(2)}) collective-permute-start(bf16[16,16,128]{2,1,0:T(8,128)(2,1)S(1)} %get-tuple-element.46.refs_0_), channel_id=1, source_target_pairs={{0,16},{4,20},{8,24},{12,28},{16,0},{20,4},{24,8},{28,12},{1,17},{... | collective-permute-start | bytes 196616 | tf_op jit(solution)/shard_map/ppermute | solution.py:439
  33.0 4.3 %collective-permute-start.9 = (bf16[16,16,128]{2,1,0:T(8,128)(2,1)S(1)}, bf16[16,16,128]{2,1,0:T(8,128)(2,1)S(1)}, u32[]{:S(2)}, u32[]{:S(2)}) collective-permute-start(bf16[16,16,128]{2,1,0:T(8,128)(2,1)S(1)} %get-tuple-element.46.refs_0_), channel_id=1, source_target_pairs={{0,8},{4,12},{8,0},{12,4},{16,24},{20,28},{24,16},{28,20},{1,9},{5... | collective-permute-start | bytes 196616 | tf_op jit(solution)/shard_map/ppermute | solution.py:439
  33.6 3.7 %collective-permute-start.12 = (bf16[16,16,128]{2,1,0:T(8,128)(2,1)S(1)}, bf16[16,16,128]{2,1,0:T(8,128)(2,1)S(1)}, u32[]{:S(2)}, u32[]{:S(2)}) collective-permute-start(bf16[16,16,128]{2,1,0:T(8,128)(2,1)S(1)} %get-tuple-element.46.refs_0_), channel_id=1, source_target_pairs={{0,4},{4,0},{8,12},{12,8},{16,20},{20,16},{24,28},{28,24},{1,5},{5... | collective-permute-start | bytes 196616 | tf_op jit(solution)/shard_map/ppermute | solution.py:439
  36.0 1.4 %collective-permute-start.15 = (bf16[16,16,128]{2,1,0:T(8,128)(2,1)S(1)}, bf16[16,16,128]{2,1,0:T(8,128)(2,1)S(1)}, u32[]{:S(2)}, u32[]{:S(2)}) collective-permute-start(bf16[16,16,128]{2,1,0:T(8,128)(2,1)S(1)} %collective-permute-done.11.refs_3_), channel_id=1, source_target_pairs={{0,4},{4,0},{8,12},{12,8},{16,20},{20,16},{24,28},{28,24},{1,5},{5... | collective-permute-start | bytes 196616 | tf_op jit(solution)/shard_map/ppermute | solution.py:439
  36.3 1.3 %collective-permute-start.14 = (bf16[16,16,128]{2,1,0:T(8,128)(2,1)S(1)}, bf16[16,16,128]{2,1,0:T(8,128)(2,1)S(1)}, u32[]{:S(2)}, u32[]{:S(2)}) collective-permute-start(bf16[16,16,128]{2,1,0:T(8,128)(2,1)S(1)} %collective-permute-done.10.refs_2_), channel_id=1, source_target_pairs={{0,4},{4,0},{8,12},{12,8},{16,20},{20,16},{24,28},{28,24},{1,5},{5... | collective-permute-start | bytes 196616 | tf_op jit(solution)/shard_map/ppermute | solution.py:439
  37.3 1.3 %collective-permute-start.13 = (bf16[16,16,128]{2,1,0:T(8,128)(2,1)S(1)}, bf16[16,16,128]{2,1,0:T(8,128)(2,1)S(1)}, u32[]{:S(2)}, u32[]{:S(2)}) collective-permute-start(bf16[16,16,128]{2,1,0:T(8,128)(2,1)S(1)} %collective-permute-done.9.refs_1_), channel_id=1, source_target_pairs={{0,4},{4,0},{8,12},{12,8},{16,20},{20,16},{24,28},{28,24},{1,5},{5... | collective-permute-start | bytes 196616 | tf_op jit(solution)/shard_map/ppermute | solution.py:439
  39.8 5.8 %collective-permute-start.16 = (bf16[128,128]{1,0:T(8,128)(2,1)S(1)}, bf16[128,128]{1,0:T(8,128)(2,1)S(1)}, u32[]{:S(2)}, u32[]{:S(2)}) collective-permute-start(bf16[128,128]{1,0:T(8,128)(2,1)S(1)} %get-tuple-element.47), channel_id=1, source_target_pairs={{0,3},{1,2},{2,1},{3,0},{4,7},{5,6},{6,5},{7,4},{8,11},{9,10},{10,... | collective-permute-start | bytes 98312 | tf_op jit(solution)/shard_map/ppermute | solution.py:439
  41.6 5.0 %collective-permute-start.17 = (bf16[128,128]{1,0:T(8,128)(2,1)S(1)}, bf16[128,128]{1,0:T(8,128)(2,1)S(1)}, u32[]{:S(2)}, u32[]{:S(2)}) collective-permute-start(bf16[128,128]{1,0:T(8,128)(2,1)S(1)} %get-tuple-element.48), channel_id=1, source_target_pairs={{0,2},{1,3},{2,0},{3,1},{4,6},{5,7},{6,4},{7,5},{8,10},{9,11},{10,... | collective-permute-start | bytes 98312 | tf_op jit(solution)/shard_map/ppermute | solution.py:439
  41.6 5.0 %collective-permute-start.18 = (bf16[128,128]{1,0:T(8,128)(2,1)S(1)}, bf16[128,128]{1,0:T(8,128)(2,1)S(1)}, u32[]{:S(2)}, u32[]{:S(2)}) collective-permute-start(bf16[128,128]{1,0:T(8,128)(2,1)S(1)} %get-tuple-element.49), channel_id=1, source_target_pairs={{0,1},{1,0},{2,3},{3,2},{4,5},{5,4},{6,7},{7,6},{8,9},{9,8},{10,11... | collective-permute-start | bytes 98312 | tf_op jit(solution)/shard_map/ppermute | solution.py:439

commit v9 on v8

--- a/solution.py
+++ b/solution.py
@@ -40,15 +40,16 @@
         inverse=jnp.asarray(inverse, F32).astype(BF16),
         taps=jnp.asarray(np.tile(tap_spec, (1, LANES // KSHIFT)), F32),
         gather=gather_table(source_local),
-        gather_half=gather_table(source_local // 2),
+        gather_half=gather_table(source_local // 2, 2),
         spread=spread_table(source_local // 2),
     )
 
 
-def gather_table(sources):
+def gather_table(sources, count=1):
     source_of = np.arange(sources * GROUP) // GROUP
     pick = source_of[:, None] == np.arange(sources)[None, :]
-    return jnp.asarray(np.tile(pick, (1, LANES // sources)), F32).astype(BF16)
+    table = np.kron(np.eye(count), np.tile(pick, (1, LANES // sources)))
+    return jnp.asarray(table, F32).astype(BF16)
 
 
 def spread_table(sources):
@@ -106,22 +107,29 @@
     diagonal = same_bin(rows, width)
     block_of = lax.broadcasted_iota(jnp.int32, (sets, GROUP, LANES), 2) // (LANES // blocks)
 
+    span = kept_ref.shape[1] // width
+
     for group in range(NG):
         vector = vector_ref[group].reshape(rows, vector_ref.shape[-1])
         matrix = [ref[group].reshape(half, ref.shape[-1]) for ref in matrix_refs]
         matrix = matrix[0] if len(matrix) == 1 else jnp.concatenate(matrix, axis=0)
         full = mm(vector, matrix, NT_DIMS)
-        kept_ref[group * rows : (group + 1) * rows, :] = jnp.where(diagonal, full, 0.0).astype(BF16)
+        place, lane = group // span * rows, group % span * width
+        kept_ref[place : place + rows, lane : lane + width] = jnp.where(
+            diagonal, full, 0.0
+        ).astype(BF16)
 
     for couple in range(NG // 2):
-        kept = kept_ref[couple * 2 * rows : (couple + 1) * 2 * rows, :]
-        spread = mm(kept, gather).reshape(2, sets, members, 2, GROUP, LANES)
+        count = 2 // span * rows
+        spread = mm(kept_ref[couple * count : (couple + 1) * count, :], gather)
         both = []
         for one in range(2):
-            value = spread[one, :, 0, 0]
+            place, lane = one // span * rows, one % span * LANES
+            part = spread[place : place + rows, lane : lane + LANES]
+            part = part.reshape(sets, members, 2, GROUP, LANES)
+            value = part[:, 0, 0]
             for block in range(1, blocks):
-                term = spread[one, :, block % members, block // members]
-                value = jnp.where(block_of == block, term, value)
+                value = jnp.where(block_of == block, part[:, block % members, block // members], value)
             both.append(value)
         store(couple * 2 * GROUP, jnp.concatenate(both, axis=1).astype(BF16))
 
@@ -232,9 +240,13 @@
     make_delays(0, half, forward_ref, deconv_ref, taps_ref, gain, delay_ref)
     forward = forward_ref[...]
     large[0].wait()
-    for place in range(fields):
-        spectra = mm(forward, focal_ref[place], NT_DIMS)
-        store_vector(vector_ref, place, spectra[:NF], spectra[NF:])
+    for place in range(0, fields, 2):
+        signals = focal_ref[place : place + 2].reshape(-1, NT)
+        receivers = signals.shape[0] // 2
+        spectra = mm(forward, signals, NT_DIMS)
+        for one in range(2):
+            field = spectra[:, one * receivers : (one + 1) * receivers]
+            store_vector(vector_ref, place + one, field[:NF], field[NF:])
     own_ref[...] = focal_ref[lax.axis_index("shot")]
     for copy in small[3:] + large[1:]:
         copy.wait()
@@ -459,7 +471,7 @@
     vector = shape((NG, focal_total, 2 * GROUP, 2 * receivers), BF16)
     half_matrix = shape((NG, half // 2, 2 * GROUP, 2 * receivers), BF16)
     half_sums = shape((sets * NF, LANES), BF16)
-    half_kept = pltpu.VMEM((NG * focal_total * 2 * GROUP, half * GROUP), BF16)
+    half_kept = pltpu.VMEM((NG // 2 * focal_total * 2 * GROUP, sources * GROUP), BF16)
     half_delays = pltpu.VMEM((half // 2, 2 * NF, LANES), BF16)
     assert sets % 2 == 0 and half * 8 == LANES
 

time: 47.7 us -> 47.6 us (level)
  no operation moved by 1% of the time
where the time goes in v9:
time: 47.6 us; the launch traced here: 47.5 us
  starting transfers between devices  20.9 us (44%)
  waiting for transfers between devices  14.7 us (31%)
  Pallas kernels  10.9 us (23%)
  between operations  0.75 us (2%)
    ppermute x19, starting transfers between devices, exchange(): lax.ppermute(value, axis, [(place, place ^ distance) for place in range(c...  20.9 us
    ppermute x19, waiting for transfers between devices, exchange(): lax.ppermute(value, axis, [(place, place ^ distance) for place in range(c...  14.7 us
    pallas_call x1, Pallas kernels, body(): call(functools.partial(first_kernel, gain), 'first', [half_matrix, half_s...  3.45 us
    pallas_call x1, Pallas kernels, body(): call(functools.partial(rest_kernel, gain), 'rest', (half_matrix, half_sum...  1.74 us
    pallas_call x2, Pallas kernels, emit(): call(emit_kernel, 'emit', jax.ShapeDtypeStruct(field.shape, field.dtype),...  1.3 us
    pallas_call x1, Pallas kernels, body(): call(functools.partial(second_kernel, pairs), 'second', [shape((NF, LANES...  1.24 us
    pallas_call x1, Pallas kernels, body(): call(adjoint_kernel, 'adjoint', [shape((pairs, 2 * NF, receivers), BF16),...  1.13 us
  transfers between devices with their start and end apart: 19, of which 14 were waited for; matrix products, arithmetic and copies ran while one was open for 0% of the time, Pallas kernels for 8%

profile of v9, /device:TPU:0, one launch (start us, length us, event | category | flops | bytes accessed | tf_op | source)
XLA Modules:
  0.0 47.5 jit_solution(9553431445867118492)
XLA Ops:
  0.6 0.0 copy-start
  0.6 3.5 %first.1 = (bf16[16,8,16,256]{3,2,1,0:T(8,128)(2,1)S(1)}, bf16[256,128]{1,0:T(8,128)(2,1)S(1)}, bf16[128,256]{1,0:T(8,128)(2,1)S(1)}, bf16[16,8,16,256]{3,2,1,0:...) custom-call(bf16[32,128,256]{2,1,0:T(8,128)(2,1)} %traces_ref.1, ...), custom_call_target="tpu_custom_call" | custom-call | flops 4000000000 | bytes 1048576 | tf_op jit(solution)/shard_map/first/pallas_call | solution.py:486
  4.1 3.1 %collective-permute-start.2 = (bf16[256,128]{1,0:T(8,128)(2,1)S(1)}, bf16[256,128]{1,0:T(8,128)(2,1)S(1)}, u32[]{:S(2)}, u32[]{:S(2)}) collective-permute-start(bf16[256,128]{1,0:T(8,128)(2,1)S(1)} %get-tuple-element.35), channel_id=1, source_target_pairs={{0,1},{1,0},{2,3},{3,2},{4,5},{5,4},{6,7},{7,6},{8,9},{9,8},{10,11... | collective-permute-start | bytes 196616 | tf_op jit(solution)/shard_map/ppermute | solution.py:451
  7.2 0.0 copy-done
  7.2 0.0 copy-start.2
  7.2 0.0 copy-start.3
  7.2 1.7 %rest.1 = (bf16[16,8,16,256]{3,2,1,0:T(8,128)(2,1)S(1)}, bf16[256,128]{1,0:T(8,128)(2,1)S(1)}) custom-call(bf16[32,128,256]{2,1,0:T(8,128)(2,1)S(1)} %copy-done, s32[32,128]{1,0:T(8,128)S(1)} %get-tuple-element.27.shift_ref, f32[32,64]{1,0:T(8,128)S(1)} %get-tuple-element.28.deconv_ref, s32[2,32]{1,0:T(2,128)S(1)} %get-tuple-element.29.onset_ref.refs_4_, ...), custom_call_target="tpu_custom_call" | custom-call | flops 3000000000 | bytes 1048576 | tf_op jit(solution)/shard_map/rest/pallas_call | solution.py:508
  8.9 0.1 collective-permute-start
  9.1 0.4 collective-permute-done.2
  9.5 3.1 %collective-permute-start.3 = (bf16[256,128]{1,0:T(8,128)(2,1)S(1)}, bf16[256,128]{1,0:T(8,128)(2,1)S(1)}, u32[]{:S(2)}, u32[]{:S(2)}) collective-permute-start(bf16[256,128]{1,0:T(8,128)(2,1)S(1)} %add_convert_fusion.3.mine_ref), channel_id=1, source_target_pairs={{0,2},{1,3},{2,0},{3,1},{4,6},{5,7},{6,4},{7,5},{8,10},{9,11},{10,... | collective-permute-start | bytes 196616 | tf_op jit(solution)/shard_map/ppermute | solution.py:451
  12.6 1.1 %collective-permute-done = bf16[256,128]{1,0:T(8,128)(2,1)S(1)} collective-permute-done((bf16[256,128]{1,0:T(8,128)(2,1)S(1)}, bf16[256,128]{1,0:T(8,128)(2,1)S(1)}, u32[]{:S(2)}, u32[]{:S(2)}) %collective-permute-start) | collective-permute-done | bytes 65568 | tf_op jit(solution)/shard_map/ppermute | solution.py:451
  13.7 2.3 %collective-permute-start.1 = (bf16[256,128]{1,0:T(8,128)(2,1)S(1)}, bf16[256,128]{1,0:T(8,128)(2,1)S(1)}, u32[]{:S(2)}, u32[]{:S(2)}) collective-permute-start(bf16[256,128]{1,0:T(8,128)(2,1)S(1)} %add_convert_fusion.4.mine_ref), channel_id=1, source_target_pairs={{0,2},{1,3},{2,0},{3,1},{4,6},{5,7},{6,4},{7,5},{8,10},{9,11},{10,... | collective-permute-start | bytes 196616 | tf_op jit(solution)/shard_map/ppermute | solution.py:451
  16.0 0.0 collective-permute-done.3.other_ref
  16.0 0.0 copy-done.2
  16.0 0.0 copy-done.3
  16.0 0.7 %mute.1 = (bf16[16,2,4,16,128]{4,3,2,1,0:T(8,128)(2,1)S(1)}, f32[2,16,256]{2,1,0:T(8,128)S(1)}) custom-call(bf16[256,128]{1,0:T(8,128)(2,1)S(1)} %add_convert_fusion.3.mine_ref, bf16[256,128]{1,0:T(8,128)(2,1)S(1)} %collective-permute-done.3.other_ref, bf16[256,256]{1,0:T(8,128)(2,1)S(1)} %get-tuple-element.30.forward_ref.refs_6_, ...), custom_call_target="tpu_custom_call" | custom-call | flops 1000000000 | bytes 1048576 | tf_op jit(solution)/shard_map/mute/pallas_call | solution.py:527
  16.7 2.9 %collective-permute-done.1.other_ref = bf16[256,128]{1,0:T(8,128)(2,1)S(1)} collective-permute-done((bf16[256,128]{1,0:T(8,128)(2,1)S(1)}, bf16[256,128]{1,0:T(8,128)(2,1)S(1)}, u32[]{:S(2)}, u32[]{:S(2)}) %collective-permute-start.1) | collective-permute-done | bytes 65568 | tf_op jit(solution)/shard_map/ppermute | solution.py:451
  19.5 0.0 copy-start.1
  19.5 1.1 %adjoint.1 = (bf16[4,256,128]{2,1,0:T(8,128)(2,1)S(1)}, bf16[256,128]{1,0:T(8,128)(2,1)S(1)}, bf16[3,256,128]{2,1,0:T(8,128)(2,1)S(1)}, f32[2,32,256]{2,1,0:T(8,128)S(1)}) custom-call(bf16[256,128]{1,0:T(8,128)(2,1)S(1)} %add_convert_fusion.4.mine_ref, bf16[256,128]{1,0:T(8,128)(2,1)S(1)} %collective-permute-done.1.other_ref, ...), custom_call_target="tpu_custom_call" | custom-call | flops 2000000000 | bytes 1048576 | tf_op jit(solution)/shard_map/adjoint/pallas_call | solution.py:535
  20.7 0.1 collective-permute-start.4
  20.7 0.5 %collective-permute-start.6 = (bf16[3,256,128]{2,1,0:T(8,128)(2,1)S(1)}, bf16[3,256,128]{2,1,0:T(8,128)(2,1)S(1)}, u32[]{:S(2)}, u32[]{:S(2)}) collective-permute-start(bf16[3,256,128]{2,1,0:T(8,128)(2,1)S(1)} %get-tuple-element.43), channel_id=1, source_target_pairs={{0,4},{4,0},{8,12},{12,8},{16,20},{20,16},{24,28},{28,24},{1,5},{5... | collective-permute-start | bytes 589832 | tf_op jit(solution)/shard_map/ppermute | solution.py:451
  21.2 0.7 %collective-permute-done.4 = bf16[256,128]{1,0:T(8,128)(2,1)S(1)} collective-permute-done((bf16[256,128]{1,0:T(8,128)(2,1)S(1)}, bf16[256,128]{1,0:T(8,128)(2,1)S(1)}, u32[]{:S(2)}, u32[]{:S(2)}) %collective-permute-start.4) | collective-permute-done | bytes 65568 | tf_op jit(solution)/shard_map/ppermute | solution.py:451
  22.0 0.0 copy-start.4
  22.0 2.5 %collective-permute-start.5 = (bf16[256,128]{1,0:T(8,128)(2,1)S(1)}, bf16[256,128]{1,0:T(8,128)(2,1)S(1)}, u32[]{:S(2)}, u32[]{:S(2)}) collective-permute-start(bf16[256,128]{1,0:T(8,128)(2,1)S(1)} %fusion), channel_id=1, source_target_pairs={{0,24},{4,28},{8,16},{12,20},{16,8},{20,12},{24,0},{28,4},{1,25},{... | collective-permute-start | bytes 196616 | tf_op jit(solution)/shard_map/ppermute | solution.py:451
  24.5 0.0 collective-permute-done.6
  24.5 0.1 fusion.3
  24.6 0.6 %collective-permute-start.8 = (bf16[256,128]{1,0:T(8,128)(2,1)S(1)}, bf16[256,128]{1,0:T(8,128)(2,1)S(1)}, u32[]{:S(2)}, u32[]{:S(2)}) collective-permute-start(bf16[256,128]{1,0:T(8,128)(2,1)S(1)} %get-tuple-element.52), channel_id=1, source_target_pairs={{0,8},{4,12},{8,0},{12,4},{16,24},{20,28},{24,16},{28,20},{1,9},{5... | collective-permute-start | bytes 196616 | tf_op jit(solution)/shard_map/ppermute | solution.py:451
  25.2 0.5 %collective-permute-start.7 = (bf16[256,128]{1,0:T(8,128)(2,1)S(1)}, bf16[256,128]{1,0:T(8,128)(2,1)S(1)}, u32[]{:S(2)}, u32[]{:S(2)}) collective-permute-start(bf16[256,128]{1,0:T(8,128)(2,1)S(1)} %get-tuple-element.53), channel_id=1, source_target_pairs={{0,16},{4,20},{8,24},{12,28},{16,0},{20,4},{24,8},{28,12},{1,17},{... | collective-permute-start | bytes 196616 | tf_op jit(solution)/shard_map/ppermute | solution.py:451
  25.7 1.8 %collective-permute-done.5.refs_0_ = bf16[256,128]{1,0:T(8,128)(2,1)S(1)} collective-permute-done((bf16[256,128]{1,0:T(8,128)(2,1)S(1)}, bf16[256,128]{1,0:T(8,128)(2,1)S(1)}, u32[]{:S(2)}, u32[]{:S(2)}) %collective-permute-start.5) | collective-permute-done | bytes 65568 | tf_op jit(solution)/shard_map/ppermute | solution.py:451
  27.5 1.4 %collective-permute-done.8.refs_2_ = bf16[256,128]{1,0:T(8,128)(2,1)S(1)} collective-permute-done((bf16[256,128]{1,0:T(8,128)(2,1)S(1)}, bf16[256,128]{1,0:T(8,128)(2,1)S(1)}, u32[]{:S(2)}, u32[]{:S(2)}) %collective-permute-start.8) | collective-permute-done | bytes 65568 | tf_op jit(solution)/shard_map/ppermute | solution.py:451
  28.9 0.5 %collective-permute-done.7.refs_1_ = bf16[256,128]{1,0:T(8,128)(2,1)S(1)} collective-permute-done((bf16[256,128]{1,0:T(8,128)(2,1)S(1)}, bf16[256,128]{1,0:T(8,128)(2,1)S(1)}, u32[]{:S(2)}, u32[]{:S(2)}) %collective-permute-start.7) | collective-permute-done | bytes 65568 | tf_op jit(solution)/shard_map/ppermute | solution.py:451
  29.5 0.0 copy-done.1
  29.5 0.5 downgoing.1
  29.9 1.6 %collective-permute-start.11 = (bf16[16,16,128]{2,1,0:T(8,128)(2,1)S(1)}, bf16[16,16,128]{2,1,0:T(8,128)(2,1)S(1)}, u32[]{:S(2)}, u32[]{:S(2)}) collective-permute-start(bf16[16,16,128]{2,1,0:T(8,128)(2,1)S(1)} %get-tuple-element.46.refs_0_), channel_id=1, source_target_pairs={{0,24},{4,28},{8,16},{12,20},{16,8},{20,12},{24,0},{28,4},{1,25},{... | collective-permute-start | bytes 196616 | tf_op jit(solution)/shard_map/ppermute | solution.py:451
  31.5 1.4 %collective-permute-start.10 = (bf16[16,16,128]{2,1,0:T(8,128)(2,1)S(1)}, bf16[16,16,128]{2,1,0:T(8,128)(2,1)S(1)}, u32[]{:S(2)}, u32[]{:S(2)}) collective-permute-start(bf16[16,16,128]{2,1,0:T(8,128)(2,1)S(1)} %get-tuple-element.46.refs_0_), channel_id=1, source_target_pairs={{0,16},{4,20},{8,24},{12,28},{16,0},{20,4},{24,8},{28,12},{1,17},{... | collective-permute-start | bytes 196616 | tf_op jit(solution)/shard_map/ppermute | solution.py:451
  33.0 0.5 %collective-permute-start.9 = (bf16[16,16,128]{2,1,0:T(8,128)(2,1)S(1)}, bf16[16,16,128]{2,1,0:T(8,128)(2,1)S(1)}, u32[]{:S(2)}, u32[]{:S(2)}) collective-permute-start(bf16[16,16,128]{2,1,0:T(8,128)(2,1)S(1)} %get-tuple-element.46.refs_0_), channel_id=1, source_target_pairs={{0,8},{4,12},{8,0},{12,4},{16,24},{20,28},{24,16},{28,20},{1,9},{5... | collective-permute-start | bytes 196616 | tf_op jit(solution)/shard_map/ppermute | solution.py:451
  33.5 0.0 collective-permute-start.12
  33.5 2.4 %collective-permute-done.11.refs_3_ = bf16[16,16,128]{2,1,0:T(8,128)(2,1)S(1)} collective-permute-done((bf16[16,16,128]{2,1,0:T(8,128)(2,1)S(1)}, bf16[16,16,128]{2,1,0:T(8,128)(2,1)S(1)}, u32[]{:S(2)}, u32[]{:S(2)}) %collective-permute-start.11) | collective-permute-done | bytes 65568 | tf_op jit(solution)/shard_map/ppermute | solution.py:451
  35.9 0.0 collective-permute-start.15
  35.9 0.3 collective-permute-done.10.refs_2_
  36.2 0.2 collective-permute-start.14
  36.4 0.8 %collective-permute-done.9.refs_1_ = bf16[16,16,128]{2,1,0:T(8,128)(2,1)S(1)} collective-permute-done((bf16[16,16,128]{2,1,0:T(8,128)(2,1)S(1)}, bf16[16,16,128]{2,1,0:T(8,128)(2,1)S(1)}, u32[]{:S(2)}, u32[]{:S(2)}) %collective-permute-start.9) | collective-permute-done | bytes 65568 | tf_op jit(solution)/shard_map/ppermute | solution.py:451
  37.2 0.0 collective-permute-start.13
  37.2 0.0 collective-permute-done.12.refs_4_
  37.2 0.0 collective-permute-done.15.refs_7_
  37.2 0.2 collective-permute-done.14.refs_6_
  37.4 1.0 %collective-permute-done.13.refs_5_ = bf16[16,16,128]{2,1,0:T(8,128)(2,1)S(1)} collective-permute-done((bf16[16,16,128]{2,1,0:T(8,128)(2,1)S(1)}, bf16[16,16,128]{2,1,0:T(8,128)(2,1)S(1)}, u32[]{:S(2)}, u32[]{:S(2)}) %collective-permute-start.13) | collective-permute-done | bytes 65568 | tf_op jit(solution)/shard_map/ppermute | solution.py:451
  38.5 0.0 copy-done.4
  38.5 1.2 %second.1 = (bf16[128,128]{1,0:T(8,128)(2,1)S(1)}, bf16[128,128]{1,0:T(8,128)(2,1)S(1)}, bf16[128,128]{1,0:T(8,128)(2,1)S(1)}, bf16[128,128]{1,0:T(8,128)(2,1)S(1)}) custom-call(bf16[16,16,128]{2,1,0:T(8,128)(2,1)S(1)} %get-tuple-element.46.refs_0_, bf16[16,16,128]{2,1,0:T(8,128)(2,1)S(1)} %collective-permute-done.9.refs_1_, ...), custom_call_target="tpu_custom_call" | custom-call | flops 1000000000 | bytes 1048576 | tf_op jit(solution)/shard_map/second/pallas_call | solution.py:571
  39.7 1.8 %collective-permute-start.16 = (bf16[128,128]{1,0:T(8,128)(2,1)S(1)}, bf16[128,128]{1,0:T(8,128)(2,1)S(1)}, u32[]{:S(2)}, u32[]{:S(2)}) collective-permute-start(bf16[128,128]{1,0:T(8,128)(2,1)S(1)} %get-tuple-element.47), channel_id=1, source_target_pairs={{0,3},{1,2},{2,1},{3,0},{4,7},{5,6},{6,5},{7,4},{8,11},{9,10},{10,... | collective-permute-start | bytes 98312 | tf_op jit(solution)/shard_map/ppermute | solution.py:451
  41.5 0.0 collective-permute-start.17
  41.6 2.6 %collective-permute-start.18 = (bf16[128,128]{1,0:T(8,128)(2,1)S(1)}, bf16[128,128]{1,0:T(8,128)(2,1)S(1)}, u32[]{:S(2)}, u32[]{:S(2)}) collective-permute-start(bf16[128,128]{1,0:T(8,128)(2,1)S(1)} %get-tuple-element.49), channel_id=1, source_target_pairs={{0,1},{1,0},{2,3},{3,2},{4,5},{5,4},{6,7},{7,6},{8,9},{9,8},{10,11... | collective-permute-start | bytes 98312 | tf_op jit(solution)/shard_map/ppermute | solution.py:451
  44.2 0.6 %emit.2 = f32[2,32,256]{2,1,0:T(8,128)} custom-call(f32[2,32,256]{2,1,0:T(8,128)S(1)} %get-tuple-element.40.field_ref), custom_call_target="tpu_custom_call" | custom-call | flops 300000000 | bytes 1048576 | tf_op jit(solution)/shard_map/emit/pallas_call | solution.py:444
  44.8 0.7 %emit.3 = f32[1,128,256]{2,1,0:T(8,128)} custom-call(f32[1,128,256]{2,1,0:T(8,128)S(1)} %get-tuple-element.45.field_ref), custom_call_target="tpu_custom_call" | custom-call | flops 300000000 | bytes 1048576 | tf_op jit(solution)/shard_map/emit/pallas_call | solution.py:444
  45.5 0.1 collective-permute-done.16.refs_0_
  45.6 1.0 %collective-permute-done.17.refs_1_ = bf16[128,128]{1,0:T(8,128)(2,1)S(1)} collective-permute-done((bf16[128,128]{1,0:T(8,128)(2,1)S(1)}, bf16[128,128]{1,0:T(8,128)(2,1)S(1)}, u32[]{:S(2)}, u32[]{:S(2)}) %collective-permute-start.17) | collective-permute-done | bytes 32800 | tf_op jit(solution)/shard_map/ppermute | solution.py:451
  46.5 0.0 collective-permute-done.18.refs_2_
  46.6 0.9 %final.1 = f32[2,32,256]{2,1,0:T(8,128)} custom-call(bf16[128,128]{1,0:T(8,128)(2,1)S(1)} %collective-permute-done.16.refs_0_, bf16[128,128]{1,0:T(8,128)(2,1)S(1)} %collective-permute-done.17.refs_1_, bf16[128,128]{1,0:T(8,128)(2,1)S(1)} %collective-permute-done.18.refs_2_, bf16[128,128]{1,0:T(8,128)(2,1)S(1)} %get-tuple-element.50.refs_3_, ...), custom_call_target="tpu_custom_call" | custom-call | flops 1000000000 | bytes 1048576 | tf_op jit(solution)/shard_map/final/pallas_call | solution.py:585
  (3 shorter events, 0.1 us)
Async XLA Ops:
  0.6 6.6 %copy-start = (bf16[32,128,256]{2,1,0:T(8,128)(2,1)S(1)}, bf16[32,128,256]{2,1,0:T(8,128)(2,1)}, u32[]{:S(2)}) copy-start(bf16[32,128,256]{2,1,0:T(8,128)(2,1)} %traces_ref.1) | copy-start | bytes 6291460
  4.1 5.3 %collective-permute-start.2 = (bf16[256,128]{1,0:T(8,128)(2,1)S(1)}, bf16[256,128]{1,0:T(8,128)(2,1)S(1)}, u32[]{:S(2)}, u32[]{:S(2)}) collective-permute-start(bf16[256,128]{1,0:T(8,128)(2,1)S(1)} %get-tuple-element.35), channel_id=1, source_target_pairs={{0,1},{1,0},{2,3},{3,2},{4,5},{5,4},{6,7},{7,6},{8,9},{9,8},{10,11... | collective-permute-start | bytes 196616 | tf_op jit(solution)/shard_map/ppermute | solution.py:451
  7.2 8.8 %copy-start.2 = (bf16[2,4,128,256]{3,2,1,0:T(8,128)(2,1)S(1)}, bf16[2,4,128,256]{3,2,1,0:T(8,128)(2,1)}, u32[]{:S(2)}) copy-start(bf16[2,4,128,256]{3,2,1,0:T(8,128)(2,1)} %constant.23.spread_ref) | copy-start | bytes 1572868
  7.2 8.8 %copy-start.3 = (bf16[256,256]{1,0:T(8,128)(2,1)S(1)}, bf16[256,256]{1,0:T(8,128)(2,1)}, u32[]{:S(2)}) copy-start(bf16[256,256]{1,0:T(8,128)(2,1)} %constant.22.inverse_ref.refs_7_.refs_5_) | copy-start | bytes 393220
  8.9 4.7 %collective-permute-start = (bf16[256,128]{1,0:T(8,128)(2,1)S(1)}, bf16[256,128]{1,0:T(8,128)(2,1)S(1)}, u32[]{:S(2)}, u32[]{:S(2)}) collective-permute-start(bf16[256,128]{1,0:T(8,128)(2,1)S(1)} %get-tuple-element.34), channel_id=1, source_target_pairs={{0,1},{1,0},{2,3},{3,2},{4,5},{5,4},{6,7},{7,6},{8,9},{9,8},{10,11... | collective-permute-start | bytes 196616 | tf_op jit(solution)/shard_map/ppermute | solution.py:451
  9.5 6.5 %collective-permute-start.3 = (bf16[256,128]{1,0:T(8,128)(2,1)S(1)}, bf16[256,128]{1,0:T(8,128)(2,1)S(1)}, u32[]{:S(2)}, u32[]{:S(2)}) collective-permute-start(bf16[256,128]{1,0:T(8,128)(2,1)S(1)} %add_convert_fusion.3.mine_ref), channel_id=1, source_target_pairs={{0,2},{1,3},{2,0},{3,1},{4,6},{5,7},{6,4},{7,5},{8,10},{9,11},{10,... | collective-permute-start | bytes 196616 | tf_op jit(solution)/shard_map/ppermute | solution.py:451
  13.7 5.8 %collective-permute-start.1 = (bf16[256,128]{1,0:T(8,128)(2,1)S(1)}, bf16[256,128]{1,0:T(8,128)(2,1)S(1)}, u32[]{:S(2)}, u32[]{:S(2)}) collective-permute-start(bf16[256,128]{1,0:T(8,128)(2,1)S(1)} %add_convert_fusion.4.mine_ref), channel_id=1, source_target_pairs={{0,2},{1,3},{2,0},{3,1},{4,6},{5,7},{6,4},{7,5},{8,10},{9,11},{10,... | collective-permute-start | bytes 196616 | tf_op jit(solution)/shard_map/ppermute | solution.py:451
  19.5 9.9 %copy-start.1 = (s32[1,128]{1,0:T(1,128)S(1)}, s32[1,128]{1,0:T(1,128)}, u32[]{:S(2)}) copy-start(s32[1,128]{1,0:T(1,128)} %refs_5_.1) | copy-start | bytes 1540
  20.7 1.3 %collective-permute-start.4 = (bf16[256,128]{1,0:T(8,128)(2,1)S(1)}, bf16[256,128]{1,0:T(8,128)(2,1)S(1)}, u32[]{:S(2)}, u32[]{:S(2)}) collective-permute-start(bf16[256,128]{1,0:T(8,128)(2,1)S(1)} %get-tuple-element.42), channel_id=1, source_target_pairs={{0,4},{4,0},{8,12},{12,8},{16,20},{20,16},{24,28},{28,24},{1,5},{5... | collective-permute-start | bytes 196616 | tf_op jit(solution)/shard_map/ppermute | solution.py:451
  20.7 3.8 %collective-permute-start.6 = (bf16[3,256,128]{2,1,0:T(8,128)(2,1)S(1)}, bf16[3,256,128]{2,1,0:T(8,128)(2,1)S(1)}, u32[]{:S(2)}, u32[]{:S(2)}) collective-permute-start(bf16[3,256,128]{2,1,0:T(8,128)(2,1)S(1)} %get-tuple-element.43), channel_id=1, source_target_pairs={{0,4},{4,0},{8,12},{12,8},{16,20},{20,16},{24,28},{28,24},{1,5},{5... | collective-permute-start | bytes 589832 | tf_op jit(solution)/shard_map/ppermute | solution.py:451
  22.0 16.5 %copy-start.4 = (bf16[256,128]{1,0:T(8,128)(2,1)S(1)}, bf16[256,128]{1,0:T(8,128)(2,1)}, u32[]{:S(2)}) copy-start(bf16[256,128]{1,0:T(8,128)(2,1)} %constant.24.refs_10_) | copy-start | bytes 196612
  22.0 5.5 %collective-permute-start.5 = (bf16[256,128]{1,0:T(8,128)(2,1)S(1)}, bf16[256,128]{1,0:T(8,128)(2,1)S(1)}, u32[]{:S(2)}, u32[]{:S(2)}) collective-permute-start(bf16[256,128]{1,0:T(8,128)(2,1)S(1)} %fusion), channel_id=1, source_target_pairs={{0,24},{4,28},{8,16},{12,20},{16,8},{20,12},{24,0},{28,4},{1,25},{... | collective-permute-start | bytes 196616 | tf_op jit(solution)/shard_map/ppermute | solution.py:451
  24.6 4.3 %collective-permute-start.8 = (bf16[256,128]{1,0:T(8,128)(2,1)S(1)}, bf16[256,128]{1,0:T(8,128)(2,1)S(1)}, u32[]{:S(2)}, u32[]{:S(2)}) collective-permute-start(bf16[256,128]{1,0:T(8,128)(2,1)S(1)} %get-tuple-element.52), channel_id=1, source_target_pairs={{0,8},{4,12},{8,0},{12,4},{16,24},{20,28},{24,16},{28,20},{1,9},{5... | collective-permute-start | bytes 196616 | tf_op jit(solution)/shard_map/ppermute | solution.py:451
  25.2 4.3 %collective-permute-start.7 = (bf16[256,128]{1,0:T(8,128)(2,1)S(1)}, bf16[256,128]{1,0:T(8,128)(2,1)S(1)}, u32[]{:S(2)}, u32[]{:S(2)}) collective-permute-start(bf16[256,128]{1,0:T(8,128)(2,1)S(1)} %get-tuple-element.53), channel_id=1, source_target_pairs={{0,16},{4,20},{8,24},{12,28},{16,0},{20,4},{24,8},{28,12},{1,17},{... | collective-permute-start | bytes 196616 | tf_op jit(solution)/shard_map/ppermute | solution.py:451
  29.9 5.9 %collective-permute-start.11 = (bf16[16,16,128]{2,1,0:T(8,128)(2,1)S(1)}, bf16[16,16,128]{2,1,0:T(8,128)(2,1)S(1)}, u32[]{:S(2)}, u32[]{:S(2)}) collective-permute-start(bf16[16,16,128]{2,1,0:T(8,128)(2,1)S(1)} %get-tuple-element.46.refs_0_), channel_id=1, source_target_pairs={{0,24},{4,28},{8,16},{12,20},{16,8},{20,12},{24,0},{28,4},{1,25},{... | collective-permute-start | bytes 196616 | tf_op jit(solution)/shard_map/ppermute | solution.py:451
  31.5 4.7 %collective-permute-start.10 = (bf16[16,16,128]{2,1,0:T(8,128)(2,1)S(1)}, bf16[16,16,128]{2,1,0:T(8,128)(2,1)S(1)}, u32[]{:S(2)}, u32[]{:S(2)}) collective-permute-start(bf16[16,16,128]{2,1,0:T(8,128)(2,1)S(1)} %get-tuple-element.46.refs_0_), channel_id=1, source_target_pairs={{0,16},{4,20},{8,24},{12,28},{16,0},{20,4},{24,8},{28,12},{1,17},{... | collective-permute-start | bytes 196616 | tf_op jit(solution)/shard_map/ppermute | solution.py:451
  33.0 4.3 %collective-permute-start.9 = (bf16[16,16,128]{2,1,0:T(8,128)(2,1)S(1)}, bf16[16,16,128]{2,1,0:T(8,128)(2,1)S(1)}, u32[]{:S(2)}, u32[]{:S(2)}) collective-permute-start(bf16[16,16,128]{2,1,0:T(8,128)(2,1)S(1)} %get-tuple-element.46.refs_0_), channel_id=1, source_target_pairs={{0,8},{4,12},{8,0},{12,4},{16,24},{20,28},{24,16},{28,20},{1,9},{5... | collective-permute-start | bytes 196616 | tf_op jit(solution)/shard_map/ppermute | solution.py:451
  33.5 3.7 %collective-permute-start.12 = (bf16[16,16,128]{2,1,0:T(8,128)(2,1)S(1)}, bf16[16,16,128]{2,1,0:T(8,128)(2,1)S(1)}, u32[]{:S(2)}, u32[]{:S(2)}) collective-permute-start(bf16[16,16,128]{2,1,0:T(8,128)(2,1)S(1)} %get-tuple-element.46.refs_0_), channel_id=1, source_target_pairs={{0,4},{4,0},{8,12},{12,8},{16,20},{20,16},{24,28},{28,24},{1,5},{5... | collective-permute-start | bytes 196616 | tf_op jit(solution)/shard_map/ppermute | solution.py:451
  35.9 1.4 %collective-permute-start.15 = (bf16[16,16,128]{2,1,0:T(8,128)(2,1)S(1)}, bf16[16,16,128]{2,1,0:T(8,128)(2,1)S(1)}, u32[]{:S(2)}, u32[]{:S(2)}) collective-permute-start(bf16[16,16,128]{2,1,0:T(8,128)(2,1)S(1)} %collective-permute-done.11.refs_3_), channel_id=1, source_target_pairs={{0,4},{4,0},{8,12},{12,8},{16,20},{20,16},{24,28},{28,24},{1,5},{5... | collective-permute-start | bytes 196616 | tf_op jit(solution)/shard_map/ppermute | solution.py:451
  36.2 1.3 %collective-permute-start.14 = (bf16[16,16,128]{2,1,0:T(8,128)(2,1)S(1)}, bf16[16,16,128]{2,1,0:T(8,128)(2,1)S(1)}, u32[]{:S(2)}, u32[]{:S(2)}) collective-permute-start(bf16[16,16,128]{2,1,0:T(8,128)(2,1)S(1)} %collective-permute-done.10.refs_2_), channel_id=1, source_target_pairs={{0,4},{4,0},{8,12},{12,8},{16,20},{20,16},{24,28},{28,24},{1,5},{5... | collective-permute-start | bytes 196616 | tf_op jit(solution)/shard_map/ppermute | solution.py:451
  37.2 1.3 %collective-permute-start.13 = (bf16[16,16,128]{2,1,0:T(8,128)(2,1)S(1)}, bf16[16,16,128]{2,1,0:T(8,128)(2,1)S(1)}, u32[]{:S(2)}, u32[]{:S(2)}) collective-permute-start(bf16[16,16,128]{2,1,0:T(8,128)(2,1)S(1)} %collective-permute-done.9.refs_1_), channel_id=1, source_target_pairs={{0,4},{4,0},{8,12},{12,8},{16,20},{20,16},{24,28},{28,24},{1,5},{5... | collective-permute-start | bytes 196616 | tf_op jit(solution)/shard_map/ppermute | solution.py:451
  39.7 5.8 %collective-permute-start.16 = (bf16[128,128]{1,0:T(8,128)(2,1)S(1)}, bf16[128,128]{1,0:T(8,128)(2,1)S(1)}, u32[]{:S(2)}, u32[]{:S(2)}) collective-permute-start(bf16[128,128]{1,0:T(8,128)(2,1)S(1)} %get-tuple-element.47), channel_id=1, source_target_pairs={{0,3},{1,2},{2,1},{3,0},{4,7},{5,6},{6,5},{7,4},{8,11},{9,10},{10,... | collective-permute-start | bytes 98312 | tf_op jit(solution)/shard_map/ppermute | solution.py:451
  41.5 5.0 %collective-permute-start.17 = (bf16[128,128]{1,0:T(8,128)(2,1)S(1)}, bf16[128,128]{1,0:T(8,128)(2,1)S(1)}, u32[]{:S(2)}, u32[]{:S(2)}) collective-permute-start(bf16[128,128]{1,0:T(8,128)(2,1)S(1)} %get-tuple-element.48), channel_id=1, source_target_pairs={{0,2},{1,3},{2,0},{3,1},{4,6},{5,7},{6,4},{7,5},{8,10},{9,11},{10,... | collective-permute-start | bytes 98312 | tf_op jit(solution)/shard_map/ppermute | solution.py:451
  41.6 5.0 %collective-permute-start.18 = (bf16[128,128]{1,0:T(8,128)(2,1)S(1)}, bf16[128,128]{1,0:T(8,128)(2,1)S(1)}, u32[]{:S(2)}, u32[]{:S(2)}) collective-permute-start(bf16[128,128]{1,0:T(8,128)(2,1)S(1)} %get-tuple-element.49), channel_id=1, source_target_pairs={{0,1},{1,0},{2,3},{3,2},{4,5},{5,4},{6,7},{7,6},{8,9},{9,8},{10,11... | collective-permute-start | bytes 98312 | tf_op jit(solution)/shard_map/ppermute | solution.py:451

commit v10 on v9

--- a/solution.py
+++ b/solution.py
@@ -96,8 +96,8 @@
     return values[:, 0].reshape(NF, receivers), values[:, 1].reshape(NF, receivers)
 
 
-def apply_matrix(matrix_refs, vector_ref, kept_ref, gather, store):
-    fields = vector_ref.shape[1]
+def apply_matrix(matrix_refs, vector_refs, kept_ref, gather, core, store):
+    fields = sum(ref.shape[1] for ref in vector_refs)
     rows = fields * 2 * GROUP
     half = matrix_refs[0].shape[1] * matrix_refs[0].shape[2]
     width = half * len(matrix_refs)
@@ -110,7 +110,8 @@
     span = kept_ref.shape[1] // width
 
     for group in range(NG):
-        vector = vector_ref[group].reshape(rows, vector_ref.shape[-1])
+        vector = [ref[group].reshape(-1, ref.shape[-1]) for ref in vector_refs]
+        vector = vector[0] if len(vector) == 1 else jnp.concatenate(vector, axis=0)
         matrix = [ref[group].reshape(half, ref.shape[-1]) for ref in matrix_refs]
         matrix = matrix[0] if len(matrix) == 1 else jnp.concatenate(matrix, axis=0)
         full = mm(vector, matrix, NT_DIMS)
@@ -126,10 +127,18 @@
         for one in range(2):
             place, lane = one // span * rows, one % span * LANES
             part = spread[place : place + rows, lane : lane + LANES]
-            part = part.reshape(sets, members, 2, GROUP, LANES)
-            value = part[:, 0, 0]
-            for block in range(1, blocks):
-                value = jnp.where(block_of == block, part[:, block % members, block // members], value)
+            if len(vector_refs) == 2:
+                part = part.reshape(2, sets, 2, GROUP, LANES)
+                ours = block_of % 2 == core
+                real = jnp.where(ours, part[0, :, 0], part[1, :, 0])
+                imag = jnp.where(ours, part[0, :, 1], part[1, :, 1])
+                value = jnp.where(block_of < 2, real, imag)
+            else:
+                part = part.reshape(sets, members, 2, GROUP, LANES)
+                value = part[:, 0, 0]
+                for block in range(1, blocks):
+                    term = part[:, block % members, block // members]
+                    value = jnp.where(block_of == block, term, value)
             both.append(value)
         store(couple * 2 * GROUP, jnp.concatenate(both, axis=1).astype(BF16))
 
@@ -192,7 +201,7 @@
         for one in range(sets):
             sum_ref[one * NF + row : one * NF + row + 2 * GROUP, :] = value[one]
 
-    apply_matrix([matrix_ref], vector_ref, kept_ref, gather, store)
+    apply_matrix([matrix_ref], [vector_ref], kept_ref, gather, None, store)
     own = onset_ref[...].astype(F32)[:, first : first + half]
     turns = LANES // (2 * half)
     own = jnp.concatenate([own[0:1], own[1:2]] * turns, axis=1)
@@ -378,25 +387,31 @@
     plus_ref[...] = interleave(spectra[:NF], spectra[NF:]).astype(BF16)
 
 
+def place_fields(field_refs, vector_ref):
+    chip = lax.axis_index("shot") // 2
+    for distance, field_ref in enumerate(field_refs):
+        slot = (chip ^ distance) ^ lax.axis_index("rcv")
+        store_vector(vector_ref, slot, *unpack(field_ref))
+
+
+def near_kernel(*refs):
+    place_fields(refs[:-1], refs[-1])
+
+
 def second_kernel(pairs, *refs):
-    near_refs, far_refs = refs[:pairs], refs[pairs : 2 * pairs]
-    first_ref, rest_ref, gather_ref = refs[2 * pairs : 2 * pairs + 3]
-    sum_refs = refs[2 * pairs + 3 : -2]
-    vector_ref, kept_ref = refs[-2:]
-    shot_index = lax.axis_index("shot")
-    rcv_index = lax.axis_index("rcv")
-    core = shot_index % 2
-    chip = shot_index // 2
-    for distance in range(pairs):
-        slot = (chip ^ distance) ^ rcv_index
-        store_vector(vector_ref, 2 * slot + core, *unpack(near_refs[distance]))
-        store_vector(vector_ref, 2 * slot + 1 - core, *unpack(far_refs[distance]))
+    first_ref, rest_ref, gather_ref, near_ref = refs[pairs : pairs + 4]
+    sum_refs = refs[pairs + 4 : -2]
+    far_ref, kept_ref = refs[-2:]
+    place_fields(refs[:pairs], far_ref)
 
     def store(row, value):
         for slot in range(pairs):
             sum_refs[slot][row : row + 2 * GROUP, :] = value[slot]
 
-    apply_matrix([first_ref, rest_ref], vector_ref, kept_ref, gather_ref[...], store)
+    core = lax.axis_index("shot") % 2
+    apply_matrix(
+        [first_ref, rest_ref], [near_ref, far_ref], kept_ref, gather_ref[...], core, store
+    )
 
 
 def final_kernel(*refs):
@@ -514,13 +529,22 @@
         work=3.0e9,
     )(traces, *loaded, start)
 
+    distances = [1 << step for step in range(rcv_count.bit_length() - 1)]
+    routes = [(distances, distances), (distances, distances[::-1])]
+
+    def hop(value, step, route):
+        pairs_of = [
+            (shot * rcv_count + rcv, shot * rcv_count + (rcv ^ route[shot % 2][step]))
+            for shot in range(shot_count)
+            for rcv in range(rcv_count)
+        ]
+        return lax.ppermute(value, ("shot", "rcv"), pairs_of)
+
     mine = [first_sum, rest_sum]
-    other = [exchange(value, "rcv", 1) for value in mine]
-    distance = 1
-    while 2 * distance < rcv_count:
-        distance *= 2
+    other = [hop(value, 0, route) for value, route in zip(mine, routes)]
+    for step in range(1, len(distances)):
         mine = [add_rounded(left, right) for left, right in zip(mine, other)]
-        other = [exchange(value, "rcv", distance) for value in mine]
+        other = [hop(value, step, route) for value, route in zip(mine, routes)]
 
     echo = shape((NG, 2, pairs, 2 * GROUP, half * GROUP), BF16)
     shared = (forward, tables["inverse"], tables["spread"])
@@ -568,16 +592,18 @@
         near.append(exchange(plus, "shot", 2 * distance))
     far = [exchange(value, "shot", 1) for value in near]
 
+    half_vector = shape((NG, pairs, 2 * GROUP, 2 * receivers), BF16)
+    near_vector = call(near_kernel, "near", half_vector, vmem(pairs), work=0.3e9)(*near)
     parts = call(
         functools.partial(second_kernel, pairs),
         "second",
         [shape((NF, LANES), BF16)] * pairs,
-        vmem(2 * pairs + 3),
+        vmem(pairs + 4),
         [
-            buffer(vector),
+            buffer(half_vector),
             pltpu.VMEM((NG * focal_total * 2 * GROUP, sources * GROUP), BF16),
         ],
-    )(*near, *far, first, rest, tables["gather"])
+    )(*far, first, rest, tables["gather"], near_vector)
 
     parts = [
         exchange(parts[distance], "rcv", distance) for distance in reversed(range(1, rcv_count))

time: 47.6 us -> 47.5 us (level)
    ppermute x0 -> x4, starting transfers between devices: none -> 8.8 us  [hop(): return lax.ppermute(value, ('shot', 'rcv'), pairs_of)]
    ppermute x19 -> x15, starting transfers between devices: 20.9 us -> 12.4 us  [exchange(): lax.ppermute(value, axis, [(place, place ^ distance) for place in range(c...]
    ppermute x19 -> x15, waiting for transfers between devices: 14.7 us -> 10.2 us  [exchange(): lax.ppermute(value, axis, [(place, place ^ distance) for place in range(c...]
    ppermute x0 -> x4, waiting for transfers between devices: none -> 4.12 us  [hop(): return lax.ppermute(value, ('shot', 'rcv'), pairs_of)]
  transfers between devices with their start and end apart: 19 -> 19, of which waited for: 14 -> 16; matrix products, arithmetic and copies ran while one was open for 0% -> 0% of each run, Pallas kernels for 8% -> 8%
where the time goes in v10:
time: 47.5 us; the launch traced here: 47.3 us
  starting transfers between devices  21.2 us (45%)
  waiting for transfers between devices  14.3 us (30%)
  Pallas kernels  10.9 us (23%)
  between operations  0.76 us (2%)
    ppermute x15, starting transfers between devices, exchange(): lax.ppermute(value, axis, [(place, place ^ distance) for place in range(c...  12.4 us
    ppermute x15, waiting for transfers between devices, exchange(): lax.ppermute(value, axis, [(place, place ^ distance) for place in range(c...  10.2 us
    ppermute x4, starting transfers between devices, hop(): return lax.ppermute(value, ('shot', 'rcv'), pairs_of)  8.8 us
    ppermute x4, waiting for transfers between devices, hop(): return lax.ppermute(value, ('shot', 'rcv'), pairs_of)  4.12 us
    pallas_call x1, Pallas kernels, body(): call(functools.partial(first_kernel, gain), 'first', [half_matrix, half_s...  3.45 us
    pallas_call x1, Pallas kernels, body(): call(functools.partial(rest_kernel, gain), 'rest', (half_matrix, half_sum...  1.74 us
    pallas_call x2, Pallas kernels, emit(): call(emit_kernel, 'emit', jax.ShapeDtypeStruct(field.shape, field.dtype),...  1.3 us
    pallas_call x1, Pallas kernels, body(): call(functools.partial(second_kernel, pairs), 'second', [shape((NF, LANES...  1.14 us
  transfers between devices with their start and end apart: 19, of which 16 were waited for; matrix products, arithmetic and copies ran while one was open for 0% of the time, Pallas kernels for 8%

profile of v10, /device:TPU:0, one launch (start us, length us, event | category | flops | bytes accessed | tf_op | source)
XLA Modules:
  0.0 47.3 jit_solution(13831795324643963100)
XLA Ops:
  0.6 0.0 copy-start
  0.6 3.5 %first.1 = (bf16[16,8,16,256]{3,2,1,0:T(8,128)(2,1)S(1)}, bf16[256,128]{1,0:T(8,128)(2,1)S(1)}, bf16[128,256]{1,0:T(8,128)(2,1)S(1)}, bf16[16,8,16,256]{3,2,1,0:...) custom-call(bf16[32,128,256]{2,1,0:T(8,128)(2,1)} %traces_ref.1, ...), custom_call_target="tpu_custom_call" | custom-call | flops 4000000000 | bytes 1048576 | tf_op jit(solution)/shard_map/first/pallas_call | solution.py:501
  4.1 3.1 %collective-permute-start.2 = (bf16[256,128]{1,0:T(8,128)(2,1)S(1)}, bf16[256,128]{1,0:T(8,128)(2,1)S(1)}, u32[]{:S(2)}, u32[]{:S(2)}) collective-permute-start(bf16[256,128]{1,0:T(8,128)(2,1)S(1)} %get-tuple-element.35), channel_id=1, source_target_pairs={{0,1},{1,0},{2,3},{3,2},{4,5},{5,4},{6,7},{7,6},{8,9},{9,8},{10,11... | collective-permute-start | bytes 196616 | tf_op jit(solution)/shard_map/ppermute | solution.py:541
  7.2 0.0 copy-done
  7.2 0.0 copy-start.2
  7.2 0.0 copy-start.3
  7.2 1.7 %rest.1 = (bf16[16,8,16,256]{3,2,1,0:T(8,128)(2,1)S(1)}, bf16[256,128]{1,0:T(8,128)(2,1)S(1)}) custom-call(bf16[32,128,256]{2,1,0:T(8,128)(2,1)S(1)} %copy-done, s32[32,128]{1,0:T(8,128)S(1)} %get-tuple-element.27.shift_ref, f32[32,64]{1,0:T(8,128)S(1)} %get-tuple-element.28.deconv_ref, s32[2,32]{1,0:T(2,128)S(1)} %get-tuple-element.29.onset_ref.refs_4_, ...), custom_call_target="tpu_custom_call" | custom-call | flops 3000000000 | bytes 1048576 | tf_op jit(solution)/shard_map/rest/pallas_call | solution.py:523
  8.9 0.1 collective-permute-start
  9.1 0.4 collective-permute-done.2
  9.5 3.1 %collective-permute-start.3 = (bf16[256,128]{1,0:T(8,128)(2,1)S(1)}, bf16[256,128]{1,0:T(8,128)(2,1)S(1)}, u32[]{:S(2)}, u32[]{:S(2)}) collective-permute-start(bf16[256,128]{1,0:T(8,128)(2,1)S(1)} %add_convert_fusion.3.mine_ref), channel_id=1, source_target_pairs={{0,2},{1,3},{2,0},{3,1},{4,6},{5,7},{6,4},{7,5},{8,10},{9,11},{10,... | collective-permute-start | bytes 196616 | tf_op jit(solution)/shard_map/ppermute | solution.py:541
  12.6 1.3 %collective-permute-done = bf16[256,128]{1,0:T(8,128)(2,1)S(1)} collective-permute-done((bf16[256,128]{1,0:T(8,128)(2,1)S(1)}, bf16[256,128]{1,0:T(8,128)(2,1)S(1)}, u32[]{:S(2)}, u32[]{:S(2)}) %collective-permute-start) | collective-permute-done | bytes 65568 | tf_op jit(solution)/shard_map/ppermute | solution.py:541
  14.0 2.5 %collective-permute-start.1 = (bf16[256,128]{1,0:T(8,128)(2,1)S(1)}, bf16[256,128]{1,0:T(8,128)(2,1)S(1)}, u32[]{:S(2)}, u32[]{:S(2)}) collective-permute-start(bf16[256,128]{1,0:T(8,128)(2,1)S(1)} %add_convert_fusion.4.mine_ref), channel_id=1, source_target_pairs={{0,2},{1,3},{2,0},{3,1},{4,5},{5,4},{6,7},{7,6},{8,10},{9,11},{10,... | collective-permute-start | bytes 196616 | tf_op jit(solution)/shard_map/ppermute | solution.py:541
  16.4 0.4 collective-permute-done.3.other_ref
  16.8 0.0 copy-done.2
  16.8 0.0 copy-done.3
  16.8 0.7 %mute.1 = (bf16[16,2,4,16,128]{4,3,2,1,0:T(8,128)(2,1)S(1)}, f32[2,16,256]{2,1,0:T(8,128)S(1)}) custom-call(bf16[256,128]{1,0:T(8,128)(2,1)S(1)} %add_convert_fusion.3.mine_ref, bf16[256,128]{1,0:T(8,128)(2,1)S(1)} %collective-permute-done.3.other_ref, bf16[256,256]{1,0:T(8,128)(2,1)S(1)} %get-tuple-element.30.forward_ref.refs_6_, ...), custom_call_target="tpu_custom_call" | custom-call | flops 1000000000 | bytes 1048576 | tf_op jit(solution)/shard_map/mute/pallas_call | solution.py:551
  17.5 2.1 %collective-permute-done.1.other_ref = bf16[256,128]{1,0:T(8,128)(2,1)S(1)} collective-permute-done((bf16[256,128]{1,0:T(8,128)(2,1)S(1)}, bf16[256,128]{1,0:T(8,128)(2,1)S(1)}, u32[]{:S(2)}, u32[]{:S(2)}) %collective-permute-start.1) | collective-permute-done | bytes 65568 | tf_op jit(solution)/shard_map/ppermute | solution.py:541
  19.5 0.0 copy-start.1
  19.5 1.1 %adjoint.1 = (bf16[4,256,128]{2,1,0:T(8,128)(2,1)S(1)}, bf16[256,128]{1,0:T(8,128)(2,1)S(1)}, bf16[3,256,128]{2,1,0:T(8,128)(2,1)S(1)}, f32[2,32,256]{2,1,0:T(8,128)S(1)}) custom-call(bf16[256,128]{1,0:T(8,128)(2,1)S(1)} %add_convert_fusion.4.mine_ref, bf16[256,128]{1,0:T(8,128)(2,1)S(1)} %collective-permute-done.1.other_ref, ...), custom_call_target="tpu_custom_call" | custom-call | flops 2000000000 | bytes 1048576 | tf_op jit(solution)/shard_map/adjoint/pallas_call | solution.py:559
  20.7 0.1 collective-permute-start.4
  20.7 0.5 %collective-permute-start.6 = (bf16[3,256,128]{2,1,0:T(8,128)(2,1)S(1)}, bf16[3,256,128]{2,1,0:T(8,128)(2,1)S(1)}, u32[]{:S(2)}, u32[]{:S(2)}) collective-permute-start(bf16[3,256,128]{2,1,0:T(8,128)(2,1)S(1)} %get-tuple-element.43), channel_id=1, source_target_pairs={{0,4},{4,0},{8,12},{12,8},{16,20},{20,16},{24,28},{28,24},{1,5},{5... | collective-permute-start | bytes 589832 | tf_op jit(solution)/shard_map/ppermute | solution.py:466
  21.2 0.7 %collective-permute-done.4 = bf16[256,128]{1,0:T(8,128)(2,1)S(1)} collective-permute-done((bf16[256,128]{1,0:T(8,128)(2,1)S(1)}, bf16[256,128]{1,0:T(8,128)(2,1)S(1)}, u32[]{:S(2)}, u32[]{:S(2)}) %collective-permute-start.4) | collective-permute-done | bytes 65568 | tf_op jit(solution)/shard_map/ppermute | solution.py:466
  22.0 2.5 %collective-permute-start.5 = (bf16[256,128]{1,0:T(8,128)(2,1)S(1)}, bf16[256,128]{1,0:T(8,128)(2,1)S(1)}, u32[]{:S(2)}, u32[]{:S(2)}) collective-permute-start(bf16[256,128]{1,0:T(8,128)(2,1)S(1)} %fusion), channel_id=1, source_target_pairs={{0,24},{4,28},{8,16},{12,20},{16,8},{20,12},{24,0},{28,4},{1,25},{... | collective-permute-start | bytes 196616 | tf_op jit(solution)/shard_map/ppermute | solution.py:466
  24.5 0.0 collective-permute-done.6
  24.5 0.1 fusion.3
  24.6 0.6 %collective-permute-start.8 = (bf16[256,128]{1,0:T(8,128)(2,1)S(1)}, bf16[256,128]{1,0:T(8,128)(2,1)S(1)}, u32[]{:S(2)}, u32[]{:S(2)}) collective-permute-start(bf16[256,128]{1,0:T(8,128)(2,1)S(1)} %get-tuple-element.52), channel_id=1, source_target_pairs={{0,8},{4,12},{8,0},{12,4},{16,24},{20,28},{24,16},{28,20},{1,9},{5... | collective-permute-start | bytes 196616 | tf_op jit(solution)/shard_map/ppermute | solution.py:466
  25.2 0.5 %collective-permute-start.7 = (bf16[256,128]{1,0:T(8,128)(2,1)S(1)}, bf16[256,128]{1,0:T(8,128)(2,1)S(1)}, u32[]{:S(2)}, u32[]{:S(2)}) collective-permute-start(bf16[256,128]{1,0:T(8,128)(2,1)S(1)} %get-tuple-element.53), channel_id=1, source_target_pairs={{0,16},{4,20},{8,24},{12,28},{16,0},{20,4},{24,8},{28,12},{1,17},{... | collective-permute-start | bytes 196616 | tf_op jit(solution)/shard_map/ppermute | solution.py:466
  25.7 1.8 %collective-permute-done.5.refs_0_ = bf16[256,128]{1,0:T(8,128)(2,1)S(1)} collective-permute-done((bf16[256,128]{1,0:T(8,128)(2,1)S(1)}, bf16[256,128]{1,0:T(8,128)(2,1)S(1)}, u32[]{:S(2)}, u32[]{:S(2)}) %collective-permute-start.5) | collective-permute-done | bytes 65568 | tf_op jit(solution)/shard_map/ppermute | solution.py:466
  27.5 1.4 %collective-permute-done.8.refs_2_ = bf16[256,128]{1,0:T(8,128)(2,1)S(1)} collective-permute-done((bf16[256,128]{1,0:T(8,128)(2,1)S(1)}, bf16[256,128]{1,0:T(8,128)(2,1)S(1)}, u32[]{:S(2)}, u32[]{:S(2)}) %collective-permute-start.8) | collective-permute-done | bytes 65568 | tf_op jit(solution)/shard_map/ppermute | solution.py:466
  28.9 0.5 %collective-permute-done.7.refs_1_ = bf16[256,128]{1,0:T(8,128)(2,1)S(1)} collective-permute-done((bf16[256,128]{1,0:T(8,128)(2,1)S(1)}, bf16[256,128]{1,0:T(8,128)(2,1)S(1)}, u32[]{:S(2)}, u32[]{:S(2)}) %collective-permute-start.7) | collective-permute-done | bytes 65568 | tf_op jit(solution)/shard_map/ppermute | solution.py:466
  29.5 0.0 copy-done.1
  29.5 0.0 copy-start.4
  29.5 0.5 downgoing.1
  29.9 1.6 %collective-permute-start.14 = (bf16[16,16,128]{2,1,0:T(8,128)(2,1)S(1)}, bf16[16,16,128]{2,1,0:T(8,128)(2,1)S(1)}, u32[]{:S(2)}, u32[]{:S(2)}) collective-permute-start(bf16[16,16,128]{2,1,0:T(8,128)(2,1)S(1)} %get-tuple-element.46.refs_0_), channel_id=1, source_target_pairs={{0,24},{4,28},{8,16},{12,20},{16,8},{20,12},{24,0},{28,4},{1,25},{... | collective-permute-start | bytes 196616 | tf_op jit(solution)/shard_map/ppermute | solution.py:466
  31.5 1.4 %collective-permute-start.12 = (bf16[16,16,128]{2,1,0:T(8,128)(2,1)S(1)}, bf16[16,16,128]{2,1,0:T(8,128)(2,1)S(1)}, u32[]{:S(2)}, u32[]{:S(2)}) collective-permute-start(bf16[16,16,128]{2,1,0:T(8,128)(2,1)S(1)} %get-tuple-element.46.refs_0_), channel_id=1, source_target_pairs={{0,16},{4,20},{8,24},{12,28},{16,0},{20,4},{24,8},{28,12},{1,17},{... | collective-permute-start | bytes 196616 | tf_op jit(solution)/shard_map/ppermute | solution.py:466
  33.0 0.5 %collective-permute-start.10 = (bf16[16,16,128]{2,1,0:T(8,128)(2,1)S(1)}, bf16[16,16,128]{2,1,0:T(8,128)(2,1)S(1)}, u32[]{:S(2)}, u32[]{:S(2)}) collective-permute-start(bf16[16,16,128]{2,1,0:T(8,128)(2,1)S(1)} %get-tuple-element.46.refs_0_), channel_id=1, source_target_pairs={{0,8},{4,12},{8,0},{12,4},{16,24},{20,28},{24,16},{28,20},{1,9},{5... | collective-permute-start | bytes 196616 | tf_op jit(solution)/shard_map/ppermute | solution.py:466
  33.5 0.0 collective-permute-start.9
  33.5 2.4 %collective-permute-done.14.refs_3_ = bf16[16,16,128]{2,1,0:T(8,128)(2,1)S(1)} collective-permute-done((bf16[16,16,128]{2,1,0:T(8,128)(2,1)S(1)}, bf16[16,16,128]{2,1,0:T(8,128)(2,1)S(1)}, u32[]{:S(2)}, u32[]{:S(2)}) %collective-permute-start.14) | collective-permute-done | bytes 65568 | tf_op jit(solution)/shard_map/ppermute | solution.py:466
  35.9 0.0 collective-permute-start.15
  35.9 0.3 collective-permute-done.12.refs_2_
  36.2 0.2 collective-permute-start.13
  36.4 0.8 %collective-permute-done.10.refs_1_ = bf16[16,16,128]{2,1,0:T(8,128)(2,1)S(1)} collective-permute-done((bf16[16,16,128]{2,1,0:T(8,128)(2,1)S(1)}, bf16[16,16,128]{2,1,0:T(8,128)(2,1)S(1)}, u32[]{:S(2)}, u32[]{:S(2)}) %collective-permute-start.10) | collective-permute-done | bytes 65568 | tf_op jit(solution)/shard_map/ppermute | solution.py:466
  37.2 0.0 collective-permute-start.11
  37.2 0.1 near.1.refs_7_
  37.3 0.0 collective-permute-done.9.refs_0_
  37.3 0.0 collective-permute-done.15.refs_3_
  37.3 0.1 collective-permute-done.13.refs_2_
  37.4 1.0 %collective-permute-done.11.refs_1_ = bf16[16,16,128]{2,1,0:T(8,128)(2,1)S(1)} collective-permute-done((bf16[16,16,128]{2,1,0:T(8,128)(2,1)S(1)}, bf16[16,16,128]{2,1,0:T(8,128)(2,1)S(1)}, u32[]{:S(2)}, u32[]{:S(2)}) %collective-permute-start.11) | collective-permute-done | bytes 65568 | tf_op jit(solution)/shard_map/ppermute | solution.py:466
  38.5 0.0 copy-done.4
  38.5 1.1 %second.1 = (bf16[128,128]{1,0:T(8,128)(2,1)S(1)}, bf16[128,128]{1,0:T(8,128)(2,1)S(1)}, bf16[128,128]{1,0:T(8,128)(2,1)S(1)}, bf16[128,128]{1,0:T(8,128)(2,1)S(1)}) custom-call(bf16[16,16,128]{2,1,0:T(8,128)(2,1)S(1)} %collective-permute-done.9.refs_0_, bf16[16,16,128]{2,1,0:T(8,128)(2,1)S(1)} %collective-permute-done.11.refs_1_, ...), custom_call_target="tpu_custom_call" | custom-call | flops 1000000000 | bytes 1048576 | tf_op jit(solution)/shard_map/second/pallas_call | solution.py:597
  39.6 1.8 %collective-permute-start.16 = (bf16[128,128]{1,0:T(8,128)(2,1)S(1)}, bf16[128,128]{1,0:T(8,128)(2,1)S(1)}, u32[]{:S(2)}, u32[]{:S(2)}) collective-permute-start(bf16[128,128]{1,0:T(8,128)(2,1)S(1)} %get-tuple-element.47), channel_id=1, source_target_pairs={{0,3},{1,2},{2,1},{3,0},{4,7},{5,6},{6,5},{7,4},{8,11},{9,10},{10,... | collective-permute-start | bytes 98312 | tf_op jit(solution)/shard_map/ppermute | solution.py:466
  41.4 0.4 collective-permute-start.17
  41.8 2.3 %collective-permute-start.18 = (bf16[128,128]{1,0:T(8,128)(2,1)S(1)}, bf16[128,128]{1,0:T(8,128)(2,1)S(1)}, u32[]{:S(2)}, u32[]{:S(2)}) collective-permute-start(bf16[128,128]{1,0:T(8,128)(2,1)S(1)} %get-tuple-element.49), channel_id=1, source_target_pairs={{0,1},{1,0},{2,3},{3,2},{4,5},{5,4},{6,7},{7,6},{8,9},{9,8},{10,11... | collective-permute-start | bytes 98312 | tf_op jit(solution)/shard_map/ppermute | solution.py:466
  44.1 0.6 %emit.2 = f32[2,32,256]{2,1,0:T(8,128)} custom-call(f32[2,32,256]{2,1,0:T(8,128)S(1)} %get-tuple-element.40.field_ref), custom_call_target="tpu_custom_call" | custom-call | flops 300000000 | bytes 1048576 | tf_op jit(solution)/shard_map/emit/pallas_call | solution.py:459
  44.7 0.7 %emit.3 = f32[1,128,256]{2,1,0:T(8,128)} custom-call(f32[1,128,256]{2,1,0:T(8,128)S(1)} %get-tuple-element.45.field_ref), custom_call_target="tpu_custom_call" | custom-call | flops 300000000 | bytes 1048576 | tf_op jit(solution)/shard_map/emit/pallas_call | solution.py:459
  45.4 0.4 collective-permute-done.16.refs_0_
  45.7 0.5 %collective-permute-done.17.refs_1_ = bf16[128,128]{1,0:T(8,128)(2,1)S(1)} collective-permute-done((bf16[128,128]{1,0:T(8,128)(2,1)S(1)}, bf16[128,128]{1,0:T(8,128)(2,1)S(1)}, u32[]{:S(2)}, u32[]{:S(2)}) %collective-permute-start.17) | collective-permute-done | bytes 32800 | tf_op jit(solution)/shard_map/ppermute | solution.py:466
  46.2 0.2 collective-permute-done.18.refs_2_
  46.4 0.9 %final.1 = f32[2,32,256]{2,1,0:T(8,128)} custom-call(bf16[128,128]{1,0:T(8,128)(2,1)S(1)} %collective-permute-done.16.refs_0_, bf16[128,128]{1,0:T(8,128)(2,1)S(1)} %collective-permute-done.17.refs_1_, bf16[128,128]{1,0:T(8,128)(2,1)S(1)} %collective-permute-done.18.refs_2_, bf16[128,128]{1,0:T(8,128)(2,1)S(1)} %get-tuple-element.50.refs_3_, ...), custom_call_target="tpu_custom_call" | custom-call | flops 1000000000 | bytes 1048576 | tf_op jit(solution)/shard_map/final/pallas_call | solution.py:611
  (3 shorter events, 0.1 us)
Async XLA Ops:
  0.6 6.6 %copy-start = (bf16[32,128,256]{2,1,0:T(8,128)(2,1)S(1)}, bf16[32,128,256]{2,1,0:T(8,128)(2,1)}, u32[]{:S(2)}) copy-start(bf16[32,128,256]{2,1,0:T(8,128)(2,1)} %traces_ref.1) | copy-start | bytes 6291460
  4.1 5.3 %collective-permute-start.2 = (bf16[256,128]{1,0:T(8,128)(2,1)S(1)}, bf16[256,128]{1,0:T(8,128)(2,1)S(1)}, u32[]{:S(2)}, u32[]{:S(2)}) collective-permute-start(bf16[256,128]{1,0:T(8,128)(2,1)S(1)} %get-tuple-element.35), channel_id=1, source_target_pairs={{0,1},{1,0},{2,3},{3,2},{4,5},{5,4},{6,7},{7,6},{8,9},{9,8},{10,11... | collective-permute-start | bytes 196616 | tf_op jit(solution)/shard_map/ppermute | solution.py:541
  7.2 9.6 %copy-start.2 = (bf16[2,4,128,256]{3,2,1,0:T(8,128)(2,1)S(1)}, bf16[2,4,128,256]{3,2,1,0:T(8,128)(2,1)}, u32[]{:S(2)}) copy-start(bf16[2,4,128,256]{3,2,1,0:T(8,128)(2,1)} %constant.23.spread_ref) | copy-start | bytes 1572868
  7.2 9.6 %copy-start.3 = (bf16[256,256]{1,0:T(8,128)(2,1)S(1)}, bf16[256,256]{1,0:T(8,128)(2,1)}, u32[]{:S(2)}) copy-start(bf16[256,256]{1,0:T(8,128)(2,1)} %constant.22.inverse_ref.refs_7_.refs_5_) | copy-start | bytes 393220
  8.9 5.0 %collective-permute-start = (bf16[256,128]{1,0:T(8,128)(2,1)S(1)}, bf16[256,128]{1,0:T(8,128)(2,1)S(1)}, u32[]{:S(2)}, u32[]{:S(2)}) collective-permute-start(bf16[256,128]{1,0:T(8,128)(2,1)S(1)} %get-tuple-element.34), channel_id=1, source_target_pairs={{0,1},{1,0},{2,3},{3,2},{4,6},{5,7},{6,4},{7,5},{8,9},{9,8},{10,11... | collective-permute-start | bytes 196616 | tf_op jit(solution)/shard_map/ppermute | solution.py:541
  9.5 7.3 %collective-permute-start.3 = (bf16[256,128]{1,0:T(8,128)(2,1)S(1)}, bf16[256,128]{1,0:T(8,128)(2,1)S(1)}, u32[]{:S(2)}, u32[]{:S(2)}) collective-permute-start(bf16[256,128]{1,0:T(8,128)(2,1)S(1)} %add_convert_fusion.3.mine_ref), channel_id=1, source_target_pairs={{0,2},{1,3},{2,0},{3,1},{4,6},{5,7},{6,4},{7,5},{8,10},{9,11},{10,... | collective-permute-start | bytes 196616 | tf_op jit(solution)/shard_map/ppermute | solution.py:541
  14.0 5.6 %collective-permute-start.1 = (bf16[256,128]{1,0:T(8,128)(2,1)S(1)}, bf16[256,128]{1,0:T(8,128)(2,1)S(1)}, u32[]{:S(2)}, u32[]{:S(2)}) collective-permute-start(bf16[256,128]{1,0:T(8,128)(2,1)S(1)} %add_convert_fusion.4.mine_ref), channel_id=1, source_target_pairs={{0,2},{1,3},{2,0},{3,1},{4,5},{5,4},{6,7},{7,6},{8,10},{9,11},{10,... | collective-permute-start | bytes 196616 | tf_op jit(solution)/shard_map/ppermute | solution.py:541
  19.5 9.9 %copy-start.1 = (s32[1,128]{1,0:T(1,128)S(1)}, s32[1,128]{1,0:T(1,128)}, u32[]{:S(2)}) copy-start(s32[1,128]{1,0:T(1,128)} %refs_5_.1) | copy-start | bytes 1540
  20.7 1.3 %collective-permute-start.4 = (bf16[256,128]{1,0:T(8,128)(2,1)S(1)}, bf16[256,128]{1,0:T(8,128)(2,1)S(1)}, u32[]{:S(2)}, u32[]{:S(2)}) collective-permute-start(bf16[256,128]{1,0:T(8,128)(2,1)S(1)} %get-tuple-element.42), channel_id=1, source_target_pairs={{0,4},{4,0},{8,12},{12,8},{16,20},{20,16},{24,28},{28,24},{1,5},{5... | collective-permute-start | bytes 196616 | tf_op jit(solution)/shard_map/ppermute | solution.py:466
  20.7 3.8 %collective-permute-start.6 = (bf16[3,256,128]{2,1,0:T(8,128)(2,1)S(1)}, bf16[3,256,128]{2,1,0:T(8,128)(2,1)S(1)}, u32[]{:S(2)}, u32[]{:S(2)}) collective-permute-start(bf16[3,256,128]{2,1,0:T(8,128)(2,1)S(1)} %get-tuple-element.43), channel_id=1, source_target_pairs={{0,4},{4,0},{8,12},{12,8},{16,20},{20,16},{24,28},{28,24},{1,5},{5... | collective-permute-start | bytes 589832 | tf_op jit(solution)/shard_map/ppermute | solution.py:466
  22.0 5.5 %collective-permute-start.5 = (bf16[256,128]{1,0:T(8,128)(2,1)S(1)}, bf16[256,128]{1,0:T(8,128)(2,1)S(1)}, u32[]{:S(2)}, u32[]{:S(2)}) collective-permute-start(bf16[256,128]{1,0:T(8,128)(2,1)S(1)} %fusion), channel_id=1, source_target_pairs={{0,24},{4,28},{8,16},{12,20},{16,8},{20,12},{24,0},{28,4},{1,25},{... | collective-permute-start | bytes 196616 | tf_op jit(solution)/shard_map/ppermute | solution.py:466
  24.6 4.3 %collective-permute-start.8 = (bf16[256,128]{1,0:T(8,128)(2,1)S(1)}, bf16[256,128]{1,0:T(8,128)(2,1)S(1)}, u32[]{:S(2)}, u32[]{:S(2)}) collective-permute-start(bf16[256,128]{1,0:T(8,128)(2,1)S(1)} %get-tuple-element.52), channel_id=1, source_target_pairs={{0,8},{4,12},{8,0},{12,4},{16,24},{20,28},{24,16},{28,20},{1,9},{5... | collective-permute-start | bytes 196616 | tf_op jit(solution)/shard_map/ppermute | solution.py:466
  25.2 4.3 %collective-permute-start.7 = (bf16[256,128]{1,0:T(8,128)(2,1)S(1)}, bf16[256,128]{1,0:T(8,128)(2,1)S(1)}, u32[]{:S(2)}, u32[]{:S(2)}) collective-permute-start(bf16[256,128]{1,0:T(8,128)(2,1)S(1)} %get-tuple-element.53), channel_id=1, source_target_pairs={{0,16},{4,20},{8,24},{12,28},{16,0},{20,4},{24,8},{28,12},{1,17},{... | collective-permute-start | bytes 196616 | tf_op jit(solution)/shard_map/ppermute | solution.py:466
  29.5 9.0 %copy-start.4 = (bf16[256,128]{1,0:T(8,128)(2,1)S(1)}, bf16[256,128]{1,0:T(8,128)(2,1)}, u32[]{:S(2)}) copy-start(bf16[256,128]{1,0:T(8,128)(2,1)} %constant.24.refs_6_) | copy-start | bytes 196612
  29.9 5.9 %collective-permute-start.14 = (bf16[16,16,128]{2,1,0:T(8,128)(2,1)S(1)}, bf16[16,16,128]{2,1,0:T(8,128)(2,1)S(1)}, u32[]{:S(2)}, u32[]{:S(2)}) collective-permute-start(bf16[16,16,128]{2,1,0:T(8,128)(2,1)S(1)} %get-tuple-element.46.refs_0_), channel_id=1, source_target_pairs={{0,24},{4,28},{8,16},{12,20},{16,8},{20,12},{24,0},{28,4},{1,25},{... | collective-permute-start | bytes 196616 | tf_op jit(solution)/shard_map/ppermute | solution.py:466
  31.5 4.7 %collective-permute-start.12 = (bf16[16,16,128]{2,1,0:T(8,128)(2,1)S(1)}, bf16[16,16,128]{2,1,0:T(8,128)(2,1)S(1)}, u32[]{:S(2)}, u32[]{:S(2)}) collective-permute-start(bf16[16,16,128]{2,1,0:T(8,128)(2,1)S(1)} %get-tuple-element.46.refs_0_), channel_id=1, source_target_pairs={{0,16},{4,20},{8,24},{12,28},{16,0},{20,4},{24,8},{28,12},{1,17},{... | collective-permute-start | bytes 196616 | tf_op jit(solution)/shard_map/ppermute | solution.py:466
  33.0 4.3 %collective-permute-start.10 = (bf16[16,16,128]{2,1,0:T(8,128)(2,1)S(1)}, bf16[16,16,128]{2,1,0:T(8,128)(2,1)S(1)}, u32[]{:S(2)}, u32[]{:S(2)}) collective-permute-start(bf16[16,16,128]{2,1,0:T(8,128)(2,1)S(1)} %get-tuple-element.46.refs_0_), channel_id=1, source_target_pairs={{0,8},{4,12},{8,0},{12,4},{16,24},{20,28},{24,16},{28,20},{1,9},{5... | collective-permute-start | bytes 196616 | tf_op jit(solution)/shard_map/ppermute | solution.py:466
  33.5 3.8 %collective-permute-start.9 = (bf16[16,16,128]{2,1,0:T(8,128)(2,1)S(1)}, bf16[16,16,128]{2,1,0:T(8,128)(2,1)S(1)}, u32[]{:S(2)}, u32[]{:S(2)}) collective-permute-start(bf16[16,16,128]{2,1,0:T(8,128)(2,1)S(1)} %get-tuple-element.46.refs_0_), channel_id=1, source_target_pairs={{0,4},{4,0},{8,12},{12,8},{16,20},{20,16},{24,28},{28,24},{1,5},{5... | collective-permute-start | bytes 196616 | tf_op jit(solution)/shard_map/ppermute | solution.py:466
  35.9 1.5 %collective-permute-start.15 = (bf16[16,16,128]{2,1,0:T(8,128)(2,1)S(1)}, bf16[16,16,128]{2,1,0:T(8,128)(2,1)S(1)}, u32[]{:S(2)}, u32[]{:S(2)}) collective-permute-start(bf16[16,16,128]{2,1,0:T(8,128)(2,1)S(1)} %collective-permute-done.14.refs_3_), channel_id=1, source_target_pairs={{0,4},{4,0},{8,12},{12,8},{16,20},{20,16},{24,28},{28,24},{1,5},{5... | collective-permute-start | bytes 196616 | tf_op jit(solution)/shard_map/ppermute | solution.py:466
  36.2 1.3 %collective-permute-start.13 = (bf16[16,16,128]{2,1,0:T(8,128)(2,1)S(1)}, bf16[16,16,128]{2,1,0:T(8,128)(2,1)S(1)}, u32[]{:S(2)}, u32[]{:S(2)}) collective-permute-start(bf16[16,16,128]{2,1,0:T(8,128)(2,1)S(1)} %collective-permute-done.12.refs_2_), channel_id=1, source_target_pairs={{0,4},{4,0},{8,12},{12,8},{16,20},{20,16},{24,28},{28,24},{1,5},{5... | collective-permute-start | bytes 196616 | tf_op jit(solution)/shard_map/ppermute | solution.py:466
  37.2 1.3 %collective-permute-start.11 = (bf16[16,16,128]{2,1,0:T(8,128)(2,1)S(1)}, bf16[16,16,128]{2,1,0:T(8,128)(2,1)S(1)}, u32[]{:S(2)}, u32[]{:S(2)}) collective-permute-start(bf16[16,16,128]{2,1,0:T(8,128)(2,1)S(1)} %collective-permute-done.10.refs_1_), channel_id=1, source_target_pairs={{0,4},{4,0},{8,12},{12,8},{16,20},{20,16},{24,28},{28,24},{1,5},{5... | collective-permute-start | bytes 196616 | tf_op jit(solution)/shard_map/ppermute | solution.py:466
  39.6 6.1 %collective-permute-start.16 = (bf16[128,128]{1,0:T(8,128)(2,1)S(1)}, bf16[128,128]{1,0:T(8,128)(2,1)S(1)}, u32[]{:S(2)}, u32[]{:S(2)}) collective-permute-start(bf16[128,128]{1,0:T(8,128)(2,1)S(1)} %get-tuple-element.47), channel_id=1, source_target_pairs={{0,3},{1,2},{2,1},{3,0},{4,7},{5,6},{6,5},{7,4},{8,11},{9,10},{10,... | collective-permute-start | bytes 98312 | tf_op jit(solution)/shard_map/ppermute | solution.py:466
  41.4 4.9 %collective-permute-start.17 = (bf16[128,128]{1,0:T(8,128)(2,1)S(1)}, bf16[128,128]{1,0:T(8,128)(2,1)S(1)}, u32[]{:S(2)}, u32[]{:S(2)}) collective-permute-start(bf16[128,128]{1,0:T(8,128)(2,1)S(1)} %get-tuple-element.48), channel_id=1, source_target_pairs={{0,2},{1,3},{2,0},{3,1},{4,6},{5,7},{6,4},{7,5},{8,10},{9,11},{10,... | collective-permute-start | bytes 98312 | tf_op jit(solution)/shard_map/ppermute | solution.py:466
  41.8 4.6 %collective-permute-start.18 = (bf16[128,128]{1,0:T(8,128)(2,1)S(1)}, bf16[128,128]{1,0:T(8,128)(2,1)S(1)}, u32[]{:S(2)}, u32[]{:S(2)}) collective-permute-start(bf16[128,128]{1,0:T(8,128)(2,1)S(1)} %get-tuple-element.49), channel_id=1, source_target_pairs={{0,1},{1,0},{2,3},{3,2},{4,5},{5,4},{6,7},{7,6},{8,9},{9,8},{10,11... | collective-permute-start | bytes 98312 | tf_op jit(solution)/shard_map/ppermute | solution.py:466

commit v11 on v10

--- a/solution.py
+++ b/solution.py
@@ -391,6 +391,8 @@
     chip = lax.axis_index("shot") // 2
     for distance, field_ref in enumerate(field_refs):
         slot = (chip ^ distance) ^ lax.axis_index("rcv")
+        swapped = (slot & ~3) | ((slot & 1) << 1) | ((slot >> 1) & 1)
+        slot = jnp.where(lax.axis_index("shot") % 2 == 0, slot, swapped)
         store_vector(vector_ref, slot, *unpack(field_ref))
 
 
@@ -592,6 +594,15 @@
         near.append(exchange(plus, "shot", 2 * distance))
     far = [exchange(value, "shot", 1) for value in near]
 
+    def scatter(value, distance):
+        swapped = (distance & ~3) | ((distance & 1) << 1) | ((distance >> 1) & 1)
+        routes = [
+            (shot * rcv_count + rcv, shot * rcv_count + (rcv ^ (swapped if shot % 2 else distance)))
+            for shot in range(shot_count)
+            for rcv in range(rcv_count)
+        ]
+        return lax.ppermute(value, ("shot", "rcv"), routes)
+
     half_vector = shape((NG, pairs, 2 * GROUP, 2 * receivers), BF16)
     near_vector = call(near_kernel, "near", half_vector, vmem(pairs), work=0.3e9)(*near)
     parts = call(
@@ -606,7 +617,7 @@
     )(*far, first, rest, tables["gather"], near_vector)
 
     parts = [
-        exchange(parts[distance], "rcv", distance) for distance in reversed(range(1, rcv_count))
+        scatter(parts[distance], distance) for distance in reversed(range(1, rcv_count))
     ] + [parts[0]]
     upgoing_second = call(
         final_kernel, "final", shape((2, sources, NT), F32), vmem(len(parts) + 2)

time: 47.5 us -> 48 us (1.011)
  waiting for transfers between devices: 14.3 us -> 14.8 us
    ppermute x15 -> x12, starting transfers between devices: 12.4 us -> 7.94 us  [exchange(): lax.ppermute(value, axis, [(place, place ^ distance) for place in range(c...]
    ppermute x0 -> x3, starting transfers between devices: none -> 4.45 us  [scatter(): return lax.ppermute(value, ('shot', 'rcv'), routes)]
    ppermute x0 -> x3, waiting for transfers between devices: none -> 1.51 us  [scatter(): return lax.ppermute(value, ('shot', 'rcv'), routes)]
    ppermute x15 -> x12, waiting for transfers between devices: 10.2 us -> 9.18 us  [exchange(): lax.ppermute(value, axis, [(place, place ^ distance) for place in range(c...]
  transfers between devices with their start and end apart: 19 -> 19, of which waited for: 16 -> 14; matrix products, arithmetic and copies ran while one was open for 0% -> 0% of each run, Pallas kernels for 8% -> 8%
where the time goes in v11:
time: 48 us; the launch traced here: 47.8 us
  starting transfers between devices  21.2 us (44%)
  waiting for transfers between devices  14.8 us (31%)
  Pallas kernels  10.9 us (23%)
  between operations  0.75 us (2%)
    ppermute x12, waiting for transfers between devices, exchange(): lax.ppermute(value, axis, [(place, place ^ distance) for place in range(c...  9.18 us
    ppermute x4, starting transfers between devices, hop(): return lax.ppermute(value, ('shot', 'rcv'), pairs_of)  8.8 us
    ppermute x12, starting transfers between devices, exchange(): lax.ppermute(value, axis, [(place, place ^ distance) for place in range(c...  7.94 us
    ppermute x3, starting transfers between devices, scatter(): return lax.ppermute(value, ('shot', 'rcv'), routes)  4.45 us
    ppermute x4, waiting for transfers between devices, hop(): return lax.ppermute(value, ('shot', 'rcv'), pairs_of)  4.12 us
    pallas_call x1, Pallas kernels, body(): call(functools.partial(first_kernel, gain), 'first', [half_matrix, half_s...  3.45 us
    pallas_call x1, Pallas kernels, body(): call(functools.partial(rest_kernel, gain), 'rest', (half_matrix, half_sum...  1.74 us
    ppermute x3, waiting for transfers between devices, scatter(): return lax.ppermute(value, ('shot', 'rcv'), routes)  1.51 us
  transfers between devices with their start and end apart: 19, of which 14 were waited for; matrix products, arithmetic and copies ran while one was open for 0% of the time, Pallas kernels for 8%

profile of v11, /device:TPU:0, one launch (start us, length us, event | category | flops | bytes accessed | tf_op | source)
XLA Modules:
  0.0 47.8 jit_solution(2009195952845650841)
XLA Ops:
  0.6 0.0 copy-start
  0.6 3.5 %first.1 = (bf16[16,8,16,256]{3,2,1,0:T(8,128)(2,1)S(1)}, bf16[256,128]{1,0:T(8,128)(2,1)S(1)}, bf16[128,256]{1,0:T(8,128)(2,1)S(1)}, bf16[16,8,16,256]{3,2,1,0:...) custom-call(bf16[32,128,256]{2,1,0:T(8,128)(2,1)} %traces_ref.1, ...), custom_call_target="tpu_custom_call" | custom-call | flops 4000000000 | bytes 1048576 | tf_op jit(solution)/shard_map/first/pallas_call | solution.py:503
  4.1 3.1 %collective-permute-start.2 = (bf16[256,128]{1,0:T(8,128)(2,1)S(1)}, bf16[256,128]{1,0:T(8,128)(2,1)S(1)}, u32[]{:S(2)}, u32[]{:S(2)}) collective-permute-start(bf16[256,128]{1,0:T(8,128)(2,1)S(1)} %get-tuple-element.35), channel_id=1, source_target_pairs={{0,1},{1,0},{2,3},{3,2},{4,5},{5,4},{6,7},{7,6},{8,9},{9,8},{10,11... | collective-permute-start | bytes 196616 | tf_op jit(solution)/shard_map/ppermute | solution.py:543
  7.2 0.0 copy-done
  7.2 0.0 copy-start.2
  7.2 0.0 copy-start.3
  7.2 1.7 %rest.1 = (bf16[16,8,16,256]{3,2,1,0:T(8,128)(2,1)S(1)}, bf16[256,128]{1,0:T(8,128)(2,1)S(1)}) custom-call(bf16[32,128,256]{2,1,0:T(8,128)(2,1)S(1)} %copy-done, s32[32,128]{1,0:T(8,128)S(1)} %get-tuple-element.27.shift_ref, f32[32,64]{1,0:T(8,128)S(1)} %get-tuple-element.28.deconv_ref, s32[2,32]{1,0:T(2,128)S(1)} %get-tuple-element.29.onset_ref.refs_4_, ...), custom_call_target="tpu_custom_call" | custom-call | flops 3000000000 | bytes 1048576 | tf_op jit(solution)/shard_map/rest/pallas_call | solution.py:525
  8.9 0.1 collective-permute-start
  9.1 0.4 collective-permute-done.2
  9.5 3.1 %collective-permute-start.3 = (bf16[256,128]{1,0:T(8,128)(2,1)S(1)}, bf16[256,128]{1,0:T(8,128)(2,1)S(1)}, u32[]{:S(2)}, u32[]{:S(2)}) collective-permute-start(bf16[256,128]{1,0:T(8,128)(2,1)S(1)} %add_convert_fusion.3.mine_ref), channel_id=1, source_target_pairs={{0,2},{1,3},{2,0},{3,1},{4,6},{5,7},{6,4},{7,5},{8,10},{9,11},{10,... | collective-permute-start | bytes 196616 | tf_op jit(solution)/shard_map/ppermute | solution.py:543
  12.6 1.3 %collective-permute-done = bf16[256,128]{1,0:T(8,128)(2,1)S(1)} collective-permute-done((bf16[256,128]{1,0:T(8,128)(2,1)S(1)}, bf16[256,128]{1,0:T(8,128)(2,1)S(1)}, u32[]{:S(2)}, u32[]{:S(2)}) %collective-permute-start) | collective-permute-done | bytes 65568 | tf_op jit(solution)/shard_map/ppermute | solution.py:543
  14.0 2.5 %collective-permute-start.1 = (bf16[256,128]{1,0:T(8,128)(2,1)S(1)}, bf16[256,128]{1,0:T(8,128)(2,1)S(1)}, u32[]{:S(2)}, u32[]{:S(2)}) collective-permute-start(bf16[256,128]{1,0:T(8,128)(2,1)S(1)} %add_convert_fusion.4.mine_ref), channel_id=1, source_target_pairs={{0,2},{1,3},{2,0},{3,1},{4,5},{5,4},{6,7},{7,6},{8,10},{9,11},{10,... | collective-permute-start | bytes 196616 | tf_op jit(solution)/shard_map/ppermute | solution.py:543
  16.4 0.4 collective-permute-done.3.other_ref
  16.8 0.0 copy-done.2
  16.8 0.0 copy-done.3
  16.8 0.7 %mute.1 = (bf16[16,2,4,16,128]{4,3,2,1,0:T(8,128)(2,1)S(1)}, f32[2,16,256]{2,1,0:T(8,128)S(1)}) custom-call(bf16[256,128]{1,0:T(8,128)(2,1)S(1)} %add_convert_fusion.3.mine_ref, bf16[256,128]{1,0:T(8,128)(2,1)S(1)} %collective-permute-done.3.other_ref, bf16[256,256]{1,0:T(8,128)(2,1)S(1)} %get-tuple-element.30.forward_ref.refs_6_, ...), custom_call_target="tpu_custom_call" | custom-call | flops 1000000000 | bytes 1048576 | tf_op jit(solution)/shard_map/mute/pallas_call | solution.py:553
  17.5 2.1 %collective-permute-done.1.other_ref = bf16[256,128]{1,0:T(8,128)(2,1)S(1)} collective-permute-done((bf16[256,128]{1,0:T(8,128)(2,1)S(1)}, bf16[256,128]{1,0:T(8,128)(2,1)S(1)}, u32[]{:S(2)}, u32[]{:S(2)}) %collective-permute-start.1) | collective-permute-done | bytes 65568 | tf_op jit(solution)/shard_map/ppermute | solution.py:543
  19.5 0.0 copy-start.1
  19.5 1.1 %adjoint.1 = (bf16[4,256,128]{2,1,0:T(8,128)(2,1)S(1)}, bf16[256,128]{1,0:T(8,128)(2,1)S(1)}, bf16[3,256,128]{2,1,0:T(8,128)(2,1)S(1)}, f32[2,32,256]{2,1,0:T(8,128)S(1)}) custom-call(bf16[256,128]{1,0:T(8,128)(2,1)S(1)} %add_convert_fusion.4.mine_ref, bf16[256,128]{1,0:T(8,128)(2,1)S(1)} %collective-permute-done.1.other_ref, ...), custom_call_target="tpu_custom_call" | custom-call | flops 2000000000 | bytes 1048576 | tf_op jit(solution)/shard_map/adjoint/pallas_call | solution.py:561
  20.7 0.1 collective-permute-start.4
  20.7 0.5 %collective-permute-start.6 = (bf16[3,256,128]{2,1,0:T(8,128)(2,1)S(1)}, bf16[3,256,128]{2,1,0:T(8,128)(2,1)S(1)}, u32[]{:S(2)}, u32[]{:S(2)}) collective-permute-start(bf16[3,256,128]{2,1,0:T(8,128)(2,1)S(1)} %get-tuple-element.43), channel_id=1, source_target_pairs={{0,4},{4,0},{8,12},{12,8},{16,20},{20,16},{24,28},{28,24},{1,5},{5... | collective-permute-start | bytes 589832 | tf_op jit(solution)/shard_map/ppermute | solution.py:468
  21.2 0.7 %collective-permute-done.4 = bf16[256,128]{1,0:T(8,128)(2,1)S(1)} collective-permute-done((bf16[256,128]{1,0:T(8,128)(2,1)S(1)}, bf16[256,128]{1,0:T(8,128)(2,1)S(1)}, u32[]{:S(2)}, u32[]{:S(2)}) %collective-permute-start.4) | collective-permute-done | bytes 65568 | tf_op jit(solution)/shard_map/ppermute | solution.py:468
  22.0 2.5 %collective-permute-start.5 = (bf16[256,128]{1,0:T(8,128)(2,1)S(1)}, bf16[256,128]{1,0:T(8,128)(2,1)S(1)}, u32[]{:S(2)}, u32[]{:S(2)}) collective-permute-start(bf16[256,128]{1,0:T(8,128)(2,1)S(1)} %fusion), channel_id=1, source_target_pairs={{0,24},{4,28},{8,16},{12,20},{16,8},{20,12},{24,0},{28,4},{1,25},{... | collective-permute-start | bytes 196616 | tf_op jit(solution)/shard_map/ppermute | solution.py:468
  24.5 0.0 collective-permute-done.6
  24.5 0.1 fusion.3
  24.6 0.6 %collective-permute-start.8 = (bf16[256,128]{1,0:T(8,128)(2,1)S(1)}, bf16[256,128]{1,0:T(8,128)(2,1)S(1)}, u32[]{:S(2)}, u32[]{:S(2)}) collective-permute-start(bf16[256,128]{1,0:T(8,128)(2,1)S(1)} %get-tuple-element.52), channel_id=1, source_target_pairs={{0,8},{4,12},{8,0},{12,4},{16,24},{20,28},{24,16},{28,20},{1,9},{5... | collective-permute-start | bytes 196616 | tf_op jit(solution)/shard_map/ppermute | solution.py:468
  25.2 0.5 %collective-permute-start.7 = (bf16[256,128]{1,0:T(8,128)(2,1)S(1)}, bf16[256,128]{1,0:T(8,128)(2,1)S(1)}, u32[]{:S(2)}, u32[]{:S(2)}) collective-permute-start(bf16[256,128]{1,0:T(8,128)(2,1)S(1)} %get-tuple-element.53), channel_id=1, source_target_pairs={{0,16},{4,20},{8,24},{12,28},{16,0},{20,4},{24,8},{28,12},{1,17},{... | collective-permute-start | bytes 196616 | tf_op jit(solution)/shard_map/ppermute | solution.py:468
  25.7 1.8 %collective-permute-done.5.refs_0_ = bf16[256,128]{1,0:T(8,128)(2,1)S(1)} collective-permute-done((bf16[256,128]{1,0:T(8,128)(2,1)S(1)}, bf16[256,128]{1,0:T(8,128)(2,1)S(1)}, u32[]{:S(2)}, u32[]{:S(2)}) %collective-permute-start.5) | collective-permute-done | bytes 65568 | tf_op jit(solution)/shard_map/ppermute | solution.py:468
  27.5 1.4 %collective-permute-done.8.refs_2_ = bf16[256,128]{1,0:T(8,128)(2,1)S(1)} collective-permute-done((bf16[256,128]{1,0:T(8,128)(2,1)S(1)}, bf16[256,128]{1,0:T(8,128)(2,1)S(1)}, u32[]{:S(2)}, u32[]{:S(2)}) %collective-permute-start.8) | collective-permute-done | bytes 65568 | tf_op jit(solution)/shard_map/ppermute | solution.py:468
  28.9 0.5 %collective-permute-done.7.refs_1_ = bf16[256,128]{1,0:T(8,128)(2,1)S(1)} collective-permute-done((bf16[256,128]{1,0:T(8,128)(2,1)S(1)}, bf16[256,128]{1,0:T(8,128)(2,1)S(1)}, u32[]{:S(2)}, u32[]{:S(2)}) %collective-permute-start.7) | collective-permute-done | bytes 65568 | tf_op jit(solution)/shard_map/ppermute | solution.py:468
  29.5 0.0 copy-done.1
  29.5 0.0 copy-start.4
  29.5 0.5 downgoing.1
  29.9 1.6 %collective-permute-start.14 = (bf16[16,16,128]{2,1,0:T(8,128)(2,1)S(1)}, bf16[16,16,128]{2,1,0:T(8,128)(2,1)S(1)}, u32[]{:S(2)}, u32[]{:S(2)}) collective-permute-start(bf16[16,16,128]{2,1,0:T(8,128)(2,1)S(1)} %get-tuple-element.46.refs_0_), channel_id=1, source_target_pairs={{0,24},{4,28},{8,16},{12,20},{16,8},{20,12},{24,0},{28,4},{1,25},{... | collective-permute-start | bytes 196616 | tf_op jit(solution)/shard_map/ppermute | solution.py:468
  31.5 1.4 %collective-permute-start.12 = (bf16[16,16,128]{2,1,0:T(8,128)(2,1)S(1)}, bf16[16,16,128]{2,1,0:T(8,128)(2,1)S(1)}, u32[]{:S(2)}, u32[]{:S(2)}) collective-permute-start(bf16[16,16,128]{2,1,0:T(8,128)(2,1)S(1)} %get-tuple-element.46.refs_0_), channel_id=1, source_target_pairs={{0,16},{4,20},{8,24},{12,28},{16,0},{20,4},{24,8},{28,12},{1,17},{... | collective-permute-start | bytes 196616 | tf_op jit(solution)/shard_map/ppermute | solution.py:468
  33.0 0.5 %collective-permute-start.10 = (bf16[16,16,128]{2,1,0:T(8,128)(2,1)S(1)}, bf16[16,16,128]{2,1,0:T(8,128)(2,1)S(1)}, u32[]{:S(2)}, u32[]{:S(2)}) collective-permute-start(bf16[16,16,128]{2,1,0:T(8,128)(2,1)S(1)} %get-tuple-element.46.refs_0_), channel_id=1, source_target_pairs={{0,8},{4,12},{8,0},{12,4},{16,24},{20,28},{24,16},{28,20},{1,9},{5... | collective-permute-start | bytes 196616 | tf_op jit(solution)/shard_map/ppermute | solution.py:468
  33.5 0.0 collective-permute-start.9
  33.5 2.4 %collective-permute-done.14.refs_3_ = bf16[16,16,128]{2,1,0:T(8,128)(2,1)S(1)} collective-permute-done((bf16[16,16,128]{2,1,0:T(8,128)(2,1)S(1)}, bf16[16,16,128]{2,1,0:T(8,128)(2,1)S(1)}, u32[]{:S(2)}, u32[]{:S(2)}) %collective-permute-start.14) | collective-permute-done | bytes 65568 | tf_op jit(solution)/shard_map/ppermute | solution.py:468
  35.9 0.0 collective-permute-start.15
  35.9 0.3 collective-permute-done.12.refs_2_
  36.2 0.2 collective-permute-start.13
  36.4 0.8 %collective-permute-done.10.refs_1_ = bf16[16,16,128]{2,1,0:T(8,128)(2,1)S(1)} collective-permute-done((bf16[16,16,128]{2,1,0:T(8,128)(2,1)S(1)}, bf16[16,16,128]{2,1,0:T(8,128)(2,1)S(1)}, u32[]{:S(2)}, u32[]{:S(2)}) %collective-permute-start.10) | collective-permute-done | bytes 65568 | tf_op jit(solution)/shard_map/ppermute | solution.py:468
  37.2 0.0 collective-permute-start.11
  37.2 0.1 near.1.refs_7_
  37.3 0.0 collective-permute-done.9.refs_0_
  37.3 0.0 collective-permute-done.15.refs_3_
  37.3 0.1 collective-permute-done.13.refs_2_
  37.4 1.0 %collective-permute-done.11.refs_1_ = bf16[16,16,128]{2,1,0:T(8,128)(2,1)S(1)} collective-permute-done((bf16[16,16,128]{2,1,0:T(8,128)(2,1)S(1)}, bf16[16,16,128]{2,1,0:T(8,128)(2,1)S(1)}, u32[]{:S(2)}, u32[]{:S(2)}) %collective-permute-start.11) | collective-permute-done | bytes 65568 | tf_op jit(solution)/shard_map/ppermute | solution.py:468
  38.5 0.0 copy-done.4
  38.5 1.1 %second.1 = (bf16[128,128]{1,0:T(8,128)(2,1)S(1)}, bf16[128,128]{1,0:T(8,128)(2,1)S(1)}, bf16[128,128]{1,0:T(8,128)(2,1)S(1)}, bf16[128,128]{1,0:T(8,128)(2,1)S(1)}) custom-call(bf16[16,16,128]{2,1,0:T(8,128)(2,1)S(1)} %collective-permute-done.9.refs_0_, bf16[16,16,128]{2,1,0:T(8,128)(2,1)S(1)} %collective-permute-done.11.refs_1_, ...), custom_call_target="tpu_custom_call" | custom-call | flops 1000000000 | bytes 1048576 | tf_op jit(solution)/shard_map/second/pallas_call | solution.py:608
  39.6 1.7 %collective-permute-start.16 = (bf16[128,128]{1,0:T(8,128)(2,1)S(1)}, bf16[128,128]{1,0:T(8,128)(2,1)S(1)}, u32[]{:S(2)}, u32[]{:S(2)}) collective-permute-start(bf16[128,128]{1,0:T(8,128)(2,1)S(1)} %get-tuple-element.47), channel_id=1, source_target_pairs={{0,3},{1,2},{2,1},{3,0},{4,7},{5,6},{6,5},{7,4},{8,11},{9,10},{10,... | collective-permute-start | bytes 98312 | tf_op jit(solution)/shard_map/ppermute | solution.py:604
  41.4 0.4 collective-permute-start.17
  41.8 2.3 %collective-permute-start.18 = (bf16[128,128]{1,0:T(8,128)(2,1)S(1)}, bf16[128,128]{1,0:T(8,128)(2,1)S(1)}, u32[]{:S(2)}, u32[]{:S(2)}) collective-permute-start(bf16[128,128]{1,0:T(8,128)(2,1)S(1)} %get-tuple-element.49), channel_id=1, source_target_pairs={{0,1},{1,0},{2,3},{3,2},{4,6},{5,7},{6,4},{7,5},{8,9},{9,8},{10,11... | collective-permute-start | bytes 98312 | tf_op jit(solution)/shard_map/ppermute | solution.py:604
  44.1 0.6 %emit.2 = f32[2,32,256]{2,1,0:T(8,128)} custom-call(f32[2,32,256]{2,1,0:T(8,128)S(1)} %get-tuple-element.40.field_ref), custom_call_target="tpu_custom_call" | custom-call | flops 300000000 | bytes 1048576 | tf_op jit(solution)/shard_map/emit/pallas_call | solution.py:461
  44.7 0.7 %emit.3 = f32[1,128,256]{2,1,0:T(8,128)} custom-call(f32[1,128,256]{2,1,0:T(8,128)S(1)} %get-tuple-element.45.field_ref), custom_call_target="tpu_custom_call" | custom-call | flops 300000000 | bytes 1048576 | tf_op jit(solution)/shard_map/emit/pallas_call | solution.py:461
  45.4 0.0 collective-permute-done.16.refs_0_
  45.4 1.5 %collective-permute-done.17.refs_1_ = bf16[128,128]{1,0:T(8,128)(2,1)S(1)} collective-permute-done((bf16[128,128]{1,0:T(8,128)(2,1)S(1)}, bf16[128,128]{1,0:T(8,128)(2,1)S(1)}, u32[]{:S(2)}, u32[]{:S(2)}) %collective-permute-start.17) | collective-permute-done | bytes 32800 | tf_op jit(solution)/shard_map/ppermute | solution.py:604
  46.9 0.0 collective-permute-done.18.refs_2_
  46.9 0.9 %final.1 = f32[2,32,256]{2,1,0:T(8,128)} custom-call(bf16[128,128]{1,0:T(8,128)(2,1)S(1)} %collective-permute-done.16.refs_0_, bf16[128,128]{1,0:T(8,128)(2,1)S(1)} %collective-permute-done.17.refs_1_, bf16[128,128]{1,0:T(8,128)(2,1)S(1)} %collective-permute-done.18.refs_2_, bf16[128,128]{1,0:T(8,128)(2,1)S(1)} %get-tuple-element.50.refs_3_, ...), custom_call_target="tpu_custom_call" | custom-call | flops 1000000000 | bytes 1048576 | tf_op jit(solution)/shard_map/final/pallas_call | solution.py:622
  (3 shorter events, 0.1 us)
Async XLA Ops:
  0.6 6.6 %copy-start = (bf16[32,128,256]{2,1,0:T(8,128)(2,1)S(1)}, bf16[32,128,256]{2,1,0:T(8,128)(2,1)}, u32[]{:S(2)}) copy-start(bf16[32,128,256]{2,1,0:T(8,128)(2,1)} %traces_ref.1) | copy-start | bytes 6291460
  4.1 5.3 %collective-permute-start.2 = (bf16[256,128]{1,0:T(8,128)(2,1)S(1)}, bf16[256,128]{1,0:T(8,128)(2,1)S(1)}, u32[]{:S(2)}, u32[]{:S(2)}) collective-permute-start(bf16[256,128]{1,0:T(8,128)(2,1)S(1)} %get-tuple-element.35), channel_id=1, source_target_pairs={{0,1},{1,0},{2,3},{3,2},{4,5},{5,4},{6,7},{7,6},{8,9},{9,8},{10,11... | collective-permute-start | bytes 196616 | tf_op jit(solution)/shard_map/ppermute | solution.py:543
  7.2 9.6 %copy-start.2 = (bf16[2,4,128,256]{3,2,1,0:T(8,128)(2,1)S(1)}, bf16[2,4,128,256]{3,2,1,0:T(8,128)(2,1)}, u32[]{:S(2)}) copy-start(bf16[2,4,128,256]{3,2,1,0:T(8,128)(2,1)} %constant.23.spread_ref) | copy-start | bytes 1572868
  7.2 9.6 %copy-start.3 = (bf16[256,256]{1,0:T(8,128)(2,1)S(1)}, bf16[256,256]{1,0:T(8,128)(2,1)}, u32[]{:S(2)}) copy-start(bf16[256,256]{1,0:T(8,128)(2,1)} %constant.22.inverse_ref.refs_7_.refs_5_) | copy-start | bytes 393220
  8.9 5.0 %collective-permute-start = (bf16[256,128]{1,0:T(8,128)(2,1)S(1)}, bf16[256,128]{1,0:T(8,128)(2,1)S(1)}, u32[]{:S(2)}, u32[]{:S(2)}) collective-permute-start(bf16[256,128]{1,0:T(8,128)(2,1)S(1)} %get-tuple-element.34), channel_id=1, source_target_pairs={{0,1},{1,0},{2,3},{3,2},{4,6},{5,7},{6,4},{7,5},{8,9},{9,8},{10,11... | collective-permute-start | bytes 196616 | tf_op jit(solution)/shard_map/ppermute | solution.py:543
  9.5 7.3 %collective-permute-start.3 = (bf16[256,128]{1,0:T(8,128)(2,1)S(1)}, bf16[256,128]{1,0:T(8,128)(2,1)S(1)}, u32[]{:S(2)}, u32[]{:S(2)}) collective-permute-start(bf16[256,128]{1,0:T(8,128)(2,1)S(1)} %add_convert_fusion.3.mine_ref), channel_id=1, source_target_pairs={{0,2},{1,3},{2,0},{3,1},{4,6},{5,7},{6,4},{7,5},{8,10},{9,11},{10,... | collective-permute-start | bytes 196616 | tf_op jit(solution)/shard_map/ppermute | solution.py:543
  14.0 5.6 %collective-permute-start.1 = (bf16[256,128]{1,0:T(8,128)(2,1)S(1)}, bf16[256,128]{1,0:T(8,128)(2,1)S(1)}, u32[]{:S(2)}, u32[]{:S(2)}) collective-permute-start(bf16[256,128]{1,0:T(8,128)(2,1)S(1)} %add_convert_fusion.4.mine_ref), channel_id=1, source_target_pairs={{0,2},{1,3},{2,0},{3,1},{4,5},{5,4},{6,7},{7,6},{8,10},{9,11},{10,... | collective-permute-start | bytes 196616 | tf_op jit(solution)/shard_map/ppermute | solution.py:543
  19.5 9.9 %copy-start.1 = (s32[1,128]{1,0:T(1,128)S(1)}, s32[1,128]{1,0:T(1,128)}, u32[]{:S(2)}) copy-start(s32[1,128]{1,0:T(1,128)} %refs_5_.1) | copy-start | bytes 1540
  20.7 1.3 %collective-permute-start.4 = (bf16[256,128]{1,0:T(8,128)(2,1)S(1)}, bf16[256,128]{1,0:T(8,128)(2,1)S(1)}, u32[]{:S(2)}, u32[]{:S(2)}) collective-permute-start(bf16[256,128]{1,0:T(8,128)(2,1)S(1)} %get-tuple-element.42), channel_id=1, source_target_pairs={{0,4},{4,0},{8,12},{12,8},{16,20},{20,16},{24,28},{28,24},{1,5},{5... | collective-permute-start | bytes 196616 | tf_op jit(solution)/shard_map/ppermute | solution.py:468
  20.7 3.8 %collective-permute-start.6 = (bf16[3,256,128]{2,1,0:T(8,128)(2,1)S(1)}, bf16[3,256,128]{2,1,0:T(8,128)(2,1)S(1)}, u32[]{:S(2)}, u32[]{:S(2)}) collective-permute-start(bf16[3,256,128]{2,1,0:T(8,128)(2,1)S(1)} %get-tuple-element.43), channel_id=1, source_target_pairs={{0,4},{4,0},{8,12},{12,8},{16,20},{20,16},{24,28},{28,24},{1,5},{5... | collective-permute-start | bytes 589832 | tf_op jit(solution)/shard_map/ppermute | solution.py:468
  22.0 5.5 %collective-permute-start.5 = (bf16[256,128]{1,0:T(8,128)(2,1)S(1)}, bf16[256,128]{1,0:T(8,128)(2,1)S(1)}, u32[]{:S(2)}, u32[]{:S(2)}) collective-permute-start(bf16[256,128]{1,0:T(8,128)(2,1)S(1)} %fusion), channel_id=1, source_target_pairs={{0,24},{4,28},{8,16},{12,20},{16,8},{20,12},{24,0},{28,4},{1,25},{... | collective-permute-start | bytes 196616 | tf_op jit(solution)/shard_map/ppermute | solution.py:468
  24.6 4.3 %collective-permute-start.8 = (bf16[256,128]{1,0:T(8,128)(2,1)S(1)}, bf16[256,128]{1,0:T(8,128)(2,1)S(1)}, u32[]{:S(2)}, u32[]{:S(2)}) collective-permute-start(bf16[256,128]{1,0:T(8,128)(2,1)S(1)} %get-tuple-element.52), channel_id=1, source_target_pairs={{0,8},{4,12},{8,0},{12,4},{16,24},{20,28},{24,16},{28,20},{1,9},{5... | collective-permute-start | bytes 196616 | tf_op jit(solution)/shard_map/ppermute | solution.py:468
  25.2 4.3 %collective-permute-start.7 = (bf16[256,128]{1,0:T(8,128)(2,1)S(1)}, bf16[256,128]{1,0:T(8,128)(2,1)S(1)}, u32[]{:S(2)}, u32[]{:S(2)}) collective-permute-start(bf16[256,128]{1,0:T(8,128)(2,1)S(1)} %get-tuple-element.53), channel_id=1, source_target_pairs={{0,16},{4,20},{8,24},{12,28},{16,0},{20,4},{24,8},{28,12},{1,17},{... | collective-permute-start | bytes 196616 | tf_op jit(solution)/shard_map/ppermute | solution.py:468
  29.5 9.0 %copy-start.4 = (bf16[256,128]{1,0:T(8,128)(2,1)S(1)}, bf16[256,128]{1,0:T(8,128)(2,1)}, u32[]{:S(2)}) copy-start(bf16[256,128]{1,0:T(8,128)(2,1)} %constant.24.refs_6_) | copy-start | bytes 196612
  29.9 5.9 %collective-permute-start.14 = (bf16[16,16,128]{2,1,0:T(8,128)(2,1)S(1)}, bf16[16,16,128]{2,1,0:T(8,128)(2,1)S(1)}, u32[]{:S(2)}, u32[]{:S(2)}) collective-permute-start(bf16[16,16,128]{2,1,0:T(8,128)(2,1)S(1)} %get-tuple-element.46.refs_0_), channel_id=1, source_target_pairs={{0,24},{4,28},{8,16},{12,20},{16,8},{20,12},{24,0},{28,4},{1,25},{... | collective-permute-start | bytes 196616 | tf_op jit(solution)/shard_map/ppermute | solution.py:468
  31.5 4.7 %collective-permute-start.12 = (bf16[16,16,128]{2,1,0:T(8,128)(2,1)S(1)}, bf16[16,16,128]{2,1,0:T(8,128)(2,1)S(1)}, u32[]{:S(2)}, u32[]{:S(2)}) collective-permute-start(bf16[16,16,128]{2,1,0:T(8,128)(2,1)S(1)} %get-tuple-element.46.refs_0_), channel_id=1, source_target_pairs={{0,16},{4,20},{8,24},{12,28},{16,0},{20,4},{24,8},{28,12},{1,17},{... | collective-permute-start | bytes 196616 | tf_op jit(solution)/shard_map/ppermute | solution.py:468
  33.0 4.3 %collective-permute-start.10 = (bf16[16,16,128]{2,1,0:T(8,128)(2,1)S(1)}, bf16[16,16,128]{2,1,0:T(8,128)(2,1)S(1)}, u32[]{:S(2)}, u32[]{:S(2)}) collective-permute-start(bf16[16,16,128]{2,1,0:T(8,128)(2,1)S(1)} %get-tuple-element.46.refs_0_), channel_id=1, source_target_pairs={{0,8},{4,12},{8,0},{12,4},{16,24},{20,28},{24,16},{28,20},{1,9},{5... | collective-permute-start | bytes 196616 | tf_op jit(solution)/shard_map/ppermute | solution.py:468
  33.5 3.8 %collective-permute-start.9 = (bf16[16,16,128]{2,1,0:T(8,128)(2,1)S(1)}, bf16[16,16,128]{2,1,0:T(8,128)(2,1)S(1)}, u32[]{:S(2)}, u32[]{:S(2)}) collective-permute-start(bf16[16,16,128]{2,1,0:T(8,128)(2,1)S(1)} %get-tuple-element.46.refs_0_), channel_id=1, source_target_pairs={{0,4},{4,0},{8,12},{12,8},{16,20},{20,16},{24,28},{28,24},{1,5},{5... | collective-permute-start | bytes 196616 | tf_op jit(solution)/shard_map/ppermute | solution.py:468
  35.9 1.5 %collective-permute-start.15 = (bf16[16,16,128]{2,1,0:T(8,128)(2,1)S(1)}, bf16[16,16,128]{2,1,0:T(8,128)(2,1)S(1)}, u32[]{:S(2)}, u32[]{:S(2)}) collective-permute-start(bf16[16,16,128]{2,1,0:T(8,128)(2,1)S(1)} %collective-permute-done.14.refs_3_), channel_id=1, source_target_pairs={{0,4},{4,0},{8,12},{12,8},{16,20},{20,16},{24,28},{28,24},{1,5},{5... | collective-permute-start | bytes 196616 | tf_op jit(solution)/shard_map/ppermute | solution.py:468
  36.2 1.3 %collective-permute-start.13 = (bf16[16,16,128]{2,1,0:T(8,128)(2,1)S(1)}, bf16[16,16,128]{2,1,0:T(8,128)(2,1)S(1)}, u32[]{:S(2)}, u32[]{:S(2)}) collective-permute-start(bf16[16,16,128]{2,1,0:T(8,128)(2,1)S(1)} %collective-permute-done.12.refs_2_), channel_id=1, source_target_pairs={{0,4},{4,0},{8,12},{12,8},{16,20},{20,16},{24,28},{28,24},{1,5},{5... | collective-permute-start | bytes 196616 | tf_op jit(solution)/shard_map/ppermute | solution.py:468
  37.2 1.3 %collective-permute-start.11 = (bf16[16,16,128]{2,1,0:T(8,128)(2,1)S(1)}, bf16[16,16,128]{2,1,0:T(8,128)(2,1)S(1)}, u32[]{:S(2)}, u32[]{:S(2)}) collective-permute-start(bf16[16,16,128]{2,1,0:T(8,128)(2,1)S(1)} %collective-permute-done.10.refs_1_), channel_id=1, source_target_pairs={{0,4},{4,0},{8,12},{12,8},{16,20},{20,16},{24,28},{28,24},{1,5},{5... | collective-permute-start | bytes 196616 | tf_op jit(solution)/shard_map/ppermute | solution.py:468
  39.6 5.8 %collective-permute-start.16 = (bf16[128,128]{1,0:T(8,128)(2,1)S(1)}, bf16[128,128]{1,0:T(8,128)(2,1)S(1)}, u32[]{:S(2)}, u32[]{:S(2)}) collective-permute-start(bf16[128,128]{1,0:T(8,128)(2,1)S(1)} %get-tuple-element.47), channel_id=1, source_target_pairs={{0,3},{1,2},{2,1},{3,0},{4,7},{5,6},{6,5},{7,4},{8,11},{9,10},{10,... | collective-permute-start | bytes 98312 | tf_op jit(solution)/shard_map/ppermute | solution.py:604
  41.4 5.5 %collective-permute-start.17 = (bf16[128,128]{1,0:T(8,128)(2,1)S(1)}, bf16[128,128]{1,0:T(8,128)(2,1)S(1)}, u32[]{:S(2)}, u32[]{:S(2)}) collective-permute-start(bf16[128,128]{1,0:T(8,128)(2,1)S(1)} %get-tuple-element.48), channel_id=1, source_target_pairs={{0,2},{1,3},{2,0},{3,1},{4,5},{5,4},{6,7},{7,6},{8,10},{9,11},{10,... | collective-permute-start | bytes 98312 | tf_op jit(solution)/shard_map/ppermute | solution.py:604
  41.8 5.1 %collective-permute-start.18 = (bf16[128,128]{1,0:T(8,128)(2,1)S(1)}, bf16[128,128]{1,0:T(8,128)(2,1)S(1)}, u32[]{:S(2)}, u32[]{:S(2)}) collective-permute-start(bf16[128,128]{1,0:T(8,128)(2,1)S(1)} %get-tuple-element.49), channel_id=1, source_target_pairs={{0,1},{1,0},{2,3},{3,2},{4,6},{5,7},{6,4},{7,5},{8,9},{9,8},{10,11... | collective-permute-start | bytes 98312 | tf_op jit(solution)/shard_map/ppermute | solution.py:604

commit v12 on v10

--- a/solution.py
+++ b/solution.py
@@ -387,22 +387,28 @@
     plus_ref[...] = interleave(spectra[:NF], spectra[NF:]).astype(BF16)
 
 
-def place_fields(field_refs, vector_ref):
+def turned(distance):
+    return (distance & ~3) | ((distance & 1) << 1) | ((distance >> 1) & 1)
+
+
+def place_fields(field_refs, vector_ref, core):
     chip = lax.axis_index("shot") // 2
     for distance, field_ref in enumerate(field_refs):
-        slot = (chip ^ distance) ^ lax.axis_index("rcv")
+        away = jnp.where(core == 0, distance, turned(distance))
+        slot = (chip ^ away) ^ lax.axis_index("rcv")
         store_vector(vector_ref, slot, *unpack(field_ref))
 
 
 def near_kernel(*refs):
-    place_fields(refs[:-1], refs[-1])
+    place_fields(refs[:-1], refs[-1], lax.axis_index("shot") % 2)
 
 
 def second_kernel(pairs, *refs):
     first_ref, rest_ref, gather_ref, near_ref = refs[pairs : pairs + 4]
     sum_refs = refs[pairs + 4 : -2]
     far_ref, kept_ref = refs[-2:]
-    place_fields(refs[:pairs], far_ref)
+    core = lax.axis_index("shot") % 2
+    place_fields(refs[:pairs], far_ref, 1 - core)
 
     def store(row, value):
         for slot in range(pairs):
@@ -589,7 +595,11 @@
 
     near = [plus]
     for distance in range(1, pairs):
-        near.append(exchange(plus, "shot", 2 * distance))
+        routes = [
+            (place, place ^ (2 * (turned(distance) if place % 2 else distance)))
+            for place in range(shot_count)
+        ]
+        near.append(lax.ppermute(plus, "shot", routes))
     far = [exchange(value, "shot", 1) for value in near]
 
     half_vector = shape((NG, pairs, 2 * GROUP, 2 * receivers), BF16)

time: 47.5 us -> 47.5 us (level)
    ppermute x15 -> x12, starting transfers between devices: 12.4 us -> 8.65 us  [exchange(): lax.ppermute(value, axis, [(place, place ^ distance) for place in range(c...]
    ppermute x0 -> x3, waiting for transfers between devices: none -> 3.72 us  [body(): near.append(lax.ppermute(plus, 'shot', routes))]
    ppermute x0 -> x3, starting transfers between devices: none -> 3.55 us  [body(): near.append(lax.ppermute(plus, 'shot', routes))]
    ppermute x15 -> x12, waiting for transfers between devices: 10.2 us -> 6.65 us  [exchange(): lax.ppermute(value, axis, [(place, place ^ distance) for place in range(c...]
  transfers between devices with their start and end apart: 19 -> 19, of which waited for: 16 -> 15; matrix products, arithmetic and copies ran while one was open for 0% -> 0% of each run, Pallas kernels for 8% -> 8%
where the time goes in v12:
time: 47.5 us; the launch traced here: 47.3 us
  starting transfers between devices  21 us (44%)
  waiting for transfers between devices  14.5 us (31%)
  Pallas kernels  10.9 us (23%)
  between operations  0.76 us (2%)
    ppermute x4, starting transfers between devices, hop(): return lax.ppermute(value, ('shot', 'rcv'), pairs_of)  8.8 us
    ppermute x12, starting transfers between devices, exchange(): lax.ppermute(value, axis, [(place, place ^ distance) for place in range(c...  8.65 us
    ppermute x12, waiting for transfers between devices, exchange(): lax.ppermute(value, axis, [(place, place ^ distance) for place in range(c...  6.65 us
    ppermute x4, waiting for transfers between devices, hop(): return lax.ppermute(value, ('shot', 'rcv'), pairs_of)  4.12 us
    ppermute x3, waiting for transfers between devices, body(): near.append(lax.ppermute(plus, 'shot', routes))  3.72 us
    ppermute x3, starting transfers between devices, body(): near.append(lax.ppermute(plus, 'shot', routes))  3.55 us
    pallas_call x1, Pallas kernels, body(): call(functools.partial(first_kernel, gain), 'first', [half_matrix, half_s...  3.45 us
    pallas_call x1, Pallas kernels, body(): call(functools.partial(rest_kernel, gain), 'rest', (half_matrix, half_sum...  1.74 us
  transfers between devices with their start and end apart: 19, of which 15 were waited for; matrix products, arithmetic and copies ran while one was open for 0% of the time, Pallas kernels for 8%

profile of v12, /device:TPU:0, one launch (start us, length us, event | category | flops | bytes accessed | tf_op | source)
XLA Modules:
  0.0 47.3 jit_solution(4499722596931727803)
XLA Ops:
  0.6 0.0 copy-start
  0.6 3.5 %first.1 = (bf16[16,8,16,256]{3,2,1,0:T(8,128)(2,1)S(1)}, bf16[256,128]{1,0:T(8,128)(2,1)S(1)}, bf16[128,256]{1,0:T(8,128)(2,1)S(1)}, bf16[16,8,16,256]{3,2,1,0:...) custom-call(bf16[32,128,256]{2,1,0:T(8,128)(2,1)} %traces_ref.1, ...), custom_call_target="tpu_custom_call" | custom-call | flops 4000000000 | bytes 1048576 | tf_op jit(solution)/shard_map/first/pallas_call | solution.py:507
  4.1 3.1 %collective-permute-start.2 = (bf16[256,128]{1,0:T(8,128)(2,1)S(1)}, bf16[256,128]{1,0:T(8,128)(2,1)S(1)}, u32[]{:S(2)}, u32[]{:S(2)}) collective-permute-start(bf16[256,128]{1,0:T(8,128)(2,1)S(1)} %get-tuple-element.35), channel_id=1, source_target_pairs={{0,1},{1,0},{2,3},{3,2},{4,5},{5,4},{6,7},{7,6},{8,9},{9,8},{10,11... | collective-permute-start | bytes 196616 | tf_op jit(solution)/shard_map/ppermute | solution.py:547
  7.2 0.0 copy-done
  7.2 0.0 copy-start.2
  7.2 0.0 copy-start.3
  7.2 1.7 %rest.1 = (bf16[16,8,16,256]{3,2,1,0:T(8,128)(2,1)S(1)}, bf16[256,128]{1,0:T(8,128)(2,1)S(1)}) custom-call(bf16[32,128,256]{2,1,0:T(8,128)(2,1)S(1)} %copy-done, s32[32,128]{1,0:T(8,128)S(1)} %get-tuple-element.27.shift_ref, f32[32,64]{1,0:T(8,128)S(1)} %get-tuple-element.28.deconv_ref, s32[2,32]{1,0:T(2,128)S(1)} %get-tuple-element.29.onset_ref.refs_4_, ...), custom_call_target="tpu_custom_call" | custom-call | flops 3000000000 | bytes 1048576 | tf_op jit(solution)/shard_map/rest/pallas_call | solution.py:529
  8.9 0.1 collective-permute-start
  9.1 0.4 collective-permute-done.2
  9.5 3.1 %collective-permute-start.3 = (bf16[256,128]{1,0:T(8,128)(2,1)S(1)}, bf16[256,128]{1,0:T(8,128)(2,1)S(1)}, u32[]{:S(2)}, u32[]{:S(2)}) collective-permute-start(bf16[256,128]{1,0:T(8,128)(2,1)S(1)} %add_convert_fusion.3.mine_ref), channel_id=1, source_target_pairs={{0,2},{1,3},{2,0},{3,1},{4,6},{5,7},{6,4},{7,5},{8,10},{9,11},{10,... | collective-permute-start | bytes 196616 | tf_op jit(solution)/shard_map/ppermute | solution.py:547
  12.6 1.3 %collective-permute-done = bf16[256,128]{1,0:T(8,128)(2,1)S(1)} collective-permute-done((bf16[256,128]{1,0:T(8,128)(2,1)S(1)}, bf16[256,128]{1,0:T(8,128)(2,1)S(1)}, u32[]{:S(2)}, u32[]{:S(2)}) %collective-permute-start) | collective-permute-done | bytes 65568 | tf_op jit(solution)/shard_map/ppermute | solution.py:547
  14.0 2.5 %collective-permute-start.1 = (bf16[256,128]{1,0:T(8,128)(2,1)S(1)}, bf16[256,128]{1,0:T(8,128)(2,1)S(1)}, u32[]{:S(2)}, u32[]{:S(2)}) collective-permute-start(bf16[256,128]{1,0:T(8,128)(2,1)S(1)} %add_convert_fusion.4.mine_ref), channel_id=1, source_target_pairs={{0,2},{1,3},{2,0},{3,1},{4,5},{5,4},{6,7},{7,6},{8,10},{9,11},{10,... | collective-permute-start | bytes 196616 | tf_op jit(solution)/shard_map/ppermute | solution.py:547
  16.4 0.4 collective-permute-done.3.other_ref
  16.8 0.0 copy-done.2
  16.8 0.0 copy-done.3
  16.8 0.7 %mute.1 = (bf16[16,2,4,16,128]{4,3,2,1,0:T(8,128)(2,1)S(1)}, f32[2,16,256]{2,1,0:T(8,128)S(1)}) custom-call(bf16[256,128]{1,0:T(8,128)(2,1)S(1)} %add_convert_fusion.3.mine_ref, bf16[256,128]{1,0:T(8,128)(2,1)S(1)} %collective-permute-done.3.other_ref, bf16[256,256]{1,0:T(8,128)(2,1)S(1)} %get-tuple-element.30.forward_ref.refs_6_, ...), custom_call_target="tpu_custom_call" | custom-call | flops 1000000000 | bytes 1048576 | tf_op jit(solution)/shard_map/mute/pallas_call | solution.py:557
  17.5 2.1 %collective-permute-done.1.other_ref = bf16[256,128]{1,0:T(8,128)(2,1)S(1)} collective-permute-done((bf16[256,128]{1,0:T(8,128)(2,1)S(1)}, bf16[256,128]{1,0:T(8,128)(2,1)S(1)}, u32[]{:S(2)}, u32[]{:S(2)}) %collective-permute-start.1) | collective-permute-done | bytes 65568 | tf_op jit(solution)/shard_map/ppermute | solution.py:547
  19.5 0.0 copy-start.1
  19.5 1.1 %adjoint.1 = (bf16[4,256,128]{2,1,0:T(8,128)(2,1)S(1)}, bf16[256,128]{1,0:T(8,128)(2,1)S(1)}, bf16[3,256,128]{2,1,0:T(8,128)(2,1)S(1)}, f32[2,32,256]{2,1,0:T(8,128)S(1)}) custom-call(bf16[256,128]{1,0:T(8,128)(2,1)S(1)} %add_convert_fusion.4.mine_ref, bf16[256,128]{1,0:T(8,128)(2,1)S(1)} %collective-permute-done.1.other_ref, ...), custom_call_target="tpu_custom_call" | custom-call | flops 2000000000 | bytes 1048576 | tf_op jit(solution)/shard_map/adjoint/pallas_call | solution.py:565
  20.7 0.1 collective-permute-start.4
  20.7 0.5 %collective-permute-start.6 = (bf16[3,256,128]{2,1,0:T(8,128)(2,1)S(1)}, bf16[3,256,128]{2,1,0:T(8,128)(2,1)S(1)}, u32[]{:S(2)}, u32[]{:S(2)}) collective-permute-start(bf16[3,256,128]{2,1,0:T(8,128)(2,1)S(1)} %get-tuple-element.43), channel_id=1, source_target_pairs={{0,4},{4,0},{8,12},{12,8},{16,20},{20,16},{24,28},{28,24},{1,5},{5... | collective-permute-start | bytes 589832 | tf_op jit(solution)/shard_map/ppermute | solution.py:472
  21.2 0.7 %collective-permute-done.4 = bf16[256,128]{1,0:T(8,128)(2,1)S(1)} collective-permute-done((bf16[256,128]{1,0:T(8,128)(2,1)S(1)}, bf16[256,128]{1,0:T(8,128)(2,1)S(1)}, u32[]{:S(2)}, u32[]{:S(2)}) %collective-permute-start.4) | collective-permute-done | bytes 65568 | tf_op jit(solution)/shard_map/ppermute | solution.py:472
  22.0 2.5 %collective-permute-start.5 = (bf16[256,128]{1,0:T(8,128)(2,1)S(1)}, bf16[256,128]{1,0:T(8,128)(2,1)S(1)}, u32[]{:S(2)}, u32[]{:S(2)}) collective-permute-start(bf16[256,128]{1,0:T(8,128)(2,1)S(1)} %fusion), channel_id=1, source_target_pairs={{0,24},{4,28},{8,16},{12,20},{16,8},{20,12},{24,0},{28,4},{1,25},{... | collective-permute-start | bytes 196616 | tf_op jit(solution)/shard_map/ppermute | solution.py:472
  24.5 0.0 collective-permute-done.6
  24.5 0.1 fusion.3
  24.6 0.6 %collective-permute-start.8 = (bf16[256,128]{1,0:T(8,128)(2,1)S(1)}, bf16[256,128]{1,0:T(8,128)(2,1)S(1)}, u32[]{:S(2)}, u32[]{:S(2)}) collective-permute-start(bf16[256,128]{1,0:T(8,128)(2,1)S(1)} %get-tuple-element.52), channel_id=1, source_target_pairs={{0,8},{4,12},{8,0},{12,4},{16,24},{20,28},{24,16},{28,20},{1,9},{5... | collective-permute-start | bytes 196616 | tf_op jit(solution)/shard_map/ppermute | solution.py:472
  25.2 0.5 %collective-permute-start.7 = (bf16[256,128]{1,0:T(8,128)(2,1)S(1)}, bf16[256,128]{1,0:T(8,128)(2,1)S(1)}, u32[]{:S(2)}, u32[]{:S(2)}) collective-permute-start(bf16[256,128]{1,0:T(8,128)(2,1)S(1)} %get-tuple-element.53), channel_id=1, source_target_pairs={{0,16},{4,20},{8,24},{12,28},{16,0},{20,4},{24,8},{28,12},{1,17},{... | collective-permute-start | bytes 196616 | tf_op jit(solution)/shard_map/ppermute | solution.py:472
  25.7 1.8 %collective-permute-done.5.refs_0_ = bf16[256,128]{1,0:T(8,128)(2,1)S(1)} collective-permute-done((bf16[256,128]{1,0:T(8,128)(2,1)S(1)}, bf16[256,128]{1,0:T(8,128)(2,1)S(1)}, u32[]{:S(2)}, u32[]{:S(2)}) %collective-permute-start.5) | collective-permute-done | bytes 65568 | tf_op jit(solution)/shard_map/ppermute | solution.py:472
  27.5 1.4 %collective-permute-done.8.refs_2_ = bf16[256,128]{1,0:T(8,128)(2,1)S(1)} collective-permute-done((bf16[256,128]{1,0:T(8,128)(2,1)S(1)}, bf16[256,128]{1,0:T(8,128)(2,1)S(1)}, u32[]{:S(2)}, u32[]{:S(2)}) %collective-permute-start.8) | collective-permute-done | bytes 65568 | tf_op jit(solution)/shard_map/ppermute | solution.py:472
  28.9 0.5 %collective-permute-done.7.refs_1_ = bf16[256,128]{1,0:T(8,128)(2,1)S(1)} collective-permute-done((bf16[256,128]{1,0:T(8,128)(2,1)S(1)}, bf16[256,128]{1,0:T(8,128)(2,1)S(1)}, u32[]{:S(2)}, u32[]{:S(2)}) %collective-permute-start.7) | collective-permute-done | bytes 65568 | tf_op jit(solution)/shard_map/ppermute | solution.py:472
  29.5 0.0 copy-done.1
  29.5 0.0 copy-start.4
  29.5 0.5 downgoing.1
  29.9 1.6 %collective-permute-start.14 = (bf16[16,16,128]{2,1,0:T(8,128)(2,1)S(1)}, bf16[16,16,128]{2,1,0:T(8,128)(2,1)S(1)}, u32[]{:S(2)}, u32[]{:S(2)}) collective-permute-start(bf16[16,16,128]{2,1,0:T(8,128)(2,1)S(1)} %get-tuple-element.46.refs_0_), channel_id=1, source_target_pairs={{0,24},{4,28},{8,16},{12,20},{16,8},{20,12},{24,0},{28,4},{1,25},{... | collective-permute-start | bytes 196616 | tf_op jit(solution)/shard_map/ppermute | solution.py:602
  31.5 1.4 %collective-permute-start.12 = (bf16[16,16,128]{2,1,0:T(8,128)(2,1)S(1)}, bf16[16,16,128]{2,1,0:T(8,128)(2,1)S(1)}, u32[]{:S(2)}, u32[]{:S(2)}) collective-permute-start(bf16[16,16,128]{2,1,0:T(8,128)(2,1)S(1)} %get-tuple-element.46.refs_0_), channel_id=1, source_target_pairs={{0,16},{4,12},{8,24},{12,4},{16,0},{20,28},{24,8},{28,20},{1,17},{... | collective-permute-start | bytes 196616 | tf_op jit(solution)/shard_map/ppermute | solution.py:602
  33.0 0.5 %collective-permute-start.10 = (bf16[16,16,128]{2,1,0:T(8,128)(2,1)S(1)}, bf16[16,16,128]{2,1,0:T(8,128)(2,1)S(1)}, u32[]{:S(2)}, u32[]{:S(2)}) collective-permute-start(bf16[16,16,128]{2,1,0:T(8,128)(2,1)S(1)} %get-tuple-element.46.refs_0_), channel_id=1, source_target_pairs={{0,8},{4,20},{8,0},{12,28},{16,24},{20,4},{24,16},{28,12},{1,9},{5... | collective-permute-start | bytes 196616 | tf_op jit(solution)/shard_map/ppermute | solution.py:602
  33.5 0.0 collective-permute-start.9
  33.5 1.7 %collective-permute-done.14.refs_3_ = bf16[16,16,128]{2,1,0:T(8,128)(2,1)S(1)} collective-permute-done((bf16[16,16,128]{2,1,0:T(8,128)(2,1)S(1)}, bf16[16,16,128]{2,1,0:T(8,128)(2,1)S(1)}, u32[]{:S(2)}, u32[]{:S(2)}) %collective-permute-start.14) | collective-permute-done | bytes 65568 | tf_op jit(solution)/shard_map/ppermute | solution.py:602
  35.2 0.0 collective-permute-start.15
  35.2 0.7 %collective-permute-done.12.refs_2_ = bf16[16,16,128]{2,1,0:T(8,128)(2,1)S(1)} collective-permute-done((bf16[16,16,128]{2,1,0:T(8,128)(2,1)S(1)}, bf16[16,16,128]{2,1,0:T(8,128)(2,1)S(1)}, u32[]{:S(2)}, u32[]{:S(2)}) %collective-permute-start.12) | collective-permute-done | bytes 65568 | tf_op jit(solution)/shard_map/ppermute | solution.py:602
  35.9 0.0 collective-permute-start.13
  35.9 1.3 %collective-permute-done.10.refs_1_ = bf16[16,16,128]{2,1,0:T(8,128)(2,1)S(1)} collective-permute-done((bf16[16,16,128]{2,1,0:T(8,128)(2,1)S(1)}, bf16[16,16,128]{2,1,0:T(8,128)(2,1)S(1)}, u32[]{:S(2)}, u32[]{:S(2)}) %collective-permute-start.10) | collective-permute-done | bytes 65568 | tf_op jit(solution)/shard_map/ppermute | solution.py:602
  37.2 0.0 collective-permute-start.11
  37.2 0.1 near.1.refs_7_
  37.3 0.0 collective-permute-done.9.refs_0_
  37.3 0.0 collective-permute-done.15.refs_3_
  37.3 0.0 collective-permute-done.13.refs_2_
  37.3 1.1 %collective-permute-done.11.refs_1_ = bf16[16,16,128]{2,1,0:T(8,128)(2,1)S(1)} collective-permute-done((bf16[16,16,128]{2,1,0:T(8,128)(2,1)S(1)}, bf16[16,16,128]{2,1,0:T(8,128)(2,1)S(1)}, u32[]{:S(2)}, u32[]{:S(2)}) %collective-permute-start.11) | collective-permute-done | bytes 65568 | tf_op jit(solution)/shard_map/ppermute | solution.py:472
  38.5 0.0 copy-done.4
  38.5 1.1 %second.1 = (bf16[128,128]{1,0:T(8,128)(2,1)S(1)}, bf16[128,128]{1,0:T(8,128)(2,1)S(1)}, bf16[128,128]{1,0:T(8,128)(2,1)S(1)}, bf16[128,128]{1,0:T(8,128)(2,1)S(1)}) custom-call(bf16[16,16,128]{2,1,0:T(8,128)(2,1)S(1)} %collective-permute-done.9.refs_0_, bf16[16,16,128]{2,1,0:T(8,128)(2,1)S(1)} %collective-permute-done.11.refs_1_, ...), custom_call_target="tpu_custom_call" | custom-call | flops 1000000000 | bytes 1048576 | tf_op jit(solution)/shard_map/second/pallas_call | solution.py:607
  39.6 1.8 %collective-permute-start.16 = (bf16[128,128]{1,0:T(8,128)(2,1)S(1)}, bf16[128,128]{1,0:T(8,128)(2,1)S(1)}, u32[]{:S(2)}, u32[]{:S(2)}) collective-permute-start(bf16[128,128]{1,0:T(8,128)(2,1)S(1)} %get-tuple-element.47), channel_id=1, source_target_pairs={{0,3},{1,2},{2,1},{3,0},{4,7},{5,6},{6,5},{7,4},{8,11},{9,10},{10,... | collective-permute-start | bytes 98312 | tf_op jit(solution)/shard_map/ppermute | solution.py:472
  41.4 0.4 collective-permute-start.17
  41.8 2.3 %collective-permute-start.18 = (bf16[128,128]{1,0:T(8,128)(2,1)S(1)}, bf16[128,128]{1,0:T(8,128)(2,1)S(1)}, u32[]{:S(2)}, u32[]{:S(2)}) collective-permute-start(bf16[128,128]{1,0:T(8,128)(2,1)S(1)} %get-tuple-element.49), channel_id=1, source_target_pairs={{0,1},{1,0},{2,3},{3,2},{4,5},{5,4},{6,7},{7,6},{8,9},{9,8},{10,11... | collective-permute-start | bytes 98312 | tf_op jit(solution)/shard_map/ppermute | solution.py:472
  44.1 0.6 %emit.2 = f32[2,32,256]{2,1,0:T(8,128)} custom-call(f32[2,32,256]{2,1,0:T(8,128)S(1)} %get-tuple-element.40.field_ref), custom_call_target="tpu_custom_call" | custom-call | flops 300000000 | bytes 1048576 | tf_op jit(solution)/shard_map/emit/pallas_call | solution.py:465
  44.7 0.7 %emit.3 = f32[1,128,256]{2,1,0:T(8,128)} custom-call(f32[1,128,256]{2,1,0:T(8,128)S(1)} %get-tuple-element.45.field_ref), custom_call_target="tpu_custom_call" | custom-call | flops 300000000 | bytes 1048576 | tf_op jit(solution)/shard_map/emit/pallas_call | solution.py:465
  45.4 0.4 collective-permute-done.16.refs_0_
  45.7 0.5 %collective-permute-done.17.refs_1_ = bf16[128,128]{1,0:T(8,128)(2,1)S(1)} collective-permute-done((bf16[128,128]{1,0:T(8,128)(2,1)S(1)}, bf16[128,128]{1,0:T(8,128)(2,1)S(1)}, u32[]{:S(2)}, u32[]{:S(2)}) %collective-permute-start.17) | collective-permute-done | bytes 32800 | tf_op jit(solution)/shard_map/ppermute | solution.py:472
  46.2 0.2 collective-permute-done.18.refs_2_
  46.4 0.9 %final.1 = f32[2,32,256]{2,1,0:T(8,128)} custom-call(bf16[128,128]{1,0:T(8,128)(2,1)S(1)} %collective-permute-done.16.refs_0_, bf16[128,128]{1,0:T(8,128)(2,1)S(1)} %collective-permute-done.17.refs_1_, bf16[128,128]{1,0:T(8,128)(2,1)S(1)} %collective-permute-done.18.refs_2_, bf16[128,128]{1,0:T(8,128)(2,1)S(1)} %get-tuple-element.50.refs_3_, ...), custom_call_target="tpu_custom_call" | custom-call | flops 1000000000 | bytes 1048576 | tf_op jit(solution)/shard_map/final/pallas_call | solution.py:621
  (3 shorter events, 0.1 us)
Async XLA Ops:
  0.6 6.6 %copy-start = (bf16[32,128,256]{2,1,0:T(8,128)(2,1)S(1)}, bf16[32,128,256]{2,1,0:T(8,128)(2,1)}, u32[]{:S(2)}) copy-start(bf16[32,128,256]{2,1,0:T(8,128)(2,1)} %traces_ref.1) | copy-start | bytes 6291460
  4.1 5.3 %collective-permute-start.2 = (bf16[256,128]{1,0:T(8,128)(2,1)S(1)}, bf16[256,128]{1,0:T(8,128)(2,1)S(1)}, u32[]{:S(2)}, u32[]{:S(2)}) collective-permute-start(bf16[256,128]{1,0:T(8,128)(2,1)S(1)} %get-tuple-element.35), channel_id=1, source_target_pairs={{0,1},{1,0},{2,3},{3,2},{4,5},{5,4},{6,7},{7,6},{8,9},{9,8},{10,11... | collective-permute-start | bytes 196616 | tf_op jit(solution)/shard_map/ppermute | solution.py:547
  7.2 9.6 %copy-start.2 = (bf16[2,4,128,256]{3,2,1,0:T(8,128)(2,1)S(1)}, bf16[2,4,128,256]{3,2,1,0:T(8,128)(2,1)}, u32[]{:S(2)}) copy-start(bf16[2,4,128,256]{3,2,1,0:T(8,128)(2,1)} %constant.23.spread_ref) | copy-start | bytes 1572868
  7.2 9.6 %copy-start.3 = (bf16[256,256]{1,0:T(8,128)(2,1)S(1)}, bf16[256,256]{1,0:T(8,128)(2,1)}, u32[]{:S(2)}) copy-start(bf16[256,256]{1,0:T(8,128)(2,1)} %constant.22.inverse_ref.refs_7_.refs_5_) | copy-start | bytes 393220
  8.9 5.0 %collective-permute-start = (bf16[256,128]{1,0:T(8,128)(2,1)S(1)}, bf16[256,128]{1,0:T(8,128)(2,1)S(1)}, u32[]{:S(2)}, u32[]{:S(2)}) collective-permute-start(bf16[256,128]{1,0:T(8,128)(2,1)S(1)} %get-tuple-element.34), channel_id=1, source_target_pairs={{0,1},{1,0},{2,3},{3,2},{4,6},{5,7},{6,4},{7,5},{8,9},{9,8},{10,11... | collective-permute-start | bytes 196616 | tf_op jit(solution)/shard_map/ppermute | solution.py:547
  9.5 7.3 %collective-permute-start.3 = (bf16[256,128]{1,0:T(8,128)(2,1)S(1)}, bf16[256,128]{1,0:T(8,128)(2,1)S(1)}, u32[]{:S(2)}, u32[]{:S(2)}) collective-permute-start(bf16[256,128]{1,0:T(8,128)(2,1)S(1)} %add_convert_fusion.3.mine_ref), channel_id=1, source_target_pairs={{0,2},{1,3},{2,0},{3,1},{4,6},{5,7},{6,4},{7,5},{8,10},{9,11},{10,... | collective-permute-start | bytes 196616 | tf_op jit(solution)/shard_map/ppermute | solution.py:547
  14.0 5.6 %collective-permute-start.1 = (bf16[256,128]{1,0:T(8,128)(2,1)S(1)}, bf16[256,128]{1,0:T(8,128)(2,1)S(1)}, u32[]{:S(2)}, u32[]{:S(2)}) collective-permute-start(bf16[256,128]{1,0:T(8,128)(2,1)S(1)} %add_convert_fusion.4.mine_ref), channel_id=1, source_target_pairs={{0,2},{1,3},{2,0},{3,1},{4,5},{5,4},{6,7},{7,6},{8,10},{9,11},{10,... | collective-permute-start | bytes 196616 | tf_op jit(solution)/shard_map/ppermute | solution.py:547
  19.5 9.9 %copy-start.1 = (s32[1,128]{1,0:T(1,128)S(1)}, s32[1,128]{1,0:T(1,128)}, u32[]{:S(2)}) copy-start(s32[1,128]{1,0:T(1,128)} %refs_5_.1) | copy-start | bytes 1540
  20.7 1.3 %collective-permute-start.4 = (bf16[256,128]{1,0:T(8,128)(2,1)S(1)}, bf16[256,128]{1,0:T(8,128)(2,1)S(1)}, u32[]{:S(2)}, u32[]{:S(2)}) collective-permute-start(bf16[256,128]{1,0:T(8,128)(2,1)S(1)} %get-tuple-element.42), channel_id=1, source_target_pairs={{0,4},{4,0},{8,12},{12,8},{16,20},{20,16},{24,28},{28,24},{1,5},{5... | collective-permute-start | bytes 196616 | tf_op jit(solution)/shard_map/ppermute | solution.py:472
  20.7 3.8 %collective-permute-start.6 = (bf16[3,256,128]{2,1,0:T(8,128)(2,1)S(1)}, bf16[3,256,128]{2,1,0:T(8,128)(2,1)S(1)}, u32[]{:S(2)}, u32[]{:S(2)}) collective-permute-start(bf16[3,256,128]{2,1,0:T(8,128)(2,1)S(1)} %get-tuple-element.43), channel_id=1, source_target_pairs={{0,4},{4,0},{8,12},{12,8},{16,20},{20,16},{24,28},{28,24},{1,5},{5... | collective-permute-start | bytes 589832 | tf_op jit(solution)/shard_map/ppermute | solution.py:472
  22.0 5.5 %collective-permute-start.5 = (bf16[256,128]{1,0:T(8,128)(2,1)S(1)}, bf16[256,128]{1,0:T(8,128)(2,1)S(1)}, u32[]{:S(2)}, u32[]{:S(2)}) collective-permute-start(bf16[256,128]{1,0:T(8,128)(2,1)S(1)} %fusion), channel_id=1, source_target_pairs={{0,24},{4,28},{8,16},{12,20},{16,8},{20,12},{24,0},{28,4},{1,25},{... | collective-permute-start | bytes 196616 | tf_op jit(solution)/shard_map/ppermute | solution.py:472
  24.6 4.3 %collective-permute-start.8 = (bf16[256,128]{1,0:T(8,128)(2,1)S(1)}, bf16[256,128]{1,0:T(8,128)(2,1)S(1)}, u32[]{:S(2)}, u32[]{:S(2)}) collective-permute-start(bf16[256,128]{1,0:T(8,128)(2,1)S(1)} %get-tuple-element.52), channel_id=1, source_target_pairs={{0,8},{4,12},{8,0},{12,4},{16,24},{20,28},{24,16},{28,20},{1,9},{5... | collective-permute-start | bytes 196616 | tf_op jit(solution)/shard_map/ppermute | solution.py:472
  25.2 4.3 %collective-permute-start.7 = (bf16[256,128]{1,0:T(8,128)(2,1)S(1)}, bf16[256,128]{1,0:T(8,128)(2,1)S(1)}, u32[]{:S(2)}, u32[]{:S(2)}) collective-permute-start(bf16[256,128]{1,0:T(8,128)(2,1)S(1)} %get-tuple-element.53), channel_id=1, source_target_pairs={{0,16},{4,20},{8,24},{12,28},{16,0},{20,4},{24,8},{28,12},{1,17},{... | collective-permute-start | bytes 196616 | tf_op jit(solution)/shard_map/ppermute | solution.py:472
  29.5 9.0 %copy-start.4 = (bf16[256,128]{1,0:T(8,128)(2,1)S(1)}, bf16[256,128]{1,0:T(8,128)(2,1)}, u32[]{:S(2)}) copy-start(bf16[256,128]{1,0:T(8,128)(2,1)} %constant.24.refs_6_) | copy-start | bytes 196612
  29.9 5.3 %collective-permute-start.14 = (bf16[16,16,128]{2,1,0:T(8,128)(2,1)S(1)}, bf16[16,16,128]{2,1,0:T(8,128)(2,1)S(1)}, u32[]{:S(2)}, u32[]{:S(2)}) collective-permute-start(bf16[16,16,128]{2,1,0:T(8,128)(2,1)S(1)} %get-tuple-element.46.refs_0_), channel_id=1, source_target_pairs={{0,24},{4,28},{8,16},{12,20},{16,8},{20,12},{24,0},{28,4},{1,25},{... | collective-permute-start | bytes 196616 | tf_op jit(solution)/shard_map/ppermute | solution.py:602
  31.5 4.4 %collective-permute-start.12 = (bf16[16,16,128]{2,1,0:T(8,128)(2,1)S(1)}, bf16[16,16,128]{2,1,0:T(8,128)(2,1)S(1)}, u32[]{:S(2)}, u32[]{:S(2)}) collective-permute-start(bf16[16,16,128]{2,1,0:T(8,128)(2,1)S(1)} %get-tuple-element.46.refs_0_), channel_id=1, source_target_pairs={{0,16},{4,12},{8,24},{12,4},{16,0},{20,28},{24,8},{28,20},{1,17},{... | collective-permute-start | bytes 196616 | tf_op jit(solution)/shard_map/ppermute | solution.py:602
  33.0 4.3 %collective-permute-start.10 = (bf16[16,16,128]{2,1,0:T(8,128)(2,1)S(1)}, bf16[16,16,128]{2,1,0:T(8,128)(2,1)S(1)}, u32[]{:S(2)}, u32[]{:S(2)}) collective-permute-start(bf16[16,16,128]{2,1,0:T(8,128)(2,1)S(1)} %get-tuple-element.46.refs_0_), channel_id=1, source_target_pairs={{0,8},{4,20},{8,0},{12,28},{16,24},{20,4},{24,16},{28,12},{1,9},{5... | collective-permute-start | bytes 196616 | tf_op jit(solution)/shard_map/ppermute | solution.py:602
  33.5 3.8 %collective-permute-start.9 = (bf16[16,16,128]{2,1,0:T(8,128)(2,1)S(1)}, bf16[16,16,128]{2,1,0:T(8,128)(2,1)S(1)}, u32[]{:S(2)}, u32[]{:S(2)}) collective-permute-start(bf16[16,16,128]{2,1,0:T(8,128)(2,1)S(1)} %get-tuple-element.46.refs_0_), channel_id=1, source_target_pairs={{0,4},{4,0},{8,12},{12,8},{16,20},{20,16},{24,28},{28,24},{1,5},{5... | collective-permute-start | bytes 196616 | tf_op jit(solution)/shard_map/ppermute | solution.py:472
  35.2 2.1 %collective-permute-start.15 = (bf16[16,16,128]{2,1,0:T(8,128)(2,1)S(1)}, bf16[16,16,128]{2,1,0:T(8,128)(2,1)S(1)}, u32[]{:S(2)}, u32[]{:S(2)}) collective-permute-start(bf16[16,16,128]{2,1,0:T(8,128)(2,1)S(1)} %collective-permute-done.14.refs_3_), channel_id=1, source_target_pairs={{0,4},{4,0},{8,12},{12,8},{16,20},{20,16},{24,28},{28,24},{1,5},{5... | collective-permute-start | bytes 196616 | tf_op jit(solution)/shard_map/ppermute | solution.py:472
  35.9 1.4 %collective-permute-start.13 = (bf16[16,16,128]{2,1,0:T(8,128)(2,1)S(1)}, bf16[16,16,128]{2,1,0:T(8,128)(2,1)S(1)}, u32[]{:S(2)}, u32[]{:S(2)}) collective-permute-start(bf16[16,16,128]{2,1,0:T(8,128)(2,1)S(1)} %collective-permute-done.12.refs_2_), channel_id=1, source_target_pairs={{0,4},{4,0},{8,12},{12,8},{16,20},{20,16},{24,28},{28,24},{1,5},{5... | collective-permute-start | bytes 196616 | tf_op jit(solution)/shard_map/ppermute | solution.py:472
  37.2 1.3 %collective-permute-start.11 = (bf16[16,16,128]{2,1,0:T(8,128)(2,1)S(1)}, bf16[16,16,128]{2,1,0:T(8,128)(2,1)S(1)}, u32[]{:S(2)}, u32[]{:S(2)}) collective-permute-start(bf16[16,16,128]{2,1,0:T(8,128)(2,1)S(1)} %collective-permute-done.10.refs_1_), channel_id=1, source_target_pairs={{0,4},{4,0},{8,12},{12,8},{16,20},{20,16},{24,28},{28,24},{1,5},{5... | collective-permute-start | bytes 196616 | tf_op jit(solution)/shard_map/ppermute | solution.py:472
  39.6 6.1 %collective-permute-start.16 = (bf16[128,128]{1,0:T(8,128)(2,1)S(1)}, bf16[128,128]{1,0:T(8,128)(2,1)S(1)}, u32[]{:S(2)}, u32[]{:S(2)}) collective-permute-start(bf16[128,128]{1,0:T(8,128)(2,1)S(1)} %get-tuple-element.47), channel_id=1, source_target_pairs={{0,3},{1,2},{2,1},{3,0},{4,7},{5,6},{6,5},{7,4},{8,11},{9,10},{10,... | collective-permute-start | bytes 98312 | tf_op jit(solution)/shard_map/ppermute | solution.py:472
  41.4 4.9 %collective-permute-start.17 = (bf16[128,128]{1,0:T(8,128)(2,1)S(1)}, bf16[128,128]{1,0:T(8,128)(2,1)S(1)}, u32[]{:S(2)}, u32[]{:S(2)}) collective-permute-start(bf16[128,128]{1,0:T(8,128)(2,1)S(1)} %get-tuple-element.48), channel_id=1, source_target_pairs={{0,2},{1,3},{2,0},{3,1},{4,6},{5,7},{6,4},{7,5},{8,10},{9,11},{10,... | collective-permute-start | bytes 98312 | tf_op jit(solution)/shard_map/ppermute | solution.py:472
  41.8 4.6 %collective-permute-start.18 = (bf16[128,128]{1,0:T(8,128)(2,1)S(1)}, bf16[128,128]{1,0:T(8,128)(2,1)S(1)}, u32[]{:S(2)}, u32[]{:S(2)}) collective-permute-start(bf16[128,128]{1,0:T(8,128)(2,1)S(1)} %get-tuple-element.49), channel_id=1, source_target_pairs={{0,1},{1,0},{2,3},{3,2},{4,5},{5,4},{6,7},{7,6},{8,9},{9,8},{10,11... | collective-permute-start | bytes 98312 | tf_op jit(solution)/shard_map/ppermute | solution.py:472
